TPU v7x, 32 devices: a whole 2x2x4 slice. The times are simulated.
32 devices in a mesh: dp: 8 (over z, core), seq: 4 (over y, x).
Axes of the slice: x: 2, y: 2, z: 4, core: 2. Of those that a mesh axis runs over, the one named last changes fastest.
Arguments:
- hidden_in: bfloat16 [2, 8, 2048, 1024], P(None, 'dp', 'seq'), may hold values from -6 to 6
- encoder_states: bfloat16 [2, 8, 512, 1024], P(None, 'dp', 'seq'), may hold values from -6 to 6
- segments: int32 [2, 8, 2048], P(None, 'dp', 'seq'), may hold values from 0 to 14, never falling along the last dimension, each value on 1 to 1280 neighbouring positions
- enc_segments: int32 [2, 8, 512], P(None, 'dp', 'seq'), may hold values from 0 to 14, never falling along the last dimension, each value on 1 to 256 neighbouring positions
- grad_out: bfloat16 [2, 8, 2048, 1024], P(None, 'dp', 'seq'), may hold values from -6 to 6
- norm_self: bfloat16 [1024], P(('dp', 'seq')), may hold values from 0.5 to 1.5
- q_self: bfloat16 [1024, 1024], P(('dp', 'seq')), may hold values from -0.046875 to 0.046875
- k_self: bfloat16 [1024, 1024], P(('dp', 'seq')), may hold values from -0.1875 to 0.1875
- v_self: bfloat16 [1024, 1024], P(('dp', 'seq')), may hold values from -0.1875 to 0.1875
- o_self: bfloat16 [1024, 1024], P(('dp', 'seq')), may hold values from -0.75 to 0.75
- rel_bias: bfloat16 [512], P(('dp', 'seq')), may hold values from -4 to 4
- norm_cross: bfloat16 [1024], P(('dp', 'seq')), may hold values from 0.5 to 1.5
- q_cross: bfloat16 [1024, 1024], P(('dp', 'seq')), may hold values from -0.046875 to 0.046875
- k_cross: bfloat16 [1024, 1024], P(('dp', 'seq')), may hold values from -0.1875 to 0.1875
- v_cross: bfloat16 [1024, 1024], P(('dp', 'seq')), may hold values from -0.1875 to 0.1875
- o_cross: bfloat16 [1024, 1024], P(('dp', 'seq')), may hold values from -0.75 to 0.75
- norm_ff: bfloat16 [1024], P(('dp', 'seq')), may hold values from 0.5 to 1.5
- wi_gate: bfloat16 [1024, 2816], P(('dp', 'seq')), may hold values from -0.1875 to 0.1875
- wi_up: bfloat16 [1024, 2816], P(('dp', 'seq')), may hold values from -0.1875 to 0.1875
- wo_ff: bfloat16 [2816, 1024], P(('dp', 'seq')), may hold values from -0.109375 to 0.109375
Outputs:
- block_out: bfloat16 [2, 8, 2048, 1024], P(None, 'dp', 'seq')
- grad_hidden_in: float32 [2, 8, 2048, 1024], P(None, 'dp', 'seq')
- grad_encoder: float32 [2, 8, 512, 1024], P(None, 'dp', 'seq')
- grad_norm_self: float32 [1024], P(('dp', 'seq'))
- grad_q_self: float32 [1024, 1024], P(('dp', 'seq'))
- grad_k_self: float32 [1024, 1024], P(('dp', 'seq'))
- grad_v_self: float32 [1024, 1024], P(('dp', 'seq'))
- grad_o_self: float32 [1024, 1024], P(('dp', 'seq'))
- grad_rel_bias: float32 [512], P(('dp', 'seq'))
- grad_norm_cross: float32 [1024], P(('dp', 'seq'))
- grad_q_cross: float32 [1024, 1024], P(('dp', 'seq'))
- grad_k_cross: float32 [1024, 1024], P(('dp', 'seq'))
- grad_v_cross: float32 [1024, 1024], P(('dp', 'seq'))
- grad_o_cross: float32 [1024, 1024], P(('dp', 'seq'))
- grad_norm_ff: float32 [1024], P(('dp', 'seq'))
- grad_wi_gate: float32 [1024, 2816], P(('dp', 'seq'))
- grad_wi_up: float32 [1024, 2816], P(('dp', 'seq'))
- grad_wo_ff: float32 [2816, 1024], P(('dp', 'seq'))
Inputs may be any that keep to these rules, and one draw needn't show every extreme that they name: `segments`: within each sequence the document numbers never fall; every number from 0 to 14 appears, one document has exactly 1280 tokens. `enc_segments`: within each sequence the numbers never fall and every document of the sequence has at least one encoder state; one has exactly 256.
All inputs are finite; a program needn't handle non-finite values.
Results may differ from a plain program's by a relative error of at most 0.023.
The roundings to bfloat16 on the way count: a program that leaves them out, or rounds other values in their place, can miss the bound.
Values may be sent and summed in bfloat16 or wider, within the bound.
A program may use at most 512 MiB of HBM per device.

v0:
```python
import math

import jax
import jax.numpy as jnp
from jax import lax
from jax.sharding import PartitionSpec as P

HEADS = 16
HEAD_DIM = 64
BUCKETS = 32
MAX_DIST = 128


EPS = 1e-06
NEG = -1e30


def norm_rows(value, gain):
    return value * lax.rsqrt(jnp.mean(value * value, axis=-1, keepdims=True) + EPS) * gain


def bucket_edges():
    half = BUCKETS // 2
    return [math.ceil(half * (MAX_DIST / half) ** (step / half)) for step in range(1, half)]


def buckets_of(distance):
    half = BUCKETS // 2
    far = half + sum(((distance >= edge).astype(jnp.int32) for edge in bucket_edges()))
    return jnp.where(distance < half, distance, far)


def by_heads(values):
    return values.reshape(values.shape[0], values.shape[1], HEADS, HEAD_DIM)


def join_heads(values):
    return values.reshape(values.shape[0], values.shape[1], HEADS * HEAD_DIM)


def project(rows, weight_matrix):
    return jnp.dot(rows, weight_matrix, preferred_element_type=jnp.float32)


def project_back(grads, weight_matrix):
    return jnp.einsum("stn,kn->stk", grads, weight_matrix, preferred_element_type=jnp.float32)


def weight_grad(rows, grads):
    return jnp.einsum("stk,stn->kn", rows, grads, preferred_element_type=jnp.float32)


def gelu_mix(gate, up_values):
    return jax.nn.gelu(gate, approximate=True) * up_values


def scores_of(q_rows, keys, bias, allowed):
    scores = jnp.einsum("sqhd,skhd->shqk", q_rows, keys, preferred_element_type=jnp.float32) + bias
    return jnp.where(allowed[:, None], scores, NEG)


def attend(q_rows, keys, values, bias, allowed):
    scores = scores_of(q_rows, keys, bias, allowed)
    largest = jnp.max(scores, axis=-1, keepdims=True)
    raised = jnp.exp(scores - largest)
    total = jnp.sum(raised, axis=-1, keepdims=True)
    probs = raised / total
    mixed = jnp.einsum(
        "shqk,skhd->sqhd", probs.astype(jnp.bfloat16), values, preferred_element_type=jnp.float32
    )
    return (join_heads(mixed).astype(jnp.bfloat16), largest + jnp.log(total))


def attend_back(q_rows, keys, values, bias, allowed, log_total, grad_mixed):
    scores = scores_of(q_rows, keys, bias, allowed)
    probs = jnp.exp(scores - log_total)
    grad_probs = jnp.einsum(
        "sqhd,skhd->shqk", grad_mixed, values, preferred_element_type=jnp.float32
    )
    inner = jnp.sum(probs * grad_probs, axis=-1, keepdims=True)
    grad_scores = (probs * (grad_probs - inner)).astype(jnp.bfloat16)
    grad_query = jnp.einsum(
        "shqk,skhd->sqhd", grad_scores, keys, preferred_element_type=jnp.float32
    )
    grad_keys = jnp.einsum(
        "shqk,sqhd->skhd", grad_scores, q_rows, preferred_element_type=jnp.float32
    )
    grad_values = jnp.einsum(
        "shqk,sqhd->skhd",
        probs.astype(jnp.bfloat16),
        grad_mixed,
        preferred_element_type=jnp.float32,
    )
    return (join_heads(grad_query), join_heads(grad_keys), join_heads(grad_values), grad_scores)


def body(
    hidden_in,
    encoder_states,
    segments,
    enc_segments,
    grad_out,
    norm_self,
    q_self,
    k_self,
    v_self,
    o_self,
    rel_bias,
    norm_cross,
    q_cross,
    k_cross,
    v_cross,
    o_cross,
    norm_ff,
    wi_gate,
    wi_up,
    wo_ff,
):
    shards = (
        norm_self,
        q_self,
        k_self,
        v_self,
        o_self,
        rel_bias,
        norm_cross,
        q_cross,
        k_cross,
        v_cross,
        o_cross,
        norm_ff,
        wi_gate,
        wi_up,
        wo_ff,
    )
    micro_count = hidden_in.shape[0]
    rows_dev = hidden_in.shape[2]
    seg_whole, enc_seg_whole = (
        lax.all_gather(segments, "seq", axis=2, tiled=True),
        lax.all_gather(enc_segments, "seq", axis=2, tiled=True),
    )
    length = seg_whole.shape[2]
    positions = lax.axis_index("seq") * rows_dev + jnp.arange(rows_dev, dtype=jnp.int32)
    columns = jnp.arange(length, dtype=jnp.int32)
    distance = jnp.maximum(positions[:, None] - columns[None, :], 0)
    bucket_indicator = (
        buckets_of(distance)[None] == jnp.arange(BUCKETS, dtype=jnp.int32)[:, None, None]
    ).astype(jnp.bfloat16)
    causal = columns[None, :] <= positions[:, None]
    grad_shards = tuple((jnp.zeros(piece.shape, jnp.float32) for piece in shards))
    outputs, grad_inputs, grad_encoders = ([], [], [])
    for micro in range(micro_count):
        params = (
            lax.all_gather(shards[0], ("dp", "seq"), axis=0, tiled=True),
            lax.all_gather(shards[1], ("dp", "seq"), axis=0, tiled=True),
            lax.all_gather(shards[2], ("dp", "seq"), axis=0, tiled=True),
            lax.all_gather(shards[3], ("dp", "seq"), axis=0, tiled=True),
            lax.all_gather(shards[4], ("dp", "seq"), axis=0, tiled=True),
            lax.all_gather(shards[5], ("dp", "seq"), axis=0, tiled=True),
            lax.all_gather(shards[6], ("dp", "seq"), axis=0, tiled=True),
            lax.all_gather(shards[7], ("dp", "seq"), axis=0, tiled=True),
            lax.all_gather(shards[8], ("dp", "seq"), axis=0, tiled=True),
            lax.all_gather(shards[9], ("dp", "seq"), axis=0, tiled=True),
            lax.all_gather(shards[10], ("dp", "seq"), axis=0, tiled=True),
            lax.all_gather(shards[11], ("dp", "seq"), axis=0, tiled=True),
            lax.all_gather(shards[12], ("dp", "seq"), axis=0, tiled=True),
            lax.all_gather(shards[13], ("dp", "seq"), axis=0, tiled=True),
            lax.all_gather(shards[14], ("dp", "seq"), axis=0, tiled=True),
        )
        (
            gain_self,
            wq,
            wk,
            wv,
            wo,
            table_flat,
            gain_cross,
            cq,
            ck,
            cv,
            co,
            gain_ff,
            w_gate,
            w_up,
            w_down,
        ) = params
        bias = jnp.einsum(
            "pia,pw->wia",
            bucket_indicator,
            table_flat.reshape(BUCKETS, HEADS),
            preferred_element_type=jnp.float32,
        )
        inputs = hidden_in[micro].astype(jnp.float32)
        encoder = encoder_states[micro]
        seg_own = segments[micro]
        self_allowed = (seg_own[:, :, None] == seg_whole[micro][:, None, :]) & causal[None]
        cross_allowed = seg_own[:, :, None] == enc_seg_whole[micro][:, None, :]
        self_norm_scale = gain_self.astype(jnp.float32)
        cross_gain = gain_cross.astype(jnp.float32)
        ff_gain = gain_ff.astype(jnp.float32)
        normed_self = norm_rows(inputs, self_norm_scale).astype(jnp.bfloat16)
        query = project(normed_self, wq).astype(jnp.bfloat16)
        key_own = project(normed_self, wk).astype(jnp.bfloat16)
        value_own = project(normed_self, wv).astype(jnp.bfloat16)
        cross_key_own = project(encoder, ck).astype(jnp.bfloat16)
        cross_value_own = project(encoder, cv).astype(jnp.bfloat16)
        keys, values, cross_keys, cross_values = (
            lax.all_gather(key_own, "seq", axis=1, tiled=True),
            lax.all_gather(value_own, "seq", axis=1, tiled=True),
            lax.all_gather(cross_key_own, "seq", axis=1, tiled=True),
            lax.all_gather(cross_value_own, "seq", axis=1, tiled=True),
        )
        mixed, self_log_normalizer = attend(
            by_heads(query), by_heads(keys), by_heads(values), bias, self_allowed
        )
        after_self = inputs + project(mixed, wo)
        normed_cross = norm_rows(after_self, cross_gain).astype(jnp.bfloat16)
        cross_query = project(normed_cross, cq).astype(jnp.bfloat16)
        cross_mixed, cross_log = attend(
            by_heads(cross_query), by_heads(cross_keys), by_heads(cross_values), 0.0, cross_allowed
        )
        after_cross = after_self + project(cross_mixed, co)
        normed_ff = norm_rows(after_cross, ff_gain).astype(jnp.bfloat16)
        gate = project(normed_ff, w_gate)
        up_values = project(normed_ff, w_up)
        hidden = gelu_mix(gate, up_values).astype(jnp.bfloat16)
        result = after_cross + project(hidden, w_down)
        outputs.append(result.astype(jnp.bfloat16))
        params = (
            lax.all_gather(shards[0], ("dp", "seq"), axis=0, tiled=True),
            lax.all_gather(shards[1], ("dp", "seq"), axis=0, tiled=True),
            lax.all_gather(shards[2], ("dp", "seq"), axis=0, tiled=True),
            lax.all_gather(shards[3], ("dp", "seq"), axis=0, tiled=True),
            lax.all_gather(shards[4], ("dp", "seq"), axis=0, tiled=True),
            lax.all_gather(shards[5], ("dp", "seq"), axis=0, tiled=True),
            lax.all_gather(shards[6], ("dp", "seq"), axis=0, tiled=True),
            lax.all_gather(shards[7], ("dp", "seq"), axis=0, tiled=True),
            lax.all_gather(shards[8], ("dp", "seq"), axis=0, tiled=True),
            lax.all_gather(shards[9], ("dp", "seq"), axis=0, tiled=True),
            lax.all_gather(shards[10], ("dp", "seq"), axis=0, tiled=True),
            lax.all_gather(shards[11], ("dp", "seq"), axis=0, tiled=True),
            lax.all_gather(shards[12], ("dp", "seq"), axis=0, tiled=True),
            lax.all_gather(shards[13], ("dp", "seq"), axis=0, tiled=True),
            lax.all_gather(shards[14], ("dp", "seq"), axis=0, tiled=True),
        )
        (
            gain_self,
            wq,
            wk,
            wv,
            wo,
            table_flat,
            gain_cross,
            cq,
            ck,
            cv,
            co,
            gain_ff,
            w_gate,
            w_up,
            w_down,
        ) = params
        grad_result = grad_out[micro].astype(jnp.float32)
        out_low = grad_out[micro]
        grad_w_down = weight_grad(hidden, out_low)
        grad_hidden = project_back(out_low, w_down)
        mix_value, mix_pull = jax.vjp(gelu_mix, gate, up_values)
        grad_gate, grad_up = mix_pull(grad_hidden)
        grad_gate = grad_gate.astype(jnp.bfloat16)
        grad_up = grad_up.astype(jnp.bfloat16)
        gate_weight_gradient = weight_grad(normed_ff, grad_gate)
        grad_w_up = weight_grad(normed_ff, grad_up)
        grad_normed_ff = project_back(grad_gate, w_gate) + project_back(grad_up, w_up)
        norm_value, norm_pull = jax.vjp(norm_rows, after_cross, ff_gain)
        ff_part, grad_gain_ff = norm_pull(grad_normed_ff)
        grad_after_cross = grad_result + ff_part
        cross_out_low = grad_after_cross.astype(jnp.bfloat16)
        grad_co = weight_grad(cross_mixed, cross_out_low)
        grad_cross_mixed = project_back(cross_out_low, co).astype(jnp.bfloat16)
        grad_cross_query, cross_key_terms, cross_value_terms, cross_scores = attend_back(
            by_heads(cross_query),
            by_heads(cross_keys),
            by_heads(cross_values),
            0.0,
            cross_allowed,
            cross_log,
            by_heads(grad_cross_mixed),
        )
        grad_cross_key, grad_cross_value = (
            lax.psum_scatter(
                cross_key_terms.astype(jnp.bfloat16), "seq", scatter_dimension=1, tiled=True
            ).astype(jnp.float32),
            lax.psum_scatter(
                cross_value_terms.astype(jnp.bfloat16), "seq", scatter_dimension=1, tiled=True
            ).astype(jnp.float32),
        )
        grad_cross_key = grad_cross_key.astype(jnp.bfloat16)
        grad_cross_value = grad_cross_value.astype(jnp.bfloat16)
        cross_key_gradient = weight_grad(encoder, grad_cross_key)
        grad_cv = weight_grad(encoder, grad_cross_value)
        grad_encoders.append(project_back(grad_cross_key, ck) + project_back(grad_cross_value, cv))
        grad_cross_query = grad_cross_query.astype(jnp.bfloat16)
        grad_cq = weight_grad(normed_cross, grad_cross_query)
        grad_normed_cross = project_back(grad_cross_query, cq)
        norm_value, norm_pull = jax.vjp(norm_rows, after_self, cross_gain)
        cross_part, grad_gain_cross = norm_pull(grad_normed_cross)
        grad_after_self = grad_after_cross + cross_part
        self_out_low = grad_after_self.astype(jnp.bfloat16)
        grad_wo = weight_grad(mixed, self_out_low)
        grad_mixed = project_back(self_out_low, wo).astype(jnp.bfloat16)
        grad_query, key_terms, value_terms, self_attention_logits = attend_back(
            by_heads(query),
            by_heads(keys),
            by_heads(values),
            bias,
            self_allowed,
            self_log_normalizer,
            by_heads(grad_mixed),
        )
        grad_table = jnp.einsum(
            "dcma,uma->uc",
            self_attention_logits,
            bucket_indicator,
            preferred_element_type=jnp.float32,
        ).reshape(-1)
        grad_key, grad_value = (
            lax.psum_scatter(
                key_terms.astype(jnp.bfloat16), "seq", scatter_dimension=1, tiled=True
            ).astype(jnp.float32),
            lax.psum_scatter(
                value_terms.astype(jnp.bfloat16), "seq", scatter_dimension=1, tiled=True
            ).astype(jnp.float32),
        )
        grad_key = grad_key.astype(jnp.bfloat16)
        grad_value = grad_value.astype(jnp.bfloat16)
        grad_query = grad_query.astype(jnp.bfloat16)
        grad_wq = weight_grad(normed_self, grad_query)
        grad_wk = weight_grad(normed_self, grad_key)
        grad_wv = weight_grad(normed_self, grad_value)
        grad_normed_self = (
            project_back(grad_query, wq) + project_back(grad_key, wk) + project_back(grad_value, wv)
        )
        norm_value, norm_pull = jax.vjp(norm_rows, inputs, self_norm_scale)
        self_part, grad_gain_self = norm_pull(grad_normed_self)
        grad_inputs.append(grad_after_self + self_part)
        local = (
            grad_gain_self,
            grad_wq,
            grad_wk,
            grad_wv,
            grad_wo,
            grad_table,
            grad_gain_cross,
            grad_cq,
            cross_key_gradient,
            grad_cv,
            grad_co,
            grad_gain_ff,
            gate_weight_gradient,
            grad_w_up,
            grad_w_down,
        )
        summed = (
            lax.psum_scatter(local[0], ("dp", "seq"), scatter_dimension=0, tiled=True),
            lax.psum_scatter(local[1], ("dp", "seq"), scatter_dimension=0, tiled=True),
            lax.psum_scatter(local[2], ("dp", "seq"), scatter_dimension=0, tiled=True),
            lax.psum_scatter(local[3], ("dp", "seq"), scatter_dimension=0, tiled=True),
            lax.psum_scatter(local[4], ("dp", "seq"), scatter_dimension=0, tiled=True),
            lax.psum_scatter(local[5], ("dp", "seq"), scatter_dimension=0, tiled=True),
            lax.psum_scatter(local[6], ("dp", "seq"), scatter_dimension=0, tiled=True),
            lax.psum_scatter(local[7], ("dp", "seq"), scatter_dimension=0, tiled=True),
            lax.psum_scatter(local[8], ("dp", "seq"), scatter_dimension=0, tiled=True),
            lax.psum_scatter(local[9], ("dp", "seq"), scatter_dimension=0, tiled=True),
            lax.psum_scatter(local[10], ("dp", "seq"), scatter_dimension=0, tiled=True),
            lax.psum_scatter(local[11], ("dp", "seq"), scatter_dimension=0, tiled=True),
            lax.psum_scatter(local[12], ("dp", "seq"), scatter_dimension=0, tiled=True),
            lax.psum_scatter(local[13], ("dp", "seq"), scatter_dimension=0, tiled=True),
            lax.psum_scatter(local[14], ("dp", "seq"), scatter_dimension=0, tiled=True),
        )
        grad_shards = tuple((before + after for before, after in zip(grad_shards, summed)))
    return (jnp.stack(outputs), jnp.stack(grad_inputs), jnp.stack(grad_encoders)) + tuple(
        grad_shards
    )


def solution(mesh):
    return jax.shard_map(
        body,
        mesh=mesh,
        in_specs=(
            P(None, "dp", "seq", None),
            P(None, "dp", "seq", None),
            P(None, "dp", "seq"),
            P(None, "dp", "seq"),
            P(None, "dp", "seq", None),
            P(("dp", "seq")),
            P(("dp", "seq"), None),
            P(("dp", "seq"), None),
            P(("dp", "seq"), None),
            P(("dp", "seq"), None),
            P(("dp", "seq")),
            P(("dp", "seq")),
            P(("dp", "seq"), None),
            P(("dp", "seq"), None),
            P(("dp", "seq"), None),
            P(("dp", "seq"), None),
            P(("dp", "seq")),
            P(("dp", "seq"), None),
            P(("dp", "seq"), None),
            P(("dp", "seq"), None),
        ),
        out_specs=(
            P(None, "dp", "seq", None),
            P(None, "dp", "seq", None),
            P(None, "dp", "seq", None),
            P(("dp", "seq")),
            P(("dp", "seq"), None),
            P(("dp", "seq"), None),
            P(("dp", "seq"), None),
            P(("dp", "seq"), None),
            P(("dp", "seq")),
            P(("dp", "seq")),
            P(("dp", "seq"), None),
            P(("dp", "seq"), None),
            P(("dp", "seq"), None),
            P(("dp", "seq"), None),
            P(("dp", "seq")),
            P(("dp", "seq"), None),
            P(("dp", "seq"), None),
            P(("dp", "seq"), None),
        ),
        check_vma=False,
    )
```

profile of v0, /device:TPU:0, one launch (start us, length us, event | category | flops | bytes accessed | tf_op | source)
XLA Modules:
  0.0 3477.2 jit_solution(10703589672805040410)
XLA Ops:
  10.6 59.4 %all-gather.36.cloned.1.call-done = bf16[1024,1024]{1,0:T(8,128)(2,1)} async-done(((bf16[32,1024]{1,0:T(8,128)(2,1)}), bf16[1024,1024]{1,0:T(8,128)(2,1)}) %all-gather.36.cloned.1.call-update) | async-done | bytes 2097168 | tf_op jit(solution)/shard_map/all_gather | solution.py:163
  76.1 52.1 %all-gather.40.cloned.1.call-done = bf16[1024,1024]{1,0:T(8,128)(2,1)} async-done(((bf16[32,1024]{1,0:T(8,128)(2,1)}), bf16[1024,1024]{1,0:T(8,128)(2,1)}) %all-gather.40.cloned.1.call-update) | async-done | bytes 2097168 | tf_op jit(solution)/shard_map/all_gather | solution.py:162
  134.8 38.6 %all-reduce.9 = (bf16[1024]{0:T(1024)(128)(2,1)S(1)}, bf16[512]{0:T(512)(128)(2,1)S(1)}, bf16[1024]{0:T(1024)(128)(2,1)S(1)}, bf16[1024]{0:T(1024)(128)(2,1)S(1)}) all-reduce(bf16[1024]{0:T(1024)(128)(2,1)S(1)} %dynamic-update-slice, bf16[512]{0:T(512)(128)(2,1)S(1)} %dynamic-update-slice.1, ...), channel_id=1, replica_groups=mesh['dp'=8,'seq'=4] {'dp','seq'}, use_global_device_ids=true, to_apply=%add | all-reduce | flops 3584 | bytes 14336
  174.0 12.4 all-gather.32.cloned.1.call-done
  190.3 54.0 %all-gather.28.cloned.1.call-done = bf16[1024,1024]{1,0:T(8,128)(2,1)} async-done(((bf16[32,1024]{1,0:T(8,128)(2,1)}), bf16[1024,1024]{1,0:T(8,128)(2,1)}) %all-gather.28.cloned.1.call-update) | async-done | bytes 2097168 | tf_op jit(solution)/shard_map/all_gather | solution.py:157
  260.2 8.0 all_gather.53
  269.4 7.2 all_gather.61
  276.7 8.3 compare_select_fusion
  290.3 25.0 iota_compare_fusion
  315.3 177.7 %copy.125 = pred[32,512,2048]{2,0,1:T(32,128)(4,1)} copy(pred[32,512,2048]{1,0,2:T(32,128)(4,1)} %iota_compare_fusion) | data formatting | bytes 67108864 | tf_op jit(solution)/shard_map/eq | solution.py:147
  497.7 36.0 %fusion.181 = f32[16,512,2048]{2,0,1:T(8,128)} fusion(pred[32,512,2048]{2,0,1:T(32,128)(4,1)} %copy.125, bf16[32,16]{1,0:T(8,128)(2,1)S(1)} %reshape.1708), kind=kOutput, calls=%fused_computation.297 | convolution fusion | flops 1073741824 | bytes 100664320 | tf_op jit(solution)/shard_map/pia,pw->wia/dot_general | solution.py:187
  561.6 73.7 %fusion.210 = (f32[16,512]{1,0:T(8,128)S(1)}, f32[16,512,2048]{2,1,0:T(8,128)}) fusion(f32[16,512,2048]{2,0,1:T(8,128)} %fusion.181, bf16[512,16,64]{0,2,1:T(8,128)(2,1)} %bitcast.438, bf16[2048,16,64]{0,2,1:T(8,128)(2,1)} %bitcast.416, pred[512,2048]{1,0:T(8,128)(4,1)S(1)} %get-tuple-element.118), kind=kOutput, calls=%fused_computation.327 | convolution fusion | flops 2197807104 | bytes 140541952 | tf_op jit(solution)/shard_map/sqhd,skhd->shqk/dot_general | solution.py:58
  635.4 22.3 fusion.5
  664.2 25.6 fusion.109
  699.3 6.7 copy.122
  706.0 67.1 %fusion.211 = (f32[16,512]{1,0:T(8,128)S(1)}, f32[16,512,2048]{2,1,0:T(8,128)}) fusion(f32[16,512,2048]{2,0,1:T(8,128)} %fusion.181, bf16[512,16,64]{0,2,1:T(8,128)(2,1)S(1)} %bitcast.440, bf16[2048,16,64]{0,2,1:T(8,128)(2,1)} %bitcast.418, pred[512,2048]{1,0:T(8,128)(4,1)S(1)} %copy-done), kind=kOutput, calls=%fused_computation.328 | convolution fusion | flops 2197807104 | bytes 140541952 | tf_op jit(solution)/shard_map/sqhd,skhd->shqk/dot_general | solution.py:58
  773.1 21.3 fusion.4
  801.1 25.6 fusion.110
  835.0 9.6 select_reduce_fusion.1
  844.6 8.8 fusion.16
  853.4 10.0 fusion.102
  868.2 8.3 select_reduce_fusion
  876.5 8.9 fusion.17
  886.1 8.4 fusion.101
  898.9 7.9 fusion.213
  906.7 41.2 %all-gather.44.cloned.1.call-done = bf16[1024,2816]{1,0:T(8,128)(2,1)} async-done(((bf16[32,2816]{1,0:T(8,128)(2,1)}), bf16[1024,2816]{1,0:T(8,128)(2,1)}) %all-gather.44.cloned.1.call-update) | async-done | bytes 5767184 | tf_op jit(solution)/shard_map/all_gather | solution.py:166
  947.9 7.8 fusion.212
  955.7 61.4 %all-gather.48.cloned.1.call-done = bf16[2816,1024]{1,0:T(8,128)(2,1)} async-done(((bf16[88,1024]{1,0:T(8,128)(2,1)}), bf16[2816,1024]{1,0:T(8,128)(2,1)}) %all-gather.48.cloned.1.call-update) | async-done | bytes 5767184 | tf_op jit(solution)/shard_map/all_gather | solution.py:168
  1017.1 13.8 multiply_convert_fusion.5
  1053.6 11.7 multiply_convert_fusion.4
  1065.3 7.3 fusion.218
  1086.2 10.8 fusion.106
  1097.1 11.7 multiply_reduce_fusion.2
  1113.5 10.7 fusion.103
  1133.3 12.8 multiply_convert_fusion.2
  1171.9 11.5 multiply_reduce_fusion.3
  1183.4 12.5 multiply_convert_fusion.3
  1211.5 7.0 convolution_convert_fusion.3
  1224.6 26.0 fusion.63
  1257.7 25.8 fusion.66
  1283.6 46.7 %multiply_reduce_fusion.1 = (f32[16,512]{1,0:T(8,128)S(1)}, f32[16,512,2048]{2,1,0:T(8,128)}) fusion(f32[16,512,2048]{2,1,0:T(8,128)} %get-tuple-element.126, f32[16,512]{1,0:T(8,128)S(1)} %copy-done.84, bf16[512,16,64]{0,2,1:T(8,128)(2,1)S(1)} %bitcast.435, bf16[2048,16,64]{0,2,1:T(8,128)(2,1)} %bitcast.423), kind=kOutput, calls=%fused_computation.7 | convolution fusion | flops 2197807104 | bytes 139526144 | tf_op jit(solution)/shard_map/sqhd,skhd->shqk/dot_general | solution.py:77
  1330.2 55.4 %multiply_convert_fusion.1 = bf16[16,512,2048]{2,1,0:T(8,128)(2,1)} fusion(f32[16,512,2048]{2,1,0:T(8,128)} %get-tuple-element.143, f32[16,512,2048]{2,1,0:T(8,128)} %get-tuple-element.126, f32[16,512]{1,0:T(8,128)S(1)} %get-tuple-element.142, f32[16,512]{1,0:T(8,128)S(1)} %copy-done.84), kind=kLoop, calls=%fused_computation.6 | loop fusion | flops 67108864 | bytes 167837696 | tf_op jit(solution)/shard_map/convert_element_type | solution.py:81
  1385.7 18.5 convolution_convert_fusion.1
  1404.4 47.0 %multiply_reduce_fusion = (f32[16,512]{1,0:T(8,128)S(1)}, f32[16,512,2048]{2,1,0:T(8,128)}) fusion(f32[16,512,2048]{2,1,0:T(8,128)} %get-tuple-element.120, f32[16,512]{1,0:T(8,128)S(1)} %log_add_fusion, bf16[512,16,64]{0,2,1:T(8,128)(2,1)S(1)} %bitcast.437, bf16[2048,16,64]{0,2,1:T(8,128)(2,1)} %bitcast.421), kind=kOutput, calls=%fused_computation.4 | convolution fusion | flops 2197807104 | bytes 139526144 | tf_op jit(solution)/shard_map/sqhd,skhd->shqk/dot_general | solution.py:77
  1451.4 53.3 %multiply_convert_fusion = bf16[16,512,2048]{2,1,0:T(8,128)(2,1)} fusion(f32[16,512,2048]{2,1,0:T(8,128)} %get-tuple-element.145, f32[16,512,2048]{2,1,0:T(8,128)} %get-tuple-element.120, f32[16,512]{1,0:T(8,128)S(1)} %get-tuple-element.144, f32[16,512]{1,0:T(8,128)S(1)} %log_add_fusion), kind=kLoop, calls=%fused_computation.3 | loop fusion | flops 67108864 | bytes 167837696 | tf_op jit(solution)/shard_map/convert_element_type | solution.py:81
  1504.7 18.5 convolution_convert_fusion
  1544.9 17.4 convolution_convert_fusion.6
  1566.8 17.3 convolution_convert_fusion.4
  1670.9 6.7 convolution_add_fusion.1
  1677.6 46.5 %copy.150 = bf16[16,512,2048]{1,0,2:T(8,128)(2,1)} copy(bf16[16,512,2048]{2,1,0:T(8,128)(2,1)} %multiply_convert_fusion) | data formatting | bytes 67108864 | tf_op jit(solution)/shard_map/convert_element_type | solution.py:81
  1724.1 46.6 %copy.149 = bf16[16,512,2048]{1,0,2:T(8,128)(2,1)} copy(bf16[16,512,2048]{2,1,0:T(8,128)(2,1)} %multiply_convert_fusion.1) | data formatting | bytes 67108864 | tf_op jit(solution)/shard_map/convert_element_type | solution.py:81
  1770.7 23.4 fusion.115
  1794.2 24.6 fusion.117
  1819.0 7.4 fusion.111
  1850.0 40.0 %all-reduce.8 = (f32[1024]{0:T(1024)S(1)}, f32[512]{0:T(512)S(1)}, f32[1024]{0:T(1024)S(1)}, f32[1024]{0:T(1024)S(1)}) all-reduce(f32[1024]{0:T(1024)S(1)} %add.520, f32[512]{0:T(512)S(1)} %reshape.1752, f32[1024]{0:T(1024)S(1)} %add.526, f32[1024]{0:T(1024)S(1)} %add.531), channel_id=33, replica_groups=mesh['dp'=8,'seq'=4] {'dp','seq'}, use_global_device_ids=true, to_apply=%region_33.34.clone | all-reduce | flops 3584 | bytes 28672
  1898.8 105.9 %reduce-scatter.46.cloned.1.call-done = f32[32,1024]{1,0:T(8,128)} async-done(((f32[1024,1024]{1,0:T(8,128)}), f32[32,1024]{1,0:T(8,128)}) %reduce-scatter.46.cloned.1.call-update) | async-done | bytes 131088 | tf_op jit(solution)/shard_map/reduce_scatter | solution.py:368
  2004.7 142.1 %reduce-scatter.40.cloned.1.call-done = f32[32,1024]{1,0:T(8,128)} async-done(((f32[1024,1024]{1,0:T(8,128)}), f32[32,1024]{1,0:T(8,128)}) %reduce-scatter.40.cloned.1.call-update) | async-done | bytes 131088 | tf_op jit(solution)/shard_map/reduce_scatter | solution.py:365
  2146.8 142.2 %reduce-scatter.68.cloned.1.call-done = f32[32,1024]{1,0:T(8,128)} async-done(((f32[1024,1024]{1,0:T(8,128)}), f32[32,1024]{1,0:T(8,128)}) %reduce-scatter.68.cloned.1.call-update) | async-done | bytes 131088
  2288.9 141.8 %reduce-scatter.66.cloned.1.call-done = f32[32,1024]{1,0:T(8,128)} async-done(((f32[1024,1024]{1,0:T(8,128)}), f32[32,1024]{1,0:T(8,128)}) %reduce-scatter.66.cloned.1.call-update) | async-done | bytes 131088
  2430.7 142.6 %reduce-scatter.44.cloned.1.call-done = f32[32,1024]{1,0:T(8,128)} async-done(((f32[1024,1024]{1,0:T(8,128)}), f32[32,1024]{1,0:T(8,128)}) %reduce-scatter.44.cloned.1.call-update) | async-done | bytes 131088 | tf_op jit(solution)/shard_map/reduce_scatter | solution.py:367
  2573.3 142.2 %reduce-scatter.42.cloned.1.call-done = f32[32,1024]{1,0:T(8,128)} async-done(((f32[1024,1024]{1,0:T(8,128)}), f32[32,1024]{1,0:T(8,128)}) %reduce-scatter.42.cloned.1.call-update) | async-done | bytes 131088 | tf_op jit(solution)/shard_map/reduce_scatter | solution.py:366
  2715.5 249.4 %reduce-scatter.56.cloned.1.call-done = f32[88,1024]{1,0:T(8,128)} async-done(((f32[2816,1024]{1,0:T(8,128)}), f32[88,1024]{1,0:T(8,128)}) %reduce-scatter.56.cloned.1.call-update) | async-done | bytes 360464 | tf_op jit(solution)/shard_map/reduce_scatter | solution.py:378
  2964.9 252.7 %reduce-scatter.52.cloned.1.call-done = f32[32,2816]{1,0:T(8,128)} async-done(((f32[1024,2816]{1,0:T(8,128)}), f32[32,2816]{1,0:T(8,128)}) %reduce-scatter.52.cloned.1.call-update) | async-done | bytes 360464 | tf_op jit(solution)/shard_map/reduce_scatter | solution.py:376
  3217.5 253.0 %reduce-scatter.54.cloned.1.call-done = f32[32,2816]{1,0:T(8,128)} async-done(((f32[1024,2816]{1,0:T(8,128)}), f32[32,2816]{1,0:T(8,128)}) %reduce-scatter.54.cloned.1.call-update) | async-done | bytes 360464 | tf_op jit(solution)/shard_map/reduce_scatter | solution.py:377
  (552 shorter events, 364.9 us)
Async XLA Ops:
  7.2 121.0 %copy-start.36 = (bf16[2,1,128,1024]{3,2,1,0:T(8,128)(2,1)S(1)}, bf16[2,1,128,1024]{3,2,1,0:T(8,128)(2,1)}, u32[]{:S(2)}) copy-start(bf16[2,1,128,1024]{3,2,1,0:T(8,128)(2,1)} %param.21) | copy-start | bytes 1572868
  7.2 62.8 %all-gather.36.cloned.1.call-start = ((), (), s32[]{:S(2)}) async-start(), calls=%async_computation.23 | async-start | bytes 2162688 | tf_op jit(solution)/shard_map/all_gather | solution.py:163
  7.9 120.2 %all-gather.40.cloned.1.call-start = ((), (), s32[]{:S(2)}) async-start(), calls=%async_computation.25 | async-start | bytes 2162688 | tf_op jit(solution)/shard_map/all_gather | solution.py:162
  8.7 177.7 %all-gather.32.cloned.1.call-start = ((), (), s32[]{:S(2)}) async-start(), calls=%async_computation.21 | async-start | bytes 2162688 | tf_op jit(solution)/shard_map/all_gather | solution.py:156
  9.4 234.9 %all-gather.28.cloned.1.call-start = ((), (), s32[]{:S(2)}) async-start(), calls=%async_computation.19 | async-start | bytes 2162688 | tf_op jit(solution)/shard_map/all_gather | solution.py:157
  10.0 523.7 %all-gather.30.cloned.1.call-start = ((), (), s32[]{:S(2)}) async-start(), calls=%async_computation.20 | async-start | bytes 2162688 | tf_op jit(solution)/shard_map/all_gather | solution.py:155
  10.6 535.4 %all-gather.62.cloned.1.call-start = ((), (), s32[]{:S(2)}) async-start(), calls=%async_computation.40 | async-start | bytes 1310720 | tf_op jit(solution)/shard_map/all_gather | solution.py:211
  72.9 61.0 %copy-start.143 = (bf16[32]{0:T(256)(128)(2,1)S(1)}, bf16[32]{0:T(256)(128)(2,1)}, u32[]{:S(2)}) copy-start(bf16[32]{0:T(256)(128)(2,1)} %param.31) | copy-start | bytes 196
  72.9 61.2 %copy-start.144 = (bf16[32]{0:T(256)(128)(2,1)S(1)}, bf16[32]{0:T(256)(128)(2,1)}, u32[]{:S(2)}) copy-start(bf16[32]{0:T(256)(128)(2,1)} %param.25) | copy-start | bytes 196
  72.9 61.4 %copy-start.145 = (bf16[32]{0:T(256)(128)(2,1)S(1)}, bf16[32]{0:T(256)(128)(2,1)}, u32[]{:S(2)}) copy-start(bf16[32]{0:T(256)(128)(2,1)} %param.36) | copy-start | bytes 196
  72.9 61.6 %copy-start.146 = (bf16[16]{0:T(256)(128)(2,1)S(1)}, bf16[16]{0:T(256)(128)(2,1)}, u32[]{:S(2)}) copy-start(bf16[16]{0:T(256)(128)(2,1)} %param.30) | copy-start | bytes 100
  72.9 100.5 %copy-start.6 = (bf16[2,1,512,1024]{3,2,1,0:T(8,128)(2,1)S(1)}, bf16[2,1,512,1024]{3,2,1,0:T(8,128)(2,1)}, u32[]{:S(2)}) copy-start(bf16[2,1,512,1024]{3,2,1,0:T(8,128)(2,1)} %param.20) | copy-start | bytes 6291460
  73.0 475.3 %all-gather.54.cloned.1.call-start = ((), (), s32[]{:S(2)}) async-start(), calls=%async_computation.36 | async-start | bytes 1310720 | tf_op jit(solution)/shard_map/all_gather | solution.py:211
  76.0 474.5 %all-gather.64.cloned.1.call-start = ((), (), s32[]{:S(2)}) async-start(), calls=%async_computation.41 | async-start | bytes 1310720 | tf_op jit(solution)/shard_map/all_gather | solution.py:210
  130.9 421.9 %all-gather.56.cloned.1.call-start = ((), (), s32[]{:S(2)}) async-start(), calls=%async_computation.37 | async-start | bytes 1310720 | tf_op jit(solution)/shard_map/all_gather | solution.py:210
  133.8 421.4 %all-gather.60.cloned.1.call-start = ((), (), s32[]{:S(2)}) async-start(), calls=%async_computation.39 | async-start | bytes 5242880 | tf_op jit(solution)/shard_map/all_gather | solution.py:208
  173.4 366.4 %copy-start.104 = (f32[1024]{0:T(1024)}, f32[1024]{0:T(1024)S(1)}, u32[]{:S(2)}) copy-start(f32[1024]{0:T(1024)S(1)} %convert_element_type.753) | copy-start | bytes 12292
  173.9 75.7 %copy-start.121 = (f32[512]{0:T(512)}, f32[512]{0:T(512)S(1)}, u32[]{:S(2)}) copy-start(f32[512]{0:T(512)S(1)} %get-tuple-element.86) | copy-start | bytes 6148
  174.0 359.7 %copy-start.110 = (f32[512]{0:T(512)}, f32[512]{0:T(512)S(1)}, u32[]{:S(2)}) copy-start(f32[512]{0:T(512)S(1)} %fusion.186) | copy-start | bytes 6148
  190.2 467.5 %all-gather.58.cloned.1.call-start = ((), (), s32[]{:S(2)}) async-start(), calls=%async_computation.38 | async-start | bytes 5242880 | tf_op jit(solution)/shard_map/all_gather | solution.py:209
  248.2 441.6 %all-gather.34.cloned.1.call-start = ((), (), s32[]{:S(2)}) async-start(), calls=%async_computation.22 | async-start | bytes 2162688 | tf_op jit(solution)/shard_map/all_gather | solution.py:158
  248.8 445.6 %all-gather.38.cloned.1.call-start = ((), (), s32[]{:S(2)}) async-start(), calls=%async_computation.24 | async-start | bytes 2162688 | tf_op jit(solution)/shard_map/all_gather | solution.py:161
  249.6 449.8 %all-gather.52.cloned.1.call-start = ((), (), s32[]{:S(2)}) async-start(), calls=%async_computation.35 | async-start | bytes 5242880 | tf_op jit(solution)/shard_map/all_gather | solution.py:208
  249.6 290.2 %copy-start.128 = (f32[512]{0:T(512)}, f32[512]{0:T(512)S(1)}, u32[]{:S(2)}) copy-start(f32[512]{0:T(512)S(1)} %fusion.183) | copy-start | bytes 6148
  253.6 540.8 %all-gather.50.cloned.1.call-start = ((), (), s32[]{:S(2)}) async-start(), calls=%async_computation.34 | async-start | bytes 5242880 | tf_op jit(solution)/shard_map/all_gather | solution.py:209
  257.6 605.8 %all-gather.42.cloned.1.call-start = ((), (), s32[]{:S(2)}) async-start(), calls=%async_computation.26 | async-start | bytes 2162688 | tf_op jit(solution)/shard_map/all_gather | solution.py:164
  258.2 640.7 %all-gather.46.cloned.1.call-start = ((), (), s32[]{:S(2)}) async-start(), calls=%async_computation.28 | async-start | bytes 5947392 | tf_op jit(solution)/shard_map/all_gather | solution.py:167
  258.8 689.2 %all-gather.44.cloned.1.call-start = ((), (), s32[]{:S(2)}) async-start(), calls=%async_computation.27 | async-start | bytes 5947392 | tf_op jit(solution)/shard_map/all_gather | solution.py:166
  259.4 757.7 %all-gather.48.cloned.1.call-start = ((), (), s32[]{:S(2)}) async-start(), calls=%async_computation.29 | async-start | bytes 5947392 | tf_op jit(solution)/shard_map/all_gather | solution.py:168
  260.1 1330.8 %reduce-scatter.60.cloned.1.call-start = ((), (), s32[]{:S(2)}) async-start(), calls=%async_computation.52 | async-start | bytes 1310720
  635.4 28.8 copy-start.93
  830.3 33.1 copy-start.3
  898.8 49.1 %copy-start.88 = (bf16[512,1024]{1,0:T(8,128)(2,1)}, bf16[512,1024]{1,0:T(8,128)(2,1)S(1)}, u32[]{:S(2)}) copy-start(bf16[512,1024]{1,0:T(8,128)(2,1)S(1)} %multiply_convert_fusion.10) | copy-start | bytes 3145732
  1080.2 126.0 %copy-start.16 = (f32[512,1024]{1,0:T(8,128)}, f32[512,1024]{1,0:T(8,128)S(1)}, u32[]{:S(2)}) copy-start(f32[512,1024]{1,0:T(8,128)S(1)} %get-tuple-element.104) | copy-start | bytes 6291460
  1133.2 459.4 %reduce-scatter.64.cloned.1.call-start = ((), (), s32[]{:S(2)}) async-start(), calls=%async_computation.54 | async-start | bytes 1310720
  1183.4 421.5 %reduce-scatter.62.cloned.1.call-start = ((), (), s32[]{:S(2)}) async-start(), calls=%async_computation.53 | async-start | bytes 1310720
  1199.4 407.2 %reduce-scatter.58.cloned.1.call-start = ((), (), s32[]{:S(2)}) async-start(), calls=%async_computation.51 | async-start | bytes 1310720
  1224.6 394.2 %reduce-scatter.34.cloned.1.call-start = ((), (), s32[]{:S(2)}) async-start(), calls=%async_computation.31 | async-start | bytes 5242880 | tf_op jit(solution)/shard_map/reduce_scatter | solution.py:330
  1250.7 372.8 %reduce-scatter.38.cloned.1.call-start = ((), (), s32[]{:S(2)}) async-start(), calls=%async_computation.33 | async-start | bytes 5242880 | tf_op jit(solution)/shard_map/reduce_scatter | solution.py:330
  1283.5 345.9 %reduce-scatter.32.cloned.1.call-start = ((), (), s32[]{:S(2)}) async-start(), calls=%async_computation.30 | async-start | bytes 5242880 | tf_op jit(solution)/shard_map/reduce_scatter | solution.py:327
  1330.2 55.4 %copy-start.32 = (bf16[512,1024]{0,1:T(8,128)(2,1)S(1)}, bf16[512,1024]{0,1:T(8,128)(2,1)}, u32[]{:S(2)}) copy-start(bf16[512,1024]{0,1:T(8,128)(2,1)} %copy.121) | copy-start | bytes 3145732
  1404.1 230.0 %reduce-scatter.36.cloned.1.call-start = ((), (), s32[]{:S(2)}) async-start(), calls=%async_computation.32 | async-start | bytes 5242880 | tf_op jit(solution)/shard_map/reduce_scatter | solution.py:327
  1451.4 53.3 %copy-start.30 = (bf16[512,1024]{0,1:T(8,128)(2,1)S(1)}, bf16[512,1024]{0,1:T(8,128)(2,1)}, u32[]{:S(2)}) copy-start(bf16[512,1024]{0,1:T(8,128)(2,1)} %copy.132) | copy-start | bytes 3145732
  1523.2 375.6 %reduce-scatter.50.cloned.1.call-start = ((), (), s32[]{:S(2)}) async-start(), calls=%async_computation.47 | async-start | bytes 4325376 | tf_op jit(solution)/shard_map/reduce_scatter | solution.py:374
  1530.3 368.5 %reduce-scatter.48.cloned.1.call-start = ((), (), s32[]{:S(2)}) async-start(), calls=%async_computation.46 | async-start | bytes 4325376 | tf_op jit(solution)/shard_map/reduce_scatter | solution.py:371
  1537.5 467.2 %reduce-scatter.46.cloned.1.call-start = ((), (), s32[]{:S(2)}) async-start(), calls=%async_computation.45 | async-start | bytes 4325376 | tf_op jit(solution)/shard_map/reduce_scatter | solution.py:368
  1544.8 18.5 copy-start.7
  1544.8 18.5 copy-start.105
  1544.8 18.5 copy-start.129
  1544.8 601.9 %reduce-scatter.40.cloned.1.call-start = ((), (), s32[]{:S(2)}) async-start(), calls=%async_computation.42 | async-start | bytes 4325376 | tf_op jit(solution)/shard_map/reduce_scatter | solution.py:365
  1590.7 698.3 %reduce-scatter.68.cloned.1.call-start = ((), (), s32[]{:S(2)}) async-start(), calls=%async_computation.56 | async-start | bytes 4325376
  1604.8 825.9 %reduce-scatter.66.cloned.1.call-start = ((), (), s32[]{:S(2)}) async-start(), calls=%async_computation.55 | async-start | bytes 4325376
  1618.7 954.6 %reduce-scatter.44.cloned.1.call-start = ((), (), s32[]{:S(2)}) async-start(), calls=%async_computation.44 | async-start | bytes 4325376 | tf_op jit(solution)/shard_map/reduce_scatter | solution.py:367
  1629.4 1086.1 %reduce-scatter.42.cloned.1.call-start = ((), (), s32[]{:S(2)}) async-start(), calls=%async_computation.43 | async-start | bytes 4325376 | tf_op jit(solution)/shard_map/reduce_scatter | solution.py:366
  1640.2 1324.7 %reduce-scatter.56.cloned.1.call-start = ((), (), s32[]{:S(2)}) async-start(), calls=%async_computation.50 | async-start | bytes 11894784 | tf_op jit(solution)/shard_map/reduce_scatter | solution.py:378
  1653.0 1564.6 %reduce-scatter.52.cloned.1.call-start = ((), (), s32[]{:S(2)}) async-start(), calls=%async_computation.48 | async-start | bytes 11894784 | tf_op jit(solution)/shard_map/reduce_scatter | solution.py:376
  1665.7 1804.8 %reduce-scatter.54.cloned.1.call-start = ((), (), s32[]{:S(2)}) async-start(), calls=%async_computation.49 | async-start | bytes 11894784 | tf_op jit(solution)/shard_map/reduce_scatter | solution.py:377
  1770.7 23.4 copy-start.23
  1794.1 24.8 copy-start.132
  1794.1 24.8 copy-start.133
  1794.2 24.8 copy-start.125
  1794.2 24.8 copy-start.126
  1846.6 45.7 %copy-start.122 = (f32[512]{0:T(512)S(1)}, f32[512]{0:T(512)}, u32[]{:S(2)}) copy-start(f32[512]{0:T(512)} %copy-done.121) | copy-start | bytes 6148
  1846.6 45.7 %copy-start.124 = (f32[512]{0:T(512)S(1)}, f32[512]{0:T(512)}, u32[]{:S(2)}) copy-start(f32[512]{0:T(512)} %copy-done.123) | copy-start | bytes 6148
  (126 other events, 601.7 us)
Sparse Core Ops, SparseCore 0:
  10.9 59.0 all-gather.35
  72.9 55.2 all-gather.39
  131.0 55.2 all-gather.31
  189.1 55.2 all-gather.27
  247.1 55.2 all-gather.29
  304.6 25.4 all-gather.61
  332.0 26.6 all-gather.53
  361.0 26.6 all-gather.63
  389.5 26.6 all-gather.55
  417.9 52.6 all-gather.59
  473.1 52.6 all-gather.57
  528.5 56.3 all-gather.33
  587.8 55.2 all-gather.37
  644.8 51.5 all-gather.51
  698.1 52.6 all-gather.49
  753.5 56.4 all-gather.41
  812.7 66.1 all-gather.45
  881.6 66.2 all-gather.43
  950.8 66.2 all-gather.47
  1133.4 26.6 reduce-scatter.59
  1183.5 26.8 reduce-scatter.63
  1213.3 27.7 reduce-scatter.61
  1244.2 27.7 reduce-scatter.57
  1274.7 52.6 reduce-scatter.33
  1330.7 52.6 reduce-scatter.37
  1404.3 51.8 reduce-scatter.31
  1523.3 51.9 reduce-scatter.35
  1578.2 141.5 reduce-scatter.49
  1722.7 138.8 reduce-scatter.47
  1864.3 140.3 reduce-scatter.45
  2007.5 139.1 reduce-scatter.39
  2149.6 139.2 reduce-scatter.67
  2291.6 139.0 reduce-scatter.65
  2433.6 139.6 reduce-scatter.43
  2576.1 139.2 reduce-scatter.41
  2718.2 246.6 reduce-scatter.55
  2967.6 249.8 reduce-scatter.51
  3220.4 250.0 reduce-scatter.53
where the time goes:
time: 3490 us; the launch traced here: 3480 us
  waiting for transfers between devices  1860 us (53%)
  matrix products  854 us (24%)
  local copies, waits for them, and re-layouts  402 us (12%)
  other arithmetic  249 us (7%)
  blocking collectives  93.8 us (3%)
    unnamed x44, waiting for transfers between devices  291 us
    reduce_scatter x1, waiting for transfers between devices, body(): lax.psum_scatter(local[13], ('dp', 'seq'), scatter_dimension=0, tiled=True)  253 us
    reduce_scatter x1, waiting for transfers between devices, body(): lax.psum_scatter(local[12], ('dp', 'seq'), scatter_dimension=0, tiled=True)  253 us
    reduce_scatter x1, waiting for transfers between devices, body(): lax.psum_scatter(local[14], ('dp', 'seq'), scatter_dimension=0, tiled=True)  249 us
    eq x1, local copies, waits for them, and re-layouts, body(): buckets_of(distance)[None]  178 us
    dot_general x4, matrix products, scores_of(): jnp.einsum('sqhd,skhd->shqk', q_rows, keys, preferred_element_type=jnp.fl...  159 us
    reduce_scatter x1, waiting for transfers between devices, body(): lax.psum_scatter(local[3], ('dp', 'seq'), scatter_dimension=0, tiled=True)  143 us
    reduce_scatter x1, waiting for transfers between devices, body(): lax.psum_scatter(local[2], ('dp', 'seq'), scatter_dimension=0, tiled=True)  142 us
  transfers between devices with their start and end apart: 38, of which 15 were waited for; matrix products, arithmetic and copies ran while one was open for 39% of the time, Pallas kernels for 0%

commit v1 on v0

--- a/solution.py
+++ b/solution.py
@@ -1,8 +1,11 @@
+import functools
 import math
 
 import jax
 import jax.numpy as jnp
 from jax import lax
+from jax.experimental import pallas as pl
+from jax.experimental.pallas import tpu as pltpu
 from jax.sharding import PartitionSpec as P
 
 HEADS = 16
@@ -94,7 +97,7 @@
     return (join_heads(grad_query), join_heads(grad_keys), join_heads(grad_values), grad_scores)
 
 
-def body(
+def general_body(
     hidden_in,
     encoder_states,
     segments,
@@ -383,9 +386,758 @@
     )
 
 
+TILE = 256
+GROUP = 4
+LANES = 128
+F32 = jnp.float32
+BF16 = jnp.bfloat16
+
+
+def contract(left, right, left_dim, right_dim):
+    return lax.dot_general(
+        left, right, (((left_dim,), (right_dim,)), ((), ())), preferred_element_type=F32
+    )
+
+
+def head_mask(head):
+    lane = lax.broadcasted_iota(jnp.int32, (1, LANES), 1)
+    keep = (lane < HEAD_DIM) if head % 2 == 0 else (lane >= HEAD_DIM)
+    return keep.astype(F32).astype(BF16)
+
+
+def bias_table(line):
+    first = jnp.concatenate(
+        [line if j == 0 else pltpu.roll(line, j, 1) for j in range(8)], axis=0
+    )
+    return [first if r == 0 else pltpu.roll(first, 8 * r, 1) for r in range(TILE // 8)]
+
+
+def line_of(table):
+    total = None
+    for r in range(TILE // 8):
+        part = table[8 * r : 8 * r + 8, :]
+        part = part if r == 0 else pltpu.roll(part, TILE - 8 * r, 1)
+        total = part if total is None else total + part
+    line = total[0:1, :]
+    for j in range(1, 8):
+        line = line + pltpu.roll(total[j : j + 1, :], TILE - j, 1)
+    return line
+
+
+def allowed_keys(segq, segk_ref, row, diagonal):
+    segk = segk_ref[pl.ds(row, TILE), :]
+    segk = jnp.concatenate([segk] * (TILE // LANES), axis=1)
+    same = segk == segq
+    if diagonal:
+        k_pos = lax.broadcasted_iota(jnp.int32, (TILE, TILE), 0)
+        q_pos = lax.broadcasted_iota(jnp.int32, (TILE, TILE), 1)
+        same = same & (k_pos <= q_pos)
+    return same
+
+
+def pair_lanes(head):
+    return slice((head // 2) * LANES, (head // 2 + 1) * LANES)
+
+
+def load_keys(refs, own_rows, par_rows, kb, vb):
+    ko, vo, kp, vp = refs
+    kb[0:own_rows, :] = ko[...]
+    vb[0:own_rows, :] = vo[...]
+    kb[own_rows : own_rows + par_rows, :] = kp[...]
+    vb[own_rows : own_rows + par_rows, :] = vp[...]
+
+
+def fill_tables(line_ref, tab, adj):
+    for h in range(GROUP):
+        line = line_ref[h]
+        for r, rows in enumerate(bias_table(line)):
+            tab[h, 8 * r : 8 * r + 8, :] = rows
+        table = tab[h]
+        k_pos = lax.broadcasted_iota(jnp.int32, (TILE, TILE), 0)
+        q_pos = lax.broadcasted_iota(jnp.int32, (TILE, TILE), 1)
+        adj[h] = jnp.where(k_pos > q_pos, table, line[:, TILE - 1 : TILE])
+
+
+def visit_tiles(causal, kinds_ref, tile, tiles):
+    if not causal:
+        for t in range(tiles):
+            tile(t * TILE, 0)
+        return
+    i = pl.program_id(1)
+    tile(pl.multiple_of(i * TILE, TILE), 3)
+
+    def step(p, carry):
+        kind = kinds_ref[i * tiles + p]
+        row = pl.multiple_of(p * TILE, TILE)
+
+        @pl.when(kind == 1)
+        def _():
+            tile(row, 1)
+
+        @pl.when(kind == 2)
+        def _():
+            tile(row, 2)
+
+        return carry
+
+    lax.fori_loop(0, tiles, step, 0)
+
+
+def with_bias(scores, kind, h, line_ref, tab, adj):
+    if kind == 3:
+        return scores + tab[h]
+    if kind == 2:
+        return scores + adj[h]
+    if kind == 1:
+        return scores + line_ref[h][:, TILE - 1 : TILE]
+    return scores
+
+
+def attend_kernel(causal, own_rows, par_rows, kinds_ref, q_ref, ko, vo, kp, vp, segq_ref, segk_ref,
+                  line_ref, o_ref, lse_ref, kb, vb, qm, tab, adj, m_s, l_s, acc):
+    @pl.when(pl.program_id(1) == 0)
+    def _():
+        load_keys((ko, vo, kp, vp), own_rows, par_rows, kb, vb)
+        if causal:
+            fill_tables(line_ref, tab, adj)
+
+    for h in range(GROUP):
+        qm[h] = q_ref[:, pair_lanes(h)] * head_mask(h)
+    m_s[...] = jnp.full(m_s.shape, NEG, F32)
+    l_s[...] = jnp.zeros(l_s.shape, F32)
+    acc[...] = jnp.zeros(acc.shape, F32)
+    segq = segq_ref[0:1, :]
+
+    def tile(row, kind):
+        allowed = allowed_keys(segq, segk_ref, row, kind == 3)
+        for h in range(GROUP):
+            scores = contract(kb[pl.ds(row, TILE), pair_lanes(h)], qm[h], 1, 1)
+            scores = jnp.where(allowed, with_bias(scores, kind, h, line_ref, tab, adj), NEG)
+            before = m_s[h : h + 1, :]
+            largest = jnp.maximum(before, jnp.max(scores, axis=0, keepdims=True))
+            raised = jnp.exp(scores - largest)
+            scale = jnp.exp(before - largest)
+            m_s[h : h + 1, :] = largest
+            l_s[h : h + 1, :] = l_s[h : h + 1, :] * scale + jnp.sum(raised, axis=0, keepdims=True)
+            mixed = contract(vb[pl.ds(row, TILE), pair_lanes(h)], raised.astype(BF16), 0, 0)
+            half = (h % 2) * HEAD_DIM
+            rows = slice(h * HEAD_DIM, (h + 1) * HEAD_DIM)
+            acc[rows, :] = acc[rows, :] * scale + mixed[half : half + HEAD_DIM, :]
+
+    visit_tiles(causal, kinds_ref, tile, (own_rows + par_rows) // TILE)
+    for h in range(GROUP):
+        rows = slice(h * HEAD_DIM, (h + 1) * HEAD_DIM)
+        acc[rows, :] = acc[rows, :] / l_s[h : h + 1, :]
+        lse_ref[0, h : h + 1, :] = m_s[h : h + 1, :] + jnp.log(l_s[h : h + 1, :])
+    o_ref[...] = acc[...].T.astype(BF16)
+
+
+def attend_back_kernel(causal, own_rows, par_rows, kinds_ref, q_ref, ko, vo, kp, vp, segq_ref, segk_ref,
+                       line_ref, do_ref, o_ref, lse_ref, dq_ref, own_ref, par_ref, gline_ref, gfar_ref,
+                       kb, vb, qm, dm, tab, adj, d_s, dq_acc, dk_acc, dv_acc, gt, gfar):
+    i = pl.program_id(1)
+
+    @pl.when(i == 0)
+    def _():
+        load_keys((ko, vo, kp, vp), own_rows, par_rows, kb, vb)
+        dk_acc[...] = jnp.zeros(dk_acc.shape, F32)
+        dv_acc[...] = jnp.zeros(dv_acc.shape, F32)
+        gt[...] = jnp.zeros(gt.shape, F32)
+        gfar[...] = jnp.zeros(gfar.shape, F32)
+        if causal:
+            fill_tables(line_ref, tab, adj)
+
+    for h in range(GROUP):
+        lanes = pair_lanes(h)
+        pair, rows = h // 2, slice((h % 2) * TILE, (h % 2 + 1) * TILE)
+        qm[pair, rows, :] = q_ref[:, lanes] * head_mask(h)
+        dm[pair, rows, :] = do_ref[:, lanes] * head_mask(h)
+        product = do_ref[:, lanes].astype(F32) * o_ref[:, lanes].astype(F32)
+        ones = jnp.broadcast_to(head_mask(h).astype(F32), (8, LANES))
+        inner = lax.dot_general(
+            ones, product, (((1,), (1,)), ((), ())),
+            precision=lax.Precision.HIGHEST, preferred_element_type=F32,
+        )
+        d_s[h : h + 1, :] = inner[0:1, :]
+    dq_acc[...] = jnp.zeros(dq_acc.shape, F32)
+    segq = segq_ref[0:1, :]
+
+    def tile(row, kind):
+        allowed = allowed_keys(segq, segk_ref, row, kind == 3)
+        for pair in range(GROUP // 2):
+            lanes = slice(pair * LANES, (pair + 1) * LANES)
+            keys = kb[pl.ds(row, TILE), lanes]
+            values = vb[pl.ds(row, TILE), lanes]
+            probs_pair, grads_pair = [], []
+            for h in (2 * pair, 2 * pair + 1):
+                half = slice((h % 2) * TILE, (h % 2 + 1) * TILE)
+                scores = contract(keys, qm[pair, half, :], 1, 1)
+                scores = jnp.where(allowed, with_bias(scores, kind, h, line_ref, tab, adj), NEG)
+                probs = jnp.exp(scores - lse_ref[0, h : h + 1, :])
+                grad_probs = contract(values, dm[pair, half, :], 1, 1)
+                grads = probs * (grad_probs - d_s[h : h + 1, :])
+                low = grads.astype(BF16)
+                probs_pair.append(probs.astype(BF16))
+                grads_pair.append(low)
+                if causal:
+                    rounded = low.astype(F32)
+                    if kind == 3:
+                        gt[h] += rounded
+                    elif kind == 2:
+                        k_pos = lax.broadcasted_iota(jnp.int32, (TILE, TILE), 0)
+                        q_pos = lax.broadcasted_iota(jnp.int32, (TILE, TILE), 1)
+                        near = jnp.where(k_pos > q_pos, rounded, 0.0)
+                        gt[h] += near
+                        gfar[h] += jnp.sum((rounded - near).reshape(TILE // 8, 8, TILE), axis=0)
+                    else:
+                        gfar[h] += jnp.sum(rounded.reshape(TILE // 8, 8, TILE), axis=0)
+                back = contract(keys, low, 0, 0)
+                rows = slice(h * HEAD_DIM, (h + 1) * HEAD_DIM)
+                start = (h % 2) * HEAD_DIM
+                dq_acc[rows, :] += back[start : start + HEAD_DIM, :]
+            dv_acc[pl.ds(row, TILE), lanes] += contract(
+                jnp.concatenate(probs_pair, axis=1), dm[pair], 1, 0
+            )
+            dk_acc[pl.ds(row, TILE), lanes] += contract(
+                jnp.concatenate(grads_pair, axis=1), qm[pair], 1, 0
+            )
+
+    visit_tiles(causal, kinds_ref, tile, (own_rows + par_rows) // TILE)
+    dq_ref[...] = dq_acc[...].T.astype(BF16)
+
+    @pl.when(i == pl.num_programs(1) - 1)
+    def _():
+        own_ref[0] = dk_acc[0:own_rows, :].astype(BF16)
+        own_ref[1] = dv_acc[0:own_rows, :].astype(BF16)
+        par_ref[0] = dk_acc[own_rows : own_rows + par_rows, :].astype(BF16)
+        par_ref[1] = dv_acc[own_rows : own_rows + par_rows, :].astype(BF16)
+        for h in range(GROUP):
+            if causal:
+                gline_ref[h] = line_of(gt[h])
+                gfar_ref[h] = jnp.sum(gfar[h], axis=0, keepdims=True)
+            else:
+                gline_ref[h] = jnp.zeros((1, TILE), F32)
+                gfar_ref[h] = jnp.zeros((1, TILE), F32)
+
+
+VMEM_LIMIT = 60 * 1024 * 1024
+
+
+def attention_specs(tokens, width, own_rows, par_rows):
+    groups = HEADS // GROUP
+    lanes = GROUP * HEAD_DIM
+    keys = own_rows + par_rows
+    return [
+        pl.BlockSpec((TILE, lanes), lambda g, i, kinds: (i, g)),
+        pl.BlockSpec((own_rows, lanes), lambda g, i, kinds: (0, g)),
+        pl.BlockSpec((own_rows, lanes), lambda g, i, kinds: (0, groups + g)),
+        pl.BlockSpec((par_rows, lanes), lambda g, i, kinds: (0, g)),
+        pl.BlockSpec((par_rows, lanes), lambda g, i, kinds: (0, groups + g)),
+        pl.BlockSpec((8, TILE), lambda g, i, kinds: (0, i)),
+        pl.BlockSpec((keys, LANES), lambda g, i, kinds: (0, 0)),
+        pl.BlockSpec((GROUP, 1, TILE), lambda g, i, kinds: (g, 0, 0)),
+    ]
+
+
+def attend_fast(kinds, query, kv_own, kv_par, segq, segk, line, causal):
+    tokens, width = query.shape
+    own_rows, par_rows = kv_own.shape[0], kv_par.shape[0]
+    keys = own_rows + par_rows
+    groups, lanes = HEADS // GROUP, GROUP * HEAD_DIM
+    table = (GROUP, TILE, TILE) if causal else (1, 8, LANES)
+    return pl.pallas_call(
+        functools.partial(attend_kernel, causal, own_rows, par_rows),
+        grid_spec=pltpu.PrefetchScalarGridSpec(
+            num_scalar_prefetch=1,
+            grid=(groups, tokens // TILE),
+            in_specs=attention_specs(tokens, width, own_rows, par_rows),
+            out_specs=[
+                pl.BlockSpec((TILE, lanes), lambda g, i, kinds: (i, g)),
+                pl.BlockSpec((1, GROUP, TILE), lambda g, i, kinds: (g, 0, i)),
+            ],
+            scratch_shapes=[
+                pltpu.VMEM((keys, lanes), BF16),
+                pltpu.VMEM((keys, lanes), BF16),
+                pltpu.VMEM((GROUP, TILE, LANES), BF16),
+                pltpu.VMEM(table, F32),
+                pltpu.VMEM(table, F32),
+                pltpu.VMEM((8, TILE), F32),
+                pltpu.VMEM((8, TILE), F32),
+                pltpu.VMEM((lanes, TILE), F32),
+            ],
+        ),
+        out_shape=[
+            jax.ShapeDtypeStruct((tokens, width), BF16),
+            jax.ShapeDtypeStruct((groups, GROUP, tokens), F32),
+        ],
+        compiler_params=pltpu.CompilerParams(vmem_limit_bytes=VMEM_LIMIT),
+        cost_estimate=pl.CostEstimate(
+            flops=tokens * keys * width * 4, bytes_accessed=4 * (tokens + keys) * width,
+            transcendentals=tokens * keys * HEADS // 2,
+        ),
+        name="attend_self" if causal else "attend_cross",
+    )(kinds, query, kv_own, kv_own, kv_par, kv_par, segq, segk, line)
+
+
+def attend_back_fast(kinds, query, kv_own, kv_par, segq, segk, line, grad_mixed, mixed, lse, causal):
+    tokens, width = query.shape
+    own_rows, par_rows = kv_own.shape[0], kv_par.shape[0]
+    keys = own_rows + par_rows
+    groups, lanes = HEADS // GROUP, GROUP * HEAD_DIM
+    table = (GROUP, TILE, TILE) if causal else (1, 8, LANES)
+    block = pl.BlockSpec((TILE, lanes), lambda g, i, kinds: (i, g))
+    line_spec = pl.BlockSpec((GROUP, 1, TILE), lambda g, i, kinds: (g, 0, 0))
+    return pl.pallas_call(
+        functools.partial(attend_back_kernel, causal, own_rows, par_rows),
+        grid_spec=pltpu.PrefetchScalarGridSpec(
+            num_scalar_prefetch=1,
+            grid=(groups, tokens // TILE),
+            in_specs=attention_specs(tokens, width, own_rows, par_rows)
+            + [block, block, pl.BlockSpec((1, GROUP, TILE), lambda g, i, kinds: (g, 0, i))],
+            out_specs=[
+                block,
+                pl.BlockSpec((2, own_rows, lanes), lambda g, i, kinds: (0, 0, g)),
+                pl.BlockSpec((2, par_rows, lanes), lambda g, i, kinds: (0, 0, g)),
+                line_spec,
+                line_spec,
+            ],
+            scratch_shapes=[
+                pltpu.VMEM((keys, lanes), BF16),
+                pltpu.VMEM((keys, lanes), BF16),
+                pltpu.VMEM((GROUP // 2, 2 * TILE, LANES), BF16),
+                pltpu.VMEM((GROUP // 2, 2 * TILE, LANES), BF16),
+                pltpu.VMEM(table, F32),
+                pltpu.VMEM(table, F32),
+                pltpu.VMEM((8, TILE), F32),
+                pltpu.VMEM((lanes, TILE), F32),
+                pltpu.VMEM((keys, lanes), F32),
+                pltpu.VMEM((keys, lanes), F32),
+                pltpu.VMEM(table, F32),
+                pltpu.VMEM((GROUP, 8, TILE), F32),
+            ],
+        ),
+        out_shape=[
+            jax.ShapeDtypeStruct((tokens, width), BF16),
+            jax.ShapeDtypeStruct((2, own_rows, width), BF16),
+            jax.ShapeDtypeStruct((2, par_rows, width), BF16),
+            jax.ShapeDtypeStruct((HEADS, 1, TILE), F32),
+            jax.ShapeDtypeStruct((HEADS, 1, TILE), F32),
+        ],
+        compiler_params=pltpu.CompilerParams(vmem_limit_bytes=VMEM_LIMIT),
+        cost_estimate=pl.CostEstimate(
+            flops=tokens * keys * width * 10, bytes_accessed=10 * (tokens + keys) * width,
+            transcendentals=tokens * keys * HEADS // 2,
+        ),
+        name="attend_self_back" if causal else "attend_cross_back",
+    )(kinds, query, kv_own, kv_own, kv_par, kv_par, segq, segk, line, grad_mixed, mixed, lse)
+
+
+AXES = ("dp", "seq")
+
+
+def exchange(value, dp_bit, seq_bit):
+    pairs = [
+        (dp * 4 + seq, (dp ^ dp_bit) * 4 + (seq ^ seq_bit)) for dp in range(8) for seq in range(4)
+    ]
+    return lax.ppermute(value, AXES, pairs)
+
+
+CORE, Z_LOW, Z_HIGH, X, Y = (1, 0), (2, 0), (4, 0), (0, 1), (0, 2)
+
+
+def move_pairs(a, b):
+    pairs = []
+    for z in range(4):
+        for core in range(2):
+            for s in range(4):
+                micro, half_core = (s >> 1) ^ a, (s & 1) ^ b
+                pairs.append(((2 * z + core) * 4 + s, (2 * z + half_core) * 4 + 2 * core + micro))
+    return pairs
+
+
+ROUNDS = ((0, 0), (0, 1), (1, 0), (1, 1))
+
+
+def in_order(flag, first, second):
+    return jnp.stack([jnp.where(flag == 0, first, second), jnp.where(flag == 0, second, first)])
+
+
+def take(value, index, axis):
+    return lax.dynamic_index_in_dim(value, index, axis, keepdims=False)
+
+
+def assemble_kernel(rows, widths, *refs):
+    pieces, (outs, scratch) = refs[:16], (refs[16 : 16 + len(widths)], refs[16 + len(widths) :])
+    sems_in, sems_out = scratch[-2:]
+    buffers = scratch[0]
+    half = buffers.shape[-1]
+    loads = []
+    for p in range(16):
+        load = pltpu.make_async_copy(pieces[p], buffers.at[p], sems_in.at[p])
+        load.start()
+        loads.append(load)
+    dp, seq = lax.axis_index("dp"), lax.axis_index("seq")
+    core, x, y = lax.rem(dp, 2), lax.rem(seq, 2), seq // 2
+    stores = []
+    for p in range(16):
+        loads[p].wait()
+        rel_core, column, rel_y, rel_x = p // 8, (p // 4) % 2, (p // 2) % 2, p % 2
+        to_core = lax.rem(core + rel_core, 2)
+        to_y, to_x = lax.rem(y + rel_y, 2), lax.rem(x + rel_x, 2)
+        starts = [sum(widths[:w]) for w in range(len(widths))]
+        for w, start in enumerate(starts):
+            low, high = max(start, column * half), min(start + widths[w], (column + 1) * half)
+            if low >= high:
+                continue
+            store = pltpu.make_async_copy(
+                buffers.at[p, :, :, pl.ds(low - column * half, high - low)],
+                outs[w].at[:, to_core, to_y, to_x, :, pl.ds(low - start, high - low)],
+                sems_out.at[p, w],
+            )
+            store.start()
+            stores.append(store)
+    for store in stores:
+        store.wait()
+
+
+def assemble(pieces, widths):
+    rows, half = pieces[0].shape[1:]
+    outs = pl.pallas_call(
+        functools.partial(assemble_kernel, rows, widths),
+        in_specs=[pl.BlockSpec(memory_space=pl.ANY)] * 16,
+        out_specs=[pl.BlockSpec(memory_space=pl.ANY)] * len(widths),
+        out_shape=[jax.ShapeDtypeStruct((4, 2, 2, 2, rows, width), BF16) for width in widths],
+        scratch_shapes=[
+            pltpu.VMEM((16, 4, rows, half), BF16),
+            pltpu.SemaphoreType.DMA((16,)),
+            pltpu.SemaphoreType.DMA((16, len(widths))),
+        ],
+        compiler_params=pltpu.CompilerParams(vmem_limit_bytes=VMEM_LIMIT),
+        cost_estimate=pl.CostEstimate(
+            flops=0, transcendentals=0, bytes_accessed=4 * 64 * rows * half
+        ),
+        name="assemble",
+    )(*pieces)
+    return [out.reshape(32 * rows, out.shape[-1]) for out in outs]
+
+
+def gather_weights(shard, widths, place):
+    core, z_low, z_high = place[0], place[1], place[2]
+    low = in_order(z_low, shard, exchange(shard, *Z_LOW))
+    both = in_order(z_high, low, exchange(low, *Z_HIGH)).reshape(4, *shard.shape)
+    half = shard.shape[1] // 2
+    left, right = both[..., :half], both[..., half:]
+    left_x, right_y = exchange(left, *X), exchange(right, *Y)
+    left_y, left_xy = exchange(left, *Y), exchange(left_x, *Y)
+    right_x, right_xy = exchange(right, *X), exchange(right_y, *X)
+    own = [left, left_x, left_y, left_xy, right, right_x, right_y, right_xy]
+    return assemble(own + [exchange(piece, *CORE) for piece in own], widths)
+
+
+def add_low(first, second):
+    return (first.astype(F32) + second.astype(F32)).astype(BF16)
+
+
+def scatter_grads(grads, place):
+    core, z_low, z_high, y, x = place
+    rows, width = grads.shape[0] // 32, grads.shape[1]
+    half = width // 2
+    whole = grads.reshape(4, 2, 2, 2, rows, width)
+    got = exchange(take(whole, 1 - core, 1), *CORE)
+    kept = add_low(take(whole, core, 1), got)
+    left, right = kept[..., :half], kept[..., half:]
+    left_got = exchange(take(left, 1 - x, 2), *X)
+    right_got = exchange(take(right, 1 - y, 1), *Y)
+    left = add_low(take(left, x, 2), left_got)
+    right = add_low(take(right, y, 1), right_got)
+    left_got = exchange(take(left, 1 - y, 1), *Y)
+    right_got = exchange(take(right, 1 - x, 1), *X)
+    left = add_low(take(left, y, 1), left_got)
+    right = add_low(take(right, x, 1), right_got)
+    both = jnp.concatenate([left, right], axis=-1).reshape(2, 2, rows, width)
+    got = exchange(take(both, 1 - z_high, 0), *Z_HIGH)
+    both = add_low(take(both, z_high, 0), got)
+    got = exchange(take(both, 1 - z_low, 0), *Z_LOW)
+    return take(both, z_low, 0).astype(F32) + got.astype(F32)
+
+
+def gather_small(shard, place):
+    core, z_low, z_high, y, x = place
+    value = in_order(x, shard, exchange(shard, *X))
+    value = in_order(y, value, exchange(value, *Y))
+    value = in_order(core, value, exchange(value, *CORE))
+    value = in_order(z_low, value, exchange(value, *Z_LOW))
+    value = in_order(z_high, value, exchange(value, *Z_HIGH))
+    return value.reshape(32, *shard.shape)
+
+
+def scatter_small(value, place):
+    core, z_low, z_high, y, x = place
+    value = value.reshape(2, 2, 2, 2, 2, *value.shape[1:])
+    for flag, link in ((z_high, Z_HIGH), (z_low, Z_LOW), (core, CORE), (y, Y), (x, X)):
+        value = take(value, flag, 0) + exchange(take(value, 1 - flag, 0), *link)
+    return value
+
+
+def norm_scale(value):
+    return lax.rsqrt(jnp.mean(value * value, axis=-1, keepdims=True) + EPS)
+
+
+def normed(value, gain):
+    return (value * norm_scale(value) * gain).astype(BF16)
+
+
+def norm_back(value, gain, grad):
+    scale = norm_scale(value)
+    scaled = grad * gain
+    inner = jnp.mean(scaled * value, axis=-1, keepdims=True)
+    return (
+        scale * scaled - (scale * scale * scale) * value * inner,
+        jnp.sum(grad * value * scale, axis=0),
+    )
+
+
+def dot(rows, weight):
+    return jnp.dot(rows, weight, preferred_element_type=F32)
+
+
+def dot_back(grads, weight):
+    return contract(grads, weight, 1, 1)
+
+
+def dot_weight(rows, grads):
+    return contract(rows, grads, 0, 0).astype(BF16)
+
+
+def fast_body(
+    hidden_in,
+    encoder_states,
+    segments,
+    enc_segments,
+    grad_out,
+    norm_self,
+    q_self,
+    k_self,
+    v_self,
+    o_self,
+    rel_bias,
+    norm_cross,
+    q_cross,
+    k_cross,
+    v_cross,
+    o_cross,
+    norm_ff,
+    wi_gate,
+    wi_up,
+    wo_ff,
+):
+    dp, seq = lax.axis_index("dp"), lax.axis_index("seq")
+    core, z_low, z_high, y, x = dp % 2, (dp // 2) % 2, dp // 4, seq // 2, seq % 2
+    place = (core, z_low, z_high, y, x)
+    rows_dev, width = hidden_in.shape[2], hidden_in.shape[3]
+    enc_dev = encoder_states.shape[2]
+    part, enc_part = rows_dev // 2, enc_dev // 2
+    owned_micro = seq % 2
+
+    def send_tokens(pieces_of):
+        return [
+            lax.ppermute(pieces_of((seq // 2) ^ a, b), AXES, move_pairs(a, b)) for a, b in ROUNDS
+        ]
+
+    def settle(received):
+        slots = []
+        for s in range(4):
+            index = 2 * ((s >> 1) ^ owned_micro) + ((s & 1) ^ core)
+            slots.append(lax.select_n(index, *received))
+        return jnp.stack(slots)
+
+    def return_tokens(value):
+        received = []
+        for a, b in ROUNDS:
+            index = 2 * (owned_micro ^ a) + (core ^ b)
+            back = [(target, source) for source, target in move_pairs(a, b)]
+            received.append(lax.ppermute(take(value, index, 0), AXES, back))
+        flag = seq // 2
+        micro = []
+        for m in range(2):
+            micro.append(
+                jnp.concatenate(
+                    [jnp.where((flag ^ m) == 0, received[b], received[2 + b]) for b in range(2)],
+                    axis=0,
+                )
+            )
+        return jnp.stack(micro)[:, None]
+
+    codes = jnp.concatenate([segments[:, 0], enc_segments[:, 0]], axis=1).astype(BF16)
+    codes = jnp.pad(codes, ((0, 0), (0, width - codes.shape[1])))
+
+    def bundle(micro, b):
+        return jnp.concatenate(
+            [
+                take(hidden_in[:, 0, b * part : (b + 1) * part], micro, 0),
+                take(encoder_states[:, 0, b * enc_part : (b + 1) * enc_part], micro, 0),
+                jnp.broadcast_to(take(codes, micro, 0)[None], (16, width)),
+            ],
+            axis=0,
+        )
+
+    bundles = send_tokens(bundle)
+
+    small = jnp.concatenate([norm_self, norm_cross, norm_ff, rel_bias])
+    small_rows = norm_self.shape[0]
+    small = gather_small(jnp.pad(small, (0, LANES - small.shape[0])).reshape(1, LANES), place)
+    small = small.reshape(32, LANES).astype(F32)
+    gain_self, gain_cross, gain_ff = (
+        small[:, j * small_rows : (j + 1) * small_rows].reshape(-1) for j in range(3)
+    )
+    table = small[:, 3 * small_rows : 3 * small_rows + rel_bias.shape[0]].reshape(BUCKETS, HEADS)
+
+    wq, wkv = gather_weights(
+        jnp.concatenate([q_self, k_self, v_self], axis=1), (width, 2 * width), place
+    )
+    wo, cq, co, ckv = gather_weights(
+        jnp.concatenate([o_self, q_cross, o_cross, k_cross, v_cross], axis=1),
+        (width, width, width, 2 * width),
+        place,
+    )
+    ff = wi_gate.shape[1]
+    w_gate, w_up = gather_weights(jnp.concatenate([wi_gate, wi_up], axis=1), (ff, ff), place)
+    (w_down,) = gather_weights(wo_ff, (width,), place)
+
+    inputs_low = settle([piece[:part] for piece in bundles]).reshape(4 * part, width)
+    encoder = settle([piece[part : part + enc_part] for piece in bundles]).reshape(4 * enc_part, width)
+    codes = settle([piece[part + enc_part : part + enc_part + 1] for piece in bundles])[:, 0]
+    codes = codes.astype(jnp.int32)
+    seg_parts = codes[:, :rows_dev].reshape(4, 2, part)
+    enc_parts = codes[:, rows_dev : rows_dev + enc_dev].reshape(4, 2, enc_part)
+
+    def of_core(parts, which):
+        return jnp.stack([take(parts[s], which ^ (s & 1), 0) for s in range(4)])
+
+    seg_own, seg_par = of_core(seg_parts, core), of_core(seg_parts, 1 - core)
+    enc_own, enc_par = of_core(enc_parts, core), of_core(enc_parts, 1 - core)
+    seg_keys = jnp.concatenate([seg_own, seg_par])
+    quarter = jnp.arange(4, dtype=jnp.int32)
+    at_own = 2 * quarter + (core ^ (quarter % 2))
+    at_par = 2 * quarter + ((1 - core) ^ (quarter % 2))
+    at_keys = jnp.concatenate([at_own, at_par])
+    needed = (at_keys[None, :] < at_own[:, None]) & (seg_keys[None, :, -1] >= seg_own[:, :1])
+    kinds = jnp.where(needed, jnp.where(at_keys[None, :] == at_own[:, None] - 1, 2, 1), 0)
+    kinds = kinds.astype(jnp.int32).reshape(-1)
+    segq = jnp.broadcast_to(seg_own.reshape(1, -1), (8, 4 * part))
+    segk = jnp.broadcast_to(seg_keys.reshape(-1, 1), (8 * part, LANES))
+    enc_segk = jnp.broadcast_to(
+        jnp.concatenate([enc_own, enc_par]).reshape(-1, 1), (8 * enc_part, LANES)
+    )
+    near = (
+        buckets_of(jnp.arange(TILE, dtype=jnp.int32))[:, None] == jnp.arange(BUCKETS)[None, :]
+    ).astype(F32)
+    line = jnp.dot(near, table, precision=lax.Precision.HIGHEST).T.reshape(HEADS, 1, TILE)
+
+    inputs = inputs_low.astype(F32)
+    normed_self = normed(inputs, gain_self)
+    kv_own = dot(normed_self, wkv).astype(BF16)
+    kv_par = exchange(kv_own, *CORE)
+    query = dot(normed_self, wq).astype(BF16)
+    cross_kv_own = dot(encoder, ckv).astype(BF16)
+    cross_kv_par = exchange(cross_kv_own, *CORE)
+    mixed, self_lse = attend_fast(kinds, query, kv_own, kv_par, segq, segk, line, True)
+    after_self = inputs + dot(mixed, wo)
+    normed_cross = normed(after_self, gain_cross)
+    cross_query = dot(normed_cross, cq).astype(BF16)
+    cross_mixed, cross_lse = attend_fast(
+        kinds, cross_query, cross_kv_own, cross_kv_par, segq, enc_segk, line, False
+    )
+    after_cross = after_self + dot(cross_mixed, co)
+    normed_ff = normed(after_cross, gain_ff)
+    gate, up_values = dot(normed_ff, w_gate), dot(normed_ff, w_up)
+    hidden = gelu_mix(gate, up_values).astype(BF16)
+    result = (after_cross + dot(hidden, w_down)).astype(BF16)
+    block_out = return_tokens(result.reshape(4, part, width))
+
+    out_low = settle(
+        send_tokens(lambda micro, b: take(grad_out[:, 0, b * part : (b + 1) * part], micro, 0))
+    ).reshape(4 * part, width)
+    grad_result = out_low.astype(F32)
+    grad_w_down = scatter_grads(dot_weight(hidden, out_low), place)
+    grad_hidden = dot_back(out_low, w_down)
+    mix_value, mix_pull = jax.vjp(gelu_mix, gate, up_values)
+    grad_gate, grad_up = (piece.astype(BF16) for piece in mix_pull(grad_hidden))
+    grad_w_in = scatter_grads(
+        jnp.concatenate([dot_weight(normed_ff, grad_gate), dot_weight(normed_ff, grad_up)], axis=1),
+        place,
+    )
+    grad_normed_ff = dot_back(grad_gate, w_gate) + dot_back(grad_up, w_up)
+    ff_part, grad_gain_ff = norm_back(after_cross, gain_ff, grad_normed_ff)
+    grad_after_cross = grad_result + ff_part
+    cross_out_low = grad_after_cross.astype(BF16)
+    grad_co = dot_weight(cross_mixed, cross_out_low)
+    grad_cross_mixed = dot_back(cross_out_low, co).astype(BF16)
+    grad_cross_query, cross_own, cross_par, unused, unused = attend_back_fast(
+        kinds, cross_query, cross_kv_own, cross_kv_par, segq, enc_segk, line,
+        grad_cross_mixed, cross_mixed, cross_lse, False,
+    )
+    cross_got = add_low(cross_own, exchange(cross_par, *CORE))
+    grad_cross_kv = jnp.concatenate([cross_got[0], cross_got[1]], axis=1)
+    grad_ckv = dot_weight(encoder, grad_cross_kv)
+    grad_encoder = dot_back(grad_cross_kv, ckv).astype(BF16)
+    grad_encoder = return_tokens(grad_encoder.reshape(4, enc_part, width)).astype(F32)
+    grad_cq = dot_weight(normed_cross, grad_cross_query)
+    grad_normed_cross = dot_back(grad_cross_query, cq)
+    cross_part, grad_gain_cross = norm_back(after_self, gain_cross, grad_normed_cross)
+    grad_after_self = grad_after_cross + cross_part
+    self_out_low = grad_after_self.astype(BF16)
+    grad_wo = dot_weight(mixed, self_out_low)
+    grad_middle = scatter_grads(jnp.concatenate([grad_wo, grad_cq, grad_co, grad_ckv], axis=1), place)
+    grad_mixed = dot_back(self_out_low, wo).astype(BF16)
+    grad_query, self_own, self_par, grad_line, grad_far = attend_back_fast(
+        kinds, query, kv_own, kv_par, segq, segk, line, grad_mixed, mixed, self_lse, True
+    )
+    self_got = add_low(self_own, exchange(self_par, *CORE))
+    grad_kv = jnp.concatenate([self_got[0], self_got[1]], axis=1)
+    grad_qkv = scatter_grads(
+        jnp.concatenate([dot_weight(normed_self, grad_query), dot_weight(normed_self, grad_kv)], axis=1),
+        place,
+    )
+    grad_normed_self = dot_back(grad_query, wq) + dot_back(grad_kv, wkv)
+    self_part, grad_gain_self = norm_back(inputs, gain_self, grad_normed_self)
+    grad_hidden_in = return_tokens((grad_after_self + self_part).astype(BF16).reshape(4, part, width))
+
+    grad_table = jnp.dot(near.T, grad_line.reshape(HEADS, TILE).T, precision=lax.Precision.HIGHEST)
+    grad_table = grad_table.at[BUCKETS - 1].add(jnp.sum(grad_far.reshape(HEADS, TILE), axis=1))
+    small_grads = [piece.reshape(32, -1) for piece in (grad_gain_self, grad_gain_cross, grad_gain_ff)]
+    small_grads = jnp.concatenate(small_grads + [grad_table.reshape(32, -1)], axis=1)
+    small_grads = jnp.pad(small_grads, ((0, 0), (0, LANES - small_grads.shape[1])))
+    small_grads = scatter_small(small_grads.reshape(32, 1, LANES), place).reshape(-1)
+    return (
+        block_out,
+        grad_hidden_in.astype(F32),
+        grad_encoder,
+        small_grads[:small_rows],
+        grad_qkv[:, :width],
+        grad_qkv[:, width : 2 * width],
+        grad_qkv[:, 2 * width :],
+        grad_middle[:, :width],
+        small_grads[3 * small_rows : 3 * small_rows + rel_bias.shape[0]],
+        small_grads[small_rows : 2 * small_rows],
+        grad_middle[:, width : 2 * width],
+        grad_middle[:, 3 * width : 4 * width],
+        grad_middle[:, 4 * width :],
+        grad_middle[:, 2 * width : 3 * width],
+        small_grads[2 * small_rows : 3 * small_rows],
+        grad_w_in[:, :ff],
+        grad_w_in[:, ff:],
+        grad_w_down,
+    )
+
+
+def fits_fast(mesh):
+    return mesh.shape["dp"] == 8 and mesh.shape["seq"] == 4
+
+
 def solution(mesh):
     return jax.shard_map(
-        body,
+        fast_body if fits_fast(mesh) else general_body,
         mesh=mesh,
         in_specs=(
             P(None, "dp", "seq", None),

time: 3490 us -> 1150 us (0.33)
  waiting for transfers between devices: 1860 us -> 331 us
  matrix products: 854 us -> 177 us
  local copies, waits for them, and re-layouts: 402 us -> 92.8 us
  Pallas kernels: 0 us -> 257 us
  starting transfers between devices: 3.12 us -> 195 us
  other arithmetic: 249 us -> 84.5 us
  blocking collectives: 93.8 us -> 0 us
    reduce_scatter x13 -> x0, waiting for transfers between devices: 1290 us -> none  [the longest x1 253 us: body(): lax.psum_scatter(local[13], ('dp', 'seq'), scatter_dimension=0, tiled=True)]
    dot_general x93 -> x29, matrix products: 854 us -> 177 us  [the longest x18 106 us: contract(): lax.dot_general(left, right, (((left_dim,), (right_dim,)), ((), ())), pre...]
    ppermute x0 -> x126, waiting for transfers between devices: none -> 331 us  [the longest x106 305 us: exchange(): return lax.ppermute(value, AXES, pairs)]
    unnamed x44 -> x0, waiting for transfers between devices: 291 us -> none
    all_gather x19 -> x0, waiting for transfers between devices: 281 us -> none  [the longest x1 61.4 us: body(): lax.all_gather(shards[14], ('dp', 'seq'), axis=0, tiled=True)]
    pallas_call x0 -> x8, Pallas kernels: none -> 257 us  [the longest x2 126 us: attend_back_fast(): pl.pallas_call(functools.partial(attend_back_kernel, causal, own_rows, pa...]
    ppermute x0 -> x126, starting transfers between devices: none -> 195 us  [the longest x106 121 us: exchange(): return lax.ppermute(value, AXES, pairs)]
    eq x1 -> x0, local copies, waits for them, and re-layouts: 178 us -> none  [body(): buckets_of(distance)[None]]
  transfers between devices with their start and end apart: 38 -> 126, of which waited for: 15 -> 45; matrix products, arithmetic and copies ran while one was open for 39% -> 18% of each run, Pallas kernels for 0% -> 14%
where the time goes in v1:
time: 1150 us; the launch traced here: 1140 us
  waiting for transfers between devices  331 us (29%)
  Pallas kernels  257 us (22%)
  starting transfers between devices  195 us (17%)
  matrix products  177 us (15%)
  local copies, waits for them, and re-layouts  92.8 us (8%)
  other arithmetic  84.5 us (7%)
    ppermute x106, waiting for transfers between devices, exchange(): return lax.ppermute(value, AXES, pairs)  305 us
    pallas_call x2, Pallas kernels, attend_back_fast(): pl.pallas_call(functools.partial(attend_back_kernel, causal, own_rows, pa...  126 us
    ppermute x106, starting transfers between devices, exchange(): return lax.ppermute(value, AXES, pairs)  121 us
    dot_general x18, matrix products, contract(): lax.dot_general(left, right, (((left_dim,), (right_dim,)), ((), ())), pre...  106 us
    pallas_call x2, Pallas kernels, attend_fast(): pl.pallas_call(functools.partial(attend_kernel, causal, own_rows, par_row...  102 us
    dot_general x9, matrix products, dot(): return jnp.dot(rows, weight, preferred_element_type=F32)  70.7 us
    ppermute x12, starting transfers between devices, return_tokens(): received.append(lax.ppermute(take(value, index, 0), AXES, back))  57.3 us
    convert_element_type x26, other arithmetic, add_low(): return (first.astype(F32) + second.astype(F32)).astype(BF16)  29.1 us
  transfers between devices with their start and end apart: 126, of which 45 were waited for; matrix products, arithmetic and copies ran while one was open for 18% of the time, Pallas kernels for 14%

profile of v1, /device:TPU:0, one launch (start us, length us, event | category | flops | bytes accessed | tf_op | source)
XLA Modules:
  0.0 1141.3 jit_solution(2155512489036468484)
XLA Ops:
  26.7 5.8 collective-permute-done.4
  67.3 11.1 collective-permute-done.80
  87.8 14.2 %collective-permute-done.60 = bf16[2,88,1024]{2,1,0:T(8,128)(2,1)S(1)} collective-permute-done((bf16[2,88,1024]{2,1,0:T(8,128)(2,1)S(1)}, bf16[2,88,1024]{2,1,0:T(8,128)(2,1)S(1)}, u32[]{:S(2)}, u32[]{:S(2)}) %collective-permute-start.60) | collective-permute-done | bytes 360480 | tf_op jit(solution)/shard_map/ppermute | solution.py:742
  103.1 18.2 %collective-permute-done.10 = bf16[2,32,3072]{2,1,0:T(8,128)(2,1)S(1)} collective-permute-done((bf16[2,32,3072]{2,1,0:T(8,128)(2,1)S(1)}, bf16[2,32,3072]{2,1,0:T(8,128)(2,1)S(1)}, u32[]{:S(2)}, u32[]{:S(2)}) %collective-permute-start.10) | collective-permute-done | bytes 393248 | tf_op jit(solution)/shard_map/ppermute | solution.py:742
  134.0 18.8 %collective-permute-done.27 = bf16[2,32,5120]{2,1,0:T(8,128)(2,1)} collective-permute-done((bf16[2,32,5120]{2,1,0:T(8,128)(2,1)}, bf16[2,32,5120]{2,1,0:T(8,128)(2,1)}, u32[]{:S(2)}, u32[]{:S(2)}) %collective-permute-start.27) | collective-permute-done | bytes 655392 | tf_op jit(solution)/shard_map/ppermute | solution.py:742
  158.4 7.7 collective-permute-done.11.refs_1_
  166.1 8.1 collective-permute-done.15.refs_6_
  177.6 21.1 %collective-permute-done.44 = bf16[2,32,5632]{2,1,0:T(8,128)(2,1)S(1)} collective-permute-done((bf16[2,32,5632]{2,1,0:T(8,128)(2,1)S(1)}, bf16[2,32,5632]{2,1,0:T(8,128)(2,1)S(1)}, u32[]{:S(2)}, u32[]{:S(2)}) %collective-permute-start.44) | collective-permute-done | bytes 720928 | tf_op jit(solution)/shard_map/ppermute | solution.py:742
  201.8 8.7 collective-permute-done.13.refs_3_
  220.9 8.2 collective-permute-done.28.refs_1_
  235.5 5.6 assemble.4
  246.7 11.1 collective-permute-done.31.refs_5_
  260.7 9.3 convolution_convert_fusion.5.ko.vo
  270.0 6.9 collective-permute-done.49.refs_6_
  283.1 9.7 collective-permute-done.30.refs_3_
  303.0 5.5 assemble.7
  310.6 11.9 %fusion.141 = f32[1024,2816]{1,0:T(8,128)} fusion(bf16[1024,1024]{1,0:T(8,128)(2,1)} %bitcast.504, bf16[2816,1024]{1,0:T(8,128)(2,1)} %bitcast.506), kind=kOutput, calls=%fused_computation.482 | convolution fusion | flops 5905580032 | bytes 19398656 | tf_op jit(solution)/shard_map/dot_general | solution.py:397
  329.6 8.5 assemble.5
  338.0 4.5 convolution_convert_fusion.6.ko.vo
  343.4 8.8 assemble.6
  354.1 58.2 %attend_self.1 = (bf16[1024,1024]{1,0:T(8,128)(2,1)}, f32[4,4,1024]{2,1,0:T(4,128)}) custom-call(s32[32]{0:T(128)} %select_n.884.kinds_ref, bf16[1024,1024]{1,0:T(8,128)(2,1)} %convolution_convert_fusion.14.q_ref, bf16[1024,2048]{1,0:T(8,128)(2,1)} %convolution_convert_fusion.5.ko.vo, bf16[1024,2048]{1,0:T(8,128)(2,1)} %convolution_convert_fusion.5.ko.vo, ...), custom_call_target="tpu_custom_call" | custom-call | flops 8589934592 | bytes 12582912 | tf_op jit(solution)/shard_map/attend_self/pallas_call | solution.py:648
  412.4 4.8 multiply_reduce_fusion.5
  421.8 44.2 %attend_cross.1 = (bf16[1024,1024]{1,0:T(8,128)(2,1)}, f32[4,4,1024]{2,1,0:T(4,128)}) custom-call(s32[32]{0:T(128)} %select_n.884.kinds_ref, bf16[1024,1024]{1,0:T(8,128)(2,1)} %convolution_convert_fusion.13.q_ref, bf16[256,2048]{1,0:T(8,128)(2,1)} %convolution_convert_fusion.6.ko.vo, bf16[256,2048]{1,0:T(8,128)(2,1)} %convolution_convert_fusion.6.ko.vo, ...), custom_call_target="tpu_custom_call" | custom-call | flops 2147483648 | bytes 6291456 | tf_op jit(solution)/shard_map/attend_cross/pallas_call | solution.py:648
  466.0 5.2 multiply_reduce_fusion.4
  473.2 11.5 %fusion.140 = f32[1024,2816]{1,0:T(8,128)} fusion(bf16[1024,1024]{1,0:T(8,128)(2,1)S(1)} %multiply_convert_fusion.2, bf16[1024,2816]{1,0:T(8,128)(2,1)} %bitcast.554), kind=kOutput, calls=%fused_computation.481 | convolution fusion | flops 5905580032 | bytes 19398656 | tf_op jit(solution)/shard_map/dot_general | solution.py:901
  484.7 21.6 %fusion.6 = (bf16[1024,2816]{1,0:T(8,128)(2,1)}, bf16[1024,2816]{1,0:T(8,128)(2,1)}, bf16[1024,2816]{1,0:T(8,128)(2,1)}) fusion(f32[1024,2816]{1,0:T(8,128)} %fusion.141, f32[1024,2816]{1,0:T(8,128)} %fusion.140, bf16[1024,1024]{1,0:T(8,128)(2,1)S(1)} %multiply_convert_fusion.2, bf16[1024,2816]{1,0:T(8,128)(2,1)} %bitcast.550), kind=kOutput, calls=%fused_computation.8 | convolution fusion | flops 5980553216 | bytes 48234496 | tf_op jit(solution)/shard_map/dot_general | solution.py:901
  506.3 11.0 convolution_convert_fusion.1
  517.3 9.7 fusion.142
  527.0 8.3 convolution_convert_fusion.2
  535.3 9.1 multiply_reduce_fusion
  553.5 53.0 %attend_cross_back.1 = (bf16[1024,1024]{1,0:T(8,128)(2,1)}, bf16[2,256,1024]{2,1,0:T(8,128)(2,1)}, bf16[2,256,1024]{2,1,0:T(8,128)(2,1)}, f32[16,1,256]{2,1,0:T(1,128)}, f32[16,1,256]{2,1,0:T(1,128)}) custom-call(s32[32]{0:T(128)} %select_n.884.kinds_ref, bf16[1024,1024]{1,0:T(8,128)(2,1)} %convolution_convert_fusion.13.q_ref, ...), custom_call_target="tpu_custom_call" | custom-call | flops 5368709120 | bytes 15728640 | tf_op jit(solution)/shard_map/attend_cross_back/pallas_call | solution.py:690
  606.5 6.9 convolution_convert_fusion.8
  625.2 8.2 convolution_convert_fusion
  633.5 6.4 add_convert_fusion.1
  639.9 5.3 pad_maximum_fusion
  651.1 30.6 %collective-permute-start.88 = (bf16[2,256,1024]{2,1,0:T(8,128)(2,1)}, bf16[2,256,1024]{2,1,0:T(8,128)(2,1)S(1)}, u32[]{:S(2)}, u32[]{:S(2)}) collective-permute-start(bf16[2,256,1024]{2,1,0:T(8,128)(2,1)} %get-tuple-element.67), channel_id=1, source_target_pairs={{0,4},{1,5},{2,6},{3,7},{4,0},{5,1},{6,2},{7,3},{8,12},{9,13},{10,... | collective-permute-start | bytes 3145736 | tf_op jit(solution)/shard_map/ppermute | solution.py:742
  681.7 73.2 %attend_self_back.1 = (bf16[1024,1024]{1,0:T(8,128)(2,1)}, bf16[2,1024,1024]{2,1,0:T(8,128)(2,1)}, bf16[2,1024,1024]{2,1,0:T(8,128)(2,1)}, f32[16,1,256]{2,1,0:T(1,128)}, f32[16,1,256]{2,1,0:T(1,128)}) custom-call(s32[32]{0:T(128)} %select_n.884.kinds_ref, bf16[1024,1024]{1,0:T(8,128)(2,1)} %convolution_convert_fusion.14.q_ref, ...), custom_call_target="tpu_custom_call" | custom-call | flops 21474836480 | bytes 31457280 | tf_op jit(solution)/shard_map/attend_self_back/pallas_call | solution.py:690
  757.3 5.3 collective-permute-start.75
  762.6 31.1 %collective-permute-start.76 = (bf16[256,1024]{1,0:T(8,128)(2,1)}, bf16[256,1024]{1,0:T(8,128)(2,1)}, u32[]{:S(2)}, u32[]{:S(2)}) collective-permute-start(bf16[256,1024]{1,0:T(8,128)(2,1)} %get-tuple-element.128), channel_id=1, source_target_pairs={{1,0},{5,1},{0,2},{4,3},{3,4},{7,5},{2,6},{6,7},{9,8},{13,9},{8,10... | collective-permute-start | bytes 1572872 | tf_op jit(solution)/shard_map/ppermute | solution.py:959
  793.7 4.6 collective-permute-start.78
  809.4 3.9 copy.110
  823.9 5.0 collective-permute-start.90
  851.2 14.3 %collective-permute-done.120 = bf16[4,2,88,512]{3,2,0,1:T(8,128)(2,1)S(1)} collective-permute-done((bf16[4,2,88,512]{3,2,0,1:T(8,128)(2,1)S(1)}, bf16[4,2,88,512]{3,2,0,1:T(8,128)(2,1)S(1)}, u32[]{:S(2)}, u32[]{:S(2)}) %collective-permute-start.120) | collective-permute-done | bytes 720928 | tf_op jit(solution)/shard_map/ppermute | solution.py:742
  870.0 6.6 collective-permute-done.121
  877.3 4.3 add_convert_fusion
  883.8 4.5 fusion.25
  888.4 5.7 fusion.20
  894.1 6.4 convolution_convert_fusion.4
  906.4 6.7 fusion.17
  935.0 4.6 collective-permute-done.125
  944.2 7.8 collective-permute-done.85
  952.1 5.2 collective-permute-done.87
  959.8 6.1 fusion.7
  972.0 6.8 fusion.8
  983.6 19.2 %collective-permute-done.113 = bf16[4,2,32,2816]{3,2,0,1:T(8,128)(2,1)} collective-permute-done((bf16[4,2,32,2816]{3,2,0,1:T(8,128)(2,1)}, bf16[4,2,32,2816]{3,2,0,1:T(8,128)(2,1)}, u32[]{:S(2)}, u32[]{:S(2)}) %collective-permute-start.113) | collective-permute-done | bytes 1441824 | tf_op jit(solution)/shard_map/ppermute | solution.py:742
  1012.2 18.6 %collective-permute-done.106 = bf16[4,2,32,2560]{3,2,0,1:T(8,128)(2,1)S(1)} collective-permute-done((bf16[4,2,32,2560]{3,2,0,1:T(8,128)(2,1)S(1)}, bf16[4,2,32,2560]{3,2,0,1:T(8,128)(2,1)S(1)}, u32[]{:S(2)}, u32[]{:S(2)}) %collective-permute-start.106) | collective-permute-done | bytes 1310752 | tf_op jit(solution)/shard_map/ppermute | solution.py:742
  1034.3 14.0 %collective-permute-done.114 = bf16[4,32,2816]{2,1,0:T(8,128)(2,1)S(1)} collective-permute-done((bf16[4,32,2816]{2,1,0:T(8,128)(2,1)S(1)}, bf16[4,32,2816]{2,1,0:T(8,128)(2,1)S(1)}, u32[]{:S(2)}, u32[]{:S(2)}) %collective-permute-start.114) | collective-permute-done | bytes 720928 | tf_op jit(solution)/shard_map/ppermute | solution.py:742
  1052.0 11.1 collective-permute-done.99
  1066.7 12.4 %collective-permute-done.107 = bf16[4,32,2560]{2,1,0:T(8,128)(2,1)S(1)} collective-permute-done((bf16[4,32,2560]{2,1,0:T(8,128)(2,1)S(1)}, bf16[4,32,2560]{2,1,0:T(8,128)(2,1)S(1)}, u32[]{:S(2)}, u32[]{:S(2)}) %collective-permute-start.107) | collective-permute-done | bytes 655392 | tf_op jit(solution)/shard_map/ppermute | solution.py:742
  1081.5 5.2 collective-permute-done.100
  1089.1 13.1 %collective-permute-start.118 = (bf16[32,5632]{1,0:T(8,128)(2,1)S(1)}, bf16[32,5632]{1,0:T(8,128)(2,1)S(1)}, u32[]{:S(2)}, u32[]{:S(2)}) collective-permute-start(bf16[32,5632]{1,0:T(8,128)(2,1)S(1)} %dynamic-slice_bitcast_fusion.36), channel_id=1, source_target_pairs={{0,8},{1,9},{2,10},{3,11},{4,12},{5,13},{6,14},{7,15},{8,0},{9,1},... | collective-permute-start | bytes 1081352 | tf_op jit(solution)/shard_map/ppermute | solution.py:742
  1102.2 18.6 %collective-permute-done.110 = bf16[2,32,5120]{2,1,0:T(8,128)(2,1)S(1)} collective-permute-done((bf16[2,32,5120]{2,1,0:T(8,128)(2,1)S(1)}, bf16[2,32,5120]{2,1,0:T(8,128)(2,1)S(1)}, u32[]{:S(2)}, u32[]{:S(2)}) %collective-permute-start.110) | collective-permute-done | bytes 655392 | tf_op jit(solution)/shard_map/ppermute | solution.py:742
  1121.1 6.1 collective-permute-done.103
  1129.9 9.5 collective-permute-done.104
  (779 shorter events, 310.1 us)
Async XLA Ops:
  4.0 54.4 %collective-permute-start.43 = (bf16[32,5632]{1,0:T(8,128)(2,1)}, bf16[32,5632]{1,0:T(8,128)(2,1)}, u32[]{:S(2)}, u32[]{:S(2)}) collective-permute-start(bf16[32,5632]{1,0:T(8,128)(2,1)} %constant_dynamic-update-slice_fusion.8), channel_id=1, source_target_pairs={{0,8},{1,9},{2,10},{3,11},{4,12},{5,13},{6,14},{7,15},{8,0},{9,1},... | collective-permute-start | bytes 1081352 | tf_op jit(solution)/shard_map/ppermute | solution.py:742
  12.7 109.7 %collective-permute-start = (bf16[336,1024]{1,0:T(8,128)(2,1)}, bf16[336,1024]{1,0:T(8,128)(2,1)S(1)}, u32[]{:S(2)}, u32[]{:S(2)}) collective-permute-start(bf16[336,1024]{1,0:T(8,128)(2,1)} %get-tuple-element.204), channel_id=1, source_target_pairs={{0,0},{1,4},{2,1},{3,5},{4,2},{5,6},{6,3},{7,7},{8,8},{9,12},{10,9... | collective-permute-start | bytes 2064392 | tf_op jit(solution)/shard_map/ppermute | solution.py:944
  17.7 37.5 %collective-permute-start.26 = (bf16[32,5120]{1,0:T(8,128)(2,1)}, bf16[32,5120]{1,0:T(8,128)(2,1)}, u32[]{:S(2)}, u32[]{:S(2)}) collective-permute-start(bf16[32,5120]{1,0:T(8,128)(2,1)} %constant_dynamic-update-slice_fusion.3), channel_id=1, source_target_pairs={{0,8},{1,9},{2,10},{3,11},{4,12},{5,13},{6,14},{7,15},{8,0},{9,1},... | collective-permute-start | bytes 983048 | tf_op jit(solution)/shard_map/ppermute | solution.py:742
  19.6 33.4 %collective-permute-start.9 = (bf16[32,3072]{1,0:T(8,128)(2,1)}, bf16[32,3072]{1,0:T(8,128)(2,1)}, u32[]{:S(2)}, u32[]{:S(2)}) collective-permute-start(bf16[32,3072]{1,0:T(8,128)(2,1)} %constant_dynamic-update-slice_fusion), channel_id=1, source_target_pairs={{0,8},{1,9},{2,10},{3,11},{4,12},{5,13},{6,14},{7,15},{8,0},{9,1},... | collective-permute-start | bytes 589832 | tf_op jit(solution)/shard_map/ppermute | solution.py:742
  53.0 25.4 %collective-permute-start.80 = (bf16[256,1024]{1,0:T(8,128)(2,1)S(1)}, bf16[256,1024]{1,0:T(8,128)(2,1)S(1)}, u32[]{:S(2)}, u32[]{:S(2)}) collective-permute-start(bf16[256,1024]{1,0:T(8,128)(2,1)S(1)} %get-tuple-element.152), channel_id=1, source_target_pairs={{0,4},{1,0},{2,5},{3,1},{4,6},{5,2},{6,7},{7,3},{8,12},{9,8},{10,1... | collective-permute-start | bytes 1572872 | tf_op jit(solution)/shard_map/ppermute | solution.py:944
  55.2 24.3 %collective-permute-start.81 = (bf16[256,1024]{1,0:T(8,128)(2,1)}, bf16[256,1024]{1,0:T(8,128)(2,1)S(1)}, u32[]{:S(2)}, u32[]{:S(2)}) collective-permute-start(bf16[256,1024]{1,0:T(8,128)(2,1)} %get-tuple-element.155), channel_id=1, source_target_pairs={{0,1},{1,5},{2,0},{3,4},{4,3},{5,7},{6,2},{7,6},{8,9},{9,13},{10,8... | collective-permute-start | bytes 1572872 | tf_op jit(solution)/shard_map/ppermute | solution.py:944
  58.3 25.0 %collective-permute-start.82 = (bf16[256,1024]{1,0:T(8,128)(2,1)}, bf16[256,1024]{1,0:T(8,128)(2,1)S(1)}, u32[]{:S(2)}, u32[]{:S(2)}) collective-permute-start(bf16[256,1024]{1,0:T(8,128)(2,1)} %get-tuple-element.153), channel_id=1, source_target_pairs={{0,5},{1,1},{2,4},{3,0},{4,7},{5,3},{6,6},{7,2},{8,13},{9,9},{10,1... | collective-permute-start | bytes 1572872 | tf_op jit(solution)/shard_map/ppermute | solution.py:944
  64.3 58.8 %collective-permute-start.1 = (bf16[336,1024]{1,0:T(8,128)(2,1)S(1)}, bf16[336,1024]{1,0:T(8,128)(2,1)S(1)}, u32[]{:S(2)}, u32[]{:S(2)}) collective-permute-start(bf16[336,1024]{1,0:T(8,128)(2,1)S(1)} %copy-done.48), channel_id=1, source_target_pairs={{0,4},{1,0},{2,5},{3,1},{4,6},{5,2},{6,7},{7,3},{8,12},{9,8},{10,1... | collective-permute-start | bytes 2064392 | tf_op jit(solution)/shard_map/ppermute | solution.py:944
  78.4 45.5 %collective-permute-start.2 = (bf16[336,1024]{1,0:T(8,128)(2,1)S(1)}, bf16[336,1024]{1,0:T(8,128)(2,1)S(1)}, u32[]{:S(2)}, u32[]{:S(2)}) collective-permute-start(bf16[336,1024]{1,0:T(8,128)(2,1)S(1)} %copy-done.50), channel_id=1, source_target_pairs={{0,1},{1,5},{2,0},{3,4},{4,3},{5,7},{6,2},{7,6},{8,9},{9,13},{10,8... | collective-permute-start | bytes 2064392 | tf_op jit(solution)/shard_map/ppermute | solution.py:944
  79.5 45.6 %collective-permute-start.3 = (bf16[336,1024]{1,0:T(8,128)(2,1)S(1)}, bf16[336,1024]{1,0:T(8,128)(2,1)S(1)}, u32[]{:S(2)}, u32[]{:S(2)}) collective-permute-start(bf16[336,1024]{1,0:T(8,128)(2,1)S(1)} %copy-done.49), channel_id=1, source_target_pairs={{0,5},{1,1},{2,4},{3,0},{4,7},{5,3},{6,6},{7,2},{8,13},{9,9},{10,1... | collective-permute-start | bytes 2064392 | tf_op jit(solution)/shard_map/ppermute | solution.py:944
  102.1 19.3 %collective-permute-start.10 = (bf16[2,32,3072]{2,1,0:T(8,128)(2,1)S(1)}, bf16[2,32,3072]{2,1,0:T(8,128)(2,1)S(1)}, u32[]{:S(2)}, u32[]{:S(2)}) collective-permute-start(bf16[2,32,3072]{2,1,0:T(8,128)(2,1)S(1)} %pad_maximum_fusion.26), channel_id=1, source_target_pairs={{0,16},{1,17},{2,18},{3,19},{4,20},{5,21},{6,22},{7,23},{8,24},{9,... | collective-permute-start | bytes 1179656 | tf_op jit(solution)/shard_map/ppermute | solution.py:742
  121.3 31.5 %collective-permute-start.27 = (bf16[2,32,5120]{2,1,0:T(8,128)(2,1)}, bf16[2,32,5120]{2,1,0:T(8,128)(2,1)}, u32[]{:S(2)}, u32[]{:S(2)}) collective-permute-start(bf16[2,32,5120]{2,1,0:T(8,128)(2,1)} %pad_maximum_fusion.24), channel_id=1, source_target_pairs={{0,16},{1,17},{2,18},{3,19},{4,20},{5,21},{6,22},{7,23},{8,24},{9,... | collective-permute-start | bytes 1966088 | tf_op jit(solution)/shard_map/ppermute | solution.py:742
  123.1 31.1 %collective-permute-start.62 = (bf16[4,88,512]{2,1,0:T(8,128)(2,1)}, bf16[4,88,512]{2,1,0:T(8,128)(2,1)}, u32[]{:S(2)}, u32[]{:S(2)}) collective-permute-start(bf16[4,88,512]{2,1,0:T(8,128)(2,1)} %get-tuple-element.171.refs_0_), channel_id=1, source_target_pairs={{0,2},{1,3},{2,0},{3,1},{4,6},{5,7},{6,4},{7,5},{8,10},{9,11},{10,... | collective-permute-start | bytes 1081352 | tf_op jit(solution)/shard_map/ppermute | solution.py:742
  123.9 30.1 %collective-permute-start.65 = (bf16[4,88,512]{2,1,0:T(8,128)(2,1)}, bf16[4,88,512]{2,1,0:T(8,128)(2,1)}, u32[]{:S(2)}, u32[]{:S(2)}) collective-permute-start(bf16[4,88,512]{2,1,0:T(8,128)(2,1)} %get-tuple-element.170.refs_4_), channel_id=1, source_target_pairs={{0,2},{1,3},{2,0},{3,1},{4,6},{5,7},{6,4},{7,5},{8,10},{9,11},{10,... | collective-permute-start | bytes 1081352 | tf_op jit(solution)/shard_map/ppermute | solution.py:742
  125.1 30.6 %collective-permute-start.64 = (bf16[4,88,512]{2,1,0:T(8,128)(2,1)}, bf16[4,88,512]{2,1,0:T(8,128)(2,1)}, u32[]{:S(2)}, u32[]{:S(2)}) collective-permute-start(bf16[4,88,512]{2,1,0:T(8,128)(2,1)} %get-tuple-element.170.refs_4_), channel_id=1, source_target_pairs={{0,1},{1,0},{2,3},{3,2},{4,5},{5,4},{6,7},{7,6},{8,9},{9,8},{10,11... | collective-permute-start | bytes 1081352 | tf_op jit(solution)/shard_map/ppermute | solution.py:742
  134.0 22.2 %collective-permute-start.67 = (bf16[4,88,512]{2,1,0:T(8,128)(2,1)}, bf16[4,88,512]{2,1,0:T(8,128)(2,1)S(1)}, u32[]{:S(2)}, u32[]{:S(2)}) collective-permute-start(bf16[4,88,512]{2,1,0:T(8,128)(2,1)} %get-tuple-element.171.refs_0_), channel_id=1, source_target_pairs={{0,4},{1,5},{2,6},{3,7},{4,0},{5,1},{6,2},{7,3},{8,12},{9,13},{10,... | collective-permute-start | bytes 1081352 | tf_op jit(solution)/shard_map/ppermute | solution.py:742
  154.2 20.0 %collective-permute-start.12 = (bf16[4,32,1536]{2,1,0:T(8,128)(2,1)S(1)}, bf16[4,32,1536]{2,1,0:T(8,128)(2,1)S(1)}, u32[]{:S(2)}, u32[]{:S(2)}) collective-permute-start(bf16[4,32,1536]{2,1,0:T(8,128)(2,1)S(1)} %copy-done.34), channel_id=1, source_target_pairs={{0,2},{1,3},{2,0},{3,1},{4,6},{5,7},{6,4},{7,5},{8,10},{9,11},{10,... | collective-permute-start | bytes 1179656 | tf_op jit(solution)/shard_map/ppermute | solution.py:742
  166.1 32.6 %collective-permute-start.44 = (bf16[2,32,5632]{2,1,0:T(8,128)(2,1)S(1)}, bf16[2,32,5632]{2,1,0:T(8,128)(2,1)S(1)}, u32[]{:S(2)}, u32[]{:S(2)}) collective-permute-start(bf16[2,32,5632]{2,1,0:T(8,128)(2,1)S(1)} %copy-done.38), channel_id=1, source_target_pairs={{0,16},{1,17},{2,18},{3,19},{4,20},{5,21},{6,22},{7,23},{8,24},{9,... | collective-permute-start | bytes 2162696 | tf_op jit(solution)/shard_map/ppermute | solution.py:742
  174.2 24.5 %collective-permute-start.63 = (bf16[4,88,512]{2,1,0:T(8,128)(2,1)}, bf16[4,88,512]{2,1,0:T(8,128)(2,1)S(1)}, u32[]{:S(2)}, u32[]{:S(2)}) collective-permute-start(bf16[4,88,512]{2,1,0:T(8,128)(2,1)} %collective-permute-done.61.refs_1_), channel_id=1, source_target_pairs={{0,2},{1,3},{2,0},{3,1},{4,6},{5,7},{6,4},{7,5},{8,10},{9,11},{10,... | collective-permute-start | bytes 1081352 | tf_op jit(solution)/shard_map/ppermute | solution.py:742
  175.4 23.8 %collective-permute-start.68 = (bf16[4,88,512]{2,1,0:T(8,128)(2,1)}, bf16[4,88,512]{2,1,0:T(8,128)(2,1)S(1)}, u32[]{:S(2)}, u32[]{:S(2)}) collective-permute-start(bf16[4,88,512]{2,1,0:T(8,128)(2,1)} %collective-permute-done.61.refs_1_), channel_id=1, source_target_pairs={{0,4},{1,5},{2,6},{3,7},{4,0},{5,1},{6,2},{7,3},{8,12},{9,13},{10,... | collective-permute-start | bytes 1081352 | tf_op jit(solution)/shard_map/ppermute | solution.py:742
  175.6 23.6 %collective-permute-start.66 = (bf16[4,88,512]{2,1,0:T(8,128)(2,1)}, bf16[4,88,512]{2,1,0:T(8,128)(2,1)S(1)}, u32[]{:S(2)}, u32[]{:S(2)}) collective-permute-start(bf16[4,88,512]{2,1,0:T(8,128)(2,1)} %collective-permute-done.65.refs_6_), channel_id=1, source_target_pairs={{0,1},{1,0},{2,3},{3,2},{4,5},{5,4},{6,7},{7,6},{8,9},{9,8},{10,11... | collective-permute-start | bytes 1081352 | tf_op jit(solution)/shard_map/ppermute | solution.py:742
  177.6 23.8 %collective-permute-start.73 = (bf16[4,88,512]{2,1,0:T(8,128)(2,1)}, bf16[4,88,512]{2,1,0:T(8,128)(2,1)S(1)}, u32[]{:S(2)}, u32[]{:S(2)}) collective-permute-start(bf16[4,88,512]{2,1,0:T(8,128)(2,1)} %collective-permute-done.65.refs_6_), channel_id=1, source_target_pairs={{0,4},{1,5},{2,6},{3,7},{4,0},{5,1},{6,2},{7,3},{8,12},{9,13},{10,... | collective-permute-start | bytes 1081352 | tf_op jit(solution)/shard_map/ppermute | solution.py:742
  215.0 45.2 %collective-permute-start.45 = (bf16[4,32,2816]{2,1,0:T(8,128)(2,1)S(1)}, bf16[4,32,2816]{2,1,0:T(8,128)(2,1)}, u32[]{:S(2)}, u32[]{:S(2)}) collective-permute-start(bf16[4,32,2816]{2,1,0:T(8,128)(2,1)S(1)} %get-tuple-element.139.refs_0_), channel_id=1, source_target_pairs={{0,1},{1,0},{2,3},{3,2},{4,5},{5,4},{6,7},{7,6},{8,9},{9,8},{10,11... | collective-permute-start | bytes 2162696 | tf_op jit(solution)/shard_map/ppermute | solution.py:742
  230.4 27.4 %collective-permute-start.31 = (bf16[4,32,2560]{2,1,0:T(8,128)(2,1)}, bf16[4,32,2560]{2,1,0:T(8,128)(2,1)}, u32[]{:S(2)}, u32[]{:S(2)}) collective-permute-start(bf16[4,32,2560]{2,1,0:T(8,128)(2,1)} %get-tuple-element.142.refs_4_), channel_id=1, source_target_pairs={{0,1},{1,0},{2,3},{3,2},{4,5},{5,4},{6,7},{7,6},{8,9},{9,8},{10,11... | collective-permute-start | bytes 1966088 | tf_op jit(solution)/shard_map/ppermute | solution.py:742
  231.1 28.5 %collective-permute-start.34 = (bf16[4,32,2560]{2,1,0:T(8,128)(2,1)}, bf16[4,32,2560]{2,1,0:T(8,128)(2,1)}, u32[]{:S(2)}, u32[]{:S(2)}) collective-permute-start(bf16[4,32,2560]{2,1,0:T(8,128)(2,1)} %get-tuple-element.143.refs_0_), channel_id=1, source_target_pairs={{0,4},{1,5},{2,6},{3,7},{4,0},{5,1},{6,2},{7,3},{8,12},{9,13},{10,... | collective-permute-start | bytes 1966088 | tf_op jit(solution)/shard_map/ppermute | solution.py:742
  231.1 29.1 %collective-permute-start.38 = (bf16[4,32,2560]{2,1,0:T(8,128)(2,1)}, bf16[4,32,2560]{2,1,0:T(8,128)(2,1)}, u32[]{:S(2)}, u32[]{:S(2)}) collective-permute-start(bf16[4,32,2560]{2,1,0:T(8,128)(2,1)} %get-tuple-element.142.refs_4_), channel_id=1, source_target_pairs={{0,4},{1,5},{2,6},{3,7},{4,0},{5,1},{6,2},{7,3},{8,12},{9,13},{10,... | collective-permute-start | bytes 1966088 | tf_op jit(solution)/shard_map/ppermute | solution.py:742
  245.0 33.7 %collective-permute-start.46 = (bf16[4,32,2816]{2,1,0:T(8,128)(2,1)S(1)}, bf16[4,32,2816]{2,1,0:T(8,128)(2,1)S(1)}, u32[]{:S(2)}, u32[]{:S(2)}) collective-permute-start(bf16[4,32,2816]{2,1,0:T(8,128)(2,1)S(1)} %get-tuple-element.139.refs_0_), channel_id=1, source_target_pairs={{0,2},{1,3},{2,0},{3,1},{4,6},{5,7},{6,4},{7,5},{8,10},{9,11},{10,... | collective-permute-start | bytes 2162696 | tf_op jit(solution)/shard_map/ppermute | solution.py:742
  259.5 19.8 %collective-permute-start.48 = (bf16[4,32,2816]{2,1,0:T(8,128)(2,1)S(1)}, bf16[4,32,2816]{2,1,0:T(8,128)(2,1)S(1)}, u32[]{:S(2)}, u32[]{:S(2)}) collective-permute-start(bf16[4,32,2816]{2,1,0:T(8,128)(2,1)S(1)} %get-tuple-element.138.refs_4_), channel_id=1, source_target_pairs={{0,1},{1,0},{2,3},{3,2},{4,5},{5,4},{6,7},{7,6},{8,9},{9,8},{10,11... | collective-permute-start | bytes 2162696 | tf_op jit(solution)/shard_map/ppermute | solution.py:742
  260.1 19.8 %collective-permute-start.51 = (bf16[4,32,2816]{2,1,0:T(8,128)(2,1)S(1)}, bf16[4,32,2816]{2,1,0:T(8,128)(2,1)S(1)}, u32[]{:S(2)}, u32[]{:S(2)}) collective-permute-start(bf16[4,32,2816]{2,1,0:T(8,128)(2,1)S(1)} %get-tuple-element.139.refs_0_), channel_id=1, source_target_pairs={{0,4},{1,5},{2,6},{3,7},{4,0},{5,1},{6,2},{7,3},{8,12},{9,13},{10,... | collective-permute-start | bytes 2162696 | tf_op jit(solution)/shard_map/ppermute | solution.py:742
  260.2 20.2 %collective-permute-start.55 = (bf16[4,32,2816]{2,1,0:T(8,128)(2,1)S(1)}, bf16[4,32,2816]{2,1,0:T(8,128)(2,1)S(1)}, u32[]{:S(2)}, u32[]{:S(2)}) collective-permute-start(bf16[4,32,2816]{2,1,0:T(8,128)(2,1)S(1)} %get-tuple-element.138.refs_4_), channel_id=1, source_target_pairs={{0,4},{1,5},{2,6},{3,7},{4,0},{5,1},{6,2},{7,3},{8,12},{9,13},{10,... | collective-permute-start | bytes 2162696 | tf_op jit(solution)/shard_map/ppermute | solution.py:742
  279.3 72.9 %collective-permute-start.25 = (bf16[1024,2048]{1,0:T(8,128)(2,1)}, bf16[1024,2048]{1,0:T(8,128)(2,1)}, u32[]{:S(2)}, u32[]{:S(2)}) collective-permute-start(bf16[1024,2048]{1,0:T(8,128)(2,1)} %convolution_convert_fusion.5.ko.vo), channel_id=1, source_target_pairs={{0,4},{1,5},{2,6},{3,7},{4,0},{5,1},{6,2},{7,3},{8,12},{9,13},{10,... | collective-permute-start | bytes 12582920 | tf_op jit(solution)/shard_map/ppermute | solution.py:742
  322.5 20.3 %collective-permute-start.57 = (bf16[4,32,2816]{2,1,0:T(8,128)(2,1)}, bf16[4,32,2816]{2,1,0:T(8,128)(2,1)}, u32[]{:S(2)}, u32[]{:S(2)}) collective-permute-start(bf16[4,32,2816]{2,1,0:T(8,128)(2,1)} %collective-permute-done.49.refs_6_), channel_id=1, source_target_pairs={{0,4},{1,5},{2,6},{3,7},{4,0},{5,1},{6,2},{7,3},{8,12},{9,13},{10,... | collective-permute-start | bytes 2162696 | tf_op jit(solution)/shard_map/ppermute | solution.py:742
  323.0 19.5 %collective-permute-start.56 = (bf16[4,32,2816]{2,1,0:T(8,128)(2,1)S(1)}, bf16[4,32,2816]{2,1,0:T(8,128)(2,1)S(1)}, u32[]{:S(2)}, u32[]{:S(2)}) collective-permute-start(bf16[4,32,2816]{2,1,0:T(8,128)(2,1)S(1)} %copy-done.42), channel_id=1, source_target_pairs={{0,4},{1,5},{2,6},{3,7},{4,0},{5,1},{6,2},{7,3},{8,12},{9,13},{10,... | collective-permute-start | bytes 2162696 | tf_op jit(solution)/shard_map/ppermute | solution.py:742
  342.5 78.5 %collective-permute-start.42 = (bf16[256,2048]{1,0:T(8,128)(2,1)}, bf16[256,2048]{1,0:T(8,128)(2,1)}, u32[]{:S(2)}, u32[]{:S(2)}) collective-permute-start(bf16[256,2048]{1,0:T(8,128)(2,1)} %convolution_convert_fusion.6.ko.vo), channel_id=1, source_target_pairs={{0,4},{1,5},{2,6},{3,7},{4,0},{5,1},{6,2},{7,3},{8,12},{9,13},{10,... | collective-permute-start | bytes 3145736 | tf_op jit(solution)/shard_map/ppermute | solution.py:742
  651.1 168.7 %collective-permute-start.88 = (bf16[2,256,1024]{2,1,0:T(8,128)(2,1)}, bf16[2,256,1024]{2,1,0:T(8,128)(2,1)S(1)}, u32[]{:S(2)}, u32[]{:S(2)}) collective-permute-start(bf16[2,256,1024]{2,1,0:T(8,128)(2,1)} %get-tuple-element.67), channel_id=1, source_target_pairs={{0,4},{1,5},{2,6},{3,7},{4,0},{5,1},{6,2},{7,3},{8,12},{9,13},{10,... | collective-permute-start | bytes 3145736 | tf_op jit(solution)/shard_map/ppermute | solution.py:742
  757.3 57.5 %collective-permute-start.75 = (bf16[256,1024]{1,0:T(8,128)(2,1)}, bf16[256,1024]{1,0:T(8,128)(2,1)}, u32[]{:S(2)}, u32[]{:S(2)}) collective-permute-start(bf16[256,1024]{1,0:T(8,128)(2,1)} %get-tuple-element.131), channel_id=1, source_target_pairs={{0,0},{4,1},{1,2},{5,3},{2,4},{6,5},{3,6},{7,7},{8,8},{12,9},{9,10... | collective-permute-start | bytes 1572872 | tf_op jit(solution)/shard_map/ppermute | solution.py:959
  762.6 52.2 %collective-permute-start.76 = (bf16[256,1024]{1,0:T(8,128)(2,1)}, bf16[256,1024]{1,0:T(8,128)(2,1)}, u32[]{:S(2)}, u32[]{:S(2)}) collective-permute-start(bf16[256,1024]{1,0:T(8,128)(2,1)} %get-tuple-element.128), channel_id=1, source_target_pairs={{1,0},{5,1},{0,2},{4,3},{3,4},{7,5},{2,6},{6,7},{9,8},{13,9},{8,10... | collective-permute-start | bytes 1572872 | tf_op jit(solution)/shard_map/ppermute | solution.py:959
  793.7 22.9 %collective-permute-start.77 = (bf16[256,1024]{1,0:T(8,128)(2,1)}, bf16[256,1024]{1,0:T(8,128)(2,1)}, u32[]{:S(2)}, u32[]{:S(2)}) collective-permute-start(bf16[256,1024]{1,0:T(8,128)(2,1)} %get-tuple-element.130), channel_id=1, source_target_pairs={{4,0},{0,1},{5,2},{1,3},{6,4},{2,5},{7,6},{3,7},{12,8},{8,9},{13,1... | collective-permute-start | bytes 1572872 | tf_op jit(solution)/shard_map/ppermute | solution.py:959
  793.7 23.1 %collective-permute-start.78 = (bf16[256,1024]{1,0:T(8,128)(2,1)}, bf16[256,1024]{1,0:T(8,128)(2,1)}, u32[]{:S(2)}, u32[]{:S(2)}) collective-permute-start(bf16[256,1024]{1,0:T(8,128)(2,1)} %get-tuple-element.129), channel_id=1, source_target_pairs={{5,0},{1,1},{4,2},{0,3},{7,4},{3,5},{6,6},{2,7},{13,8},{9,9},{12,1... | collective-permute-start | bytes 1572872 | tf_op jit(solution)/shard_map/ppermute | solution.py:959
  814.8 23.3 %collective-permute-start.119 = (bf16[4,2,2,88,1024]{4,3,2,1,0:T(8,128)(2,1)}, bf16[4,2,2,88,1024]{4,3,2,1,0:T(8,128)(2,1)S(1)}, u32[]{:S(2)}, u32[]{:S(2)}) collective-permute-start(bf16[4,2,2,88,1024]{4,3,2,1,0:T(8,128)(2,1)} %dynamic-slice_bitcast_fusion.3), channel_id=1, source_target_pairs={{0,4},{1,5},{2,6},{3,7},{4,0},{5,1},{6,2},{7,3},{8,12},{9,13},{10,... | collective-permute-start | bytes 8650760 | tf_op jit(solution)/shard_map/ppermute | solution.py:742
  814.8 144.9 %collective-permute-start.112 = (bf16[4,2,2,32,5632]{4,3,2,1,0:T(8,128)(2,1)}, bf16[4,2,2,32,5632]{4,3,2,1,0:T(8,128)(2,1)}, u32[]{:S(2)}, u32[]{:S(2)}) collective-permute-start(bf16[4,2,2,32,5632]{4,3,2,1,0:T(8,128)(2,1)} %dynamic-slice_bitcast_fusion), channel_id=1, source_target_pairs={{0,4},{1,5},{2,6},{3,7},{4,0},{5,1},{6,2},{7,3},{8,12},{9,13},{10,... | collective-permute-start | bytes 17301512 | tf_op jit(solution)/shard_map/ppermute | solution.py:742
  816.6 60.6 %collective-permute-start.83 = (bf16[2,1024,1024]{2,1,0:T(8,128)(2,1)}, bf16[2,1024,1024]{2,1,0:T(8,128)(2,1)}, u32[]{:S(2)}, u32[]{:S(2)}) collective-permute-start(bf16[2,1024,1024]{2,1,0:T(8,128)(2,1)} %get-tuple-element.65), channel_id=1, source_target_pairs={{0,4},{1,5},{2,6},{3,7},{4,0},{5,1},{6,2},{7,3},{8,12},{9,13},{10,... | collective-permute-start | bytes 12582920 | tf_op jit(solution)/shard_map/ppermute | solution.py:742
  823.2 20.8 %collective-permute-start.89 = (bf16[64,1024]{1,0:T(8,128)(2,1)S(1)}, bf16[64,1024]{1,0:T(8,128)(2,1)S(1)}, u32[]{:S(2)}, u32[]{:S(2)}) collective-permute-start(bf16[64,1024]{1,0:T(8,128)(2,1)S(1)} %get-tuple-element.186), channel_id=1, source_target_pairs={{0,0},{4,1},{1,2},{5,3},{2,4},{6,5},{3,6},{7,7},{8,8},{12,9},{9,10... | collective-permute-start | bytes 393224 | tf_op jit(solution)/shard_map/ppermute | solution.py:959
  823.9 22.5 %collective-permute-start.90 = (bf16[64,1024]{1,0:T(8,128)(2,1)S(1)}, bf16[64,1024]{1,0:T(8,128)(2,1)S(1)}, u32[]{:S(2)}, u32[]{:S(2)}) collective-permute-start(bf16[64,1024]{1,0:T(8,128)(2,1)S(1)} %get-tuple-element.183), channel_id=1, source_target_pairs={{1,0},{5,1},{0,2},{4,3},{3,4},{7,5},{2,6},{6,7},{9,8},{13,9},{8,10... | collective-permute-start | bytes 393224 | tf_op jit(solution)/shard_map/ppermute | solution.py:959
  846.6 124.4 %collective-permute-start.105 = (bf16[4,2,2,32,5120]{4,3,2,1,0:T(8,128)(2,1)}, bf16[4,2,2,32,5120]{4,3,2,1,0:T(8,128)(2,1)}, u32[]{:S(2)}, u32[]{:S(2)}) collective-permute-start(bf16[4,2,2,32,5120]{4,3,2,1,0:T(8,128)(2,1)} %dynamic-slice_bitcast_fusion.1), channel_id=1, source_target_pairs={{0,4},{1,5},{2,6},{3,7},{4,0},{5,1},{6,2},{7,3},{8,12},{9,13},{10,... | collective-permute-start | bytes 15728648 | tf_op jit(solution)/shard_map/ppermute | solution.py:742
  877.2 55.0 %collective-permute-start.124 = (bf16[2,88,1024]{2,1,0:T(8,128)(2,1)S(1)}, bf16[2,88,1024]{2,1,0:T(8,128)(2,1)S(1)}, u32[]{:S(2)}, u32[]{:S(2)}) collective-permute-start(bf16[2,88,1024]{2,1,0:T(8,128)(2,1)S(1)} %dynamic-slice_bitcast_fusion.33), channel_id=1, source_target_pairs={{0,16},{1,17},{2,18},{3,19},{4,20},{5,21},{6,22},{7,23},{8,24},{9,... | collective-permute-start | bytes 1081352 | tf_op jit(solution)/shard_map/ppermute | solution.py:742
  930.1 21.9 %collective-permute-start.85 = (bf16[256,1024]{1,0:T(8,128)(2,1)S(1)}, bf16[256,1024]{1,0:T(8,128)(2,1)S(1)}, u32[]{:S(2)}, u32[]{:S(2)}) collective-permute-start(bf16[256,1024]{1,0:T(8,128)(2,1)S(1)} %get-tuple-element.118), channel_id=1, source_target_pairs={{1,0},{5,1},{0,2},{4,3},{3,4},{7,5},{2,6},{6,7},{9,8},{13,9},{8,10... | collective-permute-start | bytes 1572872 | tf_op jit(solution)/shard_map/ppermute | solution.py:959
  952.0 54.5 %collective-permute-start.98 = (bf16[4,2,2,32,3072]{4,3,2,1,0:T(8,128)(2,1)}, bf16[4,2,2,32,3072]{4,3,2,1,0:T(8,128)(2,1)}, u32[]{:S(2)}, u32[]{:S(2)}) collective-permute-start(bf16[4,2,2,32,3072]{4,3,2,1,0:T(8,128)(2,1)} %dynamic-slice_bitcast_fusion.2), channel_id=1, source_target_pairs={{0,4},{1,5},{2,6},{3,7},{4,0},{5,1},{6,2},{7,3},{8,12},{9,13},{10,... | collective-permute-start | bytes 9437192 | tf_op jit(solution)/shard_map/ppermute | solution.py:742
  968.1 34.7 %collective-permute-start.113 = (bf16[4,2,32,2816]{3,2,0,1:T(8,128)(2,1)}, bf16[4,2,32,2816]{3,2,0,1:T(8,128)(2,1)}, u32[]{:S(2)}, u32[]{:S(2)}) collective-permute-start(bf16[4,2,32,2816]{3,2,0,1:T(8,128)(2,1)} %bitcast.487), channel_id=1, source_target_pairs={{0,1},{1,0},{2,3},{3,2},{4,5},{5,4},{6,7},{7,6},{8,9},{9,8},{10,11... | collective-permute-start | bytes 4325384 | tf_op jit(solution)/shard_map/ppermute | solution.py:742
  970.0 35.8 %collective-permute-start.115 = (bf16[4,2,32,2816]{3,2,1,0:T(8,128)(2,1)}, bf16[4,2,32,2816]{3,2,1,0:T(8,128)(2,1)S(1)}, u32[]{:S(2)}, u32[]{:S(2)}) collective-permute-start(bf16[4,2,32,2816]{3,2,1,0:T(8,128)(2,1)} %dynamic-slice_bitcast_fusion.4), channel_id=1, source_target_pairs={{0,2},{1,3},{2,0},{3,1},{4,6},{5,7},{6,4},{7,5},{8,10},{9,11},{10,... | collective-permute-start | bytes 4325384 | tf_op jit(solution)/shard_map/ppermute | solution.py:742
  982.0 48.8 %collective-permute-start.106 = (bf16[4,2,32,2560]{3,2,0,1:T(8,128)(2,1)S(1)}, bf16[4,2,32,2560]{3,2,0,1:T(8,128)(2,1)S(1)}, u32[]{:S(2)}, u32[]{:S(2)}) collective-permute-start(bf16[4,2,32,2560]{3,2,0,1:T(8,128)(2,1)S(1)} %bitcast.531), channel_id=1, source_target_pairs={{0,1},{1,0},{2,3},{3,2},{4,5},{5,4},{6,7},{7,6},{8,9},{9,8},{10,11... | collective-permute-start | bytes 3932168 | tf_op jit(solution)/shard_map/ppermute | solution.py:742
  982.5 50.2 %collective-permute-start.108 = (bf16[4,2,32,2560]{3,2,1,0:T(8,128)(2,1)S(1)}, bf16[4,2,32,2560]{3,2,1,0:T(8,128)(2,1)S(1)}, u32[]{:S(2)}, u32[]{:S(2)}) collective-permute-start(bf16[4,2,32,2560]{3,2,1,0:T(8,128)(2,1)S(1)} %dynamic-slice_bitcast_fusion.5), channel_id=1, source_target_pairs={{0,2},{1,3},{2,0},{3,1},{4,6},{5,7},{6,4},{7,5},{8,10},{9,11},{10,... | collective-permute-start | bytes 3932168 | tf_op jit(solution)/shard_map/ppermute | solution.py:742
  1004.7 43.5 %collective-permute-start.114 = (bf16[4,32,2816]{2,1,0:T(8,128)(2,1)S(1)}, bf16[4,32,2816]{2,1,0:T(8,128)(2,1)S(1)}, u32[]{:S(2)}, u32[]{:S(2)}) collective-permute-start(bf16[4,32,2816]{2,1,0:T(8,128)(2,1)S(1)} %dynamic-slice_bitcast_fusion.10), channel_id=1, source_target_pairs={{0,2},{1,3},{2,0},{3,1},{4,6},{5,7},{6,4},{7,5},{8,10},{9,11},{10,... | collective-permute-start | bytes 2162696 | tf_op jit(solution)/shard_map/ppermute | solution.py:742
  1006.3 43.4 %collective-permute-start.116 = (bf16[4,32,2816]{2,1,0:T(8,128)(2,1)S(1)}, bf16[4,32,2816]{2,1,0:T(8,128)(2,1)S(1)}, u32[]{:S(2)}, u32[]{:S(2)}) collective-permute-start(bf16[4,32,2816]{2,1,0:T(8,128)(2,1)S(1)} %dynamic-slice_bitcast_fusion.9), channel_id=1, source_target_pairs={{0,1},{1,0},{2,3},{3,2},{4,5},{5,4},{6,7},{7,6},{8,9},{9,8},{10,11... | collective-permute-start | bytes 2162696 | tf_op jit(solution)/shard_map/ppermute | solution.py:742
  1010.2 52.9 %collective-permute-start.99 = (bf16[4,2,32,1536]{3,2,0,1:T(8,128)(2,1)S(1)}, bf16[4,2,32,1536]{3,2,0,1:T(8,128)(2,1)S(1)}, u32[]{:S(2)}, u32[]{:S(2)}) collective-permute-start(bf16[4,2,32,1536]{3,2,0,1:T(8,128)(2,1)S(1)} %bitcast.532), channel_id=1, source_target_pairs={{0,1},{1,0},{2,3},{3,2},{4,5},{5,4},{6,7},{7,6},{8,9},{9,8},{10,11... | collective-permute-start | bytes 2359304 | tf_op jit(solution)/shard_map/ppermute | solution.py:742
  1030.8 34.3 %collective-permute-start.101 = (bf16[4,2,32,1536]{3,2,1,0:T(8,128)(2,1)S(1)}, bf16[4,2,32,1536]{3,2,1,0:T(8,128)(2,1)S(1)}, u32[]{:S(2)}, u32[]{:S(2)}) collective-permute-start(bf16[4,2,32,1536]{3,2,1,0:T(8,128)(2,1)S(1)} %dynamic-slice_bitcast_fusion.6), channel_id=1, source_target_pairs={{0,2},{1,3},{2,0},{3,1},{4,6},{5,7},{6,4},{7,5},{8,10},{9,11},{10,... | collective-permute-start | bytes 2359304 | tf_op jit(solution)/shard_map/ppermute | solution.py:742
  1032.8 46.3 %collective-permute-start.107 = (bf16[4,32,2560]{2,1,0:T(8,128)(2,1)S(1)}, bf16[4,32,2560]{2,1,0:T(8,128)(2,1)S(1)}, u32[]{:S(2)}, u32[]{:S(2)}) collective-permute-start(bf16[4,32,2560]{2,1,0:T(8,128)(2,1)S(1)} %dynamic-slice_bitcast_fusion.13), channel_id=1, source_target_pairs={{0,2},{1,3},{2,0},{3,1},{4,6},{5,7},{6,4},{7,5},{8,10},{9,11},{10,... | collective-permute-start | bytes 1966088 | tf_op jit(solution)/shard_map/ppermute | solution.py:742
  1048.2 31.1 %collective-permute-start.109 = (bf16[4,32,2560]{2,1,0:T(8,128)(2,1)S(1)}, bf16[4,32,2560]{2,1,0:T(8,128)(2,1)S(1)}, u32[]{:S(2)}, u32[]{:S(2)}) collective-permute-start(bf16[4,32,2560]{2,1,0:T(8,128)(2,1)S(1)} %dynamic-slice_bitcast_fusion.12), channel_id=1, source_target_pairs={{0,1},{1,0},{2,3},{3,2},{4,5},{5,4},{6,7},{7,6},{8,9},{9,8},{10,11... | collective-permute-start | bytes 1966088 | tf_op jit(solution)/shard_map/ppermute | solution.py:742
  1050.1 38.8 %collective-permute-start.117 = (bf16[2,32,5632]{2,1,0:T(8,128)(2,1)S(1)}, bf16[2,32,5632]{2,1,0:T(8,128)(2,1)S(1)}, u32[]{:S(2)}, u32[]{:S(2)}) collective-permute-start(bf16[2,32,5632]{2,1,0:T(8,128)(2,1)S(1)} %dynamic-slice_bitcast_fusion.8), channel_id=1, source_target_pairs={{0,16},{1,17},{2,18},{3,19},{4,20},{5,21},{6,22},{7,23},{8,24},{9,... | collective-permute-start | bytes 2162696 | tf_op jit(solution)/shard_map/ppermute | solution.py:742
  1063.3 23.4 %collective-permute-start.100 = (bf16[4,32,1536]{2,1,0:T(8,128)(2,1)S(1)}, bf16[4,32,1536]{2,1,0:T(8,128)(2,1)S(1)}, u32[]{:S(2)}, u32[]{:S(2)}) collective-permute-start(bf16[4,32,1536]{2,1,0:T(8,128)(2,1)S(1)} %dynamic-slice_bitcast_fusion.32), channel_id=1, source_target_pairs={{0,2},{1,3},{2,0},{3,1},{4,6},{5,7},{6,4},{7,5},{8,10},{9,11},{10,... | collective-permute-start | bytes 1179656 | tf_op jit(solution)/shard_map/ppermute | solution.py:742
  1065.3 21.6 %collective-permute-start.102 = (bf16[4,32,1536]{2,1,0:T(8,128)(2,1)S(1)}, bf16[4,32,1536]{2,1,0:T(8,128)(2,1)S(1)}, u32[]{:S(2)}, u32[]{:S(2)}) collective-permute-start(bf16[4,32,1536]{2,1,0:T(8,128)(2,1)S(1)} %dynamic-slice_bitcast_fusion.31), channel_id=1, source_target_pairs={{0,1},{1,0},{2,3},{3,2},{4,5},{5,4},{6,7},{7,6},{8,9},{9,8},{10,11... | collective-permute-start | bytes 1179656 | tf_op jit(solution)/shard_map/ppermute | solution.py:742
  1079.6 41.2 %collective-permute-start.110 = (bf16[2,32,5120]{2,1,0:T(8,128)(2,1)S(1)}, bf16[2,32,5120]{2,1,0:T(8,128)(2,1)S(1)}, u32[]{:S(2)}, u32[]{:S(2)}) collective-permute-start(bf16[2,32,5120]{2,1,0:T(8,128)(2,1)S(1)} %dynamic-slice_bitcast_fusion.11), channel_id=1, source_target_pairs={{0,16},{1,17},{2,18},{3,19},{4,20},{5,21},{6,22},{7,23},{8,24},{9,... | collective-permute-start | bytes 1966088 | tf_op jit(solution)/shard_map/ppermute | solution.py:742
  1087.1 40.1 %collective-permute-start.103 = (bf16[2,32,3072]{2,1,0:T(8,128)(2,1)S(1)}, bf16[2,32,3072]{2,1,0:T(8,128)(2,1)S(1)}, u32[]{:S(2)}, u32[]{:S(2)}) collective-permute-start(bf16[2,32,3072]{2,1,0:T(8,128)(2,1)S(1)} %dynamic-slice_bitcast_fusion.30), channel_id=1, source_target_pairs={{0,16},{1,17},{2,18},{3,19},{4,20},{5,21},{6,22},{7,23},{8,24},{9,... | collective-permute-start | bytes 1179656 | tf_op jit(solution)/shard_map/ppermute | solution.py:742
  1089.1 39.8 %collective-permute-start.118 = (bf16[32,5632]{1,0:T(8,128)(2,1)S(1)}, bf16[32,5632]{1,0:T(8,128)(2,1)S(1)}, u32[]{:S(2)}, u32[]{:S(2)}) collective-permute-start(bf16[32,5632]{1,0:T(8,128)(2,1)S(1)} %dynamic-slice_bitcast_fusion.36), channel_id=1, source_target_pairs={{0,8},{1,9},{2,10},{3,11},{4,12},{5,13},{6,14},{7,15},{8,0},{9,1},... | collective-permute-start | bytes 1081352 | tf_op jit(solution)/shard_map/ppermute | solution.py:742
  (212 other events, 2768.6 us)

commit v2 on v1

--- a/solution.py
+++ b/solution.py
@@ -758,125 +758,262 @@
 ROUNDS = ((0, 0), (0, 1), (1, 0), (1, 1))
 
 
-def in_order(flag, first, second):
-    return jnp.stack([jnp.where(flag == 0, first, second), jnp.where(flag == 0, second, first)])
-
-
 def take(value, index, axis):
     return lax.dynamic_index_in_dim(value, index, axis, keepdims=False)
 
 
-def assemble_kernel(rows, widths, *refs):
-    pieces, (outs, scratch) = refs[:16], (refs[16 : 16 + len(widths)], refs[16 + len(widths) :])
-    sems_in, sems_out = scratch[-2:]
-    buffers = scratch[0]
-    half = buffers.shape[-1]
-    loads = []
-    for p in range(16):
-        load = pltpu.make_async_copy(pieces[p], buffers.at[p], sems_in.at[p])
+def gather_kernel(count, *refs):
+    shards, wholes = refs[:count], refs[count : 2 * count]
+    local_sem, send_sem, recv_sem = refs[2 * count :]
+    dp, seq = lax.axis_index("dp"), lax.axis_index("seq")
+    z, core, y, x = dp // 2, dp % 2, seq // 2, seq % 2
+    at_z = [{"dp": ((z + k) % 4) * 2 + core, "seq": seq} for k in (1, 2, 3)]
+    at_x = {"dp": dp, "seq": seq + 1 - 2 * x}
+    at_y = {"dp": dp, "seq": seq + 2 - 4 * y}
+    at_core = {"dp": dp + 1 - 2 * core, "seq": seq}
+    partners = at_z + [at_x, at_y, at_core]
+    barrier = pltpu.get_barrier_semaphore()
+    for partner in partners:
+        pl.semaphore_signal(barrier, inc=1, device_id=partner, device_id_type=pl.DeviceIdType.MESH)
+    pl.semaphore_wait(barrier, len(partners))
+
+    def send(w, slot, source, target, device):
+        copy = pltpu.make_async_remote_copy(
+            src_ref=source,
+            dst_ref=target,
+            send_sem=send_sem.at[w, slot],
+            recv_sem=recv_sem.at[w, slot],
+            device_id=device,
+            device_id_type=pl.DeviceIdType.MESH,
+        )
+        copy.start()
+        return copy
+
+    locals_, rounds = [], [[], [], [], []]
+    for w in range(count):
+        own = wholes[w].at[z, core, y, x]
+        copy = pltpu.make_async_copy(shards[w], own, local_sem.at[w])
+        copy.start()
+        locals_.append(copy)
+        rounds[0].append([send(w, k, shards[w], own, at_z[k]) for k in range(3)])
+    for t in range(count + 2):
+        if t < count:
+            w, half = t, wholes[t].shape[-1] // 2
+            left, right = pl.ds(0, half), pl.ds(half, half)
+            locals_[w].wait()
+            for copy in rounds[0][w]:
+                copy.wait_recv()
+            one = wholes[w].at[:, core, y, x, :, left]
+            two = wholes[w].at[:, core, y, x, :, right]
+            rounds[1].append([send(w, 3, one, one, at_x), send(w, 4, two, two, at_y)])
+        if 0 <= t - 1 < count:
+            w, half = t - 1, wholes[t - 1].shape[-1] // 2
+            left, right = pl.ds(0, half), pl.ds(half, half)
+            for copy in rounds[1][w]:
+                copy.wait_recv()
+            one = wholes[w].at[:, core, y, :, :, left]
+            two = wholes[w].at[:, core, :, x, :, right]
+            rounds[2].append([send(w, 5, one, one, at_y), send(w, 6, two, two, at_x)])
+        if 0 <= t - 2 < count:
+            w = t - 2
+            for copy in rounds[2][w]:
+                copy.wait_recv()
+            both = wholes[w].at[:, core]
+            rounds[3].append([send(w, 7, both, both, at_core)])
+    for w in range(count):
+        for copy in rounds[3][w]:
+            copy.wait_recv()
+        for stage in rounds:
+            for copy in stage[w]:
+                copy.wait_send()
+
+
+def gather_weights(shards):
+    count = len(shards)
+    sent = sum(shard.size for shard in shards) * 2
+    wholes = pl.pallas_call(
+        functools.partial(gather_kernel, count),
+        in_specs=[pl.BlockSpec(memory_space=pltpu.VMEM)] * count,
+        out_specs=[pl.BlockSpec(memory_space=pl.ANY)] * count,
+        out_shape=[jax.ShapeDtypeStruct((4, 2, 2, 2, *shard.shape), BF16) for shard in shards],
+        scratch_shapes=[
+            pltpu.SemaphoreType.DMA((count,)),
+            pltpu.SemaphoreType.DMA((count, 8)),
+            pltpu.SemaphoreType.DMA((count, 8)),
+        ],
+        compiler_params=pltpu.CompilerParams(
+            vmem_limit_bytes=VMEM_LIMIT, collective_id=0, has_side_effects=True
+        ),
+        cost_estimate=pl.CostEstimate(flops=0, transcendentals=0, bytes_accessed=500 * sent),
+        name="gather_weights",
+    )(*shards)
+    return [whole.reshape(-1, whole.shape[-1]) for whole in wholes]
+
+
+def add_low(first, second):
+    return (first.astype(F32) + second.astype(F32)).astype(BF16)
+
+
+def scatter_kernel(shapes, *refs):
+    count = len(shapes)
+    grads, sums = refs[:count], refs[count : 2 * count]
+    scratch = refs[2 * count :]
+    kept, got_one, got_two, got_z = (scratch[j * count : (j + 1) * count] for j in range(4))
+    own, totals = scratch[4 * count : 5 * count], scratch[5 * count : 6 * count]
+    load_sem, store_sem, send_sem, recv_sem = scratch[6 * count :]
+    dp, seq = lax.axis_index("dp"), lax.axis_index("seq")
+    z, core, y, x = dp // 2, dp % 2, seq // 2, seq % 2
+    at_z = [{"dp": ((z + k) % 4) * 2 + core, "seq": seq} for k in (1, 2, 3)]
+    at_x = {"dp": dp, "seq": seq + 1 - 2 * x}
+    at_y = {"dp": dp, "seq": seq + 2 - 4 * y}
+    at_core = {"dp": dp + 1 - 2 * core, "seq": seq}
+    partners = at_z + [at_x, at_y, at_core]
+    barrier = pltpu.get_barrier_semaphore()
+    for partner in partners:
+        pl.semaphore_signal(barrier, inc=1, device_id=partner, device_id_type=pl.DeviceIdType.MESH)
+    pl.semaphore_wait(barrier, len(partners))
+
+    def send(w, slot, source, target, device):
+        copy = pltpu.make_async_remote_copy(
+            src_ref=source,
+            dst_ref=target,
+            send_sem=send_sem.at[w, slot],
+            recv_sem=recv_sem.at[w, slot],
+            device_id=device,
+            device_id_type=pl.DeviceIdType.MESH,
+        )
+        copy.start()
+        return copy
+
+    def halves(w):
+        half = shapes[w][1] // 2
+        return pl.ds(0, half), pl.ds(half, half)
+
+    def add(first, second, dtype):
+        return (first.astype(F32) + second.astype(F32)).astype(dtype)
+
+    stages, loads, stores = [[] for _ in range(4)], [], []
+    for w in range(count):
+        stages[0].append([send(w, 0, grads[w].at[:, 1 - core], kept[w], at_core)])
+        load = pltpu.make_async_copy(grads[w].at[:, core], own[w], load_sem.at[w])
         load.start()
         loads.append(load)
-    dp, seq = lax.axis_index("dp"), lax.axis_index("seq")
-    core, x, y = lax.rem(dp, 2), lax.rem(seq, 2), seq // 2
-    stores = []
-    for p in range(16):
-        loads[p].wait()
-        rel_core, column, rel_y, rel_x = p // 8, (p // 4) % 2, (p // 2) % 2, p % 2
-        to_core = lax.rem(core + rel_core, 2)
-        to_y, to_x = lax.rem(y + rel_y, 2), lax.rem(x + rel_x, 2)
-        starts = [sum(widths[:w]) for w in range(len(widths))]
-        for w, start in enumerate(starts):
-            low, high = max(start, column * half), min(start + widths[w], (column + 1) * half)
-            if low >= high:
-                continue
-            store = pltpu.make_async_copy(
-                buffers.at[p, :, :, pl.ds(low - column * half, high - low)],
-                outs[w].at[:, to_core, to_y, to_x, :, pl.ds(low - start, high - low)],
-                sems_out.at[p, w],
-            )
+    for t in range(count + 3):
+        if t < count:
+            w, dtype = t, kept[t].dtype
+            left, right = halves(w)
+            loads[w].wait()
+            stages[0][w][0].wait_recv()
+
+            def core_step(b, carry, w=w, dtype=dtype):
+                zz, yy, xx = b // 4, (b // 2) % 2, b % 2
+                kept[w][zz, yy, xx] = add(kept[w][zz, yy, xx], own[w][zz, yy, xx], dtype)
+                return carry
+
+            lax.fori_loop(0, 16, core_step, 0)
+            half = shapes[w][1] // 2
+            stages[1].append([
+                send(w, 1, kept[w].at[:, :, 1 - x, :, left], got_one[w].at[0], at_x),
+                send(w, 2, kept[w].at[:, 1 - y, :, :, right], got_one[w].at[1], at_y),
+            ])
+        if 0 <= t - 1 < count:
+            w, dtype = t - 1, kept[t - 1].dtype
+            left, right = halves(w)
+            half = shapes[w][1] // 2
+            for copy in stages[1][w]:
+                copy.wait_recv()
+
+            def one_step(b, carry, w=w, dtype=dtype, half=half):
+                zz, other = b // 2, b % 2
+                kept[w][zz, other, x, :, 0:half] = add(
+                    kept[w][zz, other, x, :, 0:half], got_one[w][0, zz, other], dtype
+                )
+                kept[w][zz, y, other, :, half : 2 * half] = add(
+                    kept[w][zz, y, other, :, half : 2 * half], got_one[w][1, zz, other], dtype
+                )
+                return carry
+
+            lax.fori_loop(0, 8, one_step, 0)
+            stages[2].append([
+                send(w, 3, kept[w].at[:, 1 - y, x, :, left], got_two[w].at[0], at_y),
+                send(w, 4, kept[w].at[:, y, 1 - x, :, right], got_two[w].at[1], at_x),
+            ])
+        if 0 <= t - 2 < count:
+            w, dtype = t - 2, kept[t - 2].dtype
+            half = shapes[w][1] // 2
+            for copy in stages[2][w]:
+                copy.wait_recv()
+
+            def two_step(zz, carry, w=w, dtype=dtype, half=half):
+                kept[w][zz, y, x, :, 0:half] = add(
+                    kept[w][zz, y, x, :, 0:half], got_two[w][0, zz], dtype
+                )
+                kept[w][zz, y, x, :, half : 2 * half] = add(
+                    kept[w][zz, y, x, :, half : 2 * half], got_two[w][1, zz], dtype
+                )
+                return carry
+
+            lax.fori_loop(0, 4, two_step, 0)
+            stages[3].append([
+                send(w, 5 + k, kept[w].at[(z + k + 1) % 4, y, x], got_z[w].at[k], at_z[k])
+                for k in range(3)
+            ])
+        if 0 <= t - 3 < count:
+            w = t - 3
+            for copy in stages[3][w]:
+                copy.wait_recv()
+            total = kept[w][z, y, x].astype(F32)
+            for k in range(3):
+                total = total + got_z[w][k].astype(F32)
+            totals[w][...] = total
+            store = pltpu.make_async_copy(totals[w], sums[w], store_sem.at[w])
             store.start()
             stores.append(store)
-    for store in stores:
-        store.wait()
-
-
-def assemble(pieces, widths):
-    rows, half = pieces[0].shape[1:]
-    outs = pl.pallas_call(
-        functools.partial(assemble_kernel, rows, widths),
-        in_specs=[pl.BlockSpec(memory_space=pl.ANY)] * 16,
-        out_specs=[pl.BlockSpec(memory_space=pl.ANY)] * len(widths),
-        out_shape=[jax.ShapeDtypeStruct((4, 2, 2, 2, rows, width), BF16) for width in widths],
-        scratch_shapes=[
-            pltpu.VMEM((16, 4, rows, half), BF16),
-            pltpu.SemaphoreType.DMA((16,)),
-            pltpu.SemaphoreType.DMA((16, len(widths))),
+    for w in range(count):
+        stores[w].wait()
+        for stage in stages:
+            for copy in stage[w]:
+                copy.wait_send()
+
+
+def scatter_grads(grads):
+    count = len(grads)
+    shapes = [(grad.shape[0] // 32, grad.shape[1]) for grad in grads]
+    types = [grad.dtype for grad in grads]
+
+    def buffers(*lead, halved=False):
+        return [
+            pltpu.VMEM((*lead, rows, width // 2 if halved else width), kind)
+            for (rows, width), kind in zip(shapes, types)
+        ]
+
+    return pl.pallas_call(
+        functools.partial(scatter_kernel, shapes),
+        in_specs=[pl.BlockSpec(memory_space=pl.ANY)] * count,
+        out_specs=[pl.BlockSpec(memory_space=pl.ANY)] * count,
+        out_shape=[jax.ShapeDtypeStruct(shape, F32) for shape in shapes],
+        scratch_shapes=buffers(4, 2, 2)
+        + buffers(2, 4, 2, halved=True)
+        + buffers(2, 4, halved=True)
+        + buffers(3)
+        + buffers(4, 2, 2)
+        + [pltpu.VMEM(shape, F32) for shape in shapes]
+        + [
+            pltpu.SemaphoreType.DMA((count,)),
+            pltpu.SemaphoreType.DMA((count,)),
+            pltpu.SemaphoreType.DMA((count, 8)),
+            pltpu.SemaphoreType.DMA((count, 8)),
         ],
-        compiler_params=pltpu.CompilerParams(vmem_limit_bytes=VMEM_LIMIT),
+        compiler_params=pltpu.CompilerParams(
+            vmem_limit_bytes=67043328, collective_id=1, has_side_effects=True
+        ),
         cost_estimate=pl.CostEstimate(
-            flops=0, transcendentals=0, bytes_accessed=4 * 64 * rows * half
+            flops=0, transcendentals=0, bytes_accessed=16 * sum(grad.size for grad in grads)
         ),
-        name="assemble",
-    )(*pieces)
-    return [out.reshape(32 * rows, out.shape[-1]) for out in outs]
-
-
-def gather_weights(shard, widths, place):
-    core, z_low, z_high = place[0], place[1], place[2]
-    low = in_order(z_low, shard, exchange(shard, *Z_LOW))
-    both = in_order(z_high, low, exchange(low, *Z_HIGH)).reshape(4, *shard.shape)
-    half = shard.shape[1] // 2
-    left, right = both[..., :half], both[..., half:]
-    left_x, right_y = exchange(left, *X), exchange(right, *Y)
-    left_y, left_xy = exchange(left, *Y), exchange(left_x, *Y)
-    right_x, right_xy = exchange(right, *X), exchange(right_y, *X)
-    own = [left, left_x, left_y, left_xy, right, right_x, right_y, right_xy]
-    return assemble(own + [exchange(piece, *CORE) for piece in own], widths)
-
-
-def add_low(first, second):
-    return (first.astype(F32) + second.astype(F32)).astype(BF16)
-
-
-def scatter_grads(grads, place):
-    core, z_low, z_high, y, x = place
-    rows, width = grads.shape[0] // 32, grads.shape[1]
-    half = width // 2
-    whole = grads.reshape(4, 2, 2, 2, rows, width)
-    got = exchange(take(whole, 1 - core, 1), *CORE)
-    kept = add_low(take(whole, core, 1), got)
-    left, right = kept[..., :half], kept[..., half:]
-    left_got = exchange(take(left, 1 - x, 2), *X)
-    right_got = exchange(take(right, 1 - y, 1), *Y)
-    left = add_low(take(left, x, 2), left_got)
-    right = add_low(take(right, y, 1), right_got)
-    left_got = exchange(take(left, 1 - y, 1), *Y)
-    right_got = exchange(take(right, 1 - x, 1), *X)
-    left = add_low(take(left, y, 1), left_got)
-    right = add_low(take(right, x, 1), right_got)
-    both = jnp.concatenate([left, right], axis=-1).reshape(2, 2, rows, width)
-    got = exchange(take(both, 1 - z_high, 0), *Z_HIGH)
-    both = add_low(take(both, z_high, 0), got)
-    got = exchange(take(both, 1 - z_low, 0), *Z_LOW)
-    return take(both, z_low, 0).astype(F32) + got.astype(F32)
-
-
-def gather_small(shard, place):
-    core, z_low, z_high, y, x = place
-    value = in_order(x, shard, exchange(shard, *X))
-    value = in_order(y, value, exchange(value, *Y))
-    value = in_order(core, value, exchange(value, *CORE))
-    value = in_order(z_low, value, exchange(value, *Z_LOW))
-    value = in_order(z_high, value, exchange(value, *Z_HIGH))
-    return value.reshape(32, *shard.shape)
-
-
-def scatter_small(value, place):
-    core, z_low, z_high, y, x = place
-    value = value.reshape(2, 2, 2, 2, 2, *value.shape[1:])
-    for flag, link in ((z_high, Z_HIGH), (z_low, Z_LOW), (core, CORE), (y, Y), (x, X)):
-        value = take(value, flag, 0) + exchange(take(value, 1 - flag, 0), *link)
-    return value
+        name="scatter_grads",
+    )(*[
+        grad.reshape(4, 2, 2, 2, rows, width) for grad, (rows, width) in zip(grads, shapes)
+    ])
 
 
 def norm_scale(value):
@@ -985,24 +1122,16 @@
 
     small = jnp.concatenate([norm_self, norm_cross, norm_ff, rel_bias])
     small_rows = norm_self.shape[0]
-    small = gather_small(jnp.pad(small, (0, LANES - small.shape[0])).reshape(1, LANES), place)
-    small = small.reshape(32, LANES).astype(F32)
+    small = jnp.broadcast_to(jnp.pad(small, (0, 2 * LANES - small.shape[0])), (8, 2 * LANES))
+    small, wk, wv, wq, ck, cv, wo, cq, co, w_gate, w_up, w_down = gather_weights(
+        [small, k_self, v_self, q_self, k_cross, v_cross, o_self, q_cross, o_cross, wi_gate, wi_up, wo_ff]
+    )
+    small = small.reshape(32, 8, 2 * LANES)[:, 0].astype(F32)
     gain_self, gain_cross, gain_ff = (
         small[:, j * small_rows : (j + 1) * small_rows].reshape(-1) for j in range(3)
     )
     table = small[:, 3 * small_rows : 3 * small_rows + rel_bias.shape[0]].reshape(BUCKETS, HEADS)
-
-    wq, wkv = gather_weights(
-        jnp.concatenate([q_self, k_self, v_self], axis=1), (width, 2 * width), place
-    )
-    wo, cq, co, ckv = gather_weights(
-        jnp.concatenate([o_self, q_cross, o_cross, k_cross, v_cross], axis=1),
-        (width, width, width, 2 * width),
-        place,
-    )
     ff = wi_gate.shape[1]
-    w_gate, w_up = gather_weights(jnp.concatenate([wi_gate, wi_up], axis=1), (ff, ff), place)
-    (w_down,) = gather_weights(wo_ff, (width,), place)
 
     inputs_low = settle([piece[:part] for piece in bundles]).reshape(4 * part, width)
     encoder = settle([piece[part : part + enc_part] for piece in bundles]).reshape(4 * enc_part, width)
@@ -1036,10 +1165,14 @@
 
     inputs = inputs_low.astype(F32)
     normed_self = normed(inputs, gain_self)
-    kv_own = dot(normed_self, wkv).astype(BF16)
+    kv_own = jnp.concatenate(
+        [dot(normed_self, wk).astype(BF16), dot(normed_self, wv).astype(BF16)], axis=1
+    )
     kv_par = exchange(kv_own, *CORE)
     query = dot(normed_self, wq).astype(BF16)
-    cross_kv_own = dot(encoder, ckv).astype(BF16)
+    cross_kv_own = jnp.concatenate(
+        [dot(encoder, ck).astype(BF16), dot(encoder, cv).astype(BF16)], axis=1
+    )
     cross_kv_par = exchange(cross_kv_own, *CORE)
     mixed, self_lse = attend_fast(kinds, query, kv_own, kv_par, segq, segk, line, True)
     after_self = inputs + dot(mixed, wo)
@@ -1059,14 +1192,11 @@
         send_tokens(lambda micro, b: take(grad_out[:, 0, b * part : (b + 1) * part], micro, 0))
     ).reshape(4 * part, width)
     grad_result = out_low.astype(F32)
-    grad_w_down = scatter_grads(dot_weight(hidden, out_low), place)
+    grad_w_down = dot_weight(hidden, out_low)
     grad_hidden = dot_back(out_low, w_down)
     mix_value, mix_pull = jax.vjp(gelu_mix, gate, up_values)
     grad_gate, grad_up = (piece.astype(BF16) for piece in mix_pull(grad_hidden))
-    grad_w_in = scatter_grads(
-        jnp.concatenate([dot_weight(normed_ff, grad_gate), dot_weight(normed_ff, grad_up)], axis=1),
-        place,
-    )
+    grad_w_gate, grad_w_up = dot_weight(normed_ff, grad_gate), dot_weight(normed_ff, grad_up)
     grad_normed_ff = dot_back(grad_gate, w_gate) + dot_back(grad_up, w_up)
     ff_part, grad_gain_ff = norm_back(after_cross, gain_ff, grad_normed_ff)
     grad_after_cross = grad_result + ff_part
@@ -1078,9 +1208,8 @@
         grad_cross_mixed, cross_mixed, cross_lse, False,
     )
     cross_got = add_low(cross_own, exchange(cross_par, *CORE))
-    grad_cross_kv = jnp.concatenate([cross_got[0], cross_got[1]], axis=1)
-    grad_ckv = dot_weight(encoder, grad_cross_kv)
-    grad_encoder = dot_back(grad_cross_kv, ckv).astype(BF16)
+    grad_ck, grad_cv = dot_weight(encoder, cross_got[0]), dot_weight(encoder, cross_got[1])
+    grad_encoder = (dot_back(cross_got[0], ck) + dot_back(cross_got[1], cv)).astype(BF16)
     grad_encoder = return_tokens(grad_encoder.reshape(4, enc_part, width)).astype(F32)
     grad_cq = dot_weight(normed_cross, grad_cross_query)
     grad_normed_cross = dot_back(grad_cross_query, cq)
@@ -1088,18 +1217,16 @@
     grad_after_self = grad_after_cross + cross_part
     self_out_low = grad_after_self.astype(BF16)
     grad_wo = dot_weight(mixed, self_out_low)
-    grad_middle = scatter_grads(jnp.concatenate([grad_wo, grad_cq, grad_co, grad_ckv], axis=1), place)
     grad_mixed = dot_back(self_out_low, wo).astype(BF16)
     grad_query, self_own, self_par, grad_line, grad_far = attend_back_fast(
         kinds, query, kv_own, kv_par, segq, segk, line, grad_mixed, mixed, self_lse, True
     )
     self_got = add_low(self_own, exchange(self_par, *CORE))
-    grad_kv = jnp.concatenate([self_got[0], self_got[1]], axis=1)
-    grad_qkv = scatter_grads(
-        jnp.concatenate([dot_weight(normed_self, grad_query), dot_weight(normed_self, grad_kv)], axis=1),
-        place,
-    )
-    grad_normed_self = dot_back(grad_query, wq) + dot_back(grad_kv, wkv)
+    grad_wq = dot_weight(normed_self, grad_query)
+    grad_wk, grad_wv = dot_weight(normed_self, self_got[0]), dot_weight(normed_self, self_got[1])
+    grad_normed_self = (
+        dot_back(grad_query, wq) + dot_back(self_got[0], wk) + dot_back(self_got[1], wv)
+    )
     self_part, grad_gain_self = norm_back(inputs, gain_self, grad_normed_self)
     grad_hidden_in = return_tokens((grad_after_self + self_part).astype(BF16).reshape(4, part, width))
 
@@ -1107,26 +1234,35 @@
     grad_table = grad_table.at[BUCKETS - 1].add(jnp.sum(grad_far.reshape(HEADS, TILE), axis=1))
     small_grads = [piece.reshape(32, -1) for piece in (grad_gain_self, grad_gain_cross, grad_gain_ff)]
     small_grads = jnp.concatenate(small_grads + [grad_table.reshape(32, -1)], axis=1)
-    small_grads = jnp.pad(small_grads, ((0, 0), (0, LANES - small_grads.shape[1])))
-    small_grads = scatter_small(small_grads.reshape(32, 1, LANES), place).reshape(-1)
+    small_grads = jnp.pad(small_grads, ((0, 0), (0, 2 * LANES - small_grads.shape[1])))
+    small_grads = jnp.broadcast_to(small_grads[:, None], (32, 8, 2 * LANES)).reshape(256, 2 * LANES)
+    order = [
+        grad_wk, grad_wv, grad_w_gate, grad_w_up, grad_w_down, grad_ck, grad_cv, grad_cq, grad_co,
+        grad_wo, grad_wq, small_grads,
+    ]
+    (
+        grad_wk, grad_wv, grad_w_gate, grad_w_up, grad_w_down, grad_ck, grad_cv, grad_cq, grad_co,
+        grad_wo, grad_wq, small_grads,
+    ) = scatter_grads(order)
+    small_grads = small_grads[0]
     return (
         block_out,
         grad_hidden_in.astype(F32),
         grad_encoder,
         small_grads[:small_rows],
-        grad_qkv[:, :width],
-        grad_qkv[:, width : 2 * width],
-        grad_qkv[:, 2 * width :],
-        grad_middle[:, :width],
+        grad_wq,
+        grad_wk,
+        grad_wv,
+        grad_wo,
         small_grads[3 * small_rows : 3 * small_rows + rel_bias.shape[0]],
         small_grads[small_rows : 2 * small_rows],
-        grad_middle[:, width : 2 * width],
-        grad_middle[:, 3 * width : 4 * width],
-        grad_middle[:, 4 * width :],
-        grad_middle[:, 2 * width : 3 * width],
+        grad_cq,
+        grad_ck,
+        grad_cv,
+        grad_co,
         small_grads[2 * small_rows : 3 * small_rows],
-        grad_w_in[:, :ff],
-        grad_w_in[:, ff:],
+        grad_w_gate,
+        grad_w_up,
         grad_w_down,
     )
 

time: 1150 us -> 976 us (0.85)
  Pallas kernels: 257 us -> 633 us
  waiting for transfers between devices: 331 us -> 41.9 us
  starting transfers between devices: 195 us -> 52.6 us
  local copies, waits for them, and re-layouts: 92.8 us -> 32.8 us
  other arithmetic: 84.5 us -> 32.2 us
    pallas_call x4 -> x2, Pallas kernels: 28.4 us -> 374 us  [the longest x1 200 us: scatter_grads(): pl.pallas_call(functools.partial(scatter_kernel, shapes), in_specs=[pl.Bl...]
    ppermute x106 -> x4, waiting for transfers between devices: 305 us -> 0.01 us  [exchange(): return lax.ppermute(value, AXES, pairs)]
    ppermute x106 -> x4, starting transfers between devices: 121 us -> 11.3 us  [exchange(): return lax.ppermute(value, AXES, pairs)]
    ppermute x12, starting transfers between devices: 57.3 us -> 25.2 us  [return_tokens(): received.append(lax.ppermute(take(value, index, 0), AXES, back))]
    convert_element_type x26 -> x2, other arithmetic: 29.1 us -> 4.84 us  [add_low(): return (first.astype(F32) + second.astype(F32)).astype(BF16)]
    dot_general x9 -> x11, matrix products: 70.7 us -> 52.1 us  [dot(): return jnp.dot(rows, weight, preferred_element_type=F32)]
    dot_general x18 -> x22, matrix products: 106 us -> 123 us  [contract(): lax.dot_general(left, right, (((left_dim,), (right_dim,)), ((), ())), pre...]
    pallas_call x2, Pallas kernels: 126 us -> 143 us  [attend_back_fast(): pl.pallas_call(functools.partial(attend_back_kernel, causal, own_rows, pa...]
  transfers between devices with their start and end apart: 126 -> 24, of which waited for: 45 -> 6; matrix products, arithmetic and copies ran while one was open for 18% -> 6% of each run, Pallas kernels for 14% -> 46%
where the time goes in v2:
time: 976 us; the launch traced here: 971 us
  Pallas kernels  633 us (65%)
  matrix products  176 us (18%)
  starting transfers between devices  52.6 us (5%)
  waiting for transfers between devices  41.9 us (4%)
  local copies, waits for them, and re-layouts  32.8 us (3%)
  other arithmetic  32.2 us (3%)
    pallas_call x1, Pallas kernels, scatter_grads(): pl.pallas_call(functools.partial(scatter_kernel, shapes), in_specs=[pl.Bl...  200 us
    pallas_call x1, Pallas kernels, gather_weights(): pl.pallas_call(functools.partial(gather_kernel, count), in_specs=[pl.Bloc...  174 us
    pallas_call x2, Pallas kernels, attend_back_fast(): pl.pallas_call(functools.partial(attend_back_kernel, causal, own_rows, pa...  143 us
    dot_general x22, matrix products, contract(): lax.dot_general(left, right, (((left_dim,), (right_dim,)), ((), ())), pre...  123 us
    pallas_call x2, Pallas kernels, attend_fast(): pl.pallas_call(functools.partial(attend_kernel, causal, own_rows, par_row...  117 us
    dot_general x11, matrix products, dot(): return jnp.dot(rows, weight, preferred_element_type=F32)  52.1 us
    ppermute x8, waiting for transfers between devices, send_tokens(): lax.ppermute(pieces_of(seq // 2 ^ a, b), AXES, move_pairs(a, b))  25.3 us
    ppermute x12, starting transfers between devices, return_tokens(): received.append(lax.ppermute(take(value, index, 0), AXES, back))  25.2 us
  transfers between devices with their start and end apart: 24, of which 6 were waited for; matrix products, arithmetic and copies ran while one was open for 6% of the time, Pallas kernels for 46%

profile of v2, /device:TPU:0, one launch (start us, length us, event | category | flops | bytes accessed | tf_op | source)
XLA Modules:
  0.0 971.0 jit_solution(8501339893612211183)
XLA Ops:
  0.7 1.8 fusion.84
  5.5 1.9 collective-permute-start
  8.6 1.7 collective-permute-start.10
  11.4 4.9 collective-permute-start.11
  16.5 2.8 collective-permute-start.13
  20.1 174.0 %gather_weights.1 = (bf16[4,2,2,2,8,256]{5,4,3,2,1,0:T(8,128)(2,1)}, bf16[4,2,2,2,32,1024]{5,4,3,2,1,0:T(8,128)(2,1)}, bf16[4,2,2,2,32,1024]{5,4,3,2,1,0:T(8,128...) custom-call(bf16[8,256]{1,0:T(8,128)(2,1)} %broadcast_in_dim.47.refs, ...), custom_call_target="tpu_custom_call" | custom-call | bytes 534528000 | tf_op jit(solution)/shard_map/gather_weights/pallas_call | solution.py:834
  198.6 1.6 collective-permute-start.2
  200.2 2.5 collective-permute-start.3
  203.8 1.7 select_bitcast_fusion.3
  205.6 1.6 pad_maximum_fusion.2
  207.2 8.7 collective-permute-done.1
  217.1 15.4 %collective-permute-done.3 = bf16[336,1024]{1,0:T(8,128)(2,1)S(1)} collective-permute-done((bf16[336,1024]{1,0:T(8,128)(2,1)}, bf16[336,1024]{1,0:T(8,128)(2,1)S(1)}, u32[]{:S(2)}, u32[]{:S(2)}) %collective-permute-start.3) | collective-permute-done | bytes 688160 | tf_op jit(solution)/shard_map/ppermute | solution.py:1081
  235.3 2.3 convolution_convert_fusion.15
  237.6 2.3 convolution_convert_fusion.14
  240.0 2.5 pad_maximum_fusion.ko.vo
  246.7 2.5 convolution_convert_fusion.18
  252.5 5.9 convolution_convert_fusion.16.q_ref
  260.3 73.2 %attend_self.1 = (bf16[1024,1024]{1,0:T(8,128)(2,1)}, f32[4,4,1024]{2,1,0:T(4,128)}) custom-call(s32[32]{0:T(128)} %select_n.606.kinds_ref, bf16[1024,1024]{1,0:T(8,128)(2,1)} %convolution_convert_fusion.16.q_ref, bf16[1024,2048]{1,0:T(8,128)(2,1)} %pad_maximum_fusion.ko.vo, bf16[1024,2048]{1,0:T(8,128)(2,1)} %pad_maximum_fusion.ko.vo, ...), custom_call_target="tpu_custom_call" | custom-call | flops 8589934592 | bytes 12582912 | tf_op jit(solution)/shard_map/attend_self/pallas_call | solution.py:648
  333.5 4.8 multiply_reduce_fusion.5
  338.3 3.7 convolution_convert_fusion.13.q_ref
  342.9 44.1 %attend_cross.1 = (bf16[1024,1024]{1,0:T(8,128)(2,1)}, f32[4,4,1024]{2,1,0:T(4,128)}) custom-call(s32[32]{0:T(128)} %select_n.606.kinds_ref, bf16[1024,1024]{1,0:T(8,128)(2,1)} %convolution_convert_fusion.13.q_ref, bf16[256,2048]{1,0:T(8,128)(2,1)} %copy-done.27, bf16[256,2048]{1,0:T(8,128)(2,1)} %copy-done.27, ...), custom_call_target="tpu_custom_call" | custom-call | flops 2147483648 | bytes 6291456 | tf_op jit(solution)/shard_map/attend_cross/pallas_call | solution.py:648
  387.0 5.4 multiply_reduce_fusion.4
  392.4 2.0 copy-done.6
  394.9 9.2 fusion.88
  404.1 8.9 fusion.87
  413.0 21.8 %multiply_convert_fusion = (bf16[1024,2816]{1,0:T(8,128)(2,1)}, bf16[1024,2816]{1,0:T(8,128)(2,1)}, bf16[1024,2816]{1,0:T(8,128)(2,1)}) fusion(f32[1024,2816]{1,0:T(8,128)} %fusion.87, f32[1024,2816]{1,0:T(8,128)} %fusion.88, bf16[1024,1024]{1,0:T(8,128)(2,1)S(1)} %bitcast.256, bf16[2816,1024]{1,0:T(8,128)(2,1)} %bitcast.295), kind=kOutput, calls=%fused_computation.9 | convolution fusion | flops 5980553216 | bytes 48234496 | tf_op jit(solution)/shard_map/dot_general | solution.py:397
  434.8 10.0 %fusion.89 = f32[1024,1024]{1,0:T(8,128)S(1)} fusion(bf16[1024,2816]{1,0:T(8,128)(2,1)} %get-tuple-element.121, bf16[1024,2816]{1,0:T(8,128)(2,1)} %bitcast.303), kind=kOutput, calls=%fused_computation.297 | convolution fusion | flops 5905580032 | bytes 15728640 | tf_op jit(solution)/shard_map/dot_general | solution.py:397
  444.8 9.0 multiply_reduce_fusion
  453.8 1.7 subtract_add_fusion.1
  455.5 3.7 convolution_convert_fusion.12.do_ref
  459.2 52.7 %attend_cross_back.1 = (bf16[1024,1024]{1,0:T(8,128)(2,1)}, bf16[2,256,1024]{2,1,0:T(8,128)(2,1)}, bf16[2,256,1024]{2,1,0:T(8,128)(2,1)}, f32[16,1,256]{2,1,0:T(1,128)}, f32[16,1,256]{2,1,0:T(1,128)}) custom-call(s32[32]{0:T(128)} %select_n.606.kinds_ref, bf16[1024,1024]{1,0:T(8,128)(2,1)} %convolution_convert_fusion.13.q_ref, bf16[256,2048]{1,0:T(8,128)(2,1)} %copy-done.27, ...), custom_call_target="tpu_custom_call" | custom-call | flops 5368709120 | bytes 15728640 | tf_op jit(solution)/shard_map/attend_cross_back/pallas_call | solution.py:690
  511.9 6.3 multiply_reduce_fusion.1
  518.2 3.9 convolution_convert_fusion.6
  523.7 3.7 convolution_convert_fusion.11.do_ref
  527.4 3.7 convolution_convert_fusion.4
  531.2 3.8 convolution_convert_fusion.5
  535.0 8.3 convolution_convert_fusion.2
  543.4 8.8 convolution_convert_fusion.1
  552.2 8.1 convolution_convert_fusion
  560.3 6.3 add_convert_fusion.1
  566.6 89.9 %attend_self_back.1 = (bf16[1024,1024]{1,0:T(8,128)(2,1)}, bf16[2,1024,1024]{2,1,0:T(8,128)(2,1)}, bf16[2,1024,1024]{2,1,0:T(8,128)(2,1)}, f32[16,1,256]{2,1,0:T(1,128)}, f32[16,1,256]{2,1,0:T(1,128)}) custom-call(s32[32]{0:T(128)} %select_n.606.kinds_ref, bf16[1024,1024]{1,0:T(8,128)(2,1)} %convolution_convert_fusion.16.q_ref, ...), custom_call_target="tpu_custom_call" | custom-call | flops 21474836480 | bytes 31457280 | tf_op jit(solution)/shard_map/attend_self_back/pallas_call | solution.py:690
  656.5 10.7 %collective-permute-start.14 = (bf16[2,1024,1024]{2,1,0:T(8,128)(2,1)}, bf16[2,1024,1024]{2,1,0:T(8,128)(2,1)}, u32[]{:S(2)}, u32[]{:S(2)}) collective-permute-start(bf16[2,1024,1024]{2,1,0:T(8,128)(2,1)} %get-tuple-element.85), channel_id=1, source_target_pairs={{0,4},{1,5},{2,6},{3,7},{4,0},{5,1},{6,2},{7,3},{8,12},{9,13},{10,... | collective-permute-start | bytes 12582920 | tf_op jit(solution)/shard_map/ppermute | solution.py:742
  668.6 1.7 collective-permute-start.6
  670.3 2.1 collective-permute-start.7
  672.4 4.4 fusion.90
  676.8 3.7 collective-permute-start.9
  681.5 10.4 %collective-permute-done.7 = bf16[256,1024]{1,0:T(8,128)(2,1)S(1)} collective-permute-done((bf16[256,1024]{1,0:T(8,128)(2,1)}, bf16[256,1024]{1,0:T(8,128)(2,1)S(1)}, u32[]{:S(2)}, u32[]{:S(2)}) %collective-permute-start.7) | collective-permute-done | bytes 524320 | tf_op jit(solution)/shard_map/ppermute | solution.py:1096
  691.9 3.4 collective-permute-done.9
  700.4 3.9 collective-permute-start.21
  704.3 2.2 convolution_convert_fusion.7
  706.5 2.0 convolution_convert_fusion.8
  709.0 3.4 collective-permute-start.23
  712.5 2.8 collective-permute-done.23
  716.4 4.4 add_convert_fusion
  720.8 2.4 fusion.19
  723.2 3.8 convolution_convert_fusion.9
  727.0 3.8 convolution_convert_fusion.10
  730.8 5.8 fusion.18
  736.7 6.1 convolution_convert_fusion.3
  745.6 5.4 collective-permute-start.15
  751.1 2.1 collective-permute-start.17
  753.2 1.9 collective-permute-start.18
  755.8 199.6 %scatter_grads.1 = (f32[32,1024]{1,0:T(8,128)}, f32[32,1024]{1,0:T(8,128)}, f32[32,2816]{1,0:T(8,128)}, f32[32,2816]{1,0:T(8,128)}, f32[88,1024]{1,0:T(8,128)}, ...) custom-call(bf16[4,2,2,2,32,1024]{5,4,3,2,1,0:T(8,128)(2,1)} %bitcas, ...), custom_call_target="tpu_custom_call" | custom-call | bytes 273678336 | tf_op jit(solution)/shard_map/scatter_grads/pallas_call | solution.py:990
  960.9 2.3 maximum_convert_fusion
  (332 shorter events, 53.2 us)
Async XLA Ops:
  5.5 13.8 %copy-start.51 = (bf16[16]{0:T(256)(128)(2,1)S(1)}, bf16[16]{0:T(256)(128)(2,1)}, u32[]{:S(2)}) copy-start(bf16[16]{0:T(256)(128)(2,1)} %param.32) | copy-start | bytes 100
  5.5 13.8 %copy-start.52 = (bf16[32]{0:T(256)(128)(2,1)S(1)}, bf16[32]{0:T(256)(128)(2,1)}, u32[]{:S(2)}) copy-start(bf16[32]{0:T(256)(128)(2,1)} %param.38) | copy-start | bytes 196
  5.5 13.8 %copy-start.53 = (bf16[32]{0:T(256)(128)(2,1)S(1)}, bf16[32]{0:T(256)(128)(2,1)}, u32[]{:S(2)}) copy-start(bf16[32]{0:T(256)(128)(2,1)} %param.33) | copy-start | bytes 196
  5.5 13.9 %copy-start.54 = (bf16[32]{0:T(256)(128)(2,1)S(1)}, bf16[32]{0:T(256)(128)(2,1)}, u32[]{:S(2)}) copy-start(bf16[32]{0:T(256)(128)(2,1)} %param.27) | copy-start | bytes 196
  5.5 201.7 %collective-permute-start = (bf16[336,1024]{1,0:T(8,128)(2,1)}, bf16[336,1024]{1,0:T(8,128)(2,1)S(1)}, u32[]{:S(2)}, u32[]{:S(2)}) collective-permute-start(bf16[336,1024]{1,0:T(8,128)(2,1)} %get-tuple-element.182), channel_id=1, source_target_pairs={{0,0},{1,4},{2,1},{3,5},{4,2},{5,6},{6,3},{7,7},{8,8},{9,12},{10,9... | collective-permute-start | bytes 2064392 | tf_op jit(solution)/shard_map/ppermute | solution.py:1081
  8.6 187.9 %collective-permute-start.10 = (bf16[256,1024]{1,0:T(8,128)(2,1)}, bf16[256,1024]{1,0:T(8,128)(2,1)S(1)}, u32[]{:S(2)}, u32[]{:S(2)}) collective-permute-start(bf16[256,1024]{1,0:T(8,128)(2,1)} %get-tuple-element.158), channel_id=1, source_target_pairs={{0,0},{1,4},{2,1},{3,5},{4,2},{5,6},{6,3},{7,7},{8,8},{9,12},{10,9... | collective-permute-start | bytes 1572872 | tf_op jit(solution)/shard_map/ppermute | solution.py:1081
  11.4 186.4 %collective-permute-start.11 = (bf16[256,1024]{1,0:T(8,128)(2,1)}, bf16[256,1024]{1,0:T(8,128)(2,1)S(1)}, u32[]{:S(2)}, u32[]{:S(2)}) collective-permute-start(bf16[256,1024]{1,0:T(8,128)(2,1)} %get-tuple-element.156), channel_id=1, source_target_pairs={{0,4},{1,0},{2,5},{3,1},{4,6},{5,2},{6,7},{7,3},{8,12},{9,8},{10,1... | collective-permute-start | bytes 1572872 | tf_op jit(solution)/shard_map/ppermute | solution.py:1081
  16.3 183.9 %collective-permute-start.12 = (bf16[256,1024]{1,0:T(8,128)(2,1)}, bf16[256,1024]{1,0:T(8,128)(2,1)}, u32[]{:S(2)}, u32[]{:S(2)}) collective-permute-start(bf16[256,1024]{1,0:T(8,128)(2,1)} %get-tuple-element.159), channel_id=1, source_target_pairs={{0,1},{1,5},{2,0},{3,4},{4,3},{5,7},{6,2},{7,6},{8,9},{9,13},{10,8... | collective-permute-start | bytes 1572872 | tf_op jit(solution)/shard_map/ppermute | solution.py:1081
  16.5 187.3 %collective-permute-start.13 = (bf16[256,1024]{1,0:T(8,128)(2,1)}, bf16[256,1024]{1,0:T(8,128)(2,1)}, u32[]{:S(2)}, u32[]{:S(2)}) collective-permute-start(bf16[256,1024]{1,0:T(8,128)(2,1)} %get-tuple-element.157), channel_id=1, source_target_pairs={{0,5},{1,1},{2,4},{3,0},{4,7},{5,3},{6,6},{7,2},{8,13},{9,9},{10,1... | collective-permute-start | bytes 1572872 | tf_op jit(solution)/shard_map/ppermute | solution.py:1081
  19.3 177.3 %copy-start.64 = (s32[256]{0:T(256)}, s32[256]{0:T(256)S(1)}, u32[]{:S(2)}) copy-start(s32[256]{0:T(256)S(1)} %iota_select_fusion) | copy-start | bytes 3076
  197.4 18.5 %collective-permute-start.1 = (bf16[336,1024]{1,0:T(8,128)(2,1)}, bf16[336,1024]{1,0:T(8,128)(2,1)S(1)}, u32[]{:S(2)}, u32[]{:S(2)}) collective-permute-start(bf16[336,1024]{1,0:T(8,128)(2,1)} %get-tuple-element.183), channel_id=1, source_target_pairs={{0,4},{1,0},{2,5},{3,1},{4,6},{5,2},{6,7},{7,3},{8,12},{9,8},{10,1... | collective-permute-start | bytes 2064392 | tf_op jit(solution)/shard_map/ppermute | solution.py:1081
  198.6 18.5 %collective-permute-start.2 = (bf16[336,1024]{1,0:T(8,128)(2,1)}, bf16[336,1024]{1,0:T(8,128)(2,1)S(1)}, u32[]{:S(2)}, u32[]{:S(2)}) collective-permute-start(bf16[336,1024]{1,0:T(8,128)(2,1)} %get-tuple-element.184), channel_id=1, source_target_pairs={{0,1},{1,5},{2,0},{3,4},{4,3},{5,7},{6,2},{7,6},{8,9},{9,13},{10,8... | collective-permute-start | bytes 2064392 | tf_op jit(solution)/shard_map/ppermute | solution.py:1081
  200.2 32.3 %collective-permute-start.3 = (bf16[336,1024]{1,0:T(8,128)(2,1)}, bf16[336,1024]{1,0:T(8,128)(2,1)S(1)}, u32[]{:S(2)}, u32[]{:S(2)}) collective-permute-start(bf16[336,1024]{1,0:T(8,128)(2,1)} %get-tuple-element.185), channel_id=1, source_target_pairs={{0,5},{1,1},{2,4},{3,0},{4,7},{5,3},{6,6},{7,2},{8,13},{9,9},{10,1... | collective-permute-start | bytes 2064392 | tf_op jit(solution)/shard_map/ppermute | solution.py:1081
  203.0 30.9 %copy-start.45 = (f32[1024]{0:T(1024)}, f32[1024]{0:T(1024)S(1)}, u32[]{:S(2)}) copy-start(f32[1024]{0:T(1024)S(1)} %mul.397) | copy-start | bytes 12292
  217.1 15.7 %copy-start.16 = (bf16[336,1024]{1,0:T(8,128)(2,1)}, bf16[336,1024]{1,0:T(8,128)(2,1)S(1)}, u32[]{:S(2)}) copy-start(bf16[336,1024]{1,0:T(8,128)(2,1)S(1)} %collective-permute-done.2) | copy-start | bytes 2064388
  233.9 99.6 %copy-start = (bf16[4,256,1024]{2,1,0:T(8,128)(2,1)}, bf16[4,256,1024]{2,1,0:T(8,128)(2,1)S(1)}, u32[]{:S(2)}) copy-start(bf16[4,256,1024]{2,1,0:T(8,128)(2,1)S(1)} %get-tuple-element.119) | copy-start | bytes 6291460
  242.4 15.9 %collective-permute-start.4 = (bf16[1024,2048]{1,0:T(8,128)(2,1)}, bf16[1024,2048]{1,0:T(8,128)(2,1)}, u32[]{:S(2)}, u32[]{:S(2)}) collective-permute-start(bf16[1024,2048]{1,0:T(8,128)(2,1)} %pad_maximum_fusion.ko.vo), channel_id=1, source_target_pairs={{0,4},{1,5},{2,6},{3,7},{4,0},{5,1},{6,2},{7,3},{8,12},{9,13},{10,... | collective-permute-start | bytes 12582920 | tf_op jit(solution)/shard_map/ppermute | solution.py:742
  250.1 8.3 copy-start.27
  250.1 92.0 %collective-permute-start.5 = (bf16[256,2048]{1,0:T(8,128)(2,1)S(1)}, bf16[256,2048]{1,0:T(8,128)(2,1)}, u32[]{:S(2)}, u32[]{:S(2)}) collective-permute-start(bf16[256,2048]{1,0:T(8,128)(2,1)S(1)} %pad_maximum_fusion.3.ko.vo), channel_id=1, source_target_pairs={{0,4},{1,5},{2,6},{3,7},{4,0},{5,1},{6,2},{7,3},{8,12},{9,13},{10,... | collective-permute-start | bytes 3145736 | tf_op jit(solution)/shard_map/ppermute | solution.py:742
  251.9 6.5 copy-start.43
  342.1 44.9 %copy-start.62 = (bf16[4,2,2,2,32,1024]{5,4,3,2,1,0:T(8,128)(2,1)S(1)}, bf16[4,2,2,2,32,1024]{5,4,3,2,1,0:T(8,128)(2,1)}, u32[]{:S(2)}) copy-start(bf16[4,2,2,2,32,1024]{5,4,3,2,1,0:T(8,128)(2,1)} %get-tuple-element.76) | copy-start | bytes 6291460
  387.0 7.8 slice-start.2
  387.0 7.8 slice-start.3
  394.4 9.7 slice-start.4
  394.8 9.2 copy-start.24
  394.9 9.2 slice-start.5
  404.1 8.9 copy-start.9
  434.8 10.0 %copy-start.7 = (f32[1024,1024]{1,0:T(8,128)S(1)}, f32[1024,1024]{1,0:T(8,128)}, u32[]{:S(2)}) copy-start(f32[1024,1024]{1,0:T(8,128)} %copy-done.6) | copy-start | bytes 12582916
  434.8 10.0 %copy-start.72 = (bf16[1024,2816]{1,0:T(8,128)(2,1)S(1)}, bf16[1024,2816]{1,0:T(8,128)(2,1)}, u32[]{:S(2)}) copy-start(bf16[1024,2816]{1,0:T(8,128)(2,1)} %get-tuple-element.120) | copy-start | bytes 17301508
  511.9 6.3 copy-start.14
  511.9 6.3 copy-start.69
  527.4 7.6 slice-start.8
  531.2 12.2 %slice-start.6 = ((s8[5767168]{0:T(1024)(128)(4,1)}), s8[4194304]{0:T(1024)(128)(4,1)S(1)}, s32[]{:S(2)}) async-start(s8[5767168]{0:T(1024)(128)(4,1)} %bitcast.319), calls=%async_computation.6 | async-start | bytes 8388608
  535.0 8.4 slice-start.7
  535.0 17.1 %slice-start.10 = ((s8[5767168]{0:T(1024)(128)(4,1)}), s8[1572864]{0:T(1024)(128)(4,1)S(1)}, s32[]{:S(2)}) async-start(s8[5767168]{0:T(1024)(128)(4,1)} %bitcast.323), calls=%async_computation.10 | async-start | bytes 3145728
  543.4 8.8 slice-start.11
  543.4 16.9 %slice-start = ((s8[5767168]{0:T(1024)(128)(4,1)}), s8[4194304]{0:T(1024)(128)(4,1)S(1)}, s32[]{:S(2)}) async-start(s8[5767168]{0:T(1024)(128)(4,1)} %bitcast.296), calls=%async_computation | async-start | bytes 8388608
  552.2 8.1 copy-start.8
  552.2 8.1 slice-start.1
  656.5 15.9 %copy-start.59 = (bf16[4,2,2,2,32,1024]{5,4,3,2,1,0:T(8,128)(2,1)S(1)}, bf16[4,2,2,2,32,1024]{5,4,3,2,1,0:T(8,128)(2,1)}, u32[]{:S(2)}) copy-start(bf16[4,2,2,2,32,1024]{5,4,3,2,1,0:T(8,128)(2,1)} %get-tuple-element.67) | copy-start | bytes 6291460
  656.5 15.9 %copy-start.71 = (bf16[1024,1024]{1,0:T(8,128)(2,1)S(1)}, bf16[1024,1024]{1,0:T(8,128)(2,1)}, u32[]{:S(2)}) copy-start(bf16[1024,1024]{1,0:T(8,128)(2,1)} %get-tuple-element.83) | copy-start | bytes 6291460
  656.5 59.9 %collective-permute-start.14 = (bf16[2,1024,1024]{2,1,0:T(8,128)(2,1)}, bf16[2,1024,1024]{2,1,0:T(8,128)(2,1)}, u32[]{:S(2)}, u32[]{:S(2)}) collective-permute-start(bf16[2,1024,1024]{2,1,0:T(8,128)(2,1)} %get-tuple-element.85), channel_id=1, source_target_pairs={{0,4},{1,5},{2,6},{3,7},{4,0},{5,1},{6,2},{7,3},{8,12},{9,13},{10,... | collective-permute-start | bytes 12582920 | tf_op jit(solution)/shard_map/ppermute | solution.py:742
  668.6 12.4 %collective-permute-start.6 = (bf16[256,1024]{1,0:T(8,128)(2,1)}, bf16[256,1024]{1,0:T(8,128)(2,1)S(1)}, u32[]{:S(2)}, u32[]{:S(2)}) collective-permute-start(bf16[256,1024]{1,0:T(8,128)(2,1)} %get-tuple-element.149), channel_id=1, source_target_pairs={{0,0},{4,1},{1,2},{5,3},{2,4},{6,5},{3,6},{7,7},{8,8},{12,9},{9,10... | collective-permute-start | bytes 1572872 | tf_op jit(solution)/shard_map/ppermute | solution.py:1096
  670.3 21.5 %collective-permute-start.7 = (bf16[256,1024]{1,0:T(8,128)(2,1)}, bf16[256,1024]{1,0:T(8,128)(2,1)S(1)}, u32[]{:S(2)}, u32[]{:S(2)}) collective-permute-start(bf16[256,1024]{1,0:T(8,128)(2,1)} %get-tuple-element.146), channel_id=1, source_target_pairs={{1,0},{5,1},{0,2},{4,3},{3,4},{7,5},{2,6},{6,7},{9,8},{13,9},{8,10... | collective-permute-start | bytes 1572872 | tf_op jit(solution)/shard_map/ppermute | solution.py:1096
  672.4 8.1 copy-start.65
  672.4 8.1 copy-start.66
  672.4 8.3 copy-start.48
  676.8 15.1 %collective-permute-start.8 = (bf16[256,1024]{1,0:T(8,128)(2,1)}, bf16[256,1024]{1,0:T(8,128)(2,1)S(1)}, u32[]{:S(2)}, u32[]{:S(2)}) collective-permute-start(bf16[256,1024]{1,0:T(8,128)(2,1)} %get-tuple-element.148), channel_id=1, source_target_pairs={{4,0},{0,1},{5,2},{1,3},{6,4},{2,5},{7,6},{3,7},{12,8},{8,9},{13,1... | collective-permute-start | bytes 1572872 | tf_op jit(solution)/shard_map/ppermute | solution.py:1096
  676.8 18.6 %collective-permute-start.9 = (bf16[256,1024]{1,0:T(8,128)(2,1)}, bf16[256,1024]{1,0:T(8,128)(2,1)S(1)}, u32[]{:S(2)}, u32[]{:S(2)}) collective-permute-start(bf16[256,1024]{1,0:T(8,128)(2,1)} %get-tuple-element.147), channel_id=1, source_target_pairs={{5,0},{1,1},{4,2},{0,3},{7,4},{3,5},{6,6},{2,7},{13,8},{9,9},{12,1... | collective-permute-start | bytes 1572872 | tf_op jit(solution)/shard_map/ppermute | solution.py:1096
  681.0 16.1 %collective-permute-start.19 = (bf16[2,256,1024]{2,1,0:T(8,128)(2,1)}, bf16[2,256,1024]{2,1,0:T(8,128)(2,1)S(1)}, u32[]{:S(2)}, u32[]{:S(2)}) collective-permute-start(bf16[2,256,1024]{2,1,0:T(8,128)(2,1)} %get-tuple-element.87), channel_id=1, source_target_pairs={{0,4},{1,5},{2,6},{3,7},{4,0},{5,1},{6,2},{7,3},{8,12},{9,13},{10,... | collective-permute-start | bytes 3145736 | tf_op jit(solution)/shard_map/ppermute | solution.py:742
  699.7 12.7 %collective-permute-start.20 = (bf16[64,1024]{1,0:T(8,128)(2,1)S(1)}, bf16[64,1024]{1,0:T(8,128)(2,1)S(1)}, u32[]{:S(2)}, u32[]{:S(2)}) collective-permute-start(bf16[64,1024]{1,0:T(8,128)(2,1)S(1)} %get-tuple-element.171), channel_id=1, source_target_pairs={{0,0},{4,1},{1,2},{5,3},{2,4},{6,5},{3,6},{7,7},{8,8},{12,9},{9,10... | collective-permute-start | bytes 393224 | tf_op jit(solution)/shard_map/ppermute | solution.py:1096
  700.4 12.1 %collective-permute-start.21 = (bf16[64,1024]{1,0:T(8,128)(2,1)S(1)}, bf16[64,1024]{1,0:T(8,128)(2,1)S(1)}, u32[]{:S(2)}, u32[]{:S(2)}) collective-permute-start(bf16[64,1024]{1,0:T(8,128)(2,1)S(1)} %get-tuple-element.168), channel_id=1, source_target_pairs={{1,0},{5,1},{0,2},{4,3},{3,4},{7,5},{2,6},{6,7},{9,8},{13,9},{8,10... | collective-permute-start | bytes 393224 | tf_op jit(solution)/shard_map/ppermute | solution.py:1096
  706.5 9.9 %copy-start.12 = (bf16[2,1024,1024]{2,1,0:T(8,128)(2,1)S(1)}, bf16[2,1024,1024]{2,1,0:T(8,128)(2,1)}, u32[]{:S(2)}) copy-start(bf16[2,1024,1024]{2,1,0:T(8,128)(2,1)} %get-tuple-element.84) | copy-start | bytes 12582916
  708.5 3.9 collective-permute-start.22
  709.0 6.3 collective-permute-start.23
  745.6 212.5 %collective-permute-start.15 = (bf16[256,1024]{1,0:T(8,128)(2,1)}, bf16[256,1024]{1,0:T(8,128)(2,1)}, u32[]{:S(2)}, u32[]{:S(2)}) collective-permute-start(bf16[256,1024]{1,0:T(8,128)(2,1)} %get-tuple-element.139), channel_id=1, source_target_pairs={{0,0},{4,1},{1,2},{5,3},{2,4},{6,5},{3,6},{7,7},{8,8},{12,9},{9,10... | collective-permute-start | bytes 1572872 | tf_op jit(solution)/shard_map/ppermute | solution.py:1096
  751.0 207.1 %collective-permute-start.16 = (bf16[256,1024]{1,0:T(8,128)(2,1)}, bf16[256,1024]{1,0:T(8,128)(2,1)}, u32[]{:S(2)}, u32[]{:S(2)}) collective-permute-start(bf16[256,1024]{1,0:T(8,128)(2,1)} %get-tuple-element.136), channel_id=1, source_target_pairs={{1,0},{5,1},{0,2},{4,3},{3,4},{7,5},{2,6},{6,7},{9,8},{13,9},{8,10... | collective-permute-start | bytes 1572872 | tf_op jit(solution)/shard_map/ppermute | solution.py:1096
  751.1 208.3 %collective-permute-start.17 = (bf16[256,1024]{1,0:T(8,128)(2,1)}, bf16[256,1024]{1,0:T(8,128)(2,1)}, u32[]{:S(2)}, u32[]{:S(2)}) collective-permute-start(bf16[256,1024]{1,0:T(8,128)(2,1)} %get-tuple-element.138), channel_id=1, source_target_pairs={{4,0},{0,1},{5,2},{1,3},{6,4},{2,5},{7,6},{3,7},{12,8},{8,9},{13,1... | collective-permute-start | bytes 1572872 | tf_op jit(solution)/shard_map/ppermute | solution.py:1096
  753.2 206.2 %collective-permute-start.18 = (bf16[256,1024]{1,0:T(8,128)(2,1)}, bf16[256,1024]{1,0:T(8,128)(2,1)}, u32[]{:S(2)}, u32[]{:S(2)}) collective-permute-start(bf16[256,1024]{1,0:T(8,128)(2,1)} %get-tuple-element.137), channel_id=1, source_target_pairs={{5,0},{1,1},{4,2},{0,3},{7,4},{3,5},{6,6},{2,7},{13,8},{9,9},{12,1... | collective-permute-start | bytes 1572872 | tf_op jit(solution)/shard_map/ppermute | solution.py:1096
  960.9 6.3 copy-start.36
  960.9 6.9 copy-start.35
  960.9 7.6 copy-start.34
  960.9 8.3 copy-start.33
  960.9 9.0 copy-start.32
  (45 other events, 150.5 us)

commit v3 on v2

--- a/solution.py
+++ b/solution.py
@@ -387,8 +387,9 @@
 
 
 TILE = 256
-GROUP = 4
+GROUP = 8
 LANES = 128
+AHEAD = 2
 F32 = jnp.float32
 BF16 = jnp.bfloat16
 
@@ -424,127 +425,190 @@
     return line
 
 
-def allowed_keys(segq, segk_ref, row, diagonal):
-    segk = segk_ref[pl.ds(row, TILE), :]
-    segk = jnp.concatenate([segk] * (TILE // LANES), axis=1)
-    same = segk == segq
-    if diagonal:
-        k_pos = lax.broadcasted_iota(jnp.int32, (TILE, TILE), 0)
-        q_pos = lax.broadcasted_iota(jnp.int32, (TILE, TILE), 1)
-        same = same & (k_pos <= q_pos)
-    return same
+def positions():
+    return (
+        lax.broadcasted_iota(jnp.int32, (TILE, TILE), 0),
+        lax.broadcasted_iota(jnp.int32, (TILE, TILE), 1),
+    )
 
 
 def pair_lanes(head):
     return slice((head // 2) * LANES, (head // 2 + 1) * LANES)
 
 
-def load_keys(refs, own_rows, par_rows, kb, vb):
-    ko, vo, kp, vp = refs
-    kb[0:own_rows, :] = ko[...]
-    vb[0:own_rows, :] = vo[...]
-    kb[own_rows : own_rows + par_rows, :] = kp[...]
-    vb[own_rows : own_rows + par_rows, :] = vp[...]
+def head_rows(head):
+    return slice(head * HEAD_DIM, (head + 1) * HEAD_DIM)
+
+
+def place_tiles(causal, meta_ref, own, par):
+    moves = []
+    count = own.shape[0] // TILE
+    for ref, base in ((own, 0), (par, count)):
+        for s in range(count):
+            target = meta_ref[base + s] + 1 if causal else base + s
+            moves.append((ref, s, target))
+    return moves
+
+
+def rows_at(tile):
+    return pl.ds(pl.multiple_of(tile * TILE, TILE), TILE)
 
 
 def fill_tables(line_ref, tab, adj):
     for h in range(GROUP):
         line = line_ref[h]
-        for r, rows in enumerate(bias_table(line)):
-            tab[h, 8 * r : 8 * r + 8, :] = rows
-        table = tab[h]
-        k_pos = lax.broadcasted_iota(jnp.int32, (TILE, TILE), 0)
-        q_pos = lax.broadcasted_iota(jnp.int32, (TILE, TILE), 1)
-        adj[h] = jnp.where(k_pos > q_pos, table, line[:, TILE - 1 : TILE])
-
-
-def visit_tiles(causal, kinds_ref, tile, tiles):
+        far = line[:, TILE - 1 : TILE]
+        for r, rows in enumerate(bias_table(line - far)):
+            adj[h, 8 * r : 8 * r + 8, :] = rows
+        k_pos, q_pos = positions()
+        table = adj[h]
+        tab[h] = jnp.where(k_pos <= q_pos, table, NEG)
+        adj[h] = jnp.where(k_pos > q_pos, table, 0.0)
+
+
+BIAS_LANE, EMPTY_LANE = 16, 17
+
+
+def lane_of():
+    return lax.broadcasted_iota(jnp.int32, (1, LANES), 1) % HEAD_DIM
+
+
+def by_parity(lanes):
+    even = (jnp.arange(LANES) < HEAD_DIM)[None, :]
+    zero = jnp.zeros_like(lanes)
+    return jnp.stack([jnp.where(even, zero, lanes), jnp.where(even, lanes, zero)])
+
+
+def key_lanes(codes):
+    lane = jnp.arange(LANES, dtype=jnp.int32)[None, :] % HEAD_DIM
+    documents = (codes[:, None] == lane) & (lane < BIAS_LANE)
+    ones = (lane >= BIAS_LANE) & (lane < EMPTY_LANE)
+    return by_parity((documents | ones | ((lane == EMPTY_LANE) & (codes[:, None] < 0))).astype(BF16))
+
+
+def query_lanes(codes):
+    lane = jnp.arange(LANES, dtype=jnp.int32)[None, :] % HEAD_DIM
+    other = ((codes[:, None] != lane) & (lane < BIAS_LANE)) | (lane == EMPTY_LANE)
+    return by_parity(jnp.where(other, NEG, 0.0).astype(BF16))
+
+
+def with_lanes(head, rows, lanes):
+    return rows * head_mask(head) + lanes
+
+
+def far_lane(head, line_ref):
+    lane = lax.broadcasted_iota(jnp.int32, (1, LANES), 1)
+    at = BIAS_LANE + (HEAD_DIM if head % 2 == 0 else 0)
+    return jnp.where(lane == at, line_ref[head][:, TILE - 1 : TILE], 0.0).astype(BF16)
+
+
+def query_with_lanes(causal, h, q_ref, qext_ref, line_ref):
+    rows = with_lanes(h, q_ref[:, pair_lanes(h)], qext_ref[h % 2])
+    return rows + far_lane(h, line_ref) if causal else rows
+
+
+def visit_pairs(causal, meta_ref, region):
     if not causal:
-        for t in range(tiles):
-            tile(t * TILE, 0)
+        region(0, False)
         return
     i = pl.program_id(1)
-    tile(pl.multiple_of(i * TILE, TILE), 3)
-
-    def step(p, carry):
-        kind = kinds_ref[i * tiles + p]
-        row = pl.multiple_of(p * TILE, TILE)
-
-        @pl.when(kind == 1)
-        def _():
-            tile(row, 1)
-
-        @pl.when(kind == 2)
-        def _():
-            tile(row, 2)
-
-        return carry
-
-    lax.fori_loop(0, tiles, step, 0)
-
-
-def with_bias(scores, kind, h, line_ref, tab, adj):
-    if kind == 3:
-        return scores + tab[h]
-    if kind == 2:
-        return scores + adj[h]
-    if kind == 1:
-        return scores + line_ref[h][:, TILE - 1 : TILE]
+    own = meta_ref[i]
+    region(own, True)
+    lax.fori_loop(0, meta_ref[8 + i], lambda j, c: (region(own - 2 * (j + 1), False), c)[1], 0)
+
+
+def biased(scores, causal, near, j, h, tab, adj):
+    if causal and near:
+        return scores + (tab[h] if j else adj[h])
     return scores
 
 
-def attend_kernel(causal, own_rows, par_rows, kinds_ref, q_ref, ko, vo, kp, vp, segq_ref, segk_ref,
-                  line_ref, o_ref, lse_ref, kb, vb, qm, tab, adj, m_s, l_s, acc):
+def attend_kernel(causal, meta_ref, q_ref, ko, vo, kp, vp, qext_ref, kext_ref, line_ref,
+                  o_ref, lse_ref, kb, vt, qx, tab, adj, m_s, l_s, acc):
     @pl.when(pl.program_id(1) == 0)
     def _():
-        load_keys((ko, vo, kp, vp), own_rows, par_rows, kb, vb)
+        for ref, s, target in place_tiles(causal, meta_ref, ko, kp):
+            for h in range(GROUP):
+                kb[h, rows_at(target), :] = with_lanes(
+                    h, ref[s * TILE : (s + 1) * TILE, pair_lanes(h)], kext_ref[h % 2, rows_at(target), :]
+                )
+        for ref, s, target in place_tiles(causal, meta_ref, vo, vp):
+            vt[target] = ref[s * TILE : (s + 1) * TILE, :].T
         if causal:
+            for h in range(GROUP):
+                kb[h, 0:TILE, :] = kext_ref[h % 2, 0:TILE, :]
+            vt[0] = jnp.zeros(vt.shape[1:], BF16)
             fill_tables(line_ref, tab, adj)
 
     for h in range(GROUP):
-        qm[h] = q_ref[:, pair_lanes(h)] * head_mask(h)
+        qx[h] = query_with_lanes(causal, h, q_ref, qext_ref, line_ref)
     m_s[...] = jnp.full(m_s.shape, NEG, F32)
     l_s[...] = jnp.zeros(l_s.shape, F32)
     acc[...] = jnp.zeros(acc.shape, F32)
-    segq = segq_ref[0:1, :]
-
-    def tile(row, kind):
-        allowed = allowed_keys(segq, segk_ref, row, kind == 3)
+
+    def region(tile, near):
+        def scores_of_head(h):
+            return [contract(kb[h, rows_at(tile + j), :], qx[h], 1, 1) for j in range(2)]
+
+        ready = [scores_of_head(h) for h in range(AHEAD)]
         for h in range(GROUP):
-            scores = contract(kb[pl.ds(row, TILE), pair_lanes(h)], qm[h], 1, 1)
-            scores = jnp.where(allowed, with_bias(scores, kind, h, line_ref, tab, adj), NEG)
+            if h + AHEAD < GROUP:
+                ready.append(scores_of_head(h + AHEAD))
+            scores = [biased(ready[h][j], causal, near, j, h, tab, adj) for j in range(2)]
             before = m_s[h : h + 1, :]
-            largest = jnp.maximum(before, jnp.max(scores, axis=0, keepdims=True))
-            raised = jnp.exp(scores - largest)
+            largest = jnp.maximum(
+                before, jnp.max(jnp.maximum(scores[0], scores[1]), axis=0, keepdims=True)
+            )
+            raised = [jnp.exp(piece - largest) for piece in scores]
             scale = jnp.exp(before - largest)
             m_s[h : h + 1, :] = largest
-            l_s[h : h + 1, :] = l_s[h : h + 1, :] * scale + jnp.sum(raised, axis=0, keepdims=True)
-            mixed = contract(vb[pl.ds(row, TILE), pair_lanes(h)], raised.astype(BF16), 0, 0)
-            half = (h % 2) * HEAD_DIM
-            rows = slice(h * HEAD_DIM, (h + 1) * HEAD_DIM)
-            acc[rows, :] = acc[rows, :] * scale + mixed[half : half + HEAD_DIM, :]
-
-    visit_tiles(causal, kinds_ref, tile, (own_rows + par_rows) // TILE)
+            l_s[h : h + 1, :] = l_s[h : h + 1, :] * scale + jnp.sum(
+                raised[0] + raised[1], axis=0, keepdims=True
+            )
+            rows = head_rows(h)
+            mixed = contract(vt[tile, rows, :], raised[0].astype(BF16), 1, 0) + contract(
+                vt[tile + 1, rows, :], raised[1].astype(BF16), 1, 0
+            )
+            acc[rows, :] = acc[rows, :] * scale + mixed
+
+    visit_pairs(causal, meta_ref, region)
     for h in range(GROUP):
-        rows = slice(h * HEAD_DIM, (h + 1) * HEAD_DIM)
+        rows = head_rows(h)
         acc[rows, :] = acc[rows, :] / l_s[h : h + 1, :]
         lse_ref[0, h : h + 1, :] = m_s[h : h + 1, :] + jnp.log(l_s[h : h + 1, :])
     o_ref[...] = acc[...].T.astype(BF16)
 
 
-def attend_back_kernel(causal, own_rows, par_rows, kinds_ref, q_ref, ko, vo, kp, vp, segq_ref, segk_ref,
-                       line_ref, do_ref, o_ref, lse_ref, dq_ref, own_ref, par_ref, gline_ref, gfar_ref,
-                       kb, vb, qm, dm, tab, adj, d_s, dq_acc, dk_acc, dv_acc, gt, gfar):
+def attend_back_kernel(causal, meta_ref, q_ref, ko, vo, kp, vp, qext_ref, kext_ref, line_ref,
+                       do_ref, o_ref, lse_ref, dq_ref, own_ref, par_ref, gline_ref, gall_ref,
+                       kb, vb, kt, qm, dm, qx, d_s, tab, adj, dq_acc, dk_acc, dv_acc, gt, gall):
     i = pl.program_id(1)
 
     @pl.when(i == 0)
     def _():
-        load_keys((ko, vo, kp, vp), own_rows, par_rows, kb, vb)
+        for ref, s, target in place_tiles(causal, meta_ref, ko, kp):
+            for h in range(GROUP):
+                kb[h, rows_at(target), :] = with_lanes(
+                    h, ref[s * TILE : (s + 1) * TILE, pair_lanes(h)], kext_ref[h % 2, rows_at(target), :]
+                )
+        for ref, s, target in place_tiles(causal, meta_ref, vo, vp):
+            vb[rows_at(target), :] = ref[s * TILE : (s + 1) * TILE, :]
+        for ref, s, target in place_tiles(causal, meta_ref, ko, kp):
+            turned = ref[s * TILE : (s + 1) * TILE, :].T
+            for h in range(GROUP):
+                kt[target, h, 0:HEAD_DIM, :] = turned[head_rows(h), :]
         dk_acc[...] = jnp.zeros(dk_acc.shape, F32)
         dv_acc[...] = jnp.zeros(dv_acc.shape, F32)
-        gt[...] = jnp.zeros(gt.shape, F32)
-        gfar[...] = jnp.zeros(gfar.shape, F32)
         if causal:
+            for h in range(GROUP):
+                kb[h, 0:TILE, :] = kext_ref[h % 2, 0:TILE, :]
+            vb[0:TILE, :] = jnp.zeros((TILE, vb.shape[1]), BF16)
+            kt[0] = jnp.zeros(kt.shape[1:], BF16)
+            for t in range(kt.shape[0]):
+                for h in range(GROUP):
+                    kt[t, h, HEAD_DIM:, :] = jnp.ones((kt.shape[2] - HEAD_DIM, TILE), BF16)
+            gt[...] = jnp.zeros(gt.shape, F32)
+            gall[...] = jnp.zeros(gall.shape, F32)
             fill_tables(line_ref, tab, adj)
 
     for h in range(GROUP):
@@ -552,112 +616,116 @@
         pair, rows = h // 2, slice((h % 2) * TILE, (h % 2 + 1) * TILE)
         qm[pair, rows, :] = q_ref[:, lanes] * head_mask(h)
         dm[pair, rows, :] = do_ref[:, lanes] * head_mask(h)
+        qx[h] = query_with_lanes(causal, h, q_ref, qext_ref, line_ref)
+    both = jnp.concatenate([head_mask(0)] * 8 + [head_mask(1)] * 8, axis=0)
+    for pair in range(GROUP // 2):
+        lanes = pair_lanes(2 * pair)
         product = do_ref[:, lanes].astype(F32) * o_ref[:, lanes].astype(F32)
-        ones = jnp.broadcast_to(head_mask(h).astype(F32), (8, LANES))
-        inner = lax.dot_general(
-            ones, product, (((1,), (1,)), ((), ())),
-            precision=lax.Precision.HIGHEST, preferred_element_type=F32,
-        )
-        d_s[h : h + 1, :] = inner[0:1, :]
+        high = product.astype(BF16)
+        low = (product - high.astype(F32)).astype(BF16)
+        inner = contract(both, high, 1, 1) + contract(both, low, 1, 1)
+        d_s[2 * pair : 2 * pair + 1, :] = inner[0:1, :]
+        d_s[2 * pair + 1 : 2 * pair + 2, :] = inner[8:9, :]
     dq_acc[...] = jnp.zeros(dq_acc.shape, F32)
-    segq = segq_ref[0:1, :]
-
-    def tile(row, kind):
-        allowed = allowed_keys(segq, segk_ref, row, kind == 3)
-        for pair in range(GROUP // 2):
-            lanes = slice(pair * LANES, (pair + 1) * LANES)
-            keys = kb[pl.ds(row, TILE), lanes]
-            values = vb[pl.ds(row, TILE), lanes]
-            probs_pair, grads_pair = [], []
-            for h in (2 * pair, 2 * pair + 1):
-                half = slice((h % 2) * TILE, (h % 2 + 1) * TILE)
-                scores = contract(keys, qm[pair, half, :], 1, 1)
-                scores = jnp.where(allowed, with_bias(scores, kind, h, line_ref, tab, adj), NEG)
-                probs = jnp.exp(scores - lse_ref[0, h : h + 1, :])
-                grad_probs = contract(values, dm[pair, half, :], 1, 1)
+
+    def region(tile, near):
+        def products_of_head(h):
+            half = slice((h % 2) * TILE, (h % 2 + 1) * TILE)
+            return [
+                (
+                    contract(kb[h, rows_at(tile + j), :], qx[h], 1, 1),
+                    contract(vb[rows_at(tile + j), pair_lanes(h)], dm[h // 2, half, :], 1, 1),
+                )
+                for j in range(2)
+            ]
+
+        ready = [products_of_head(h) for h in range(AHEAD)]
+        probs_low, grads_low = {}, {}
+        for h in range(GROUP):
+            if h + AHEAD < GROUP:
+                ready.append(products_of_head(h + AHEAD))
+            back = None
+            for j in range(2):
+                scores, grad_probs = ready[h][j]
+                probs = jnp.exp(biased(scores, causal, near, j, h, tab, adj) - lse_ref[0, h : h + 1, :])
                 grads = probs * (grad_probs - d_s[h : h + 1, :])
                 low = grads.astype(BF16)
-                probs_pair.append(probs.astype(BF16))
-                grads_pair.append(low)
-                if causal:
+                probs_low[h, j], grads_low[h, j] = probs.astype(BF16), low
+                if causal and near:
                     rounded = low.astype(F32)
-                    if kind == 3:
-                        gt[h] += rounded
-                    elif kind == 2:
-                        k_pos = lax.broadcasted_iota(jnp.int32, (TILE, TILE), 0)
-                        q_pos = lax.broadcasted_iota(jnp.int32, (TILE, TILE), 1)
-                        near = jnp.where(k_pos > q_pos, rounded, 0.0)
-                        gt[h] += near
-                        gfar[h] += jnp.sum((rounded - near).reshape(TILE // 8, 8, TILE), axis=0)
-                    else:
-                        gfar[h] += jnp.sum(rounded.reshape(TILE // 8, 8, TILE), axis=0)
-                back = contract(keys, low, 0, 0)
-                rows = slice(h * HEAD_DIM, (h + 1) * HEAD_DIM)
-                start = (h % 2) * HEAD_DIM
-                dq_acc[rows, :] += back[start : start + HEAD_DIM, :]
-            dv_acc[pl.ds(row, TILE), lanes] += contract(
-                jnp.concatenate(probs_pair, axis=1), dm[pair], 1, 0
-            )
-            dk_acc[pl.ds(row, TILE), lanes] += contract(
-                jnp.concatenate(grads_pair, axis=1), qm[pair], 1, 0
-            )
-
-    visit_tiles(causal, kinds_ref, tile, (own_rows + par_rows) // TILE)
+                    if j == 0:
+                        k_pos, q_pos = positions()
+                        rounded = jnp.where(k_pos > q_pos, rounded, 0.0)
+                    gt[h] += rounded
+                part = contract(kt[tile + j, h], low, 1, 0)
+                back = part if back is None else back + part
+            dq_acc[head_rows(h), :] += back[0:HEAD_DIM, :]
+            if causal:
+                gall[h : h + 1, :] += back[HEAD_DIM : HEAD_DIM + 1, :]
+            if h % 2 == 1:
+                pair = h // 2
+                lanes = pair_lanes(h)
+                for j in range(2):
+                    dv_acc[rows_at(tile + j), lanes] += contract(
+                        jnp.concatenate([probs_low[h - 1, j], probs_low[h, j]], axis=1), dm[pair], 1, 0
+                    )
+                    dk_acc[rows_at(tile + j), lanes] += contract(
+                        jnp.concatenate([grads_low[h - 1, j], grads_low[h, j]], axis=1), qm[pair], 1, 0
+                    )
+
+    visit_pairs(causal, meta_ref, region)
     dq_ref[...] = dq_acc[...].T.astype(BF16)
 
     @pl.when(i == pl.num_programs(1) - 1)
     def _():
-        own_ref[0] = dk_acc[0:own_rows, :].astype(BF16)
-        own_ref[1] = dv_acc[0:own_rows, :].astype(BF16)
-        par_ref[0] = dk_acc[own_rows : own_rows + par_rows, :].astype(BF16)
-        par_ref[1] = dv_acc[own_rows : own_rows + par_rows, :].astype(BF16)
+        for j, total in enumerate((dk_acc, dv_acc)):
+            for ref, s, target in place_tiles(causal, meta_ref, own_ref.at[j], par_ref.at[j]):
+                ref[s * TILE : (s + 1) * TILE, :] = total[rows_at(target), :].astype(BF16)
         for h in range(GROUP):
             if causal:
                 gline_ref[h] = line_of(gt[h])
-                gfar_ref[h] = jnp.sum(gfar[h], axis=0, keepdims=True)
+                gall_ref[h] = gall[h : h + 1, :]
             else:
                 gline_ref[h] = jnp.zeros((1, TILE), F32)
-                gfar_ref[h] = jnp.zeros((1, TILE), F32)
+                gall_ref[h] = jnp.zeros((1, TILE), F32)
 
 
 VMEM_LIMIT = 60 * 1024 * 1024
 
 
-def attention_specs(tokens, width, own_rows, par_rows):
+def attention_specs(own_rows, par_rows, keys):
     groups = HEADS // GROUP
     lanes = GROUP * HEAD_DIM
-    keys = own_rows + par_rows
     return [
-        pl.BlockSpec((TILE, lanes), lambda g, i, kinds: (i, g)),
-        pl.BlockSpec((own_rows, lanes), lambda g, i, kinds: (0, g)),
-        pl.BlockSpec((own_rows, lanes), lambda g, i, kinds: (0, groups + g)),
-        pl.BlockSpec((par_rows, lanes), lambda g, i, kinds: (0, g)),
-        pl.BlockSpec((par_rows, lanes), lambda g, i, kinds: (0, groups + g)),
-        pl.BlockSpec((8, TILE), lambda g, i, kinds: (0, i)),
-        pl.BlockSpec((keys, LANES), lambda g, i, kinds: (0, 0)),
-        pl.BlockSpec((GROUP, 1, TILE), lambda g, i, kinds: (g, 0, 0)),
+        pl.BlockSpec((TILE, lanes), lambda g, i, meta: (i, g)),
+        pl.BlockSpec((own_rows, lanes), lambda g, i, meta: (0, g)),
+        pl.BlockSpec((own_rows, lanes), lambda g, i, meta: (0, groups + g)),
+        pl.BlockSpec((par_rows, lanes), lambda g, i, meta: (0, g)),
+        pl.BlockSpec((par_rows, lanes), lambda g, i, meta: (0, groups + g)),
+        pl.BlockSpec((2, TILE, LANES), lambda g, i, meta: (0, i, 0)),
+        pl.BlockSpec((2, keys, LANES), lambda g, i, meta: (0, 0, 0)),
+        pl.BlockSpec((GROUP, 1, TILE), lambda g, i, meta: (g, 0, 0)),
     ]
 
 
-def attend_fast(kinds, query, kv_own, kv_par, segq, segk, line, causal):
+def attend_fast(meta, query, kv_own, kv_par, qext, kext, line, causal):
     tokens, width = query.shape
-    own_rows, par_rows = kv_own.shape[0], kv_par.shape[0]
-    keys = own_rows + par_rows
+    own_rows, par_rows, keys = kv_own.shape[0], kv_par.shape[0], kext.shape[1]
     groups, lanes = HEADS // GROUP, GROUP * HEAD_DIM
     table = (GROUP, TILE, TILE) if causal else (1, 8, LANES)
     return pl.pallas_call(
-        functools.partial(attend_kernel, causal, own_rows, par_rows),
+        functools.partial(attend_kernel, causal),
         grid_spec=pltpu.PrefetchScalarGridSpec(
             num_scalar_prefetch=1,
             grid=(groups, tokens // TILE),
-            in_specs=attention_specs(tokens, width, own_rows, par_rows),
+            in_specs=attention_specs(own_rows, par_rows, keys),
             out_specs=[
-                pl.BlockSpec((TILE, lanes), lambda g, i, kinds: (i, g)),
-                pl.BlockSpec((1, GROUP, TILE), lambda g, i, kinds: (g, 0, i)),
+                pl.BlockSpec((TILE, lanes), lambda g, i, meta: (i, g)),
+                pl.BlockSpec((1, GROUP, TILE), lambda g, i, meta: (g, 0, i)),
             ],
             scratch_shapes=[
-                pltpu.VMEM((keys, lanes), BF16),
-                pltpu.VMEM((keys, lanes), BF16),
+                pltpu.VMEM((GROUP, keys, LANES), BF16),
+                pltpu.VMEM((keys // TILE, lanes, TILE), BF16),
                 pltpu.VMEM((GROUP, TILE, LANES), BF16),
                 pltpu.VMEM(table, F32),
                 pltpu.VMEM(table, F32),
@@ -676,44 +744,45 @@
             transcendentals=tokens * keys * HEADS // 2,
         ),
         name="attend_self" if causal else "attend_cross",
-    )(kinds, query, kv_own, kv_own, kv_par, kv_par, segq, segk, line)
-
-
-def attend_back_fast(kinds, query, kv_own, kv_par, segq, segk, line, grad_mixed, mixed, lse, causal):
+    )(meta, query, kv_own, kv_own, kv_par, kv_par, qext, kext, line)
+
+
+def attend_back_fast(meta, query, kv_own, kv_par, qext, kext, line, grad_mixed, mixed, lse, causal):
     tokens, width = query.shape
-    own_rows, par_rows = kv_own.shape[0], kv_par.shape[0]
-    keys = own_rows + par_rows
+    own_rows, par_rows, keys = kv_own.shape[0], kv_par.shape[0], kext.shape[1]
     groups, lanes = HEADS // GROUP, GROUP * HEAD_DIM
     table = (GROUP, TILE, TILE) if causal else (1, 8, LANES)
-    block = pl.BlockSpec((TILE, lanes), lambda g, i, kinds: (i, g))
-    line_spec = pl.BlockSpec((GROUP, 1, TILE), lambda g, i, kinds: (g, 0, 0))
+    block = pl.BlockSpec((TILE, lanes), lambda g, i, meta: (i, g))
+    line_spec = pl.BlockSpec((GROUP, 1, TILE), lambda g, i, meta: (g, 0, 0))
     return pl.pallas_call(
-        functools.partial(attend_back_kernel, causal, own_rows, par_rows),
+        functools.partial(attend_back_kernel, causal),
         grid_spec=pltpu.PrefetchScalarGridSpec(
             num_scalar_prefetch=1,
             grid=(groups, tokens // TILE),
-            in_specs=attention_specs(tokens, width, own_rows, par_rows)
-            + [block, block, pl.BlockSpec((1, GROUP, TILE), lambda g, i, kinds: (g, 0, i))],
+            in_specs=attention_specs(own_rows, par_rows, keys)
+            + [block, block, pl.BlockSpec((1, GROUP, TILE), lambda g, i, meta: (g, 0, i))],
             out_specs=[
                 block,
-                pl.BlockSpec((2, own_rows, lanes), lambda g, i, kinds: (0, 0, g)),
-                pl.BlockSpec((2, par_rows, lanes), lambda g, i, kinds: (0, 0, g)),
+                pl.BlockSpec((2, own_rows, lanes), lambda g, i, meta: (0, 0, g)),
+                pl.BlockSpec((2, par_rows, lanes), lambda g, i, meta: (0, 0, g)),
                 line_spec,
                 line_spec,
             ],
             scratch_shapes=[
+                pltpu.VMEM((GROUP, keys, LANES), BF16),
                 pltpu.VMEM((keys, lanes), BF16),
-                pltpu.VMEM((keys, lanes), BF16),
+                pltpu.VMEM((keys // TILE, GROUP, HEAD_DIM + (16 if causal else 0), TILE), BF16),
                 pltpu.VMEM((GROUP // 2, 2 * TILE, LANES), BF16),
                 pltpu.VMEM((GROUP // 2, 2 * TILE, LANES), BF16),
+                pltpu.VMEM((GROUP, TILE, LANES), BF16),
+                pltpu.VMEM((8, TILE), F32),
                 pltpu.VMEM(table, F32),
                 pltpu.VMEM(table, F32),
-                pltpu.VMEM((8, TILE), F32),
                 pltpu.VMEM((lanes, TILE), F32),
                 pltpu.VMEM((keys, lanes), F32),
                 pltpu.VMEM((keys, lanes), F32),
                 pltpu.VMEM(table, F32),
-                pltpu.VMEM((GROUP, 8, TILE), F32),
+                pltpu.VMEM((8, TILE), F32),
             ],
         ),
         out_shape=[
@@ -729,7 +798,7 @@
             transcendentals=tokens * keys * HEADS // 2,
         ),
         name="attend_self_back" if causal else "attend_cross_back",
-    )(kinds, query, kv_own, kv_own, kv_par, kv_par, segq, segk, line, grad_mixed, mixed, lse)
+    )(meta, query, kv_own, kv_own, kv_par, kv_par, qext, kext, line, grad_mixed, mixed, lse)
 
 
 AXES = ("dp", "seq")
@@ -762,30 +831,98 @@
     return lax.dynamic_index_in_dim(value, index, axis, keepdims=False)
 
 
-def gather_kernel(count, *refs):
-    shards, wholes = refs[:count], refs[count : 2 * count]
-    local_sem, send_sem, recv_sem = refs[2 * count :]
-    dp, seq = lax.axis_index("dp"), lax.axis_index("seq")
-    z, core, y, x = dp // 2, dp % 2, seq // 2, seq % 2
-    at_z = [{"dp": ((z + k) % 4) * 2 + core, "seq": seq} for k in (1, 2, 3)]
-    at_x = {"dp": dp, "seq": seq + 1 - 2 * x}
-    at_y = {"dp": dp, "seq": seq + 2 - 4 * y}
-    at_core = {"dp": dp + 1 - 2 * core, "seq": seq}
-    partners = at_z + [at_x, at_y, at_core]
-    barrier = pltpu.get_barrier_semaphore()
-    for partner in partners:
-        pl.semaphore_signal(barrier, inc=1, device_id=partner, device_id_type=pl.DeviceIdType.MESH)
-    pl.semaphore_wait(barrier, len(partners))
+MESH = pl.DeviceIdType.MESH
+
+
+class Links:
+    def __init__(self):
+        dp, seq = lax.axis_index("dp"), lax.axis_index("seq")
+        self.seq = seq
+        self.z, self.core, self.y, self.x = dp // 2, dp % 2, seq // 2, seq % 2
+        self.at_z = [{"dp": ((self.z + k) % 4) * 2 + self.core, "seq": seq} for k in (1, 2, 3)]
+        self.at_x = {"dp": dp, "seq": seq + 1 - 2 * self.x}
+        self.at_y = {"dp": dp, "seq": seq + 2 - 4 * self.y}
+        self.at_core = {"dp": dp + 1 - 2 * self.core, "seq": seq}
+
+    def at_plane(self, core, seq):
+        return {"dp": 2 * self.z + core, "seq": seq}
+
+    def greet(self):
+        partners = list(self.at_z)
+        for flip in (0, 1):
+            for k in range(4):
+                if flip or k:
+                    core = 1 - self.core if flip else self.core
+                    partners.append(self.at_plane(core, (self.seq + k) % 4))
+        barrier = pltpu.get_barrier_semaphore()
+        for partner in partners:
+            pl.semaphore_signal(barrier, inc=1, device_id=partner, device_id_type=MESH)
+        pl.semaphore_wait(barrier, len(partners))
+
+
+def remote(source, target, send_sem, recv_sem, device):
+    return pltpu.make_async_remote_copy(
+        src_ref=source,
+        dst_ref=target,
+        send_sem=send_sem,
+        recv_sem=recv_sem,
+        device_id=device,
+        device_id_type=MESH,
+    )
+
+
+def move_tokens(links, sources, targets, parts, local_sem, send_sem, recv_sem):
+    waits = []
+    for r, (a, b) in enumerate(ROUNDS):
+        micro = 1 - links.y if a else links.y
+        core = 1 - links.x if b else links.x
+        chip = 2 * links.core + micro
+        stays = (core == links.core) & (chip == links.seq)
+        for n, (source, target, part) in enumerate(zip(sources, targets, parts)):
+            if part is None:
+                piece = source.at[micro]
+            else:
+                piece = source.at[micro, 0, pl.ds(b * part, part)]
+            slot = target.at[links.seq]
+            here = pltpu.make_async_copy(piece, slot, local_sem.at[r, n])
+            away = remote(piece, slot, send_sem.at[r, n], recv_sem.at[r, n], links.at_plane(core, chip))
+
+            @pl.when(stays)
+            def _(here=here):
+                here.start()
+
+            @pl.when(jnp.logical_not(stays))
+            def _(away=away):
+                away.start()
+
+            waits.append((stays, here, away))
+
+    def finish():
+        for stays, here, away in waits:
+            @pl.when(stays)
+            def _(here=here):
+                here.wait()
+
+            @pl.when(jnp.logical_not(stays))
+            def _(away=away):
+                away.wait()
+
+    return finish
+
+
+def gather_kernel(count, parts, *refs):
+    tokens = len(parts)
+    shards, moved = refs[:count], refs[count : count + tokens]
+    refs = refs[count + tokens :]
+    wholes, settled = refs[:count], refs[count : count + tokens]
+    local_sem, send_sem, recv_sem, move_local, move_send, move_recv = refs[count + tokens :]
+    links = Links()
+    z, core, y, x = links.z, links.core, links.y, links.x
+    links.greet()
+    finish = move_tokens(links, moved, settled, parts, move_local, move_send, move_recv)
 
     def send(w, slot, source, target, device):
-        copy = pltpu.make_async_remote_copy(
-            src_ref=source,
-            dst_ref=target,
-            send_sem=send_sem.at[w, slot],
-            recv_sem=recv_sem.at[w, slot],
-            device_id=device,
-            device_id_type=pl.DeviceIdType.MESH,
-        )
+        copy = remote(source, target, send_sem.at[w, slot], recv_sem.at[w, slot], device)
         copy.start()
         return copy
 
@@ -795,7 +932,7 @@
         copy = pltpu.make_async_copy(shards[w], own, local_sem.at[w])
         copy.start()
         locals_.append(copy)
-        rounds[0].append([send(w, k, shards[w], own, at_z[k]) for k in range(3)])
+        rounds[0].append([send(w, k, shards[w], own, links.at_z[k]) for k in range(3)])
     for t in range(count + 2):
         if t < count:
             w, half = t, wholes[t].shape[-1] // 2
@@ -805,7 +942,7 @@
                 copy.wait_recv()
             one = wholes[w].at[:, core, y, x, :, left]
             two = wholes[w].at[:, core, y, x, :, right]
-            rounds[1].append([send(w, 3, one, one, at_x), send(w, 4, two, two, at_y)])
+            rounds[1].append([send(w, 3, one, one, links.at_x), send(w, 4, two, two, links.at_y)])
         if 0 <= t - 1 < count:
             w, half = t - 1, wholes[t - 1].shape[-1] // 2
             left, right = pl.ds(0, half), pl.ds(half, half)
@@ -813,75 +950,115 @@
                 copy.wait_recv()
             one = wholes[w].at[:, core, y, :, :, left]
             two = wholes[w].at[:, core, :, x, :, right]
-            rounds[2].append([send(w, 5, one, one, at_y), send(w, 6, two, two, at_x)])
+            rounds[2].append([send(w, 5, one, one, links.at_y), send(w, 6, two, two, links.at_x)])
         if 0 <= t - 2 < count:
             w = t - 2
             for copy in rounds[2][w]:
                 copy.wait_recv()
             both = wholes[w].at[:, core]
-            rounds[3].append([send(w, 7, both, both, at_core)])
+            rounds[3].append([send(w, 7, both, both, links.at_core)])
     for w in range(count):
         for copy in rounds[3][w]:
             copy.wait_recv()
         for stage in rounds:
             for copy in stage[w]:
                 copy.wait_send()
-
-
-def gather_weights(shards):
+    finish()
+
+
+def gather_weights(shards, moved):
     count = len(shards)
     sent = sum(shard.size for shard in shards) * 2
-    wholes = pl.pallas_call(
-        functools.partial(gather_kernel, count),
-        in_specs=[pl.BlockSpec(memory_space=pltpu.VMEM)] * count,
-        out_specs=[pl.BlockSpec(memory_space=pl.ANY)] * count,
-        out_shape=[jax.ShapeDtypeStruct((4, 2, 2, 2, *shard.shape), BF16) for shard in shards],
+    parts = [None if value.ndim == 3 else value.shape[2] // 2 for value in moved]
+    settled = [
+        jax.ShapeDtypeStruct((4, value.shape[1] if part is None else part, value.shape[-1]), BF16)
+        for value, part in zip(moved, parts)
+    ]
+    outs = pl.pallas_call(
+        functools.partial(gather_kernel, count, parts),
+        in_specs=[pl.BlockSpec(memory_space=pltpu.VMEM)] * count
+        + [pl.BlockSpec(memory_space=pl.ANY)] * len(moved),
+        out_specs=[pl.BlockSpec(memory_space=pl.ANY)] * (count + len(moved)),
+        out_shape=[jax.ShapeDtypeStruct((4, 2, 2, 2, *shard.shape), BF16) for shard in shards] + settled,
         scratch_shapes=[
             pltpu.SemaphoreType.DMA((count,)),
             pltpu.SemaphoreType.DMA((count, 8)),
             pltpu.SemaphoreType.DMA((count, 8)),
+            pltpu.SemaphoreType.DMA((4, len(moved))),
+            pltpu.SemaphoreType.DMA((4, len(moved))),
+            pltpu.SemaphoreType.DMA((4, len(moved))),
         ],
         compiler_params=pltpu.CompilerParams(
             vmem_limit_bytes=VMEM_LIMIT, collective_id=0, has_side_effects=True
         ),
         cost_estimate=pl.CostEstimate(flops=0, transcendentals=0, bytes_accessed=500 * sent),
         name="gather_weights",
-    )(*shards)
-    return [whole.reshape(-1, whole.shape[-1]) for whole in wholes]
+    )(*shards, *moved)
+    return [whole.reshape(-1, whole.shape[-1]) for whole in outs[:count]], outs[count:]
 
 
 def add_low(first, second):
     return (first.astype(F32) + second.astype(F32)).astype(BF16)
 
 
-def scatter_kernel(shapes, *refs):
+def return_tokens_kernel(links, source, target, part, local_sem, send_sem, recv_sem):
+    waits = []
+    mine = 2 * (links.seq % 2) + links.core
+    for s in range(4):
+        half = (links.core + s) % 2
+        slot = target.at[links.seq % 2, pl.ds(pl.multiple_of(half * part, part), part)]
+        stays = (links.y == links.core) & (links.seq == s)
+        here = pltpu.make_async_copy(source.at[s], slot, local_sem)
+        away = remote(source.at[s], slot, send_sem.at[s], recv_sem.at[mine], links.at_plane(links.y, s))
+
+        @pl.when(stays)
+        def _(here=here):
+            here.start()
+
+        @pl.when(jnp.logical_not(stays))
+        def _(away=away):
+            away.start()
+
+        waits.append((stays, here, away))
+
+    def finish():
+        for stays, here, away in waits:
+            @pl.when(stays)
+            def _(here=here):
+                here.wait()
+
+            @pl.when(jnp.logical_not(stays))
+            def _(away=away):
+                away.wait_send()
+
+        for j in range(4):
+            arrived = remote(
+                source.at[0], target.at[0, pl.ds(0, part)], send_sem.at[0], recv_sem.at[j],
+                links.at_core,
+            )
+
+            @pl.when(jnp.logical_not((links.y == links.core) & (mine == j)))
+            def _(arrived=arrived):
+                arrived.wait_recv()
+
+    return finish
+
+
+def scatter_kernel(shapes, part, *refs):
     count = len(shapes)
-    grads, sums = refs[:count], refs[count : 2 * count]
-    scratch = refs[2 * count :]
+    grads, tokens, sums, returned = refs[:count], refs[count], refs[count + 1 : 2 * count + 1], refs[2 * count + 1]
+    scratch = refs[2 * count + 2 :]
     kept, got_one, got_two, got_z = (scratch[j * count : (j + 1) * count] for j in range(4))
     own, totals = scratch[4 * count : 5 * count], scratch[5 * count : 6 * count]
-    load_sem, store_sem, send_sem, recv_sem = scratch[6 * count :]
-    dp, seq = lax.axis_index("dp"), lax.axis_index("seq")
-    z, core, y, x = dp // 2, dp % 2, seq // 2, seq % 2
-    at_z = [{"dp": ((z + k) % 4) * 2 + core, "seq": seq} for k in (1, 2, 3)]
-    at_x = {"dp": dp, "seq": seq + 1 - 2 * x}
-    at_y = {"dp": dp, "seq": seq + 2 - 4 * y}
-    at_core = {"dp": dp + 1 - 2 * core, "seq": seq}
-    partners = at_z + [at_x, at_y, at_core]
-    barrier = pltpu.get_barrier_semaphore()
-    for partner in partners:
-        pl.semaphore_signal(barrier, inc=1, device_id=partner, device_id_type=pl.DeviceIdType.MESH)
-    pl.semaphore_wait(barrier, len(partners))
+    load_sem, store_sem, send_sem, recv_sem, back_local, back_send, back_recv = scratch[6 * count :]
+    links = Links()
+    z, core, y, x = links.z, links.core, links.y, links.x
+    at_z, at_x, at_y, at_core = links.at_z, links.at_x, links.at_y, links.at_core
+    links.greet()
+    finish = return_tokens_kernel(links, tokens, returned, part, back_local, back_send, back_recv)
 
     def send(w, slot, source, target, device):
-        copy = pltpu.make_async_remote_copy(
-            src_ref=source,
-            dst_ref=target,
-            send_sem=send_sem.at[w, slot],
-            recv_sem=recv_sem.at[w, slot],
-            device_id=device,
-            device_id_type=pl.DeviceIdType.MESH,
-        )
+        copy = remote(source, target, send_sem.at[w, slot], recv_sem.at[w, slot], device)
         copy.start()
         return copy
 
@@ -974,9 +1151,11 @@
         for stage in stages:
             for copy in stage[w]:
                 copy.wait_send()
-
-
-def scatter_grads(grads):
+    finish()
+
+
+def scatter_grads(grads, tokens):
+    part = tokens.shape[1]
     count = len(grads)
     shapes = [(grad.shape[0] // 32, grad.shape[1]) for grad in grads]
     types = [grad.dtype for grad in grads]
@@ -988,10 +1167,11 @@
         ]
 
     return pl.pallas_call(
-        functools.partial(scatter_kernel, shapes),
-        in_specs=[pl.BlockSpec(memory_space=pl.ANY)] * count,
-        out_specs=[pl.BlockSpec(memory_space=pl.ANY)] * count,
-        out_shape=[jax.ShapeDtypeStruct(shape, F32) for shape in shapes],
+        functools.partial(scatter_kernel, shapes, part),
+        in_specs=[pl.BlockSpec(memory_space=pl.ANY)] * (count + 1),
+        out_specs=[pl.BlockSpec(memory_space=pl.ANY)] * (count + 1),
+        out_shape=[jax.ShapeDtypeStruct(shape, F32) for shape in shapes]
+        + [jax.ShapeDtypeStruct((2, 2 * part, tokens.shape[2]), BF16)],
         scratch_shapes=buffers(4, 2, 2)
         + buffers(2, 4, 2, halved=True)
         + buffers(2, 4, halved=True)
@@ -1003,6 +1183,9 @@
             pltpu.SemaphoreType.DMA((count,)),
             pltpu.SemaphoreType.DMA((count, 8)),
             pltpu.SemaphoreType.DMA((count, 8)),
+            pltpu.SemaphoreType.DMA,
+            pltpu.SemaphoreType.DMA((4,)),
+            pltpu.SemaphoreType.DMA((4,)),
         ],
         compiler_params=pltpu.CompilerParams(
             vmem_limit_bytes=67043328, collective_id=1, has_side_effects=True
@@ -1013,7 +1196,7 @@
         name="scatter_grads",
     )(*[
         grad.reshape(4, 2, 2, 2, rows, width) for grad, (rows, width) in zip(grads, shapes)
-    ])
+    ], tokens)
 
 
 def norm_scale(value):
@@ -1107,25 +1290,16 @@
 
     codes = jnp.concatenate([segments[:, 0], enc_segments[:, 0]], axis=1).astype(BF16)
     codes = jnp.pad(codes, ((0, 0), (0, width - codes.shape[1])))
-
-    def bundle(micro, b):
-        return jnp.concatenate(
-            [
-                take(hidden_in[:, 0, b * part : (b + 1) * part], micro, 0),
-                take(encoder_states[:, 0, b * enc_part : (b + 1) * enc_part], micro, 0),
-                jnp.broadcast_to(take(codes, micro, 0)[None], (16, width)),
-            ],
-            axis=0,
-        )
-
-    bundles = send_tokens(bundle)
+    codes = jnp.broadcast_to(codes[:, None], (2, 8, width))
 
     small = jnp.concatenate([norm_self, norm_cross, norm_ff, rel_bias])
     small_rows = norm_self.shape[0]
     small = jnp.broadcast_to(jnp.pad(small, (0, 2 * LANES - small.shape[0])), (8, 2 * LANES))
-    small, wk, wv, wq, ck, cv, wo, cq, co, w_gate, w_up, w_down = gather_weights(
-        [small, k_self, v_self, q_self, k_cross, v_cross, o_self, q_cross, o_cross, wi_gate, wi_up, wo_ff]
-    )
+    wholes, (inputs_low, encoder, codes) = gather_weights(
+        [small, k_self, v_self, q_self, k_cross, v_cross, o_self, q_cross, o_cross, wi_gate, wi_up, wo_ff],
+        [hidden_in, encoder_states, codes],
+    )
+    small, wk, wv, wq, ck, cv, wo, cq, co, w_gate, w_up, w_down = wholes
     small = small.reshape(32, 8, 2 * LANES)[:, 0].astype(F32)
     gain_self, gain_cross, gain_ff = (
         small[:, j * small_rows : (j + 1) * small_rows].reshape(-1) for j in range(3)
@@ -1133,31 +1307,27 @@
     table = small[:, 3 * small_rows : 3 * small_rows + rel_bias.shape[0]].reshape(BUCKETS, HEADS)
     ff = wi_gate.shape[1]
 
-    inputs_low = settle([piece[:part] for piece in bundles]).reshape(4 * part, width)
-    encoder = settle([piece[part : part + enc_part] for piece in bundles]).reshape(4 * enc_part, width)
-    codes = settle([piece[part + enc_part : part + enc_part + 1] for piece in bundles])[:, 0]
-    codes = codes.astype(jnp.int32)
+    inputs_low = inputs_low.reshape(4 * part, width)
+    encoder = encoder.reshape(4 * enc_part, width)
+    codes = codes[:, 0].astype(jnp.int32)
     seg_parts = codes[:, :rows_dev].reshape(4, 2, part)
     enc_parts = codes[:, rows_dev : rows_dev + enc_dev].reshape(4, 2, enc_part)
 
     def of_core(parts, which):
         return jnp.stack([take(parts[s], which ^ (s & 1), 0) for s in range(4)])
 
-    seg_own, seg_par = of_core(seg_parts, core), of_core(seg_parts, 1 - core)
+    seg_own = of_core(seg_parts, core)
     enc_own, enc_par = of_core(enc_parts, core), of_core(enc_parts, 1 - core)
-    seg_keys = jnp.concatenate([seg_own, seg_par])
     quarter = jnp.arange(4, dtype=jnp.int32)
     at_own = 2 * quarter + (core ^ (quarter % 2))
     at_par = 2 * quarter + ((1 - core) ^ (quarter % 2))
-    at_keys = jnp.concatenate([at_own, at_par])
-    needed = (at_keys[None, :] < at_own[:, None]) & (seg_keys[None, :, -1] >= seg_own[:, :1])
-    kinds = jnp.where(needed, jnp.where(at_keys[None, :] == at_own[:, None] - 1, 2, 1), 0)
-    kinds = kinds.astype(jnp.int32).reshape(-1)
-    segq = jnp.broadcast_to(seg_own.reshape(1, -1), (8, 4 * part))
-    segk = jnp.broadcast_to(seg_keys.reshape(-1, 1), (8 * part, LANES))
-    enc_segk = jnp.broadcast_to(
-        jnp.concatenate([enc_own, enc_par]).reshape(-1, 1), (8 * enc_part, LANES)
-    )
+    tile_last = seg_parts.reshape(8, part)[:, -1]
+    first_tile = jnp.sum((tile_last[None, :] < seg_own[:, :1]).astype(jnp.int32), axis=1)
+    pairs = jnp.maximum(at_own - first_tile, 0) // 2
+    meta = jnp.concatenate([at_own, at_par, pairs]).astype(jnp.int32)
+    seg_keys = jnp.concatenate([jnp.full((part,), -1, jnp.int32), seg_parts.reshape(-1)])
+    query_codes, key_codes = query_lanes(seg_own.reshape(-1)), key_lanes(seg_keys)
+    cross_codes = key_lanes(jnp.concatenate([enc_own, enc_par]).reshape(-1))
     near = (
         buckets_of(jnp.arange(TILE, dtype=jnp.int32))[:, None] == jnp.arange(BUCKETS)[None, :]
     ).astype(F32)
@@ -1174,12 +1344,14 @@
         [dot(encoder, ck).astype(BF16), dot(encoder, cv).astype(BF16)], axis=1
     )
     cross_kv_par = exchange(cross_kv_own, *CORE)
-    mixed, self_lse = attend_fast(kinds, query, kv_own, kv_par, segq, segk, line, True)
+    kv_par, cross_kv_par, late_grad = lax.optimization_barrier((kv_par, cross_kv_par, grad_out))
+    out_parts = send_tokens(lambda micro, b: take(late_grad[:, 0, b * part : (b + 1) * part], micro, 0))
+    mixed, self_lse = attend_fast(meta, query, kv_own, kv_par, query_codes, key_codes, line, True)
     after_self = inputs + dot(mixed, wo)
     normed_cross = normed(after_self, gain_cross)
     cross_query = dot(normed_cross, cq).astype(BF16)
     cross_mixed, cross_lse = attend_fast(
-        kinds, cross_query, cross_kv_own, cross_kv_par, segq, enc_segk, line, False
+        meta, cross_query, cross_kv_own, cross_kv_par, query_codes, cross_codes, line, False
     )
     after_cross = after_self + dot(cross_mixed, co)
     normed_ff = normed(after_cross, gain_ff)
@@ -1188,9 +1360,7 @@
     result = (after_cross + dot(hidden, w_down)).astype(BF16)
     block_out = return_tokens(result.reshape(4, part, width))
 
-    out_low = settle(
-        send_tokens(lambda micro, b: take(grad_out[:, 0, b * part : (b + 1) * part], micro, 0))
-    ).reshape(4 * part, width)
+    out_low = settle(out_parts).reshape(4 * part, width)
     grad_result = out_low.astype(F32)
     grad_w_down = dot_weight(hidden, out_low)
     grad_hidden = dot_back(out_low, w_down)
@@ -1204,9 +1374,10 @@
     grad_co = dot_weight(cross_mixed, cross_out_low)
     grad_cross_mixed = dot_back(cross_out_low, co).astype(BF16)
     grad_cross_query, cross_own, cross_par, unused, unused = attend_back_fast(
-        kinds, cross_query, cross_kv_own, cross_kv_par, segq, enc_segk, line,
+        meta, cross_query, cross_kv_own, cross_kv_par, query_codes, cross_codes, line,
         grad_cross_mixed, cross_mixed, cross_lse, False,
     )
+    grad_cross_query, block_out = lax.optimization_barrier((grad_cross_query, block_out))
     cross_got = add_low(cross_own, exchange(cross_par, *CORE))
     grad_ck, grad_cv = dot_weight(encoder, cross_got[0]), dot_weight(encoder, cross_got[1])
     grad_encoder = (dot_back(cross_got[0], ck) + dot_back(cross_got[1], cv)).astype(BF16)
@@ -1218,9 +1389,10 @@
     self_out_low = grad_after_self.astype(BF16)
     grad_wo = dot_weight(mixed, self_out_low)
     grad_mixed = dot_back(self_out_low, wo).astype(BF16)
-    grad_query, self_own, self_par, grad_line, grad_far = attend_back_fast(
-        kinds, query, kv_own, kv_par, segq, segk, line, grad_mixed, mixed, self_lse, True
-    )
+    grad_query, self_own, self_par, grad_line, grad_all = attend_back_fast(
+        meta, query, kv_own, kv_par, query_codes, key_codes, line, grad_mixed, mixed, self_lse, True
+    )
+    grad_query, grad_encoder = lax.optimization_barrier((grad_query, grad_encoder))
     self_got = add_low(self_own, exchange(self_par, *CORE))
     grad_wq = dot_weight(normed_self, grad_query)
     grad_wk, grad_wv = dot_weight(normed_self, self_got[0]), dot_weight(normed_self, self_got[1])
@@ -1228,10 +1400,11 @@
         dot_back(grad_query, wq) + dot_back(self_got[0], wk) + dot_back(self_got[1], wv)
     )
     self_part, grad_gain_self = norm_back(inputs, gain_self, grad_normed_self)
-    grad_hidden_in = return_tokens((grad_after_self + self_part).astype(BF16).reshape(4, part, width))
+    grad_hidden_in = (grad_after_self + self_part).astype(BF16).reshape(4, part, width)
 
     grad_table = jnp.dot(near.T, grad_line.reshape(HEADS, TILE).T, precision=lax.Precision.HIGHEST)
-    grad_table = grad_table.at[BUCKETS - 1].add(jnp.sum(grad_far.reshape(HEADS, TILE), axis=1))
+    grad_far = jnp.sum((grad_all - grad_line).reshape(HEADS, TILE), axis=1)
+    grad_table = grad_table.at[BUCKETS - 1].add(grad_far)
     small_grads = [piece.reshape(32, -1) for piece in (grad_gain_self, grad_gain_cross, grad_gain_ff)]
     small_grads = jnp.concatenate(small_grads + [grad_table.reshape(32, -1)], axis=1)
     small_grads = jnp.pad(small_grads, ((0, 0), (0, 2 * LANES - small_grads.shape[1])))
@@ -1242,12 +1415,12 @@
     ]
     (
         grad_wk, grad_wv, grad_w_gate, grad_w_up, grad_w_down, grad_ck, grad_cv, grad_cq, grad_co,
-        grad_wo, grad_wq, small_grads,
-    ) = scatter_grads(order)
+        grad_wo, grad_wq, small_grads, grad_hidden_in,
+    ) = scatter_grads(order, grad_hidden_in)
     small_grads = small_grads[0]
     return (
         block_out,
-        grad_hidden_in.astype(F32),
+        grad_hidden_in.astype(F32)[:, None],
         grad_encoder,
         small_grads[:small_rows],
         grad_wq,

time: 976 us -> 818 us (0.84)
  Pallas kernels: 633 us -> 531 us
  waiting for transfers between devices: 41.9 us -> 3.26 us
  starting transfers between devices: 52.6 us -> 40.4 us
    pallas_call x6, Pallas kernels: 633 us -> 531 us  [the longest x1 184 us: scatter_grads(): pl.pallas_call(functools.partial(scatter_kernel, shapes, part), in_specs=...]
    ppermute x8 -> x4, waiting for transfers between devices: 25.3 us -> 0.01 us  [send_tokens(): lax.ppermute(pieces_of(seq // 2 ^ a, b), AXES, move_pairs(a, b))]
    ppermute x12 -> x8, waiting for transfers between devices: 16.6 us -> 3.24 us  [return_tokens(): received.append(lax.ppermute(take(value, index, 0), AXES, back))]
    ppermute x12 -> x8, starting transfers between devices: 25.2 us -> 20.3 us  [return_tokens(): received.append(lax.ppermute(take(value, index, 0), AXES, back))]
  transfers between devices with their start and end apart: 24 -> 16, of which waited for: 6 -> 1; matrix products, arithmetic and copies ran while one was open for 6% -> 13% of each run, Pallas kernels for 46% -> 20%
where the time goes in v3:
time: 818 us; the launch traced here: 814 us
  Pallas kernels  531 us (65%)
  matrix products  170 us (21%)
  other arithmetic  40.4 us (5%)
  starting transfers between devices  40.4 us (5%)
  local copies, waits for them, and re-layouts  26.4 us (3%)
    pallas_call x1, Pallas kernels, scatter_grads(): pl.pallas_call(functools.partial(scatter_kernel, shapes, part), in_specs=...  184 us
    pallas_call x1, Pallas kernels, gather_weights(): pl.pallas_call(functools.partial(gather_kernel, count, parts), in_specs=[...  183 us
    dot_general x22, matrix products, contract(): lax.dot_general(left, right, (((left_dim,), (right_dim,)), ((), ())), pre...  117 us
    pallas_call x2, Pallas kernels, attend_back_fast(): pl.pallas_call(functools.partial(attend_back_kernel, causal), grid_spec=p...  91.5 us
    pallas_call x2, Pallas kernels, attend_fast(): pl.pallas_call(functools.partial(attend_kernel, causal), grid_spec=pltpu....  72.5 us
    dot_general x11, matrix products, dot(): return jnp.dot(rows, weight, preferred_element_type=F32)  51.9 us
    ppermute x8, starting transfers between devices, return_tokens(): received.append(lax.ppermute(take(value, index, 0), AXES, back))  20.3 us
  transfers between devices with their start and end apart: 16, of which 1 were waited for; matrix products, arithmetic and copies ran while one was open for 13% of the time, Pallas kernels for 20%

profile of v3, /device:TPU:0, one launch (start us, length us, event | category | flops | bytes accessed | tf_op | source)
XLA Modules:
  0.0 814.0 jit_solution(12073584936780683834)
XLA Ops:
  4.1 183.4 %gather_weights.1 = (bf16[4,2,2,2,8,256]{5,4,3,2,1,0:T(8,128)(2,1)}, bf16[4,2,2,2,32,1024]{5,4,3,2,1,0:T(8,128)(2,1)}, bf16[4,2,2,2,32,1024]{5,4,3,2,1,0:T(8,128...) custom-call(bf16[8,256]{1,0:T(8,128)(2,1)} %broadcast_in_dim.103.ref, ...), custom_call_target="tpu_custom_call" | custom-call | bytes 534528000 | tf_op jit(solution)/shard_map/gather_weights/pallas_call | solution.py:977
  188.6 2.2 fusion.7
  190.8 2.1 fusion.9
  193.0 2.3 convolution_convert_fusion.15
  195.4 2.3 convolution_convert_fusion.14
  197.7 2.6 pad_maximum_fusion.ko.vo
  208.7 2.0 broadcast_select_fusion.1
  211.3 1.1 pad_maximum_fusion.2.kext_ref
  212.5 3.7 convolution_convert_fusion.16.q_ref
  216.4 1.1 dynamic-slice_bitcast_fusion.7
  217.5 1.7 collective-permute-start.2
  219.2 1.1 dynamic-slice_bitcast_fusion.6
  222.3 4.3 collective-permute-start.5
  226.6 44.8 %attend_self.1 = (bf16[1024,1024]{1,0:T(8,128)(2,1)}, f32[2,8,1024]{2,1,0:T(8,128)}) custom-call(s32[12]{0:T(128)} %pad_add_fusion.1.meta_ref, bf16[1024,1024]{1,0:T(8,128)(2,1)} %convolution_convert_fusion.16.q_ref, bf16[1024,2048]{1,0:T(8,128)(2,1)} %pad_maximum_fusion.ko.vo, bf16[1024,2048]{1,0:T(8,128)(2,1)} %pad_maximum_fusion.ko.vo, ...), custom_call_target="tpu_custom_call" | custom-call | flops 9663676416 | bytes 13631488 | tf_op jit(solution)/shard_map/attend_self/pallas_call | solution.py:716
  271.4 4.8 multiply_reduce_fusion.5
  276.9 1.3 copy-done.7
  278.2 3.7 convolution_convert_fusion.13.q_ref
  281.9 27.7 %attend_cross.1 = (bf16[1024,1024]{1,0:T(8,128)(2,1)}, f32[2,8,1024]{2,1,0:T(8,128)}) custom-call(s32[12]{0:T(128)} %pad_add_fusion.1.meta_ref, bf16[1024,1024]{1,0:T(8,128)(2,1)} %convolution_convert_fusion.13.q_ref, bf16[256,2048]{1,0:T(8,128)(2,1)} %copy-done.23, bf16[256,2048]{1,0:T(8,128)(2,1)} %copy-done.23, ...), custom_call_target="tpu_custom_call" | custom-call | flops 2147483648 | bytes 6291456 | tf_op jit(solution)/shard_map/attend_cross/pallas_call | solution.py:716
  309.7 5.4 multiply_reduce_fusion.4
  315.1 2.0 copy-done.5
  317.5 8.8 %fusion.80 = f32[1024,2816]{1,0:T(8,128)} fusion(bf16[1024,1024]{1,0:T(8,128)(2,1)S(1)} %multiply_convert_fusion.2, bf16[1024,2816]{1,0:T(8,128)(2,1)S(1)} %bitcast.260), kind=kOutput, calls=%fused_computation.257 | convolution fusion | flops 5905580032 | bytes 19398656 | tf_op jit(solution)/shard_map/dot_general | solution.py:1221
  326.4 8.8 %fusion.79 = f32[1024,2816]{1,0:T(8,128)} fusion(bf16[1024,1024]{1,0:T(8,128)(2,1)S(1)} %multiply_convert_fusion.2, bf16[1024,2816]{1,0:T(8,128)(2,1)S(1)} %bitcast.253), kind=kOutput, calls=%fused_computation.256 | convolution fusion | flops 5905580032 | bytes 19398656 | tf_op jit(solution)/shard_map/dot_general | solution.py:1221
  335.2 1.3 select_bitcast_fusion.3
  336.7 21.7 %multiply_convert_fusion = (bf16[1024,2816]{1,0:T(8,128)(2,1)}, bf16[1024,2816]{1,0:T(8,128)(2,1)}, bf16[1024,2816]{1,0:T(8,128)(2,1)}) fusion(f32[1024,2816]{1,0:T(8,128)} %fusion.79, f32[1024,2816]{1,0:T(8,128)} %fusion.80, bf16[1024,1024]{1,0:T(8,128)(2,1)S(1)} %bitcast.209, bf16[2816,1024]{1,0:T(8,128)(2,1)} %bitcast.261), kind=kOutput, calls=%fused_computation.9 | convolution fusion | flops 5980553216 | bytes 48234496 | tf_op jit(solution)/shard_map/dot_general | solution.py:398
  358.4 10.6 %add_convert_fusion.1 = bf16[1024,1024]{1,0:T(8,128)(2,1)S(1)} fusion(f32[1024,1024]{1,0:T(8,128)} %copy-done.5, bf16[1024,2816]{1,0:T(8,128)(2,1)} %get-tuple-element.210, bf16[2816,1024]{1,0:T(8,128)(2,1)} %bitcast.262), kind=kOutput, calls=%fused_computation.41 | convolution fusion | flops 5907677184 | bytes 17825792 | tf_op jit(solution)/shard_map/dot_general | solution.py:1221
  369.1 8.3 %convolution_convert_fusion = bf16[2816,1024]{1,0:T(8,128)(2,1)} fusion(bf16[1024,2816]{1,0:T(8,128)(2,1)S(1)} %copy-done.64, bf16[1024,1024]{1,0:T(8,128)(2,1)S(1)} %bitcast.210), kind=kOutput, calls=%fused_computation.13 | convolution fusion | flops 5908463616 | bytes 13631488 | tf_op jit(solution)/shard_map/dot_general | solution.py:398
  377.4 9.8 %fusion.81 = f32[1024,1024]{1,0:T(8,128)} fusion(bf16[1024,2816]{1,0:T(8,128)(2,1)S(1)} %copy-done.63, bf16[1024,2816]{1,0:T(8,128)(2,1)} %bitcast.257), kind=kOutput, calls=%fused_computation.258 | convolution fusion | flops 5905580032 | bytes 15728640 | tf_op jit(solution)/shard_map/dot_general | solution.py:398
  387.2 8.5 %convolution_convert_fusion.2 = bf16[1024,2816]{1,0:T(8,128)(2,1)} fusion(bf16[1024,1024]{1,0:T(8,128)(2,1)S(1)} %copy-done.19, bf16[1024,2816]{1,0:T(8,128)(2,1)S(1)} %copy-done.63), kind=kOutput, calls=%fused_computation.15 | convolution fusion | flops 5908463616 | bytes 13631488 | tf_op jit(solution)/shard_map/dot_general | solution.py:398
  395.7 1.4 dynamic-slice_bitcast_fusion.2
  397.1 1.7 collective-permute-start.6
  398.8 8.0 collective-permute-start.7
  406.7 8.7 %convolution_convert_fusion.1 = bf16[1024,2816]{1,0:T(8,128)(2,1)} fusion(bf16[1024,1024]{1,0:T(8,128)(2,1)S(1)} %copy-done.19, bf16[1024,2816]{1,0:T(8,128)(2,1)S(1)} %bitcast.276), kind=kOutput, calls=%fused_computation.14 | convolution fusion | flops 5908463616 | bytes 13631488 | tf_op jit(solution)/shard_map/dot_general | solution.py:398
  415.4 8.7 %multiply_reduce_fusion = (f32[1024]{0:T(1024)S(1)}, f32[1024]{0:T(1024)S(1)}, f32[1024,1024]{1,0:T(8,128)S(1)}) fusion(f32[1024,1024]{1,0:T(8,128)S(1)} %copy-done.6, f32[1024]{0:T(1024)S(1)} %get-tuple-element.260, f32[1024]{0:T(1024)S(1)} %mul.350, f32[1024,1024]{1,0:T(8,128)} %fusion.81, bf16[1024,2816]{1,0:T(8,128)(2,1)S(1)} %bitcast.276, ...), kind=kOutput, calls=%fused_computation.36 | convolution fusion | flops 5912918016 | bytes 24133632 | tf_op jit(solution)/shard_map/dot_general | solution.py:398
  424.2 1.5 subtract_add_fusion.1
  425.8 3.7 convolution_convert_fusion.12.do_ref
  429.5 3.7 convolution_convert_fusion.5
  433.3 4.1 collective-permute-start.9
  437.3 28.5 %attend_cross_back.1 = (bf16[1024,1024]{1,0:T(8,128)(2,1)}, bf16[2,256,1024]{2,1,0:T(8,128)(2,1)}, bf16[2,256,1024]{2,1,0:T(8,128)(2,1)}, f32[16,1,256]{2,1,0:T(1,128)}, f32[16,1,256]{2,1,0:T(1,128)}) custom-call(s32[12]{0:T(128)} %pad_add_fusion.1.meta_ref, bf16[1024,1024]{1,0:T(8,128)(2,1)} %convolution_convert_fusion.13.q_ref, ...), custom_call_target="tpu_custom_call" | custom-call | flops 5368709120 | bytes 15728640 | tf_op jit(solution)/shard_map/attend_cross_back/pallas_call | solution.py:757
  466.4 1.5 maximum_bitcast_fusion
  468.3 1.4 copy-done.8
  470.4 2.6 multiply_reduce_fusion.1
  473.1 1.2 subtract_add_fusion
  474.7 3.7 convolution_convert_fusion.11.do_ref
  478.4 63.1 %attend_self_back.1 = (bf16[1024,1024]{1,0:T(8,128)(2,1)}, bf16[2,1024,1024]{2,1,0:T(8,128)(2,1)}, bf16[2,1024,1024]{2,1,0:T(8,128)(2,1)}, f32[16,1,256]{2,1,0:T(1,128)}, f32[16,1,256]{2,1,0:T(1,128)}) custom-call(s32[12]{0:T(128)} %pad_add_fusion.1.meta_ref, bf16[1024,1024]{1,0:T(8,128)(2,1)} %convolution_convert_fusion.16.q_ref, ...), custom_call_target="tpu_custom_call" | custom-call | flops 24159191040 | bytes 34078720 | tf_op jit(solution)/shard_map/attend_self_back/pallas_call | solution.py:757
  544.1 11.1 %collective-permute-start.10 = (bf16[2,1024,1024]{2,1,0:T(8,128)(2,1)}, bf16[2,1024,1024]{2,1,0:T(8,128)(2,1)}, u32[]{:S(2)}, u32[]{:S(2)}) collective-permute-start(bf16[2,1024,1024]{2,1,0:T(8,128)(2,1)} %get-tuple-element.103), channel_id=1, source_target_pairs={{0,4},{1,5},{2,6},{3,7},{4,0},{5,1},{6,2},{7,3},{8,12},{9,13},{10,... | collective-permute-start | bytes 12582920 | tf_op jit(solution)/shard_map/ppermute | solution.py:811
  555.3 6.7 convolution_convert_fusion.4
  562.0 4.0 convolution_convert_fusion.6
  569.1 2.9 collective-permute-start.13
  572.1 2.0 convolution_convert_fusion.7
  574.1 2.1 convolution_convert_fusion.8
  576.2 3.0 collective-permute-start.15
  579.2 3.2 collective-permute-done.15
  583.6 2.4 fusion.82
  586.0 4.4 add_convert_fusion
  590.5 2.4 fusion.19
  592.8 3.8 convolution_convert_fusion.9
  596.7 3.8 convolution_convert_fusion.10
  600.5 5.2 fusion.18
  605.8 5.4 fusion.17
  611.3 3.7 convolution_convert_fusion.3
  615.7 183.7 %scatter_grads.1 = (f32[32,1024]{1,0:T(8,128)}, f32[32,1024]{1,0:T(8,128)}, f32[32,2816]{1,0:T(8,128)}, f32[32,2816]{1,0:T(8,128)}, f32[88,1024]{1,0:T(8,128)}, ...) custom-call(bf16[4,2,2,2,32,1024]{5,4,3,2,1,0:T(8,128)(2,1)} %bitcas, ...), custom_call_target="tpu_custom_call" | custom-call | bytes 273678336 | tf_op jit(solution)/shard_map/scatter_grads/pallas_call | solution.py:1169
  799.5 1.4 slice_bitcast_fusion.12
  800.9 1.3 slice_bitcast_fusion.14
  802.1 4.2 bitcast_convert_fusion
  (279 shorter events, 34.2 us)
Async XLA Ops:
  188.6 6.7 copy-start.37
  188.6 4.4 copy-start.47
  193.0 19.5 %copy-start.14 = (bf16[4,256,1024]{2,1,0:T(8,128)(2,1)}, bf16[4,256,1024]{2,1,0:T(8,128)(2,1)S(1)}, u32[]{:S(2)}) copy-start(bf16[4,256,1024]{2,1,0:T(8,128)(2,1)S(1)} %fusion.9) | copy-start | bytes 6291460
  200.3 15.9 %collective-permute-start = (bf16[1024,2048]{1,0:T(8,128)(2,1)}, bf16[1024,2048]{1,0:T(8,128)(2,1)}, u32[]{:S(2)}, u32[]{:S(2)}) collective-permute-start(bf16[1024,2048]{1,0:T(8,128)(2,1)} %pad_maximum_fusion.ko.vo), channel_id=1, source_target_pairs={{0,4},{1,5},{2,6},{3,7},{4,0},{5,1},{6,2},{7,3},{8,12},{9,13},{10,... | collective-permute-start | bytes 12582920 | tf_op jit(solution)/shard_map/ppermute | solution.py:811
  202.4 13.8 %copy-start.23 = (bf16[256,2048]{1,0:T(8,128)(2,1)}, bf16[256,2048]{1,0:T(8,128)(2,1)S(1)}, u32[]{:S(2)}) copy-start(bf16[256,2048]{1,0:T(8,128)(2,1)S(1)} %pad_maximum_fusion.3.ko.vo) | copy-start | bytes 3145732
  202.4 13.8 %collective-permute-start.1 = (bf16[256,2048]{1,0:T(8,128)(2,1)S(1)}, bf16[256,2048]{1,0:T(8,128)(2,1)}, u32[]{:S(2)}, u32[]{:S(2)}) collective-permute-start(bf16[256,2048]{1,0:T(8,128)(2,1)S(1)} %pad_maximum_fusion.3.ko.vo), channel_id=1, source_target_pairs={{0,4},{1,5},{2,6},{3,7},{4,0},{5,1},{6,2},{7,3},{8,12},{9,13},{10,... | collective-permute-start | bytes 3145736 | tf_op jit(solution)/shard_map/ppermute | solution.py:811
  204.3 11.8 %copy-start.56 = (s32[256]{0:T(256)}, s32[256]{0:T(256)S(1)}, u32[]{:S(2)}) copy-start(s32[256]{0:T(256)S(1)} %iota_select_fusion) | copy-start | bytes 3076
  205.7 71.2 %copy-start.39 = (f32[1024]{0:T(1024)}, f32[1024]{0:T(1024)S(1)}, u32[]{:S(2)}) copy-start(f32[1024]{0:T(1024)S(1)} %mul.342) | copy-start | bytes 12292
  205.7 10.4 %copy-start.35 = (f32[1,2,4,128]{3,1,2,0:T(2,128)}, f32[1,2,4,128]{3,1,2,0:T(2,128)S(1)}, u32[]{:S(2)}) copy-start(f32[1,2,4,128]{3,1,2,0:T(2,128)S(1)} %copy.79) | copy-start | bytes 12292
  205.7 6.7 copy-start.49
  217.5 117.7 %collective-permute-start.2 = (bf16[256,1024]{1,0:T(8,128)(2,1)}, bf16[256,1024]{1,0:T(8,128)(2,1)S(1)}, u32[]{:S(2)}, u32[]{:S(2)}) collective-permute-start(bf16[256,1024]{1,0:T(8,128)(2,1)} %get-tuple-element.231), channel_id=1, source_target_pairs={{0,0},{1,4},{2,1},{3,5},{4,2},{5,6},{6,3},{7,7},{8,8},{9,12},{10,9... | collective-permute-start | bytes 1572872 | tf_op jit(solution)/shard_map/ppermute | solution.py:1264
  220.2 115.0 %collective-permute-start.3 = (bf16[256,1024]{1,0:T(8,128)(2,1)}, bf16[256,1024]{1,0:T(8,128)(2,1)S(1)}, u32[]{:S(2)}, u32[]{:S(2)}) collective-permute-start(bf16[256,1024]{1,0:T(8,128)(2,1)} %get-tuple-element.229), channel_id=1, source_target_pairs={{0,4},{1,0},{2,5},{3,1},{4,6},{5,2},{6,7},{7,3},{8,12},{9,8},{10,1... | collective-permute-start | bytes 1572872 | tf_op jit(solution)/shard_map/ppermute | solution.py:1264
  221.3 113.9 %collective-permute-start.4 = (bf16[256,1024]{1,0:T(8,128)(2,1)}, bf16[256,1024]{1,0:T(8,128)(2,1)S(1)}, u32[]{:S(2)}, u32[]{:S(2)}) collective-permute-start(bf16[256,1024]{1,0:T(8,128)(2,1)} %get-tuple-element.232), channel_id=1, source_target_pairs={{0,1},{1,5},{2,0},{3,4},{4,3},{5,7},{6,2},{7,6},{8,9},{9,13},{10,8... | collective-permute-start | bytes 1572872 | tf_op jit(solution)/shard_map/ppermute | solution.py:1264
  222.3 49.1 %copy-start = (bf16[4,256,1024]{2,1,0:T(8,128)(2,1)S(1)}, bf16[4,256,1024]{2,1,0:T(8,128)(2,1)}, u32[]{:S(2)}) copy-start(bf16[4,256,1024]{2,1,0:T(8,128)(2,1)} %get-tuple-element.78) | copy-start | bytes 6291460
  222.3 112.9 %collective-permute-start.5 = (bf16[256,1024]{1,0:T(8,128)(2,1)}, bf16[256,1024]{1,0:T(8,128)(2,1)}, u32[]{:S(2)}, u32[]{:S(2)}) collective-permute-start(bf16[256,1024]{1,0:T(8,128)(2,1)} %get-tuple-element.230), channel_id=1, source_target_pairs={{0,5},{1,1},{2,4},{3,0},{4,7},{5,3},{6,6},{7,2},{8,13},{9,9},{10,1... | collective-permute-start | bytes 1572872 | tf_op jit(solution)/shard_map/ppermute | solution.py:1264
  271.4 6.8 copy-start.52
  276.9 5.0 copy-start.41
  281.9 27.8 %copy-start.54 = (bf16[4,2,2,2,32,1024]{5,4,3,2,1,0:T(8,128)(2,1)S(1)}, bf16[4,2,2,2,32,1024]{5,4,3,2,1,0:T(8,128)(2,1)}, u32[]{:S(2)}) copy-start(bf16[4,2,2,2,32,1024]{5,4,3,2,1,0:T(8,128)(2,1)} %get-tuple-element.93) | copy-start | bytes 6291460
  309.6 7.8 slice-start.4
  309.7 7.8 slice-start.5
  317.0 9.3 %slice-start = ((s8[5767168]{0:T(1024)(128)(4,1)}), s8[4194304]{0:T(1024)(128)(4,1)S(1)}, s32[]{:S(2)}) async-start(s8[5767168]{0:T(1024)(128)(4,1)} %bitcast.251), calls=%async_computation | async-start | bytes 8388608
  317.5 8.9 %copy-start.18 = (bf16[1024,1024]{1,0:T(8,128)(2,1)}, bf16[1024,1024]{1,0:T(8,128)(2,1)S(1)}, u32[]{:S(2)}) copy-start(bf16[1024,1024]{1,0:T(8,128)(2,1)S(1)} %multiply_convert_fusion.2) | copy-start | bytes 6291460
  317.5 8.8 %slice-start.1 = ((s8[5767168]{0:T(1024)(128)(4,1)}), s8[1572864]{0:T(1024)(128)(4,1)S(1)}, s32[]{:S(2)}) async-start(s8[5767168]{0:T(1024)(128)(4,1)} %bitcast.251), calls=%async_computation.1 | async-start | bytes 3145728
  358.4 10.6 %copy-start.64 = (bf16[1024,2816]{1,0:T(8,128)(2,1)S(1)}, bf16[1024,2816]{1,0:T(8,128)(2,1)}, u32[]{:S(2)}) copy-start(bf16[1024,2816]{1,0:T(8,128)(2,1)} %get-tuple-element.210) | copy-start | bytes 17301508
  369.1 8.4 %copy-start.63 = (bf16[1024,2816]{1,0:T(8,128)(2,1)S(1)}, bf16[1024,2816]{1,0:T(8,128)(2,1)}, u32[]{:S(2)}) copy-start(bf16[1024,2816]{1,0:T(8,128)(2,1)} %get-tuple-element.211) | copy-start | bytes 17301508
  377.4 9.8 %copy-start.19 = (bf16[1024,1024]{1,0:T(8,128)(2,1)S(1)}, bf16[1024,1024]{1,0:T(8,128)(2,1)}, u32[]{:S(2)}) copy-start(bf16[1024,1024]{1,0:T(8,128)(2,1)} %copy-done.18) | copy-start | bytes 6291460
  377.4 29.3 %slice-start.6 = ((s8[5767168]{0:T(1024)(128)(4,1)}), s8[4194304]{0:T(1024)(128)(4,1)S(1)}, s32[]{:S(2)}) async-start(s8[5767168]{0:T(1024)(128)(4,1)} %bitcast.275), calls=%async_computation.6 | async-start | bytes 8388608
  387.2 19.5 %slice-start.7 = ((s8[5767168]{0:T(1024)(128)(4,1)}), s8[1572864]{0:T(1024)(128)(4,1)S(1)}, s32[]{:S(2)}) async-start(s8[5767168]{0:T(1024)(128)(4,1)} %bitcast.275), calls=%async_computation.7 | async-start | bytes 3145728
  387.2 28.2 %slice-start.2 = ((s8[5767168]{0:T(1024)(128)(4,1)}), s8[4194304]{0:T(1024)(128)(4,1)S(1)}, s32[]{:S(2)}) async-start(s8[5767168]{0:T(1024)(128)(4,1)} %bitcast.254), calls=%async_computation.2 | async-start | bytes 8388608
  395.7 19.8 %slice-start.3 = ((s8[5767168]{0:T(1024)(128)(4,1)}), s8[1572864]{0:T(1024)(128)(4,1)S(1)}, s32[]{:S(2)}) async-start(s8[5767168]{0:T(1024)(128)(4,1)} %bitcast.254), calls=%async_computation.3 | async-start | bytes 3145728
  397.1 68.9 %collective-permute-start.6 = (bf16[256,1024]{1,0:T(8,128)(2,1)}, bf16[256,1024]{1,0:T(8,128)(2,1)S(1)}, u32[]{:S(2)}, u32[]{:S(2)}) collective-permute-start(bf16[256,1024]{1,0:T(8,128)(2,1)} %get-tuple-element.218), channel_id=1, source_target_pairs={{0,0},{4,1},{1,2},{5,3},{2,4},{6,5},{3,6},{7,7},{8,8},{12,9},{9,10... | collective-permute-start | bytes 1572872 | tf_op jit(solution)/shard_map/ppermute | solution.py:1279
  398.8 67.2 %collective-permute-start.7 = (bf16[256,1024]{1,0:T(8,128)(2,1)}, bf16[256,1024]{1,0:T(8,128)(2,1)S(1)}, u32[]{:S(2)}, u32[]{:S(2)}) collective-permute-start(bf16[256,1024]{1,0:T(8,128)(2,1)} %get-tuple-element.215), channel_id=1, source_target_pairs={{1,0},{5,1},{0,2},{4,3},{3,4},{7,5},{2,6},{6,7},{9,8},{13,9},{8,10... | collective-permute-start | bytes 1572872 | tf_op jit(solution)/shard_map/ppermute | solution.py:1279
  406.7 8.7 %copy-start.6 = (f32[1024,1024]{1,0:T(8,128)S(1)}, f32[1024,1024]{1,0:T(8,128)}, u32[]{:S(2)}) copy-start(f32[1024,1024]{1,0:T(8,128)} %copy-done.5) | copy-start | bytes 12582916
  433.3 32.8 %collective-permute-start.8 = (bf16[256,1024]{1,0:T(8,128)(2,1)}, bf16[256,1024]{1,0:T(8,128)(2,1)S(1)}, u32[]{:S(2)}, u32[]{:S(2)}) collective-permute-start(bf16[256,1024]{1,0:T(8,128)(2,1)} %get-tuple-element.217), channel_id=1, source_target_pairs={{4,0},{0,1},{5,2},{1,3},{6,4},{2,5},{7,6},{3,7},{12,8},{8,9},{13,1... | collective-permute-start | bytes 1572872 | tf_op jit(solution)/shard_map/ppermute | solution.py:1279
  433.3 32.8 %collective-permute-start.9 = (bf16[256,1024]{1,0:T(8,128)(2,1)}, bf16[256,1024]{1,0:T(8,128)(2,1)S(1)}, u32[]{:S(2)}, u32[]{:S(2)}) collective-permute-start(bf16[256,1024]{1,0:T(8,128)(2,1)} %get-tuple-element.216), channel_id=1, source_target_pairs={{5,0},{1,1},{4,2},{0,3},{7,4},{3,5},{6,6},{2,7},{13,8},{9,9},{12,1... | collective-permute-start | bytes 1572872 | tf_op jit(solution)/shard_map/ppermute | solution.py:1279
  465.8 100.2 %collective-permute-start.11 = (bf16[2,256,1024]{2,1,0:T(8,128)(2,1)}, bf16[2,256,1024]{2,1,0:T(8,128)(2,1)S(1)}, u32[]{:S(2)}, u32[]{:S(2)}) collective-permute-start(bf16[2,256,1024]{2,1,0:T(8,128)(2,1)} %get-tuple-element.105), channel_id=1, source_target_pairs={{0,4},{1,5},{2,6},{3,7},{4,0},{5,1},{6,2},{7,3},{8,12},{9,13},{10,... | collective-permute-start | bytes 3145736 | tf_op jit(solution)/shard_map/ppermute | solution.py:811
  466.2 4.2 copy-start.53
  478.4 63.1 %copy-start.57 = (s32[256]{0:T(256)S(1)}, s32[256]{0:T(256)}, u32[]{:S(2)}) copy-start(s32[256]{0:T(256)} %copy-done.56) | copy-start | bytes 3076
  544.1 41.8 %collective-permute-start.10 = (bf16[2,1024,1024]{2,1,0:T(8,128)(2,1)}, bf16[2,1024,1024]{2,1,0:T(8,128)(2,1)}, u32[]{:S(2)}, u32[]{:S(2)}) collective-permute-start(bf16[2,1024,1024]{2,1,0:T(8,128)(2,1)} %get-tuple-element.103), channel_id=1, source_target_pairs={{0,4},{1,5},{2,6},{3,7},{4,0},{5,1},{6,2},{7,3},{8,12},{9,13},{10,... | collective-permute-start | bytes 12582920 | tf_op jit(solution)/shard_map/ppermute | solution.py:811
  555.3 6.7 copy-start.9
  555.3 6.7 copy-start.60
  562.0 4.0 copy-start.22
  562.0 4.5 copy-start.12
  566.5 5.6 copy-start.21
  568.5 10.7 %collective-permute-start.12 = (bf16[64,1024]{1,0:T(8,128)(2,1)S(1)}, bf16[64,1024]{1,0:T(8,128)(2,1)S(1)}, u32[]{:S(2)}, u32[]{:S(2)}) collective-permute-start(bf16[64,1024]{1,0:T(8,128)(2,1)S(1)} %get-tuple-element.236), channel_id=1, source_target_pairs={{0,0},{4,1},{1,2},{5,3},{2,4},{6,5},{3,6},{7,7},{8,8},{12,9},{9,10... | collective-permute-start | bytes 393224 | tf_op jit(solution)/shard_map/ppermute | solution.py:1279
  569.1 10.1 %collective-permute-start.13 = (bf16[64,1024]{1,0:T(8,128)(2,1)S(1)}, bf16[64,1024]{1,0:T(8,128)(2,1)S(1)}, u32[]{:S(2)}, u32[]{:S(2)}) collective-permute-start(bf16[64,1024]{1,0:T(8,128)(2,1)S(1)} %get-tuple-element.233), channel_id=1, source_target_pairs={{1,0},{5,1},{0,2},{4,3},{3,4},{7,5},{2,6},{6,7},{9,8},{13,9},{8,10... | collective-permute-start | bytes 393224 | tf_op jit(solution)/shard_map/ppermute | solution.py:1279
  574.1 9.5 %copy-start.50 = (bf16[4,2,2,2,32,1024]{5,4,3,2,1,0:T(8,128)(2,1)S(1)}, bf16[4,2,2,2,32,1024]{5,4,3,2,1,0:T(8,128)(2,1)}, u32[]{:S(2)}) copy-start(bf16[4,2,2,2,32,1024]{5,4,3,2,1,0:T(8,128)(2,1)} %get-tuple-element.80) | copy-start | bytes 6291460
  574.1 9.5 %copy-start.61 = (bf16[1024,1024]{1,0:T(8,128)(2,1)S(1)}, bf16[1024,1024]{1,0:T(8,128)(2,1)}, u32[]{:S(2)}) copy-start(bf16[1024,1024]{1,0:T(8,128)(2,1)} %get-tuple-element.107) | copy-start | bytes 6291460
  576.2 3.0 collective-permute-start.14
  576.2 6.3 collective-permute-start.15
  586.0 4.5 copy-start.48
  600.5 5.4 copy-start.44
  605.8 5.5 copy-start.62
  799.4 6.9 copy-start.34
  799.4 7.5 copy-start.33
  799.4 8.2 %copy-start.32 = (f32[32,1024]{1,0:T(8,128)S(1)}, f32[32,1024]{1,0:T(8,128)}, u32[]{:S(2)}) copy-start(f32[32,1024]{1,0:T(8,128)} %get-tuple-element.312) | copy-start | bytes 393220
  799.4 8.8 %copy-start.31 = (f32[32,1024]{1,0:T(8,128)S(1)}, f32[32,1024]{1,0:T(8,128)}, u32[]{:S(2)}) copy-start(f32[32,1024]{1,0:T(8,128)} %get-tuple-element.313) | copy-start | bytes 393220
  799.4 9.5 %copy-start.30 = (f32[32,1024]{1,0:T(8,128)S(1)}, f32[32,1024]{1,0:T(8,128)}, u32[]{:S(2)}) copy-start(f32[32,1024]{1,0:T(8,128)} %get-tuple-element.316) | copy-start | bytes 393220
  799.4 10.1 %copy-start.29 = (f32[32,1024]{1,0:T(8,128)S(1)}, f32[32,1024]{1,0:T(8,128)}, u32[]{:S(2)}) copy-start(f32[32,1024]{1,0:T(8,128)} %get-tuple-element.317) | copy-start | bytes 393220
  799.4 10.8 %copy-start.28 = (f32[32,1024]{1,0:T(8,128)S(1)}, f32[32,1024]{1,0:T(8,128)}, u32[]{:S(2)}) copy-start(f32[32,1024]{1,0:T(8,128)} %get-tuple-element.318) | copy-start | bytes 393220
  799.5 11.4 %copy-start.27 = (f32[32,1024]{1,0:T(8,128)S(1)}, f32[32,1024]{1,0:T(8,128)}, u32[]{:S(2)}) copy-start(f32[32,1024]{1,0:T(8,128)} %get-tuple-element.319) | copy-start | bytes 393220
  802.1 9.4 %copy-start.26 = (f32[32,2816]{1,0:T(8,128)S(1)}, f32[32,2816]{1,0:T(8,128)}, u32[]{:S(2)}) copy-start(f32[32,2816]{1,0:T(8,128)} %get-tuple-element.321) | copy-start | bytes 1081348
  802.1 10.2 %copy-start.25 = (f32[32,2816]{1,0:T(8,128)S(1)}, f32[32,2816]{1,0:T(8,128)}, u32[]{:S(2)}) copy-start(f32[32,2816]{1,0:T(8,128)} %get-tuple-element.322) | copy-start | bytes 1081348
  802.1 10.9 %copy-start.24 = (f32[88,1024]{1,0:T(8,128)S(1)}, f32[88,1024]{1,0:T(8,128)}, u32[]{:S(2)}) copy-start(f32[88,1024]{1,0:T(8,128)} %get-tuple-element.323) | copy-start | bytes 1081348
  (25 other events, 74.0 us)

commit v4 on v3

--- a/solution.py
+++ b/solution.py
@@ -440,12 +440,20 @@
     return slice(head * HEAD_DIM, (head + 1) * HEAD_DIM)
 
 
+def tile_places():
+    core = lax.axis_index("dp") % 2
+    own = [2 * s + (core + s) % 2 for s in range(4)]
+    par = [2 * s + (1 - core + s) % 2 for s in range(4)]
+    return own + par + [tile // 2 for tile in own]
+
+
 def place_tiles(causal, meta_ref, own, par):
     moves = []
     count = own.shape[0] // TILE
+    places = tile_places() if causal and meta_ref is None else meta_ref
     for ref, base in ((own, 0), (par, count)):
         for s in range(count):
-            target = meta_ref[base + s] + 1 if causal else base + s
+            target = places[base + s] + 1 if causal else base + s
             moves.append((ref, s, target))
     return moves
 
@@ -512,9 +520,13 @@
         region(0, False)
         return
     i = pl.program_id(1)
-    own = meta_ref[i]
+    if meta_ref is None:
+        own = 2 * i + (lax.axis_index("dp") + i) % 2
+        pairs = own // 2
+    else:
+        own, pairs = meta_ref[i], meta_ref[8 + i]
     region(own, True)
-    lax.fori_loop(0, meta_ref[8 + i], lambda j, c: (region(own - 2 * (j + 1), False), c)[1], 0)
+    lax.fori_loop(0, pairs, lambda j, c: (region(own - 2 * (j + 1), False), c)[1], 0)
 
 
 def biased(scores, causal, near, j, h, tab, adj):
@@ -708,6 +720,23 @@
     ]
 
 
+def without_meta(spec):
+    return pl.BlockSpec(spec.block_shape, lambda g, i: spec.index_map(g, i, None))
+
+
+def attention_scratch(keys, lanes, table):
+    return [
+        pltpu.VMEM((GROUP, keys, LANES), BF16),
+        pltpu.VMEM((keys // TILE, lanes, TILE), BF16),
+        pltpu.VMEM((GROUP, TILE, LANES), BF16),
+        pltpu.VMEM(table, F32),
+        pltpu.VMEM(table, F32),
+        pltpu.VMEM((8, TILE), F32),
+        pltpu.VMEM((8, TILE), F32),
+        pltpu.VMEM((lanes, TILE), F32),
+    ]
+
+
 def attend_fast(meta, query, kv_own, kv_par, qext, kext, line, causal):
     tokens, width = query.shape
     own_rows, par_rows, keys = kv_own.shape[0], kv_par.shape[0], kext.shape[1]
@@ -723,16 +752,7 @@
                 pl.BlockSpec((TILE, lanes), lambda g, i, meta: (i, g)),
                 pl.BlockSpec((1, GROUP, TILE), lambda g, i, meta: (g, 0, i)),
             ],
-            scratch_shapes=[
-                pltpu.VMEM((GROUP, keys, LANES), BF16),
-                pltpu.VMEM((keys // TILE, lanes, TILE), BF16),
-                pltpu.VMEM((GROUP, TILE, LANES), BF16),
-                pltpu.VMEM(table, F32),
-                pltpu.VMEM(table, F32),
-                pltpu.VMEM((8, TILE), F32),
-                pltpu.VMEM((8, TILE), F32),
-                pltpu.VMEM((lanes, TILE), F32),
-            ],
+            scratch_shapes=attention_scratch(keys, lanes, table),
         ),
         out_shape=[
             jax.ShapeDtypeStruct((tokens, width), BF16),
@@ -910,6 +930,66 @@
     return finish
 
 
+class Gather:
+    def __init__(self, links, shards, wholes, local_sem, send_sem, recv_sem):
+        self.links, self.shards, self.wholes = links, shards, wholes
+        self.local_sem, self.send_sem, self.recv_sem = local_sem, send_sem, recv_sem
+
+    def copy(self, w, slot, source, target, device):
+        return remote(source, target, self.send_sem.at[w, slot], self.recv_sem.at[w, slot], device)
+
+    def copies(self, stage, w):
+        links, whole = self.links, self.wholes[w]
+        z, core, y, x = links.z, links.core, links.y, links.x
+        half = whole.shape[-1] // 2
+        left, right = pl.ds(0, half), pl.ds(half, half)
+        if stage == 0:
+            own = whole.at[z, core, y, x]
+            return [self.copy(w, k, self.shards[w], own, links.at_z[k]) for k in range(3)]
+        if stage == 1:
+            one, two = whole.at[:, core, y, x, :, left], whole.at[:, core, y, x, :, right]
+            return [self.copy(w, 3, one, one, links.at_x), self.copy(w, 4, two, two, links.at_y)]
+        if stage == 2:
+            one, two = whole.at[:, core, y, :, :, left], whole.at[:, core, :, x, :, right]
+            return [self.copy(w, 5, one, one, links.at_y), self.copy(w, 6, two, two, links.at_x)]
+        both = whole.at[:, core]
+        return [self.copy(w, 7, both, both, links.at_core)]
+
+    def local(self, w):
+        links = self.links
+        own = self.wholes[w].at[links.z, links.core, links.y, links.x]
+        return pltpu.make_async_copy(self.shards[w], own, self.local_sem.at[w])
+
+    def begin(self):
+        for w in range(len(self.shards)):
+            self.local(w).start()
+            for copy in self.copies(0, w):
+                copy.start()
+
+    def advance(self, stage, w):
+        if stage == 1:
+            self.local(w).wait()
+        for copy in self.copies(stage - 1, w):
+            copy.wait_recv()
+        for copy in self.copies(stage, w):
+            copy.start()
+
+    def steps(self):
+        count = len(self.shards)
+        order = []
+        for t in range(count + 2):
+            order += [(stage, t - stage + 1) for stage in (1, 2, 3) if 0 <= t - stage + 1 < count]
+        return order
+
+    def end(self):
+        for w in range(len(self.shards)):
+            for copy in self.copies(3, w):
+                copy.wait_recv()
+            for stage in range(4):
+                for copy in self.copies(stage, w):
+                    copy.wait_send()
+
+
 def gather_kernel(count, parts, *refs):
     tokens = len(parts)
     shards, moved = refs[:count], refs[count : count + tokens]
@@ -917,53 +997,93 @@
     wholes, settled = refs[:count], refs[count : count + tokens]
     local_sem, send_sem, recv_sem, move_local, move_send, move_recv = refs[count + tokens :]
     links = Links()
-    z, core, y, x = links.z, links.core, links.y, links.x
     links.greet()
+    gather = Gather(links, shards, wholes, local_sem, send_sem, recv_sem)
+    gather.begin()
     finish = move_tokens(links, moved, settled, parts, move_local, move_send, move_recv)
-
-    def send(w, slot, source, target, device):
-        copy = remote(source, target, send_sem.at[w, slot], recv_sem.at[w, slot], device)
-        copy.start()
-        return copy
-
-    locals_, rounds = [], [[], [], [], []]
-    for w in range(count):
-        own = wholes[w].at[z, core, y, x]
-        copy = pltpu.make_async_copy(shards[w], own, local_sem.at[w])
-        copy.start()
-        locals_.append(copy)
-        rounds[0].append([send(w, k, shards[w], own, links.at_z[k]) for k in range(3)])
-    for t in range(count + 2):
-        if t < count:
-            w, half = t, wholes[t].shape[-1] // 2
-            left, right = pl.ds(0, half), pl.ds(half, half)
-            locals_[w].wait()
-            for copy in rounds[0][w]:
-                copy.wait_recv()
-            one = wholes[w].at[:, core, y, x, :, left]
-            two = wholes[w].at[:, core, y, x, :, right]
-            rounds[1].append([send(w, 3, one, one, links.at_x), send(w, 4, two, two, links.at_y)])
-        if 0 <= t - 1 < count:
-            w, half = t - 1, wholes[t - 1].shape[-1] // 2
-            left, right = pl.ds(0, half), pl.ds(half, half)
-            for copy in rounds[1][w]:
-                copy.wait_recv()
-            one = wholes[w].at[:, core, y, :, :, left]
-            two = wholes[w].at[:, core, :, x, :, right]
-            rounds[2].append([send(w, 5, one, one, links.at_y), send(w, 6, two, two, links.at_x)])
-        if 0 <= t - 2 < count:
-            w = t - 2
-            for copy in rounds[2][w]:
-                copy.wait_recv()
-            both = wholes[w].at[:, core]
-            rounds[3].append([send(w, 7, both, both, links.at_core)])
-    for w in range(count):
-        for copy in rounds[3][w]:
-            copy.wait_recv()
-        for stage in rounds:
-            for copy in stage[w]:
-                copy.wait_send()
+    for stage, w in gather.steps():
+        gather.advance(stage, w)
+    gather.end()
     finish()
+
+
+def attend_gather_kernel(count, q_ref, ko, vo, kp, vp, qext_ref, kext_ref, line_ref, *refs):
+    sources, (o_ref, lse_ref), refs = refs[:count], refs[count : count + 2], refs[count + 2 :]
+    wholes, scratch = refs[:count], refs[count : count + 8]
+    shards = refs[count + 8 : 2 * count + 8]
+    load_sem, local_sem, send_sem, recv_sem = refs[2 * count + 8 :]
+    links = Links()
+    gather = Gather(links, shards, wholes, local_sem, send_sem, recv_sem)
+    step = pl.program_id(0) * pl.num_programs(1) + pl.program_id(1)
+    total = (HEADS * HEAD_DIM // q_ref.shape[1]) * 4
+    steps = gather.steps()
+
+    @pl.when(step == 0)
+    def _():
+        links.greet()
+        loads = [pltpu.make_async_copy(sources[w], shards[w], load_sem.at[w]) for w in range(count)]
+        for load in loads:
+            load.start()
+        for load in loads:
+            load.wait()
+        gather.begin()
+
+    attend_kernel(True, None, q_ref, ko, vo, kp, vp, qext_ref, kext_ref, line_ref, o_ref, lse_ref, *scratch)
+    served = 0
+    for n in range(total):
+        upto = len(steps) if n == total - 1 else GATHER_PACE[n] if n < len(GATHER_PACE) else served
+        if upto > served:
+            @pl.when(step == n)
+            def _(first=served, last=upto, n=n):
+                for stage, w in steps[first:last]:
+                    gather.advance(stage, w)
+                if n == total - 1:
+                    gather.end()
+
+            served = upto
+
+
+GATHER_PACE = (1, 4, 7, 9, 11, 13, 15)
+
+
+def attend_gather(query, kv_own, kv_par, qext, kext, line, shards):
+    tokens, width = query.shape
+    own_rows, par_rows, keys = kv_own.shape[0], kv_par.shape[0], kext.shape[1]
+    groups, lanes, count = HEADS // GROUP, GROUP * HEAD_DIM, len(shards)
+    table = (GROUP, TILE, TILE)
+    whole = pl.BlockSpec(memory_space=pl.ANY)
+    outs = pl.pallas_call(
+        functools.partial(attend_gather_kernel, count),
+        grid=(groups, tokens // TILE),
+        in_specs=[without_meta(spec) for spec in attention_specs(own_rows, par_rows, keys)] + [whole] * count,
+        out_specs=[
+            pl.BlockSpec((TILE, lanes), lambda g, i: (i, g)),
+            pl.BlockSpec((1, GROUP, TILE), lambda g, i: (g, 0, i)),
+        ]
+        + [whole] * count,
+        scratch_shapes=attention_scratch(keys, lanes, table)
+        + [pltpu.VMEM(shard.shape, BF16) for shard in shards]
+        + [
+            pltpu.SemaphoreType.DMA((count,)),
+            pltpu.SemaphoreType.DMA((count,)),
+            pltpu.SemaphoreType.DMA((count, 8)),
+            pltpu.SemaphoreType.DMA((count, 8)),
+        ],
+        out_shape=[
+            jax.ShapeDtypeStruct((tokens, width), BF16),
+            jax.ShapeDtypeStruct((groups, GROUP, tokens), F32),
+        ]
+        + [jax.ShapeDtypeStruct((4, 2, 2, 2, *shard.shape), BF16) for shard in shards],
+        compiler_params=pltpu.CompilerParams(
+            vmem_limit_bytes=VMEM_LIMIT, collective_id=2, has_side_effects=True
+        ),
+        cost_estimate=pl.CostEstimate(
+            flops=tokens * keys * width * 4, bytes_accessed=4 * (tokens + keys) * width,
+            transcendentals=tokens * keys * HEADS // 2,
+        ),
+        name="attend_gather",
+    )(query, kv_own, kv_own, kv_par, kv_par, qext, kext, line, *shards)
+    return outs[0], outs[1], [whole.reshape(-1, whole.shape[-1]) for whole in outs[2:]]
 
 
 def gather_weights(shards, moved):
@@ -1296,10 +1416,9 @@
     small_rows = norm_self.shape[0]
     small = jnp.broadcast_to(jnp.pad(small, (0, 2 * LANES - small.shape[0])), (8, 2 * LANES))
     wholes, (inputs_low, encoder, codes) = gather_weights(
-        [small, k_self, v_self, q_self, k_cross, v_cross, o_self, q_cross, o_cross, wi_gate, wi_up, wo_ff],
-        [hidden_in, encoder_states, codes],
-    )
-    small, wk, wv, wq, ck, cv, wo, cq, co, w_gate, w_up, w_down = wholes
+        [small, k_self, v_self, q_self], [hidden_in, encoder_states, codes]
+    )
+    small, wk, wv, wq = wholes
     small = small.reshape(32, 8, 2 * LANES)[:, 0].astype(F32)
     gain_self, gain_cross, gain_ff = (
         small[:, j * small_rows : (j + 1) * small_rows].reshape(-1) for j in range(3)
@@ -1340,13 +1459,17 @@
     )
     kv_par = exchange(kv_own, *CORE)
     query = dot(normed_self, wq).astype(BF16)
+    mixed, self_lse, wholes = attend_gather(
+        query, kv_own, kv_par, query_codes, key_codes, line,
+        [k_cross, v_cross, o_self, q_cross, o_cross, wi_gate, wi_up, wo_ff],
+    )
+    ck, cv, wo, cq, co, w_gate, w_up, w_down = wholes
     cross_kv_own = jnp.concatenate(
         [dot(encoder, ck).astype(BF16), dot(encoder, cv).astype(BF16)], axis=1
     )
     cross_kv_par = exchange(cross_kv_own, *CORE)
-    kv_par, cross_kv_par, late_grad = lax.optimization_barrier((kv_par, cross_kv_par, grad_out))
+    cross_kv_par, late_grad = lax.optimization_barrier((cross_kv_par, grad_out))
     out_parts = send_tokens(lambda micro, b: take(late_grad[:, 0, b * part : (b + 1) * part], micro, 0))
-    mixed, self_lse = attend_fast(meta, query, kv_own, kv_par, query_codes, key_codes, line, True)
     after_self = inputs + dot(mixed, wo)
     normed_cross = normed(after_self, gain_cross)
     cross_query = dot(normed_cross, cq).astype(BF16)

time: 818 us -> 801 us (0.979)
  Pallas kernels: 531 us -> 518 us
    pallas_call x0 -> x1, Pallas kernels: none -> 150 us  [attend_gather(): pl.pallas_call(functools.partial(attend_gather_kernel, count), grid=(grou...]
    pallas_call x1, Pallas kernels: 183 us -> 67.6 us  [gather_weights(): pl.pallas_call(functools.partial(gather_kernel, count, parts), in_specs=[...]
    pallas_call x2 -> x1, Pallas kernels: 72.5 us -> 19.4 us  [attend_fast(): pl.pallas_call(functools.partial(attend_kernel, causal), grid_spec=pltpu....]
    dot_general x11, matrix products: 51.9 us -> 70.3 us  [dot(): return jnp.dot(rows, weight, preferred_element_type=F32)]
    dot_general x22, matrix products: 117 us -> 104 us  [contract(): lax.dot_general(left, right, (((left_dim,), (right_dim,)), ((), ())), pre...]
  transfers between devices with their start and end apart: 16 -> 16, of which waited for: 1 -> 1; matrix products, arithmetic and copies ran while one was open for 13% -> 12% of each run, Pallas kernels for 20% -> 14%
where the time goes in v4:
time: 801 us; the launch traced here: 796 us
  Pallas kernels  518 us (65%)
  matrix products  175 us (22%)
  other arithmetic  39.5 us (5%)
  starting transfers between devices  33.9 us (4%)
  local copies, waits for them, and re-layouts  23.9 us (3%)
    pallas_call x1, Pallas kernels, scatter_grads(): pl.pallas_call(functools.partial(scatter_kernel, shapes, part), in_specs=...  189 us
    pallas_call x1, Pallas kernels, attend_gather(): pl.pallas_call(functools.partial(attend_gather_kernel, count), grid=(grou...  150 us
    dot_general x22, matrix products, contract(): lax.dot_general(left, right, (((left_dim,), (right_dim,)), ((), ())), pre...  104 us
    pallas_call x2, Pallas kernels, attend_back_fast(): pl.pallas_call(functools.partial(attend_back_kernel, causal), grid_spec=p...  91.8 us
    dot_general x11, matrix products, dot(): return jnp.dot(rows, weight, preferred_element_type=F32)  70.3 us
    pallas_call x1, Pallas kernels, gather_weights(): pl.pallas_call(functools.partial(gather_kernel, count, parts), in_specs=[...  67.6 us
    pallas_call x1, Pallas kernels, attend_fast(): pl.pallas_call(functools.partial(attend_kernel, causal), grid_spec=pltpu....  19.4 us
  transfers between devices with their start and end apart: 16, of which 1 were waited for; matrix products, arithmetic and copies ran while one was open for 12% of the time, Pallas kernels for 14%

profile of v4, /device:TPU:0, one launch (start us, length us, event | category | flops | bytes accessed | tf_op | source)
XLA Modules:
  0.0 796.2 jit_solution(3729861695905282661)
XLA Ops:
  4.1 67.6 %gather_weights.1 = (bf16[4,2,2,2,8,256]{5,4,3,2,1,0:T(8,128)(2,1)}, bf16[4,2,2,2,32,1024]{5,4,3,2,1,0:T(8,128)(2,1)}, bf16[4,2,2,2,32,1024]{5,4,3,2,1,0:T(8,128...) custom-call(bf16[8,256]{1,0:T(8,128)(2,1)} %broadcast_in_dim.103.ref, ...), custom_call_target="tpu_custom_call" | custom-call | bytes 100352000 | tf_op jit(solution)/shard_map/gather_weights/pallas_call | solution.py:1097
  72.7 2.2 fusion.7
  75.0 2.1 fusion.9
  77.1 2.4 convolution_convert_fusion.15
  79.5 2.4 convolution_convert_fusion.14
  81.9 2.5 pad_maximum_fusion.ko.vo
  91.6 2.2 broadcast_select_fusion.1
  93.8 1.1 pad_maximum_fusion.2.kext_ref
  95.0 3.7 convolution_convert_fusion.16.q_ref
  98.7 149.8 %attend_gather.1 = (bf16[1024,1024]{1,0:T(8,128)(2,1)}, f32[2,8,1024]{2,1,0:T(8,128)}, bf16[4,2,2,2,32,1024]{5,4,3,2,1,0:T(8,128)(2,1)}, bf16[4,2,2,2,32,1024]{5...) custom-call(bf16[1024,1024]{1,0:T(8,128)(2,1)} %convolution_convert_, ...), custom_call_target="tpu_custom_call" | custom-call | flops 9663676416 | bytes 13631488 | tf_op jit(solution)/shard_map/attend_gather/pallas_call | solution.py:1055
  248.6 2.4 convolution_convert_fusion.18
  251.1 2.3 convolution_convert_fusion.17
  253.9 2.5 multiply_reduce_fusion.5
  257.2 3.7 convolution_convert_fusion.13.q_ref
  262.8 2.5 collective-permute-start.3
  265.8 3.9 collective-permute-start.5
  269.7 19.4 %attend_cross.1 = (bf16[1024,1024]{1,0:T(8,128)(2,1)}, f32[2,8,1024]{2,1,0:T(8,128)}) custom-call(s32[12]{0:T(128)} %pad_add_fusion.1.meta_ref, bf16[1024,1024]{1,0:T(8,128)(2,1)} %convolution_convert_fusion.13.q_ref, bf16[256,2048]{1,0:T(8,128)(2,1)} %copy-done.21, bf16[256,2048]{1,0:T(8,128)(2,1)} %copy-done.21, bf16[256,2048]{1,0:T(8,128)(2,1)} %copy-done.49, ...), custom_call_target="tpu_custom_call" | custom-call | flops 2147483648 | bytes 6291456 | tf_op jit(solution)/shard_map/attend_cross/pallas_call | solution.py:745
  289.1 6.0 multiply_reduce_fusion.4
  295.1 2.0 copy-done.5
  297.6 8.8 %fusion.80 = f32[1024,2816]{1,0:T(8,128)} fusion(bf16[1024,1024]{1,0:T(8,128)(2,1)S(1)} %multiply_convert_fusion.2, bf16[1024,2816]{1,0:T(8,128)(2,1)S(1)} %bitcast.259), kind=kOutput, calls=%fused_computation.257 | convolution fusion | flops 5905580032 | bytes 19398656 | tf_op jit(solution)/shard_map/dot_general | solution.py:1341
  307.0 8.9 %fusion.79 = f32[1024,2816]{1,0:T(8,128)} fusion(bf16[1024,1024]{1,0:T(8,128)(2,1)S(1)} %bitcast.209, bf16[2816,1024]{1,0:T(8,128)(2,1)S(1)} %bitcast.268), kind=kOutput, calls=%fused_computation.256 | convolution fusion | flops 5905580032 | bytes 19398656 | tf_op jit(solution)/shard_map/dot_general | solution.py:398
  315.8 25.5 %multiply_convert_fusion = (bf16[1024,2816]{1,0:T(8,128)(2,1)}, bf16[1024,2816]{1,0:T(8,128)(2,1)}, bf16[1024,2816]{1,0:T(8,128)(2,1)}) fusion(f32[1024,2816]{1,0:T(8,128)} %fusion.80, f32[1024,2816]{1,0:T(8,128)} %fusion.79, bf16[1024,1024]{1,0:T(8,128)(2,1)} %copy-done.16, bf16[1024,2816]{1,0:T(8,128)(2,1)} %bitcast.263), kind=kOutput, calls=%fused_computation.9 | convolution fusion | flops 5980553216 | bytes 48234496 | tf_op jit(solution)/shard_map/dot_general | solution.py:1341
  341.3 10.6 %add_convert_fusion.1 = bf16[1024,1024]{1,0:T(8,128)(2,1)S(1)} fusion(f32[1024,1024]{1,0:T(8,128)} %copy-done.5, bf16[1024,2816]{1,0:T(8,128)(2,1)} %get-tuple-element.208, bf16[2816,1024]{1,0:T(8,128)(2,1)} %bitcast.265), kind=kOutput, calls=%fused_computation.41 | convolution fusion | flops 5907677184 | bytes 17825792 | tf_op jit(solution)/shard_map/dot_general | solution.py:1341
  351.9 8.1 %convolution_convert_fusion = bf16[2816,1024]{1,0:T(8,128)(2,1)} fusion(bf16[1024,2816]{1,0:T(8,128)(2,1)S(1)} %copy-done.64, bf16[1024,1024]{1,0:T(8,128)(2,1)S(1)} %bitcast.210), kind=kOutput, calls=%fused_computation.13 | convolution fusion | flops 5908463616 | bytes 13631488 | tf_op jit(solution)/shard_map/dot_general | solution.py:398
  360.1 9.9 %fusion.81 = f32[1024,1024]{1,0:T(8,128)} fusion(bf16[1024,2816]{1,0:T(8,128)(2,1)S(1)} %copy-done.63, bf16[1024,2816]{1,0:T(8,128)(2,1)} %bitcast.264), kind=kOutput, calls=%fused_computation.258 | convolution fusion | flops 5905580032 | bytes 15728640 | tf_op jit(solution)/shard_map/dot_general | solution.py:398
  370.0 8.5 %convolution_convert_fusion.1 = bf16[1024,2816]{1,0:T(8,128)(2,1)} fusion(bf16[1024,1024]{1,0:T(8,128)(2,1)S(1)} %copy-done.17, bf16[1024,2816]{1,0:T(8,128)(2,1)S(1)} %copy-done.63), kind=kOutput, calls=%fused_computation.14 | convolution fusion | flops 5908463616 | bytes 13631488 | tf_op jit(solution)/shard_map/dot_general | solution.py:398
  378.5 1.4 dynamic-slice_bitcast_fusion.2
  379.9 1.7 collective-permute-start.6
  381.6 1.4 collective-permute-start.7
  383.0 8.3 %convolution_convert_fusion.2 = bf16[1024,2816]{1,0:T(8,128)(2,1)} fusion(bf16[1024,1024]{1,0:T(8,128)(2,1)S(1)} %copy-done.17, bf16[1024,2816]{1,0:T(8,128)(2,1)S(1)} %bitcast.276), kind=kOutput, calls=%fused_computation.15 | convolution fusion | flops 5908463616 | bytes 13631488 | tf_op jit(solution)/shard_map/dot_general | solution.py:398
  391.3 8.7 %multiply_reduce_fusion = (f32[1024]{0:T(1024)S(1)}, f32[1024]{0:T(1024)S(1)}, f32[1024,1024]{1,0:T(8,128)S(1)}) fusion(f32[1024,1024]{1,0:T(8,128)S(1)} %copy-done.6, f32[1024]{0:T(1024)S(1)} %get-tuple-element.258, f32[1024]{0:T(1024)S(1)} %mul.350, f32[1024,1024]{1,0:T(8,128)} %fusion.81, bf16[1024,2816]{1,0:T(8,128)(2,1)S(1)} %bitcast.276, ...), kind=kOutput, calls=%fused_computation.36 | convolution fusion | flops 5912918016 | bytes 24133632 | tf_op jit(solution)/shard_map/dot_general | solution.py:398
  400.1 1.5 subtract_add_fusion.1
  401.7 3.7 convolution_convert_fusion.12.do_ref
  405.4 3.7 convolution_convert_fusion.5
  409.1 1.5 collective-permute-start.8
  410.6 2.0 collective-permute-start.9
  412.6 28.5 %attend_cross_back.1 = (bf16[1024,1024]{1,0:T(8,128)(2,1)}, bf16[2,256,1024]{2,1,0:T(8,128)(2,1)}, bf16[2,256,1024]{2,1,0:T(8,128)(2,1)}, f32[16,1,256]{2,1,0:T(1,128)}, f32[16,1,256]{2,1,0:T(1,128)}) custom-call(s32[12]{0:T(128)} %pad_add_fusion.1.meta_ref, bf16[1024,1024]{1,0:T(8,128)(2,1)} %convolution_convert_fusion.13.q_ref, ...), custom_call_target="tpu_custom_call" | custom-call | flops 5368709120 | bytes 15728640 | tf_op jit(solution)/shard_map/attend_cross_back/pallas_call | solution.py:777
  441.1 1.6 collective-permute-start.11
  443.2 1.5 maximum_bitcast_fusion
  445.2 1.4 copy-done.8
  447.3 2.6 multiply_reduce_fusion.1
  450.0 1.2 subtract_add_fusion
  451.5 3.7 convolution_convert_fusion.11.do_ref
  455.3 63.3 %attend_self_back.1 = (bf16[1024,1024]{1,0:T(8,128)(2,1)}, bf16[2,1024,1024]{2,1,0:T(8,128)(2,1)}, bf16[2,1024,1024]{2,1,0:T(8,128)(2,1)}, f32[16,1,256]{2,1,0:T(1,128)}, f32[16,1,256]{2,1,0:T(1,128)}) custom-call(s32[12]{0:T(128)} %pad_add_fusion.1.meta_ref, bf16[1024,1024]{1,0:T(8,128)(2,1)} %convolution_convert_fusion.16.q_ref, ...), custom_call_target="tpu_custom_call" | custom-call | flops 24159191040 | bytes 34078720 | tf_op jit(solution)/shard_map/attend_self_back/pallas_call | solution.py:777
  521.0 10.6 %collective-permute-start.10 = (bf16[2,1024,1024]{2,1,0:T(8,128)(2,1)}, bf16[2,1024,1024]{2,1,0:T(8,128)(2,1)}, u32[]{:S(2)}, u32[]{:S(2)}) collective-permute-start(bf16[2,1024,1024]{2,1,0:T(8,128)(2,1)} %get-tuple-element.101), channel_id=1, source_target_pairs={{0,4},{1,5},{2,6},{3,7},{4,0},{5,1},{6,2},{7,3},{8,12},{9,13},{10,... | collective-permute-start | bytes 12582920 | tf_op jit(solution)/shard_map/ppermute | solution.py:831
  531.7 6.7 convolution_convert_fusion.4
  538.4 4.0 convolution_convert_fusion.6
  545.5 2.9 collective-permute-start.13
  548.5 2.0 convolution_convert_fusion.7
  550.5 2.1 convolution_convert_fusion.8
  552.6 3.0 collective-permute-start.15
  555.7 3.2 collective-permute-done.15
  560.0 2.4 fusion.82
  562.4 4.4 add_convert_fusion
  566.8 2.4 fusion.19
  569.2 3.8 convolution_convert_fusion.9
  573.1 3.7 convolution_convert_fusion.10
  576.8 5.2 fusion.18
  582.2 5.4 fusion.17
  587.7 3.7 convolution_convert_fusion.3
  592.1 189.4 %scatter_grads.1 = (f32[32,1024]{1,0:T(8,128)}, f32[32,1024]{1,0:T(8,128)}, f32[32,2816]{1,0:T(8,128)}, f32[32,2816]{1,0:T(8,128)}, f32[88,1024]{1,0:T(8,128)}, ...) custom-call(bf16[4,2,2,2,32,1024]{5,4,3,2,1,0:T(8,128)(2,1)} %bitcas, ...), custom_call_target="tpu_custom_call" | custom-call | bytes 273678336 | tf_op jit(solution)/shard_map/scatter_grads/pallas_call | solution.py:1289
  781.6 1.4 slice_bitcast_fusion.12
  783.0 1.3 slice_bitcast_fusion.14
  784.3 4.2 bitcast_convert_fusion
  (279 shorter events, 33.0 us)
Async XLA Ops:
  72.7 6.8 copy-start.35
  72.7 4.4 copy-start.45
  77.1 17.9 %copy-start.13 = (bf16[4,256,1024]{2,1,0:T(8,128)(2,1)}, bf16[4,256,1024]{2,1,0:T(8,128)(2,1)S(1)}, u32[]{:S(2)}) copy-start(bf16[4,256,1024]{2,1,0:T(8,128)(2,1)S(1)} %fusion.9) | copy-start | bytes 6291460
  84.3 14.4 %collective-permute-start = (bf16[1024,2048]{1,0:T(8,128)(2,1)}, bf16[1024,2048]{1,0:T(8,128)(2,1)}, u32[]{:S(2)}, u32[]{:S(2)}) collective-permute-start(bf16[1024,2048]{1,0:T(8,128)(2,1)} %pad_maximum_fusion.ko.vo), channel_id=1, source_target_pairs={{0,4},{1,5},{2,6},{3,7},{4,0},{5,1},{6,2},{7,3},{8,12},{9,13},{10,... | collective-permute-start | bytes 12582920 | tf_op jit(solution)/shard_map/ppermute | solution.py:831
  87.7 169.4 %copy-start.37 = (f32[1024]{0:T(1024)}, f32[1024]{0:T(1024)S(1)}, u32[]{:S(2)}) copy-start(f32[1024]{0:T(1024)S(1)} %mul.342) | copy-start | bytes 12292
  88.0 10.7 %copy-start.33 = (f32[1,2,4,128]{3,1,2,0:T(2,128)}, f32[1,2,4,128]{3,1,2,0:T(2,128)S(1)}, u32[]{:S(2)}) copy-start(f32[1,2,4,128]{3,1,2,0:T(2,128)S(1)} %copy.79) | copy-start | bytes 12292
  88.0 7.0 copy-start.47
  98.7 149.9 %copy-start.18 = (bf16[4,64,1024]{2,1,0:T(8,128)(2,1)S(1)}, bf16[4,64,1024]{2,1,0:T(8,128)(2,1)}, u32[]{:S(2)}) copy-start(bf16[4,64,1024]{2,1,0:T(8,128)(2,1)} %get-tuple-element.85) | copy-start | bytes 1572868
  248.6 5.4 copy-start
  248.6 5.3 copy-start.50
  248.6 5.3 copy-start.60
  253.5 7.4 collective-permute-start.1
  256.5 4.4 copy-start.7
  261.2 45.2 %collective-permute-start.2 = (bf16[256,1024]{1,0:T(8,128)(2,1)S(1)}, bf16[256,1024]{1,0:T(8,128)(2,1)S(1)}, u32[]{:S(2)}, u32[]{:S(2)}) collective-permute-start(bf16[256,1024]{1,0:T(8,128)(2,1)S(1)} %get-tuple-element.229), channel_id=1, source_target_pairs={{0,0},{1,4},{2,1},{3,5},{4,2},{5,6},{6,3},{7,7},{8,8},{9,12},{10,9... | collective-permute-start | bytes 1572872 | tf_op jit(solution)/shard_map/ppermute | solution.py:1384
  262.8 43.6 %collective-permute-start.3 = (bf16[256,1024]{1,0:T(8,128)(2,1)}, bf16[256,1024]{1,0:T(8,128)(2,1)S(1)}, u32[]{:S(2)}, u32[]{:S(2)}) collective-permute-start(bf16[256,1024]{1,0:T(8,128)(2,1)} %get-tuple-element.227), channel_id=1, source_target_pairs={{0,4},{1,0},{2,5},{3,1},{4,6},{5,2},{6,7},{7,3},{8,12},{9,8},{10,1... | collective-permute-start | bytes 1572872 | tf_op jit(solution)/shard_map/ppermute | solution.py:1384
  265.3 41.1 %collective-permute-start.4 = (bf16[256,1024]{1,0:T(8,128)(2,1)S(1)}, bf16[256,1024]{1,0:T(8,128)(2,1)S(1)}, u32[]{:S(2)}, u32[]{:S(2)}) collective-permute-start(bf16[256,1024]{1,0:T(8,128)(2,1)S(1)} %get-tuple-element.230), channel_id=1, source_target_pairs={{0,1},{1,5},{2,0},{3,4},{4,3},{5,7},{6,2},{7,6},{8,9},{9,13},{10,8... | collective-permute-start | bytes 1572872 | tf_op jit(solution)/shard_map/ppermute | solution.py:1384
  265.8 40.6 %collective-permute-start.5 = (bf16[256,1024]{1,0:T(8,128)(2,1)S(1)}, bf16[256,1024]{1,0:T(8,128)(2,1)S(1)}, u32[]{:S(2)}, u32[]{:S(2)}) collective-permute-start(bf16[256,1024]{1,0:T(8,128)(2,1)S(1)} %get-tuple-element.228), channel_id=1, source_target_pairs={{0,5},{1,1},{2,4},{3,0},{4,7},{5,3},{6,6},{7,2},{8,13},{9,9},{10,1... | collective-permute-start | bytes 1572872 | tf_op jit(solution)/shard_map/ppermute | solution.py:1384
  289.1 8.5 %slice-start = ((s8[5767168]{0:T(1024)(128)(4,1)}), s8[4194304]{0:T(1024)(128)(4,1)S(1)}, s32[]{:S(2)}) async-start(s8[5767168]{0:T(1024)(128)(4,1)} %bitcast.257), calls=%async_computation | async-start | bytes 8388608
  289.1 8.5 %slice-start.1 = ((s8[5767168]{0:T(1024)(128)(4,1)}), s8[1572864]{0:T(1024)(128)(4,1)S(1)}, s32[]{:S(2)}) async-start(s8[5767168]{0:T(1024)(128)(4,1)} %bitcast.257), calls=%async_computation.1 | async-start | bytes 3145728
  297.5 8.9 %copy-start.16 = (bf16[1024,1024]{1,0:T(8,128)(2,1)}, bf16[1024,1024]{1,0:T(8,128)(2,1)S(1)}, u32[]{:S(2)}) copy-start(bf16[1024,1024]{1,0:T(8,128)(2,1)S(1)} %multiply_convert_fusion.2) | copy-start | bytes 6291460
  297.5 9.4 %slice-start.4 = ((s8[5767168]{0:T(1024)(128)(4,1)}), s8[4194304]{0:T(1024)(128)(4,1)S(1)}, s32[]{:S(2)}) async-start(s8[5767168]{0:T(1024)(128)(4,1)} %bitcast.266), calls=%async_computation.4 | async-start | bytes 8388608
  297.6 9.4 %slice-start.5 = ((s8[5767168]{0:T(1024)(128)(4,1)}), s8[1572864]{0:T(1024)(128)(4,1)S(1)}, s32[]{:S(2)}) async-start(s8[5767168]{0:T(1024)(128)(4,1)} %bitcast.266), calls=%async_computation.5 | async-start | bytes 3145728
  341.3 10.6 %copy-start.64 = (bf16[1024,2816]{1,0:T(8,128)(2,1)S(1)}, bf16[1024,2816]{1,0:T(8,128)(2,1)}, u32[]{:S(2)}) copy-start(bf16[1024,2816]{1,0:T(8,128)(2,1)} %get-tuple-element.208) | copy-start | bytes 17301508
  351.9 8.2 %copy-start.63 = (bf16[1024,2816]{1,0:T(8,128)(2,1)S(1)}, bf16[1024,2816]{1,0:T(8,128)(2,1)}, u32[]{:S(2)}) copy-start(bf16[1024,2816]{1,0:T(8,128)(2,1)} %get-tuple-element.210) | copy-start | bytes 17301508
  360.1 9.9 %copy-start.17 = (bf16[1024,1024]{1,0:T(8,128)(2,1)S(1)}, bf16[1024,1024]{1,0:T(8,128)(2,1)}, u32[]{:S(2)}) copy-start(bf16[1024,1024]{1,0:T(8,128)(2,1)} %copy-done.16) | copy-start | bytes 6291460
  360.1 23.0 %slice-start.6 = ((s8[5767168]{0:T(1024)(128)(4,1)}), s8[4194304]{0:T(1024)(128)(4,1)S(1)}, s32[]{:S(2)}) async-start(s8[5767168]{0:T(1024)(128)(4,1)} %bitcast.275), calls=%async_computation.6 | async-start | bytes 8388608
  370.0 13.0 %slice-start.7 = ((s8[5767168]{0:T(1024)(128)(4,1)}), s8[1572864]{0:T(1024)(128)(4,1)S(1)}, s32[]{:S(2)}) async-start(s8[5767168]{0:T(1024)(128)(4,1)} %bitcast.275), calls=%async_computation.7 | async-start | bytes 3145728
  370.0 21.3 %slice-start.2 = ((s8[5767168]{0:T(1024)(128)(4,1)}), s8[4194304]{0:T(1024)(128)(4,1)S(1)}, s32[]{:S(2)}) async-start(s8[5767168]{0:T(1024)(128)(4,1)} %bitcast.260), calls=%async_computation.2 | async-start | bytes 8388608
  378.5 12.8 %slice-start.3 = ((s8[5767168]{0:T(1024)(128)(4,1)}), s8[1572864]{0:T(1024)(128)(4,1)S(1)}, s32[]{:S(2)}) async-start(s8[5767168]{0:T(1024)(128)(4,1)} %bitcast.260), calls=%async_computation.3 | async-start | bytes 3145728
  379.9 63.0 %collective-permute-start.6 = (bf16[256,1024]{1,0:T(8,128)(2,1)}, bf16[256,1024]{1,0:T(8,128)(2,1)S(1)}, u32[]{:S(2)}, u32[]{:S(2)}) collective-permute-start(bf16[256,1024]{1,0:T(8,128)(2,1)} %get-tuple-element.216), channel_id=1, source_target_pairs={{0,0},{4,1},{1,2},{5,3},{2,4},{6,5},{3,6},{7,7},{8,8},{12,9},{9,10... | collective-permute-start | bytes 1572872 | tf_op jit(solution)/shard_map/ppermute | solution.py:1399
  381.6 61.3 %collective-permute-start.7 = (bf16[256,1024]{1,0:T(8,128)(2,1)}, bf16[256,1024]{1,0:T(8,128)(2,1)S(1)}, u32[]{:S(2)}, u32[]{:S(2)}) collective-permute-start(bf16[256,1024]{1,0:T(8,128)(2,1)} %get-tuple-element.213), channel_id=1, source_target_pairs={{1,0},{5,1},{0,2},{4,3},{3,4},{7,5},{2,6},{6,7},{9,8},{13,9},{8,10... | collective-permute-start | bytes 1572872 | tf_op jit(solution)/shard_map/ppermute | solution.py:1399
  383.0 8.3 %copy-start.6 = (f32[1024,1024]{1,0:T(8,128)S(1)}, f32[1024,1024]{1,0:T(8,128)}, u32[]{:S(2)}) copy-start(f32[1024,1024]{1,0:T(8,128)} %copy-done.5) | copy-start | bytes 12582916
  409.1 33.8 %collective-permute-start.8 = (bf16[256,1024]{1,0:T(8,128)(2,1)}, bf16[256,1024]{1,0:T(8,128)(2,1)S(1)}, u32[]{:S(2)}, u32[]{:S(2)}) collective-permute-start(bf16[256,1024]{1,0:T(8,128)(2,1)} %get-tuple-element.215), channel_id=1, source_target_pairs={{4,0},{0,1},{5,2},{1,3},{6,4},{2,5},{7,6},{3,7},{12,8},{8,9},{13,1... | collective-permute-start | bytes 1572872 | tf_op jit(solution)/shard_map/ppermute | solution.py:1399
  410.6 32.3 %collective-permute-start.9 = (bf16[256,1024]{1,0:T(8,128)(2,1)}, bf16[256,1024]{1,0:T(8,128)(2,1)S(1)}, u32[]{:S(2)}, u32[]{:S(2)}) collective-permute-start(bf16[256,1024]{1,0:T(8,128)(2,1)} %get-tuple-element.214), channel_id=1, source_target_pairs={{5,0},{1,1},{4,2},{0,3},{7,4},{3,5},{6,6},{2,7},{13,8},{9,9},{12,1... | collective-permute-start | bytes 1572872 | tf_op jit(solution)/shard_map/ppermute | solution.py:1399
  441.1 101.3 %collective-permute-start.11 = (bf16[2,256,1024]{2,1,0:T(8,128)(2,1)}, bf16[2,256,1024]{2,1,0:T(8,128)(2,1)S(1)}, u32[]{:S(2)}, u32[]{:S(2)}) collective-permute-start(bf16[2,256,1024]{2,1,0:T(8,128)(2,1)} %get-tuple-element.103), channel_id=1, source_target_pairs={{0,4},{1,5},{2,6},{3,7},{4,0},{5,1},{6,2},{7,3},{8,12},{9,13},{10,... | collective-permute-start | bytes 3145736 | tf_op jit(solution)/shard_map/ppermute | solution.py:831
  443.1 4.2 copy-start.53
  455.3 63.3 %copy-start.56 = (s32[256]{0:T(256)S(1)}, s32[256]{0:T(256)}, u32[]{:S(2)}) copy-start(s32[256]{0:T(256)} %copy-done.55) | copy-start | bytes 3076
  521.0 41.4 %collective-permute-start.10 = (bf16[2,1024,1024]{2,1,0:T(8,128)(2,1)}, bf16[2,1024,1024]{2,1,0:T(8,128)(2,1)}, u32[]{:S(2)}, u32[]{:S(2)}) collective-permute-start(bf16[2,1024,1024]{2,1,0:T(8,128)(2,1)} %get-tuple-element.101), channel_id=1, source_target_pairs={{0,4},{1,5},{2,6},{3,7},{4,0},{5,1},{6,2},{7,3},{8,12},{9,13},{10,... | collective-permute-start | bytes 12582920 | tf_op jit(solution)/shard_map/ppermute | solution.py:831
  531.7 6.7 copy-start.9
  531.7 6.7 copy-start.59
  538.4 4.0 copy-start.20
  538.4 4.4 copy-start.11
  542.9 5.6 copy-start.19
  544.8 10.8 %collective-permute-start.12 = (bf16[64,1024]{1,0:T(8,128)(2,1)S(1)}, bf16[64,1024]{1,0:T(8,128)(2,1)S(1)}, u32[]{:S(2)}, u32[]{:S(2)}) collective-permute-start(bf16[64,1024]{1,0:T(8,128)(2,1)S(1)} %get-tuple-element.234), channel_id=1, source_target_pairs={{0,0},{4,1},{1,2},{5,3},{2,4},{6,5},{3,6},{7,7},{8,8},{12,9},{9,10... | collective-permute-start | bytes 393224 | tf_op jit(solution)/shard_map/ppermute | solution.py:1399
  545.5 10.1 %collective-permute-start.13 = (bf16[64,1024]{1,0:T(8,128)(2,1)S(1)}, bf16[64,1024]{1,0:T(8,128)(2,1)S(1)}, u32[]{:S(2)}, u32[]{:S(2)}) collective-permute-start(bf16[64,1024]{1,0:T(8,128)(2,1)S(1)} %get-tuple-element.231), channel_id=1, source_target_pairs={{1,0},{5,1},{0,2},{4,3},{3,4},{7,5},{2,6},{6,7},{9,8},{13,9},{8,10... | collective-permute-start | bytes 393224 | tf_op jit(solution)/shard_map/ppermute | solution.py:1399
  550.5 9.5 %copy-start.48 = (bf16[4,2,2,2,32,1024]{5,4,3,2,1,0:T(8,128)(2,1)S(1)}, bf16[4,2,2,2,32,1024]{5,4,3,2,1,0:T(8,128)(2,1)}, u32[]{:S(2)}) copy-start(bf16[4,2,2,2,32,1024]{5,4,3,2,1,0:T(8,128)(2,1)} %get-tuple-element.79) | copy-start | bytes 6291460
  550.5 9.5 %copy-start.61 = (bf16[1024,1024]{1,0:T(8,128)(2,1)S(1)}, bf16[1024,1024]{1,0:T(8,128)(2,1)}, u32[]{:S(2)}) copy-start(bf16[1024,1024]{1,0:T(8,128)(2,1)} %get-tuple-element.105) | copy-start | bytes 6291460
  552.6 3.1 collective-permute-start.14
  552.6 6.3 collective-permute-start.15
  562.4 4.5 copy-start.46
  573.1 3.8 copy-start.44
  576.8 5.4 copy-start.42
  582.2 5.4 copy-start.62
  781.5 6.9 copy-start.32
  781.6 7.6 copy-start.31
  781.6 8.2 %copy-start.30 = (f32[32,1024]{1,0:T(8,128)S(1)}, f32[32,1024]{1,0:T(8,128)}, u32[]{:S(2)}) copy-start(f32[32,1024]{1,0:T(8,128)} %get-tuple-element.310) | copy-start | bytes 393220
  781.6 8.9 %copy-start.29 = (f32[32,1024]{1,0:T(8,128)S(1)}, f32[32,1024]{1,0:T(8,128)}, u32[]{:S(2)}) copy-start(f32[32,1024]{1,0:T(8,128)} %get-tuple-element.311) | copy-start | bytes 393220
  781.6 9.5 %copy-start.28 = (f32[32,1024]{1,0:T(8,128)S(1)}, f32[32,1024]{1,0:T(8,128)}, u32[]{:S(2)}) copy-start(f32[32,1024]{1,0:T(8,128)} %get-tuple-element.314) | copy-start | bytes 393220
  781.6 10.1 %copy-start.27 = (f32[32,1024]{1,0:T(8,128)S(1)}, f32[32,1024]{1,0:T(8,128)}, u32[]{:S(2)}) copy-start(f32[32,1024]{1,0:T(8,128)} %get-tuple-element.315) | copy-start | bytes 393220
  781.6 10.8 %copy-start.26 = (f32[32,1024]{1,0:T(8,128)S(1)}, f32[32,1024]{1,0:T(8,128)}, u32[]{:S(2)}) copy-start(f32[32,1024]{1,0:T(8,128)} %get-tuple-element.316) | copy-start | bytes 393220
  781.6 11.4 %copy-start.25 = (f32[32,1024]{1,0:T(8,128)S(1)}, f32[32,1024]{1,0:T(8,128)}, u32[]{:S(2)}) copy-start(f32[32,1024]{1,0:T(8,128)} %get-tuple-element.317) | copy-start | bytes 393220
  784.3 9.4 %copy-start.24 = (f32[32,2816]{1,0:T(8,128)S(1)}, f32[32,2816]{1,0:T(8,128)}, u32[]{:S(2)}) copy-start(f32[32,2816]{1,0:T(8,128)} %get-tuple-element.319) | copy-start | bytes 1081348
  784.3 10.2 %copy-start.23 = (f32[32,2816]{1,0:T(8,128)S(1)}, f32[32,2816]{1,0:T(8,128)}, u32[]{:S(2)}) copy-start(f32[32,2816]{1,0:T(8,128)} %get-tuple-element.320) | copy-start | bytes 1081348
  784.3 10.9 %copy-start.22 = (f32[88,1024]{1,0:T(8,128)S(1)}, f32[88,1024]{1,0:T(8,128)}, u32[]{:S(2)}) copy-start(f32[88,1024]{1,0:T(8,128)} %get-tuple-element.321) | copy-start | bytes 1081348
  (25 other events, 70.7 us)

commit v5 on v4

--- a/solution.py
+++ b/solution.py
@@ -463,7 +463,7 @@
 
 
 def fill_tables(line_ref, tab, adj):
-    for h in range(GROUP):
+    for h in range(line_ref.shape[0]):
         line = line_ref[h]
         far = line[:, TILE - 1 : TILE]
         for r, rows in enumerate(bias_table(line - far)):
@@ -595,11 +595,12 @@
                        do_ref, o_ref, lse_ref, dq_ref, own_ref, par_ref, gline_ref, gall_ref,
                        kb, vb, kt, qm, dm, qx, d_s, tab, adj, dq_acc, dk_acc, dv_acc, gt, gall):
     i = pl.program_id(1)
+    group = q_ref.shape[1] // HEAD_DIM
 
     @pl.when(i == 0)
     def _():
         for ref, s, target in place_tiles(causal, meta_ref, ko, kp):
-            for h in range(GROUP):
+            for h in range(group):
                 kb[h, rows_at(target), :] = with_lanes(
                     h, ref[s * TILE : (s + 1) * TILE, pair_lanes(h)], kext_ref[h % 2, rows_at(target), :]
                 )
@@ -607,30 +608,30 @@
             vb[rows_at(target), :] = ref[s * TILE : (s + 1) * TILE, :]
         for ref, s, target in place_tiles(causal, meta_ref, ko, kp):
             turned = ref[s * TILE : (s + 1) * TILE, :].T
-            for h in range(GROUP):
+            for h in range(group):
                 kt[target, h, 0:HEAD_DIM, :] = turned[head_rows(h), :]
         dk_acc[...] = jnp.zeros(dk_acc.shape, F32)
         dv_acc[...] = jnp.zeros(dv_acc.shape, F32)
         if causal:
-            for h in range(GROUP):
+            for h in range(group):
                 kb[h, 0:TILE, :] = kext_ref[h % 2, 0:TILE, :]
             vb[0:TILE, :] = jnp.zeros((TILE, vb.shape[1]), BF16)
             kt[0] = jnp.zeros(kt.shape[1:], BF16)
             for t in range(kt.shape[0]):
-                for h in range(GROUP):
+                for h in range(group):
                     kt[t, h, HEAD_DIM:, :] = jnp.ones((kt.shape[2] - HEAD_DIM, TILE), BF16)
             gt[...] = jnp.zeros(gt.shape, F32)
             gall[...] = jnp.zeros(gall.shape, F32)
             fill_tables(line_ref, tab, adj)
 
-    for h in range(GROUP):
+    for h in range(group):
         lanes = pair_lanes(h)
         pair, rows = h // 2, slice((h % 2) * TILE, (h % 2 + 1) * TILE)
         qm[pair, rows, :] = q_ref[:, lanes] * head_mask(h)
         dm[pair, rows, :] = do_ref[:, lanes] * head_mask(h)
         qx[h] = query_with_lanes(causal, h, q_ref, qext_ref, line_ref)
     both = jnp.concatenate([head_mask(0)] * 8 + [head_mask(1)] * 8, axis=0)
-    for pair in range(GROUP // 2):
+    for pair in range(group // 2):
         lanes = pair_lanes(2 * pair)
         product = do_ref[:, lanes].astype(F32) * o_ref[:, lanes].astype(F32)
         high = product.astype(BF16)
@@ -653,8 +654,8 @@
 
         ready = [products_of_head(h) for h in range(AHEAD)]
         probs_low, grads_low = {}, {}
-        for h in range(GROUP):
-            if h + AHEAD < GROUP:
+        for h in range(group):
+            if h + AHEAD < group:
                 ready.append(products_of_head(h + AHEAD))
             back = None
             for j in range(2):
@@ -693,7 +694,7 @@
         for j, total in enumerate((dk_acc, dv_acc)):
             for ref, s, target in place_tiles(causal, meta_ref, own_ref.at[j], par_ref.at[j]):
                 ref[s * TILE : (s + 1) * TILE, :] = total[rows_at(target), :].astype(BF16)
-        for h in range(GROUP):
+        for h in range(group):
             if causal:
                 gline_ref[h] = line_of(gt[h])
                 gall_ref[h] = gall[h : h + 1, :]
@@ -705,9 +706,9 @@
 VMEM_LIMIT = 60 * 1024 * 1024
 
 
-def attention_specs(own_rows, par_rows, keys):
-    groups = HEADS // GROUP
-    lanes = GROUP * HEAD_DIM
+def attention_specs(own_rows, par_rows, keys, group=GROUP):
+    groups = HEADS // group
+    lanes = group * HEAD_DIM
     return [
         pl.BlockSpec((TILE, lanes), lambda g, i, meta: (i, g)),
         pl.BlockSpec((own_rows, lanes), lambda g, i, meta: (0, g)),
@@ -716,7 +717,7 @@
         pl.BlockSpec((par_rows, lanes), lambda g, i, meta: (0, groups + g)),
         pl.BlockSpec((2, TILE, LANES), lambda g, i, meta: (0, i, 0)),
         pl.BlockSpec((2, keys, LANES), lambda g, i, meta: (0, 0, 0)),
-        pl.BlockSpec((GROUP, 1, TILE), lambda g, i, meta: (g, 0, 0)),
+        pl.BlockSpec((group, 1, TILE), lambda g, i, meta: (g, 0, 0)),
     ]
 
 
@@ -767,6 +768,27 @@
     )(meta, query, kv_own, kv_own, kv_par, kv_par, qext, kext, line)
 
 
+def back_scratch(keys, group, causal):
+    lanes = group * HEAD_DIM
+    table = (group, TILE, TILE) if causal else (1, 8, LANES)
+    return [
+        pltpu.VMEM((group, keys, LANES), BF16),
+        pltpu.VMEM((keys, lanes), BF16),
+        pltpu.VMEM((keys // TILE, group, HEAD_DIM + (16 if causal else 0), TILE), BF16),
+        pltpu.VMEM((group // 2, 2 * TILE, LANES), BF16),
+        pltpu.VMEM((group // 2, 2 * TILE, LANES), BF16),
+        pltpu.VMEM((group, TILE, LANES), BF16),
+        pltpu.VMEM((8, TILE), F32),
+        pltpu.VMEM(table, F32),
+        pltpu.VMEM(table, F32),
+        pltpu.VMEM((lanes, TILE), F32),
+        pltpu.VMEM((keys, lanes), F32),
+        pltpu.VMEM((keys, lanes), F32),
+        pltpu.VMEM(table, F32),
+        pltpu.VMEM((8, TILE), F32),
+    ]
+
+
 def attend_back_fast(meta, query, kv_own, kv_par, qext, kext, line, grad_mixed, mixed, lse, causal):
     tokens, width = query.shape
     own_rows, par_rows, keys = kv_own.shape[0], kv_par.shape[0], kext.shape[1]
@@ -788,22 +810,7 @@
                 line_spec,
                 line_spec,
             ],
-            scratch_shapes=[
-                pltpu.VMEM((GROUP, keys, LANES), BF16),
-                pltpu.VMEM((keys, lanes), BF16),
-                pltpu.VMEM((keys // TILE, GROUP, HEAD_DIM + (16 if causal else 0), TILE), BF16),
-                pltpu.VMEM((GROUP // 2, 2 * TILE, LANES), BF16),
-                pltpu.VMEM((GROUP // 2, 2 * TILE, LANES), BF16),
-                pltpu.VMEM((GROUP, TILE, LANES), BF16),
-                pltpu.VMEM((8, TILE), F32),
-                pltpu.VMEM(table, F32),
-                pltpu.VMEM(table, F32),
-                pltpu.VMEM((lanes, TILE), F32),
-                pltpu.VMEM((keys, lanes), F32),
-                pltpu.VMEM((keys, lanes), F32),
-                pltpu.VMEM(table, F32),
-                pltpu.VMEM((8, TILE), F32),
-            ],
+            scratch_shapes=back_scratch(keys, GROUP, causal),
         ),
         out_shape=[
             jax.ShapeDtypeStruct((tokens, width), BF16),
@@ -933,6 +940,7 @@
 class Gather:
     def __init__(self, links, shards, wholes, local_sem, send_sem, recv_sem):
         self.links, self.shards, self.wholes = links, shards, wholes
+        self.along_z = [len(shard.shape) == 3 for shard in shards]
         self.local_sem, self.send_sem, self.recv_sem = local_sem, send_sem, recv_sem
 
     def copy(self, w, slot, source, target, device):
@@ -948,6 +956,12 @@
             return [self.copy(w, k, self.shards[w], own, links.at_z[k]) for k in range(3)]
         if stage == 1:
             one, two = whole.at[:, core, y, x, :, left], whole.at[:, core, y, x, :, right]
+            if self.along_z[w]:
+                shard = self.shards[w]
+                return [
+                    self.copy(w, 3, shard.at[:, :, left], one, links.at_x),
+                    self.copy(w, 4, shard.at[:, :, right], two, links.at_y),
+                ]
             return [self.copy(w, 3, one, one, links.at_x), self.copy(w, 4, two, two, links.at_y)]
         if stage == 2:
             one, two = whole.at[:, core, y, :, :, left], whole.at[:, core, :, x, :, right]
@@ -957,17 +971,18 @@
 
     def local(self, w):
         links = self.links
-        own = self.wholes[w].at[links.z, links.core, links.y, links.x]
+        z = slice(None) if self.along_z[w] else links.z
+        own = self.wholes[w].at[z, links.core, links.y, links.x]
         return pltpu.make_async_copy(self.shards[w], own, self.local_sem.at[w])
 
     def begin(self):
         for w in range(len(self.shards)):
             self.local(w).start()
-            for copy in self.copies(0, w):
+            for copy in self.copies(1 if self.along_z[w] else 0, w):
                 copy.start()
 
     def advance(self, stage, w):
-        if stage == 1:
+        if stage == (2 if self.along_z[w] else 1):
             self.local(w).wait()
         for copy in self.copies(stage - 1, w):
             copy.wait_recv()
@@ -985,26 +1000,39 @@
         for w in range(len(self.shards)):
             for copy in self.copies(3, w):
                 copy.wait_recv()
-            for stage in range(4):
+            for stage in range(1 if self.along_z[w] else 0, 4):
                 for copy in self.copies(stage, w):
                     copy.wait_send()
 
 
-def gather_kernel(count, parts, *refs):
+def gather_kernel(count, later, parts, *refs):
     tokens = len(parts)
-    shards, moved = refs[:count], refs[count : count + tokens]
-    refs = refs[count + tokens :]
-    wholes, settled = refs[:count], refs[count : count + tokens]
-    local_sem, send_sem, recv_sem, move_local, move_send, move_recv = refs[count + tokens :]
+    shards, early, moved = refs[:count], refs[count : count + later], refs[count + later : count + later + tokens]
+    refs = refs[count + later + tokens :]
+    wholes, lines, settled = refs[:count], refs[count : count + later], refs[count + later : count + later + tokens]
+    refs = refs[count + later + tokens :]
+    local_sem, send_sem, recv_sem, z_local, z_send, z_recv, move_local, move_send, move_recv = refs
     links = Links()
     links.greet()
     gather = Gather(links, shards, wholes, local_sem, send_sem, recv_sem)
     gather.begin()
     finish = move_tokens(links, moved, settled, parts, move_local, move_send, move_recv)
+    waits = []
+    for w in range(later):
+        own = lines[w].at[links.z]
+        here = pltpu.make_async_copy(early[w], own, z_local.at[w])
+        here.start()
+        waits.append(here)
+        for k in range(3):
+            away = remote(early[w], own, z_send.at[w, k], z_recv.at[w, k], links.at_z[k])
+            away.start()
+            waits.append(away)
     for stage, w in gather.steps():
         gather.advance(stage, w)
     gather.end()
     finish()
+    for copy in waits:
+        copy.wait()
 
 
 def attend_gather_kernel(count, q_ref, ko, vo, kp, vp, qext_ref, kext_ref, line_ref, *refs):
@@ -1016,8 +1044,6 @@
     gather = Gather(links, shards, wholes, local_sem, send_sem, recv_sem)
     step = pl.program_id(0) * pl.num_programs(1) + pl.program_id(1)
     total = (HEADS * HEAD_DIM // q_ref.shape[1]) * 4
-    steps = gather.steps()
-
     @pl.when(step == 0)
     def _():
         links.greet()
@@ -1029,21 +1055,22 @@
         gather.begin()
 
     attend_kernel(True, None, q_ref, ko, vo, kp, vp, qext_ref, kext_ref, line_ref, o_ref, lse_ref, *scratch)
-    served = 0
     for n in range(total):
-        upto = len(steps) if n == total - 1 else GATHER_PACE[n] if n < len(GATHER_PACE) else served
-        if upto > served:
+        todo = [item for at, item in GATHER_PLAN if at == n]
+        if todo or n == total - 1:
             @pl.when(step == n)
-            def _(first=served, last=upto, n=n):
-                for stage, w in steps[first:last]:
+            def _(todo=todo, n=n):
+                for stage, w in todo:
                     gather.advance(stage, w)
                 if n == total - 1:
                     gather.end()
 
-            served = upto
-
-
-GATHER_PACE = (1, 4, 7, 9, 11, 13, 15)
+
+GATHER_PLAN = (
+    (0, (1, 3)), (1, (2, 0)), (1, (1, 4)), (2, (2, 1)), (2, (1, 5)), (3, (2, 2)), (3, (1, 6)), (4, (1, 7)),
+    (5, (2, 3)), (5, (3, 0)), (6, (2, 4)), (6, (2, 5)), (7, (3, 1)), (7, (2, 6)), (7, (2, 7)), (7, (3, 2)),
+    (7, (3, 3)), (7, (3, 4)), (7, (3, 5)), (7, (3, 6)), (7, (3, 7)),
+)
 
 
 def attend_gather(query, kv_own, kv_par, qext, kext, line, shards):
@@ -1073,7 +1100,7 @@
             jax.ShapeDtypeStruct((tokens, width), BF16),
             jax.ShapeDtypeStruct((groups, GROUP, tokens), F32),
         ]
-        + [jax.ShapeDtypeStruct((4, 2, 2, 2, *shard.shape), BF16) for shard in shards],
+        + [jax.ShapeDtypeStruct((4, 2, 2, 2, *shard.shape[-2:]), BF16) for shard in shards],
         compiler_params=pltpu.CompilerParams(
             vmem_limit_bytes=VMEM_LIMIT, collective_id=2, has_side_effects=True
         ),
@@ -1086,8 +1113,8 @@
     return outs[0], outs[1], [whole.reshape(-1, whole.shape[-1]) for whole in outs[2:]]
 
 
-def gather_weights(shards, moved):
-    count = len(shards)
+def gather_weights(shards, early, moved):
+    count, later, tokens = len(shards), len(early), len(moved)
     sent = sum(shard.size for shard in shards) * 2
     parts = [None if value.ndim == 3 else value.shape[2] // 2 for value in moved]
     settled = [
@@ -1095,26 +1122,32 @@
         for value, part in zip(moved, parts)
     ]
     outs = pl.pallas_call(
-        functools.partial(gather_kernel, count, parts),
-        in_specs=[pl.BlockSpec(memory_space=pltpu.VMEM)] * count
-        + [pl.BlockSpec(memory_space=pl.ANY)] * len(moved),
-        out_specs=[pl.BlockSpec(memory_space=pl.ANY)] * (count + len(moved)),
-        out_shape=[jax.ShapeDtypeStruct((4, 2, 2, 2, *shard.shape), BF16) for shard in shards] + settled,
+        functools.partial(gather_kernel, count, later, parts),
+        in_specs=[pl.BlockSpec(memory_space=pltpu.VMEM)] * (count + later)
+        + [pl.BlockSpec(memory_space=pl.ANY)] * tokens,
+        out_specs=[pl.BlockSpec(memory_space=pl.ANY)] * (count + later + tokens),
+        out_shape=[jax.ShapeDtypeStruct((4, 2, 2, 2, *shard.shape), BF16) for shard in shards]
+        + [jax.ShapeDtypeStruct((4, *shard.shape), BF16) for shard in early]
+        + settled,
         scratch_shapes=[
             pltpu.SemaphoreType.DMA((count,)),
             pltpu.SemaphoreType.DMA((count, 8)),
             pltpu.SemaphoreType.DMA((count, 8)),
-            pltpu.SemaphoreType.DMA((4, len(moved))),
-            pltpu.SemaphoreType.DMA((4, len(moved))),
-            pltpu.SemaphoreType.DMA((4, len(moved))),
+            pltpu.SemaphoreType.DMA((later,)),
+            pltpu.SemaphoreType.DMA((later, 3)),
+            pltpu.SemaphoreType.DMA((later, 3)),
+            pltpu.SemaphoreType.DMA((4, tokens)),
+            pltpu.SemaphoreType.DMA((4, tokens)),
+            pltpu.SemaphoreType.DMA((4, tokens)),
         ],
         compiler_params=pltpu.CompilerParams(
             vmem_limit_bytes=VMEM_LIMIT, collective_id=0, has_side_effects=True
         ),
         cost_estimate=pl.CostEstimate(flops=0, transcendentals=0, bytes_accessed=500 * sent),
         name="gather_weights",
-    )(*shards, *moved)
-    return [whole.reshape(-1, whole.shape[-1]) for whole in outs[:count]], outs[count:]
+    )(*shards, *early, *moved)
+    wholes = [whole.reshape(-1, whole.shape[-1]) for whole in outs[:count]]
+    return wholes, outs[count : count + later], outs[count + later :]
 
 
 def add_low(first, second):
@@ -1122,7 +1155,7 @@
 
 
 def return_tokens_kernel(links, source, target, part, local_sem, send_sem, recv_sem):
-    waits = []
+    waits, starts = [], []
     mine = 2 * (links.seq % 2) + links.core
     for s in range(4):
         half = (links.core + s) % 2
@@ -1131,14 +1164,16 @@
         here = pltpu.make_async_copy(source.at[s], slot, local_sem)
         away = remote(source.at[s], slot, send_sem.at[s], recv_sem.at[mine], links.at_plane(links.y, s))
 
-        @pl.when(stays)
-        def _(here=here):
-            here.start()
-
-        @pl.when(jnp.logical_not(stays))
-        def _(away=away):
-            away.start()
-
+        def start(stays=stays, here=here, away=away):
+            @pl.when(stays)
+            def _():
+                here.start()
+
+            @pl.when(jnp.logical_not(stays))
+            def _():
+                away.start()
+
+        starts.append(start)
         waits.append((stays, here, away))
 
     def finish():
@@ -1161,124 +1196,115 @@
             def _(arrived=arrived):
                 arrived.wait_recv()
 
-    return finish
-
-
-def scatter_kernel(shapes, part, *refs):
+    return starts, finish
+
+
+class Scatter:
+    def __init__(self, links, grads, sums, scratch):
+        count = len(grads)
+        self.links, self.grads, self.sums = links, grads, sums
+        self.kept, self.got_one, self.got_two, self.got_z, self.own, self.totals = (
+            scratch[j * count : (j + 1) * count] for j in range(6)
+        )
+        self.load_sem, self.store_sem, self.send_sem, self.recv_sem = scratch[6 * count :]
+
+    def copy(self, w, slot, source, target, device):
+        return remote(source, target, self.send_sem.at[w, slot], self.recv_sem.at[w, slot], device)
+
+    def copies(self, stage, w):
+        links, kept = self.links, self.kept[w]
+        z, core, y, x = links.z, links.core, links.y, links.x
+        half = kept.shape[-1] // 2
+        left, right = pl.ds(0, half), pl.ds(half, half)
+        if stage == 0:
+            return [self.copy(w, 0, self.grads[w].at[:, 1 - core], kept, links.at_core)]
+        if stage == 1:
+            got = self.got_one[w]
+            return [
+                self.copy(w, 1, kept.at[:, :, 1 - x, :, left], got.at[0], links.at_x),
+                self.copy(w, 2, kept.at[:, 1 - y, :, :, right], got.at[1], links.at_y),
+            ]
+        if stage == 2:
+            got = self.got_two[w]
+            return [
+                self.copy(w, 3, kept.at[:, 1 - y, x, :, left], got.at[0], links.at_y),
+                self.copy(w, 4, kept.at[:, y, 1 - x, :, right], got.at[1], links.at_x),
+            ]
+        return [
+            self.copy(w, 5 + k, kept.at[(z + k + 1) % 4, y, x], self.got_z[w].at[k], links.at_z[k])
+            for k in range(3)
+        ]
+
+    def load(self, w):
+        return pltpu.make_async_copy(self.grads[w].at[:, self.links.core], self.own[w], self.load_sem.at[w])
+
+    def store(self, w):
+        return pltpu.make_async_copy(self.totals[w], self.sums[w], self.store_sem.at[w])
+
+    def begin(self):
+        for w in range(len(self.grads)):
+            for copy in self.copies(0, w):
+                copy.start()
+            self.load(w).start()
+
+    def advance(self, stage, w):
+        kept, own, one, two = self.kept[w], self.own[w], self.got_one[w], self.got_two[w]
+        z, y, x = self.links.z, self.links.y, self.links.x
+        half, kind = kept.shape[-1] // 2, kept.dtype
+
+        def add(first, second):
+            return (first.astype(F32) + second.astype(F32)).astype(kind)
+
+        def core_step(b, carry):
+            zz, yy, xx = b // 4, (b // 2) % 2, b % 2
+            kept[zz, yy, xx] = add(kept[zz, yy, xx], own[zz, yy, xx])
+            return carry
+
+        def one_step(b, carry):
+            zz, other = b // 2, b % 2
+            kept[zz, other, x, :, 0:half] = add(kept[zz, other, x, :, 0:half], one[0, zz, other])
+            kept[zz, y, other, :, half : 2 * half] = add(
+                kept[zz, y, other, :, half : 2 * half], one[1, zz, other]
+            )
+            return carry
+
+        def two_step(zz, carry):
+            kept[zz, y, x, :, 0:half] = add(kept[zz, y, x, :, 0:half], two[0, zz])
+            kept[zz, y, x, :, half : 2 * half] = add(kept[zz, y, x, :, half : 2 * half], two[1, zz])
+            return carry
+
+        if stage == 1:
+            self.load(w).wait()
+        for copy in self.copies(stage - 1, w):
+            copy.wait_recv()
+        if stage < 4:
+            lax.fori_loop(0, (16, 8, 4)[stage - 1], (core_step, one_step, two_step)[stage - 1], 0)
+            for copy in self.copies(stage, w):
+                copy.start()
+        else:
+            total = kept[z, y, x].astype(F32)
+            for k in range(3):
+                total = total + self.got_z[w][k].astype(F32)
+            self.totals[w][...] = total
+            self.store(w).start()
+
+    def steps(self):
+        count = len(self.grads)
+        order = []
+        for t in range(count + 3):
+            order += [(stage, t - stage + 1) for stage in (1, 2, 3, 4) if 0 <= t - stage + 1 < count]
+        return order
+
+    def end(self):
+        for w in range(len(self.grads)):
+            self.store(w).wait()
+            for stage in range(4):
+                for copy in self.copies(stage, w):
+                    copy.wait_send()
+
+
+def scatter_scratch(shapes, types):
     count = len(shapes)
-    grads, tokens, sums, returned = refs[:count], refs[count], refs[count + 1 : 2 * count + 1], refs[2 * count + 1]
-    scratch = refs[2 * count + 2 :]
-    kept, got_one, got_two, got_z = (scratch[j * count : (j + 1) * count] for j in range(4))
-    own, totals = scratch[4 * count : 5 * count], scratch[5 * count : 6 * count]
-    load_sem, store_sem, send_sem, recv_sem, back_local, back_send, back_recv = scratch[6 * count :]
-    links = Links()
-    z, core, y, x = links.z, links.core, links.y, links.x
-    at_z, at_x, at_y, at_core = links.at_z, links.at_x, links.at_y, links.at_core
-    links.greet()
-    finish = return_tokens_kernel(links, tokens, returned, part, back_local, back_send, back_recv)
-
-    def send(w, slot, source, target, device):
-        copy = remote(source, target, send_sem.at[w, slot], recv_sem.at[w, slot], device)
-        copy.start()
-        return copy
-
-    def halves(w):
-        half = shapes[w][1] // 2
-        return pl.ds(0, half), pl.ds(half, half)
-
-    def add(first, second, dtype):
-        return (first.astype(F32) + second.astype(F32)).astype(dtype)
-
-    stages, loads, stores = [[] for _ in range(4)], [], []
-    for w in range(count):
-        stages[0].append([send(w, 0, grads[w].at[:, 1 - core], kept[w], at_core)])
-        load = pltpu.make_async_copy(grads[w].at[:, core], own[w], load_sem.at[w])
-        load.start()
-        loads.append(load)
-    for t in range(count + 3):
-        if t < count:
-            w, dtype = t, kept[t].dtype
-            left, right = halves(w)
-            loads[w].wait()
-            stages[0][w][0].wait_recv()
-
-            def core_step(b, carry, w=w, dtype=dtype):
-                zz, yy, xx = b // 4, (b // 2) % 2, b % 2
-                kept[w][zz, yy, xx] = add(kept[w][zz, yy, xx], own[w][zz, yy, xx], dtype)
-                return carry
-
-            lax.fori_loop(0, 16, core_step, 0)
-            half = shapes[w][1] // 2
-            stages[1].append([
-                send(w, 1, kept[w].at[:, :, 1 - x, :, left], got_one[w].at[0], at_x),
-                send(w, 2, kept[w].at[:, 1 - y, :, :, right], got_one[w].at[1], at_y),
-            ])
-        if 0 <= t - 1 < count:
-            w, dtype = t - 1, kept[t - 1].dtype
-            left, right = halves(w)
-            half = shapes[w][1] // 2
-            for copy in stages[1][w]:
-                copy.wait_recv()
-
-            def one_step(b, carry, w=w, dtype=dtype, half=half):
-                zz, other = b // 2, b % 2
-                kept[w][zz, other, x, :, 0:half] = add(
-                    kept[w][zz, other, x, :, 0:half], got_one[w][0, zz, other], dtype
-                )
-                kept[w][zz, y, other, :, half : 2 * half] = add(
-                    kept[w][zz, y, other, :, half : 2 * half], got_one[w][1, zz, other], dtype
-                )
-                return carry
-
-            lax.fori_loop(0, 8, one_step, 0)
-            stages[2].append([
-                send(w, 3, kept[w].at[:, 1 - y, x, :, left], got_two[w].at[0], at_y),
-                send(w, 4, kept[w].at[:, y, 1 - x, :, right], got_two[w].at[1], at_x),
-            ])
-        if 0 <= t - 2 < count:
-            w, dtype = t - 2, kept[t - 2].dtype
-            half = shapes[w][1] // 2
-            for copy in stages[2][w]:
-                copy.wait_recv()
-
-            def two_step(zz, carry, w=w, dtype=dtype, half=half):
-                kept[w][zz, y, x, :, 0:half] = add(
-                    kept[w][zz, y, x, :, 0:half], got_two[w][0, zz], dtype
-                )
-                kept[w][zz, y, x, :, half : 2 * half] = add(
-                    kept[w][zz, y, x, :, half : 2 * half], got_two[w][1, zz], dtype
-                )
-                return carry
-
-            lax.fori_loop(0, 4, two_step, 0)
-            stages[3].append([
-                send(w, 5 + k, kept[w].at[(z + k + 1) % 4, y, x], got_z[w].at[k], at_z[k])
-                for k in range(3)
-            ])
-        if 0 <= t - 3 < count:
-            w = t - 3
-            for copy in stages[3][w]:
-                copy.wait_recv()
-            total = kept[w][z, y, x].astype(F32)
-            for k in range(3):
-                total = total + got_z[w][k].astype(F32)
-            totals[w][...] = total
-            store = pltpu.make_async_copy(totals[w], sums[w], store_sem.at[w])
-            store.start()
-            stores.append(store)
-    for w in range(count):
-        stores[w].wait()
-        for stage in stages:
-            for copy in stage[w]:
-                copy.wait_send()
-    finish()
-
-
-def scatter_grads(grads, tokens):
-    part = tokens.shape[1]
-    count = len(grads)
-    shapes = [(grad.shape[0] // 32, grad.shape[1]) for grad in grads]
-    types = [grad.dtype for grad in grads]
 
     def buffers(*lead, halved=False):
         return [
@@ -1286,13 +1312,8 @@
             for (rows, width), kind in zip(shapes, types)
         ]
 
-    return pl.pallas_call(
-        functools.partial(scatter_kernel, shapes, part),
-        in_specs=[pl.BlockSpec(memory_space=pl.ANY)] * (count + 1),
-        out_specs=[pl.BlockSpec(memory_space=pl.ANY)] * (count + 1),
-        out_shape=[jax.ShapeDtypeStruct(shape, F32) for shape in shapes]
-        + [jax.ShapeDtypeStruct((2, 2 * part, tokens.shape[2]), BF16)],
-        scratch_shapes=buffers(4, 2, 2)
+    return (
+        buffers(4, 2, 2)
         + buffers(2, 4, 2, halved=True)
         + buffers(2, 4, halved=True)
         + buffers(3)
@@ -1303,6 +1324,137 @@
             pltpu.SemaphoreType.DMA((count,)),
             pltpu.SemaphoreType.DMA((count, 8)),
             pltpu.SemaphoreType.DMA((count, 8)),
+        ]
+    )
+
+
+def rows_by_device(grads):
+    return [grad.reshape(4, 2, 2, 2, grad.shape[0] // 32, grad.shape[1]) for grad in grads]
+
+
+def scatter_kernel(count, part, *refs):
+    grads, tokens, sums, returned = refs[:count], refs[count], refs[count + 1 : 2 * count + 1], refs[2 * count + 1]
+    scratch, (back_local, back_send, back_recv) = refs[2 * count + 2 : -3], refs[-3:]
+    links = Links()
+    links.greet()
+    scatter = Scatter(links, grads, sums, scratch)
+    scatter.begin()
+    starts, finish = return_tokens_kernel(links, tokens, returned, part, back_local, back_send, back_recv)
+    for start in starts:
+        start()
+    for stage, w in scatter.steps():
+        scatter.advance(stage, w)
+    scatter.end()
+    finish()
+
+
+def attend_scatter_kernel(count, *refs):
+    inputs, grads, tokens, refs = refs[:11], refs[11 : 11 + count], refs[11 + count], refs[12 + count :]
+    outs, sums, returned, refs = refs[:5], refs[5 : 5 + count], refs[5 + count], refs[6 + count :]
+    scratch, buffers, (back_local, back_send, back_recv) = refs[:14], refs[14:-3], refs[-3:]
+    links = Links()
+    scatter = Scatter(links, grads, sums, buffers)
+    step = pl.program_id(0) * pl.num_programs(1) + pl.program_id(1)
+    total = (HEADS * HEAD_DIM // inputs[0].shape[1]) * 4
+
+    def tokens_back():
+        return return_tokens_kernel(
+            links, tokens, returned, tokens.shape[1], back_local, back_send, back_recv
+        )
+
+    @pl.when(step == 0)
+    def _():
+        links.greet()
+        scatter.begin()
+        for start in tokens_back()[0]:
+            start()
+
+    attend_back_kernel(True, None, *inputs, *outs, *scratch)
+    for n in range(total):
+        todo = [item for at, item in SCATTER_PACE if at == n]
+        if todo or n == total - 1:
+            @pl.when(step == n)
+            def _(todo=todo, n=n):
+                for stage, w in todo:
+                    scatter.advance(stage, w)
+                if n == total - 1:
+                    scatter.end()
+                    tokens_back()[1]()
+
+
+SCATTER_PACE = (
+    (1, (1, 0)), (3, (1, 1)), (4, (2, 0)), (4, (1, 2)), (7, (2, 1)), (7, (1, 3)), (8, (3, 0)), (9, (1, 4)),
+    (11, (2, 2)), (12, (3, 1)), (12, (2, 3)), (13, (4, 0)), (13, (2, 4)), (14, (3, 2)), (14, (3, 3)),
+    (15, (3, 4)), (15, (4, 1)), (15, (4, 2)), (15, (4, 3)), (15, (4, 4)),
+)
+
+
+def attend_scatter(query, kv_own, kv_par, qext, kext, line, grad_mixed, mixed, lse, grads, back):
+    tokens, width = query.shape
+    own_rows, par_rows, keys = kv_own.shape[0], kv_par.shape[0], kext.shape[1]
+    group, count = GROUP // 2, len(grads)
+    groups, lanes = HEADS // group, group * HEAD_DIM
+    block = pl.BlockSpec((TILE, lanes), lambda g, i: (i, g))
+    line_spec = pl.BlockSpec((group, 1, TILE), lambda g, i: (g, 0, 0))
+    whole = pl.BlockSpec(memory_space=pl.ANY)
+    shapes = [(grad.shape[0] // 32, grad.shape[1]) for grad in grads]
+    outs = pl.pallas_call(
+        functools.partial(attend_scatter_kernel, count),
+        grid=(groups, tokens // TILE),
+        in_specs=[without_meta(spec) for spec in attention_specs(own_rows, par_rows, keys, group)]
+        + [block, block, pl.BlockSpec((1, group, TILE), lambda g, i: (g, 0, i))]
+        + [whole] * (count + 1),
+        out_specs=[
+            block,
+            pl.BlockSpec((2, own_rows, lanes), lambda g, i: (0, 0, g)),
+            pl.BlockSpec((2, par_rows, lanes), lambda g, i: (0, 0, g)),
+            line_spec,
+            line_spec,
+        ]
+        + [whole] * (count + 1),
+        scratch_shapes=back_scratch(keys, group, True)
+        + scatter_scratch(shapes, [grad.dtype for grad in grads])
+        + [
+            pltpu.SemaphoreType.DMA,
+            pltpu.SemaphoreType.DMA((4,)),
+            pltpu.SemaphoreType.DMA((4,)),
+        ],
+        out_shape=[
+            jax.ShapeDtypeStruct((tokens, width), BF16),
+            jax.ShapeDtypeStruct((2, own_rows, width), BF16),
+            jax.ShapeDtypeStruct((2, par_rows, width), BF16),
+            jax.ShapeDtypeStruct((HEADS, 1, TILE), F32),
+            jax.ShapeDtypeStruct((HEADS, 1, TILE), F32),
+        ]
+        + [jax.ShapeDtypeStruct(shape, F32) for shape in shapes]
+        + [jax.ShapeDtypeStruct((2, 2 * back.shape[1], width), BF16)],
+        compiler_params=pltpu.CompilerParams(
+            vmem_limit_bytes=67043328, collective_id=3, has_side_effects=True
+        ),
+        cost_estimate=pl.CostEstimate(
+            flops=tokens * keys * width * 10, bytes_accessed=10 * (tokens + keys) * width,
+            transcendentals=tokens * keys * HEADS // 2,
+        ),
+        name="attend_scatter",
+    )(query, kv_own, kv_own, kv_par, kv_par, qext, kext, line, grad_mixed, mixed,
+      lse.reshape(groups, group, tokens), *rows_by_device(grads), back)
+    return outs[:5], outs[5 : 5 + count], outs[5 + count]
+
+
+def scatter_grads(grads, tokens):
+    part = tokens.shape[1]
+    count = len(grads)
+    shapes = [(grad.shape[0] // 32, grad.shape[1]) for grad in grads]
+    types = [grad.dtype for grad in grads]
+
+    return pl.pallas_call(
+        functools.partial(scatter_kernel, count, part),
+        in_specs=[pl.BlockSpec(memory_space=pl.ANY)] * (count + 1),
+        out_specs=[pl.BlockSpec(memory_space=pl.ANY)] * (count + 1),
+        out_shape=[jax.ShapeDtypeStruct(shape, F32) for shape in shapes]
+        + [jax.ShapeDtypeStruct((2, 2 * part, tokens.shape[2]), BF16)],
+        scratch_shapes=scatter_scratch(shapes, types)
+        + [
             pltpu.SemaphoreType.DMA,
             pltpu.SemaphoreType.DMA((4,)),
             pltpu.SemaphoreType.DMA((4,)),
@@ -1314,9 +1466,7 @@
             flops=0, transcendentals=0, bytes_accessed=16 * sum(grad.size for grad in grads)
         ),
         name="scatter_grads",
-    )(*[
-        grad.reshape(4, 2, 2, 2, rows, width) for grad, (rows, width) in zip(grads, shapes)
-    ], tokens)
+    )(*rows_by_device(grads), tokens)
 
 
 def norm_scale(value):
@@ -1415,8 +1565,8 @@
     small = jnp.concatenate([norm_self, norm_cross, norm_ff, rel_bias])
     small_rows = norm_self.shape[0]
     small = jnp.broadcast_to(jnp.pad(small, (0, 2 * LANES - small.shape[0])), (8, 2 * LANES))
-    wholes, (inputs_low, encoder, codes) = gather_weights(
-        [small, k_self, v_self, q_self], [hidden_in, encoder_states, codes]
+    wholes, ff_lines, (inputs_low, encoder, codes) = gather_weights(
+        [small, k_self, v_self, q_self], [wi_gate, wi_up, wo_ff], [hidden_in, encoder_states, codes]
     )
     small, wk, wv, wq = wholes
     small = small.reshape(32, 8, 2 * LANES)[:, 0].astype(F32)
@@ -1461,9 +1611,9 @@
     query = dot(normed_self, wq).astype(BF16)
     mixed, self_lse, wholes = attend_gather(
         query, kv_own, kv_par, query_codes, key_codes, line,
-        [k_cross, v_cross, o_self, q_cross, o_cross, wi_gate, wi_up, wo_ff],
-    )
-    ck, cv, wo, cq, co, w_gate, w_up, w_down = wholes
+        [*ff_lines, k_cross, v_cross, o_self, q_cross, o_cross],
+    )
+    w_gate, w_up, w_down, ck, cv, wo, cq, co = wholes
     cross_kv_own = jnp.concatenate(
         [dot(encoder, ck).astype(BF16), dot(encoder, cv).astype(BF16)], axis=1
     )
@@ -1504,7 +1654,7 @@
     cross_got = add_low(cross_own, exchange(cross_par, *CORE))
     grad_ck, grad_cv = dot_weight(encoder, cross_got[0]), dot_weight(encoder, cross_got[1])
     grad_encoder = (dot_back(cross_got[0], ck) + dot_back(cross_got[1], cv)).astype(BF16)
-    grad_encoder = return_tokens(grad_encoder.reshape(4, enc_part, width)).astype(F32)
+    grad_encoder = grad_encoder.reshape(4, enc_part, width)
     grad_cq = dot_weight(normed_cross, grad_cross_query)
     grad_normed_cross = dot_back(grad_cross_query, cq)
     cross_part, grad_gain_cross = norm_back(after_self, gain_cross, grad_normed_cross)
@@ -1512,10 +1662,14 @@
     self_out_low = grad_after_self.astype(BF16)
     grad_wo = dot_weight(mixed, self_out_low)
     grad_mixed = dot_back(self_out_low, wo).astype(BF16)
-    grad_query, self_own, self_par, grad_line, grad_all = attend_back_fast(
-        meta, query, kv_own, kv_par, query_codes, key_codes, line, grad_mixed, mixed, self_lse, True
-    )
-    grad_query, grad_encoder = lax.optimization_barrier((grad_query, grad_encoder))
+    (grad_query, self_own, self_par, grad_line, grad_all), ff_grads, grad_encoder = (
+        attend_scatter(
+            query, kv_own, kv_par, query_codes, key_codes, line, grad_mixed, mixed, self_lse,
+            [grad_w_gate, grad_w_up, grad_w_down, grad_co, grad_cq], grad_encoder,
+        )
+    )
+    grad_w_gate, grad_w_up, grad_w_down, grad_co, grad_cq = ff_grads
+    grad_encoder = grad_encoder.astype(F32)[:, None]
     self_got = add_low(self_own, exchange(self_par, *CORE))
     grad_wq = dot_weight(normed_self, grad_query)
     grad_wk, grad_wv = dot_weight(normed_self, self_got[0]), dot_weight(normed_self, self_got[1])
@@ -1533,11 +1687,11 @@
     small_grads = jnp.pad(small_grads, ((0, 0), (0, 2 * LANES - small_grads.shape[1])))
     small_grads = jnp.broadcast_to(small_grads[:, None], (32, 8, 2 * LANES)).reshape(256, 2 * LANES)
     order = [
-        grad_wk, grad_wv, grad_w_gate, grad_w_up, grad_w_down, grad_ck, grad_cv, grad_cq, grad_co,
+        grad_ck, grad_cv, grad_wk, grad_wv,
         grad_wo, grad_wq, small_grads,
     ]
     (
-        grad_wk, grad_wv, grad_w_gate, grad_w_up, grad_w_down, grad_ck, grad_cv, grad_cq, grad_co,
+        grad_ck, grad_cv, grad_wk, grad_wv,
         grad_wo, grad_wq, small_grads, grad_hidden_in,
     ) = scatter_grads(order, grad_hidden_in)
     small_grads = small_grads[0]

time: 801 us -> 734 us (0.916)
  Pallas kernels: 518 us -> 463 us
  starting transfers between devices: 33.9 us -> 16.4 us
    pallas_call x2 -> x1, Pallas kernels: 91.8 us -> 28.3 us  [attend_back_fast(): pl.pallas_call(functools.partial(attend_back_kernel, causal), grid_spec=p...]
    pallas_call x2 -> x3, Pallas kernels: 257 us -> 287 us  [the longest x1 126 us: attend_scatter(): pl.pallas_call(functools.partial(attend_scatter_kernel, count), grid=(gro...]
    pallas_call x1, Pallas kernels: 150 us -> 128 us  [attend_gather(): pl.pallas_call(functools.partial(attend_gather_kernel, count), grid=(grou...]
    ppermute x4, starting transfers between devices: 13.1 us -> 2.17 us  [exchange(): return lax.ppermute(value, AXES, pairs)]
  transfers between devices with their start and end apart: 16 -> 12, of which waited for: 1 -> 0; matrix products, arithmetic and copies ran while one was open for 12% -> 10% of each run, Pallas kernels for 14% -> 7%
where the time goes in v5:
time: 734 us; the launch traced here: 727 us
  Pallas kernels  463 us (63%)
  matrix products  181 us (25%)
  other arithmetic  39 us (5%)
  local copies, waits for them, and re-layouts  26 us (4%)
  starting transfers between devices  16.4 us (2%)
    pallas_call x1, Pallas kernels, attend_gather(): pl.pallas_call(functools.partial(attend_gather_kernel, count), grid=(grou...  128 us
    pallas_call x1, Pallas kernels, attend_scatter(): pl.pallas_call(functools.partial(attend_scatter_kernel, count), grid=(gro...  126 us
    dot_general x22, matrix products, contract(): lax.dot_general(left, right, (((left_dim,), (right_dim,)), ((), ())), pre...  106 us
    pallas_call x1, Pallas kernels, scatter_grads(): pl.pallas_call(functools.partial(scatter_kernel, count, part), in_specs=[...  90.8 us
    dot_general x11, matrix products, dot(): return jnp.dot(rows, weight, preferred_element_type=F32)  74.8 us
    pallas_call x1, Pallas kernels, gather_weights(): pl.pallas_call(functools.partial(gather_kernel, count, later, parts), in_...  70.1 us
    pallas_call x1, Pallas kernels, attend_back_fast(): pl.pallas_call(functools.partial(attend_back_kernel, causal), grid_spec=p...  28.3 us
    pallas_call x1, Pallas kernels, attend_fast(): pl.pallas_call(functools.partial(attend_kernel, causal), grid_spec=pltpu....  19.6 us
  transfers between devices with their start and end apart: 12, of which 0 were waited for; matrix products, arithmetic and copies ran while one was open for 10% of the time, Pallas kernels for 7%

profile of v5, /device:TPU:0, one launch (start us, length us, event | category | flops | bytes accessed | tf_op | source)
XLA Modules:
  0.0 727.3 jit_solution(1781744959236998964)
XLA Ops:
  4.1 70.1 %gather_weights.1 = (bf16[4,2,2,2,8,256]{5,4,3,2,1,0:T(8,128)(2,1)}, bf16[4,2,2,2,32,1024]{5,4,3,2,1,0:T(8,128)(2,1)}, bf16[4,2,2,2,32,1024]{5,4,3,2,1,0:T(8,128...) custom-call(bf16[8,256]{1,0:T(8,128)(2,1)} %broadcast_in_dim.108.ref, ...), custom_call_target="tpu_custom_call" | custom-call | bytes 100352000 | tf_op jit(solution)/shard_map/gather_weights/pallas_call | solution.py:1124
  74.2 0.9 slice.181
  75.3 2.2 fusion.7
  78.1 2.1 fusion.9
  80.3 2.4 convolution_convert_fusion.15
  82.6 2.4 convolution_convert_fusion.14
  85.0 2.5 pad_maximum_fusion.ko.vo.refs_1_.refs_2_
  93.4 1.9 broadcast_select_fusion.1
  95.3 1.1 pad_maximum_fusion.2.kext_ref.refs_6_
  96.4 3.7 convolution_convert_fusion.16.q_ref.refs_0_
  100.1 127.9 %attend_gather.1 = (bf16[1024,1024]{1,0:T(8,128)(2,1)}, f32[2,8,1024]{2,1,0:T(8,128)}, bf16[4,2,2,2,32,2816]{5,4,3,2,1,0:T(8,128)(2,1)}, bf16[4,2,2,2,32,2816]{5...) custom-call(bf16[1024,1024]{1,0:T(8,128)(2,1)} %convolution_convert_, ...), custom_call_target="tpu_custom_call" | custom-call | flops 9663676416 | bytes 13631488 | tf_op jit(solution)/shard_map/attend_gather/pallas_call | solution.py:1082
  228.1 2.4 convolution_convert_fusion.18
  230.5 2.3 convolution_convert_fusion.17
  233.4 4.4 multiply_reduce_fusion.5
  239.1 6.7 convolution_convert_fusion.13.q_ref
  246.7 0.9 dynamic-slice_bitcast_fusion.6
  247.6 2.8 collective-permute-start.3
  250.6 4.3 collective-permute-start.5
  254.9 19.6 %attend_cross.1 = (bf16[1024,1024]{1,0:T(8,128)(2,1)}, f32[2,8,1024]{2,1,0:T(8,128)}) custom-call(s32[12]{0:T(128)} %pad_add_fusion.1.meta_ref, bf16[1024,1024]{1,0:T(8,128)(2,1)} %convolution_convert_fusion.13.q_ref, bf16[256,2048]{1,0:T(8,128)(2,1)} %copy-done.21, bf16[256,2048]{1,0:T(8,128)(2,1)} %copy-done.21, ...), custom_call_target="tpu_custom_call" | custom-call | flops 2147483648 | bytes 6291456 | tf_op jit(solution)/shard_map/attend_cross/pallas_call | solution.py:746
  274.5 6.0 multiply_reduce_fusion.4
  280.6 2.0 copy-done.5
  283.0 8.8 %fusion.81 = f32[1024,2816]{1,0:T(8,128)} fusion(bf16[1024,1024]{1,0:T(8,128)(2,1)S(1)} %multiply_convert_fusion.2, bf16[1024,2816]{1,0:T(8,128)(2,1)S(1)} %bitcast.253), kind=kOutput, calls=%fused_computation.248 | convolution fusion | flops 5905580032 | bytes 19398656 | tf_op jit(solution)/shard_map/dot_general | solution.py:1491
  292.4 8.9 %fusion.80 = f32[1024,2816]{1,0:T(8,128)} fusion(bf16[1024,1024]{1,0:T(8,128)(2,1)S(1)} %bitcast.205, bf16[2816,1024]{1,0:T(8,128)(2,1)S(1)} %bitcast.262), kind=kOutput, calls=%fused_computation.247 | convolution fusion | flops 5905580032 | bytes 19398656 | tf_op jit(solution)/shard_map/dot_general | solution.py:398
  301.3 25.2 %multiply_convert_fusion = (bf16[1024,2816]{1,0:T(8,128)(2,1)}, bf16[1024,2816]{1,0:T(8,128)(2,1)}, bf16[1024,2816]{1,0:T(8,128)(2,1)}) fusion(f32[1024,2816]{1,0:T(8,128)} %fusion.81, f32[1024,2816]{1,0:T(8,128)} %fusion.80, bf16[1024,1024]{1,0:T(8,128)(2,1)} %copy-done.16, bf16[1024,2816]{1,0:T(8,128)(2,1)} %bitcast.257), kind=kOutput, calls=%fused_computation.9 | convolution fusion | flops 5980553216 | bytes 48234496 | tf_op jit(solution)/shard_map/dot_general | solution.py:1491
  326.5 10.6 %add_convert_fusion.1 = bf16[1024,1024]{1,0:T(8,128)(2,1)S(1)} fusion(f32[1024,1024]{1,0:T(8,128)} %copy-done.5, bf16[1024,2816]{1,0:T(8,128)(2,1)} %get-tuple-element.212, bf16[2816,1024]{1,0:T(8,128)(2,1)} %bitcast.259), kind=kOutput, calls=%fused_computation.41 | convolution fusion | flops 5907677184 | bytes 17825792 | tf_op jit(solution)/shard_map/dot_general | solution.py:1491
  337.1 8.1 %convolution_convert_fusion = bf16[2816,1024]{1,0:T(8,128)(2,1)} fusion(bf16[1024,2816]{1,0:T(8,128)(2,1)S(1)} %copy-done.63, bf16[1024,1024]{1,0:T(8,128)(2,1)S(1)} %bitcast.206), kind=kOutput, calls=%fused_computation.13 | convolution fusion | flops 5908463616 | bytes 13631488 | tf_op jit(solution)/shard_map/dot_general | solution.py:398
  345.2 10.0 %fusion.82 = f32[1024,1024]{1,0:T(8,128)} fusion(bf16[1024,2816]{1,0:T(8,128)(2,1)S(1)} %copy-done.61, bf16[1024,2816]{1,0:T(8,128)(2,1)} %bitcast.258), kind=kOutput, calls=%fused_computation.249 | convolution fusion | flops 5905580032 | bytes 15728640 | tf_op jit(solution)/shard_map/dot_general | solution.py:398
  355.2 8.3 %convolution_convert_fusion.1 = bf16[1024,2816]{1,0:T(8,128)(2,1)} fusion(bf16[1024,1024]{1,0:T(8,128)(2,1)S(1)} %copy-done.17, bf16[1024,2816]{1,0:T(8,128)(2,1)S(1)} %copy-done.61), kind=kOutput, calls=%fused_computation.14 | convolution fusion | flops 5908463616 | bytes 13631488 | tf_op jit(solution)/shard_map/dot_general | solution.py:398
  363.5 8.5 %convolution_convert_fusion.2 = bf16[1024,2816]{1,0:T(8,128)(2,1)} fusion(bf16[1024,1024]{1,0:T(8,128)(2,1)S(1)} %copy-done.17, bf16[1024,2816]{1,0:T(8,128)(2,1)S(1)} %bitcast.272), kind=kOutput, calls=%fused_computation.15 | convolution fusion | flops 5908463616 | bytes 13631488 | tf_op jit(solution)/shard_map/dot_general | solution.py:398
  372.0 9.5 %multiply_reduce_fusion = (f32[1024]{0:T(1024)}, f32[1024]{0:T(1024)S(1)}, f32[1024,1024]{1,0:T(8,128)S(1)}) fusion(f32[1024,1024]{1,0:T(8,128)S(1)} %copy-done.6, f32[1024]{0:T(1024)S(1)} %get-tuple-element.254, f32[1024]{0:T(1024)S(1)} %mul.346, f32[1024,1024]{1,0:T(8,128)S(1)} %copy-done.62, bf16[1024,2816]{1,0:T(8,128)(2,1)} %get-tuple-element.213, ...), kind=kOutput, calls=%fused_computation.36 | convolution fusion | flops 5912918016 | bytes 24133632 | tf_op jit(solution)/shard_map/dot_general | solution.py:398
  381.4 2.0 subtract_add_fusion.1
  383.4 3.7 convolution_convert_fusion.12.do_ref
  387.1 1.0 dynamic-slice_bitcast_fusion.2
  388.1 1.7 collective-permute-start.6
  389.8 1.1 collective-permute-start.7
  391.0 3.8 convolution_convert_fusion.8
  394.7 1.5 collective-permute-start.8
  396.2 2.0 collective-permute-start.9
  398.2 28.3 %attend_cross_back.1 = (bf16[1024,1024]{1,0:T(8,128)(2,1)}, bf16[2,256,1024]{2,1,0:T(8,128)(2,1)}, bf16[2,256,1024]{2,1,0:T(8,128)(2,1)}, f32[16,1,256]{2,1,0:T(1,128)}, f32[16,1,256]{2,1,0:T(1,128)}) custom-call(s32[12]{0:T(128)} %pad_add_fusion.1.meta_ref, bf16[1024,1024]{1,0:T(8,128)(2,1)} %convolution_convert_fusion.13.q_ref, ...), custom_call_target="tpu_custom_call" | custom-call | flops 5368709120 | bytes 15728640 | tf_op jit(solution)/shard_map/attend_cross_back/pallas_call | solution.py:799
  426.5 1.6 collective-permute-start.10
  428.5 1.5 maximum_bitcast_fusion
  430.4 1.4 copy-done.9
  432.5 3.2 multiply_reduce_fusion.1
  435.7 1.4 subtract_add_fusion
  437.3 3.7 convolution_convert_fusion.9.refs_8_
  441.0 3.9 convolution_convert_fusion.7
  446.9 1.5 fusion.21
  448.4 125.8 %attend_scatter.1 = (bf16[1024,1024]{1,0:T(8,128)(2,1)}, bf16[2,1024,1024]{2,1,0:T(8,128)(2,1)}, bf16[2,1024,1024]{2,1,0:T(8,128)(2,1)}, f32[16,1,256]{2,1,0:T(1...) custom-call(bf16[1024,1024]{1,0:T(8,128)(2,1)} %convolution_convert_, ...), custom_call_target="tpu_custom_call" | custom-call | flops 24159191040 | bytes 34078720 | tf_op jit(solution)/shard_map/attend_scatter/pallas_call | solution.py:1401
  576.6 6.7 convolution_convert_fusion.4
  584.2 1.1 bitcast_convert_fusion.1
  585.3 2.1 convolution_convert_fusion.10
  587.4 2.1 convolution_convert_fusion.11
  589.5 2.4 fusion.83
  591.9 4.4 add_convert_fusion
  596.3 2.4 fusion.19
  598.7 3.8 convolution_convert_fusion.5
  602.5 3.8 convolution_convert_fusion.6
  606.3 5.2 fusion.18
  611.7 5.5 fusion.17
  617.2 3.7 convolution_convert_fusion.3
  621.6 90.8 %scatter_grads.1 = (f32[32,1024]{1,0:T(8,128)}, f32[32,1024]{1,0:T(8,128)}, f32[32,1024]{1,0:T(8,128)}, f32[32,1024]{1,0:T(8,128)}, f32[32,1024]{1,0:T(8,128)}, ...) custom-call(bf16[4,2,2,2,32,1024]{5,4,3,2,1,0:T(8,128)(2,1)} %bitcast.203, ...), custom_call_target="tpu_custom_call" | custom-call | bytes 101711872 | tf_op jit(solution)/shard_map/scatter_grads/pallas_call | solution.py:1450
  712.5 1.4 slice_bitcast_fusion.14
  713.9 1.3 slice_bitcast_fusion.16
  715.2 4.2 bitcast_convert_fusion
  (265 shorter events, 29.0 us)
Async XLA Ops:
  75.3 7.4 %copy-start.35 = (f32[1024]{0:T(1024)}, f32[1024]{0:T(1024)S(1)}, u32[]{:S(2)}) copy-start(f32[1024]{0:T(1024)S(1)} %mul.332) | copy-start | bytes 12292
  75.3 5.0 copy-start.46
  80.2 16.2 %copy-start.13 = (bf16[4,256,1024]{2,1,0:T(8,128)(2,1)}, bf16[4,256,1024]{2,1,0:T(8,128)(2,1)S(1)}, u32[]{:S(2)}) copy-start(bf16[4,256,1024]{2,1,0:T(8,128)(2,1)S(1)} %fusion.9) | copy-start | bytes 6291460
  87.5 12.6 %collective-permute-start = (bf16[1024,2048]{1,0:T(8,128)(2,1)}, bf16[1024,2048]{1,0:T(8,128)(2,1)}, u32[]{:S(2)}, u32[]{:S(2)}) collective-permute-start(bf16[1024,2048]{1,0:T(8,128)(2,1)} %pad_maximum_fusion.ko.vo.refs_1_.refs_2_), channel_id=1, source_target_pairs={{0,4},{1,5},{2,6},{3,7},{4,0},{5,1},{6,2},{7,3},{8,12},{9,13},{10,... | collective-permute-start | bytes 12582920 | tf_op jit(solution)/shard_map/ppermute | solution.py:838
  88.4 11.7 %copy-start.54 = (s32[256]{0:T(256)}, s32[256]{0:T(256)S(1)}, u32[]{:S(2)}) copy-start(s32[256]{0:T(256)S(1)} %iota_select_fusion) | copy-start | bytes 3076
  90.1 148.9 %copy-start.37 = (f32[1024]{0:T(1024)}, f32[1024]{0:T(1024)S(1)}, u32[]{:S(2)}) copy-start(f32[1024]{0:T(1024)S(1)} %mul.338) | copy-start | bytes 12292
  90.4 6.1 copy-start.48
  100.1 128.0 %copy-start.18 = (bf16[4,64,1024]{2,1,0:T(8,128)(2,1)S(1)}, bf16[4,64,1024]{2,1,0:T(8,128)(2,1)}, u32[]{:S(2)}) copy-start(bf16[4,64,1024]{2,1,0:T(8,128)(2,1)} %get-tuple-element.90) | copy-start | bytes 1572868
  228.1 5.4 copy-start
  228.1 5.3 copy-start.50
  228.1 5.3 copy-start.58
  232.9 4.8 copy-start.21
  233.0 12.8 %collective-permute-start.1 = (bf16[256,2048]{1,0:T(8,128)(2,1)S(1)}, bf16[256,2048]{1,0:T(8,128)(2,1)}, u32[]{:S(2)}, u32[]{:S(2)}) collective-permute-start(bf16[256,2048]{1,0:T(8,128)(2,1)S(1)} %pad_maximum_fusion.3.ko.vo), channel_id=1, source_target_pairs={{0,4},{1,5},{2,6},{3,7},{4,0},{5,1},{6,2},{7,3},{8,12},{9,13},{10,... | collective-permute-start | bytes 3145736 | tf_op jit(solution)/shard_map/ppermute | solution.py:838
  233.4 4.4 copy-start.34
  239.0 6.7 copy-start.39
  239.1 6.7 copy-start.12
  246.0 45.8 %collective-permute-start.2 = (bf16[256,1024]{1,0:T(8,128)(2,1)S(1)}, bf16[256,1024]{1,0:T(8,128)(2,1)S(1)}, u32[]{:S(2)}, u32[]{:S(2)}) collective-permute-start(bf16[256,1024]{1,0:T(8,128)(2,1)S(1)} %get-tuple-element.233), channel_id=1, source_target_pairs={{0,0},{1,4},{2,1},{3,5},{4,2},{5,6},{6,3},{7,7},{8,8},{9,12},{10,9... | collective-permute-start | bytes 1572872 | tf_op jit(solution)/shard_map/ppermute | solution.py:1534
  247.6 44.2 %collective-permute-start.3 = (bf16[256,1024]{1,0:T(8,128)(2,1)}, bf16[256,1024]{1,0:T(8,128)(2,1)S(1)}, u32[]{:S(2)}, u32[]{:S(2)}) collective-permute-start(bf16[256,1024]{1,0:T(8,128)(2,1)} %get-tuple-element.231), channel_id=1, source_target_pairs={{0,4},{1,0},{2,5},{3,1},{4,6},{5,2},{6,7},{7,3},{8,12},{9,8},{10,1... | collective-permute-start | bytes 1572872 | tf_op jit(solution)/shard_map/ppermute | solution.py:1534
  250.5 41.3 %collective-permute-start.4 = (bf16[256,1024]{1,0:T(8,128)(2,1)S(1)}, bf16[256,1024]{1,0:T(8,128)(2,1)S(1)}, u32[]{:S(2)}, u32[]{:S(2)}) collective-permute-start(bf16[256,1024]{1,0:T(8,128)(2,1)S(1)} %get-tuple-element.234), channel_id=1, source_target_pairs={{0,1},{1,5},{2,0},{3,4},{4,3},{5,7},{6,2},{7,6},{8,9},{9,13},{10,8... | collective-permute-start | bytes 1572872 | tf_op jit(solution)/shard_map/ppermute | solution.py:1534
  250.6 41.2 %collective-permute-start.5 = (bf16[256,1024]{1,0:T(8,128)(2,1)S(1)}, bf16[256,1024]{1,0:T(8,128)(2,1)S(1)}, u32[]{:S(2)}, u32[]{:S(2)}) collective-permute-start(bf16[256,1024]{1,0:T(8,128)(2,1)S(1)} %get-tuple-element.232), channel_id=1, source_target_pairs={{0,5},{1,1},{2,4},{3,0},{4,7},{5,3},{6,6},{7,2},{8,13},{9,9},{10,1... | collective-permute-start | bytes 1572872 | tf_op jit(solution)/shard_map/ppermute | solution.py:1534
  274.5 8.4 %slice-start = ((s8[5767168]{0:T(1024)(128)(4,1)}), s8[4194304]{0:T(1024)(128)(4,1)S(1)}, s32[]{:S(2)}) async-start(s8[5767168]{0:T(1024)(128)(4,1)} %bitcast.251), calls=%async_computation | async-start | bytes 8388608
  274.5 8.5 %slice-start.1 = ((s8[5767168]{0:T(1024)(128)(4,1)}), s8[1572864]{0:T(1024)(128)(4,1)S(1)}, s32[]{:S(2)}) async-start(s8[5767168]{0:T(1024)(128)(4,1)} %bitcast.251), calls=%async_computation.1 | async-start | bytes 3145728
  282.9 8.9 %copy-start.16 = (bf16[1024,1024]{1,0:T(8,128)(2,1)}, bf16[1024,1024]{1,0:T(8,128)(2,1)S(1)}, u32[]{:S(2)}) copy-start(bf16[1024,1024]{1,0:T(8,128)(2,1)S(1)} %multiply_convert_fusion.2) | copy-start | bytes 6291460
  283.0 9.4 %slice-start.4 = ((s8[5767168]{0:T(1024)(128)(4,1)}), s8[4194304]{0:T(1024)(128)(4,1)S(1)}, s32[]{:S(2)}) async-start(s8[5767168]{0:T(1024)(128)(4,1)} %bitcast.260), calls=%async_computation.4 | async-start | bytes 8388608
  283.0 9.4 %slice-start.5 = ((s8[5767168]{0:T(1024)(128)(4,1)}), s8[1572864]{0:T(1024)(128)(4,1)S(1)}, s32[]{:S(2)}) async-start(s8[5767168]{0:T(1024)(128)(4,1)} %bitcast.260), calls=%async_computation.5 | async-start | bytes 3145728
  326.5 10.6 %copy-start.63 = (bf16[1024,2816]{1,0:T(8,128)(2,1)S(1)}, bf16[1024,2816]{1,0:T(8,128)(2,1)}, u32[]{:S(2)}) copy-start(bf16[1024,2816]{1,0:T(8,128)(2,1)} %get-tuple-element.212) | copy-start | bytes 17301508
  337.1 8.1 %copy-start.61 = (bf16[1024,2816]{1,0:T(8,128)(2,1)S(1)}, bf16[1024,2816]{1,0:T(8,128)(2,1)}, u32[]{:S(2)}) copy-start(bf16[1024,2816]{1,0:T(8,128)(2,1)} %get-tuple-element.214) | copy-start | bytes 17301508
  345.2 10.0 %copy-start.17 = (bf16[1024,1024]{1,0:T(8,128)(2,1)S(1)}, bf16[1024,1024]{1,0:T(8,128)(2,1)}, u32[]{:S(2)}) copy-start(bf16[1024,1024]{1,0:T(8,128)(2,1)} %copy-done.16) | copy-start | bytes 6291460
  345.2 18.3 %slice-start.6 = ((s8[5767168]{0:T(1024)(128)(4,1)}), s8[4194304]{0:T(1024)(128)(4,1)S(1)}, s32[]{:S(2)}) async-start(s8[5767168]{0:T(1024)(128)(4,1)} %bitcast.271), calls=%async_computation.6 | async-start | bytes 8388608
  355.2 8.3 %slice-start.7 = ((s8[5767168]{0:T(1024)(128)(4,1)}), s8[1572864]{0:T(1024)(128)(4,1)S(1)}, s32[]{:S(2)}) async-start(s8[5767168]{0:T(1024)(128)(4,1)} %bitcast.271), calls=%async_computation.7 | async-start | bytes 3145728
  355.2 16.8 %slice-start.2 = ((s8[5767168]{0:T(1024)(128)(4,1)}), s8[4194304]{0:T(1024)(128)(4,1)S(1)}, s32[]{:S(2)}) async-start(s8[5767168]{0:T(1024)(128)(4,1)} %bitcast.254), calls=%async_computation.2 | async-start | bytes 8388608
  363.5 8.5 %slice-start.3 = ((s8[5767168]{0:T(1024)(128)(4,1)}), s8[1572864]{0:T(1024)(128)(4,1)S(1)}, s32[]{:S(2)}) async-start(s8[5767168]{0:T(1024)(128)(4,1)} %bitcast.254), calls=%async_computation.3 | async-start | bytes 3145728
  363.5 8.5 %copy-start.6 = (f32[1024,1024]{1,0:T(8,128)S(1)}, f32[1024,1024]{1,0:T(8,128)}, u32[]{:S(2)}) copy-start(f32[1024,1024]{1,0:T(8,128)} %copy-done.5) | copy-start | bytes 12582916
  363.5 8.5 %copy-start.62 = (f32[1024,1024]{1,0:T(8,128)S(1)}, f32[1024,1024]{1,0:T(8,128)}, u32[]{:S(2)}) copy-start(f32[1024,1024]{1,0:T(8,128)} %fusion.82) | copy-start | bytes 12582916
  383.4 7.5 %copy-start.3 = (f32[1024,1024]{1,0:T(8,128)}, f32[1024,1024]{1,0:T(8,128)S(1)}, u32[]{:S(2)}) copy-start(f32[1024,1024]{1,0:T(8,128)S(1)} %subtract_add_fusion.1) | copy-start | bytes 12582916
  388.1 40.0 %collective-permute-start.6 = (bf16[256,1024]{1,0:T(8,128)(2,1)}, bf16[256,1024]{1,0:T(8,128)(2,1)S(1)}, u32[]{:S(2)}, u32[]{:S(2)}) collective-permute-start(bf16[256,1024]{1,0:T(8,128)(2,1)} %get-tuple-element.220), channel_id=1, source_target_pairs={{0,0},{4,1},{1,2},{5,3},{2,4},{6,5},{3,6},{7,7},{8,8},{12,9},{9,10... | collective-permute-start | bytes 1572872 | tf_op jit(solution)/shard_map/ppermute | solution.py:1549
  389.8 38.3 %collective-permute-start.7 = (bf16[256,1024]{1,0:T(8,128)(2,1)S(1)}, bf16[256,1024]{1,0:T(8,128)(2,1)S(1)}, u32[]{:S(2)}, u32[]{:S(2)}) collective-permute-start(bf16[256,1024]{1,0:T(8,128)(2,1)S(1)} %get-tuple-element.217), channel_id=1, source_target_pairs={{1,0},{5,1},{0,2},{4,3},{3,4},{7,5},{2,6},{6,7},{9,8},{13,9},{8,10... | collective-permute-start | bytes 1572872 | tf_op jit(solution)/shard_map/ppermute | solution.py:1549
  394.7 33.5 %collective-permute-start.8 = (bf16[256,1024]{1,0:T(8,128)(2,1)S(1)}, bf16[256,1024]{1,0:T(8,128)(2,1)S(1)}, u32[]{:S(2)}, u32[]{:S(2)}) collective-permute-start(bf16[256,1024]{1,0:T(8,128)(2,1)S(1)} %get-tuple-element.219), channel_id=1, source_target_pairs={{4,0},{0,1},{5,2},{1,3},{6,4},{2,5},{7,6},{3,7},{12,8},{8,9},{13,1... | collective-permute-start | bytes 1572872 | tf_op jit(solution)/shard_map/ppermute | solution.py:1549
  396.2 32.0 %collective-permute-start.9 = (bf16[256,1024]{1,0:T(8,128)(2,1)S(1)}, bf16[256,1024]{1,0:T(8,128)(2,1)S(1)}, u32[]{:S(2)}, u32[]{:S(2)}) collective-permute-start(bf16[256,1024]{1,0:T(8,128)(2,1)S(1)} %get-tuple-element.218), channel_id=1, source_target_pairs={{5,0},{1,1},{4,2},{0,3},{7,4},{3,5},{6,6},{2,7},{13,8},{9,9},{12,1... | collective-permute-start | bytes 1572872 | tf_op jit(solution)/shard_map/ppermute | solution.py:1549
  426.5 18.5 %collective-permute-start.10 = (bf16[2,256,1024]{2,1,0:T(8,128)(2,1)}, bf16[2,256,1024]{2,1,0:T(8,128)(2,1)S(1)}, u32[]{:S(2)}, u32[]{:S(2)}) collective-permute-start(bf16[2,256,1024]{2,1,0:T(8,128)(2,1)} %get-tuple-element.104), channel_id=1, source_target_pairs={{0,4},{1,5},{2,6},{3,7},{4,0},{5,1},{6,2},{7,3},{8,12},{9,13},{10,... | collective-permute-start | bytes 3145736 | tf_op jit(solution)/shard_map/ppermute | solution.py:838
  428.3 4.2 copy-start.52
  441.0 4.3 copy-start.11
  574.3 17.6 %collective-permute-start.11 = (bf16[2,1024,1024]{2,1,0:T(8,128)(2,1)}, bf16[2,1024,1024]{2,1,0:T(8,128)(2,1)}, u32[]{:S(2)}, u32[]{:S(2)}) collective-permute-start(bf16[2,1024,1024]{2,1,0:T(8,128)(2,1)} %get-tuple-element.108), channel_id=1, source_target_pairs={{0,4},{1,5},{2,6},{3,7},{4,0},{5,1},{6,2},{7,3},{8,12},{9,13},{10,... | collective-permute-start | bytes 12582920 | tf_op jit(solution)/shard_map/ppermute | solution.py:838
  576.5 6.7 copy-start.42
  576.5 6.7 copy-start.43
  576.5 7.0 copy-start.55
  576.5 7.7 %copy-start.22 = (bf16[2,128,1024]{2,1,0:T(8,128)(2,1)S(1)}, bf16[2,128,1024]{2,1,0:T(8,128)(2,1)}, u32[]{:S(2)}) copy-start(bf16[2,128,1024]{2,1,0:T(8,128)(2,1)} %get-tuple-element.113) | copy-start | bytes 1572868
  576.6 8.8 %copy-start.8 = (bf16[2,256,1024]{2,1,0:T(8,128)(2,1)S(1)}, bf16[2,256,1024]{2,1,0:T(8,128)(2,1)}, u32[]{:S(2)}) copy-start(bf16[2,256,1024]{2,1,0:T(8,128)(2,1)} %copy-done.7) | copy-start | bytes 3145732
  576.6 8.8 %copy-start.19 = (bf16[4,64,1024]{2,1,0:T(8,128)(2,1)S(1)}, bf16[4,64,1024]{2,1,0:T(8,128)(2,1)}, u32[]{:S(2)}) copy-start(bf16[4,64,1024]{2,1,0:T(8,128)(2,1)} %get-tuple-element.90) | copy-start | bytes 1572868
  584.2 5.2 copy-start.49
  584.2 5.2 copy-start.59
  591.9 4.5 copy-start.47
  611.7 5.5 copy-start.60
  712.5 6.9 copy-start.33
  712.5 7.6 %copy-start.32 = (f32[32,1024]{1,0:T(8,128)S(1)}, f32[32,1024]{1,0:T(8,128)}, u32[]{:S(2)}) copy-start(f32[32,1024]{1,0:T(8,128)} %get-tuple-element.305) | copy-start | bytes 393220
  712.5 8.2 %copy-start.31 = (f32[32,1024]{1,0:T(8,128)S(1)}, f32[32,1024]{1,0:T(8,128)}, u32[]{:S(2)}) copy-start(f32[32,1024]{1,0:T(8,128)} %get-tuple-element.306) | copy-start | bytes 393220
  712.5 8.8 %copy-start.30 = (f32[32,1024]{1,0:T(8,128)S(1)}, f32[32,1024]{1,0:T(8,128)}, u32[]{:S(2)}) copy-start(f32[32,1024]{1,0:T(8,128)} %get-tuple-element.307) | copy-start | bytes 393220
  712.5 9.5 %copy-start.27 = (f32[32,1024]{1,0:T(8,128)S(1)}, f32[32,1024]{1,0:T(8,128)}, u32[]{:S(2)}) copy-start(f32[32,1024]{1,0:T(8,128)} %get-tuple-element.310) | copy-start | bytes 393220
  712.5 10.1 %copy-start.29 = (f32[32,1024]{1,0:T(8,128)S(1)}, f32[32,1024]{1,0:T(8,128)}, u32[]{:S(2)}) copy-start(f32[32,1024]{1,0:T(8,128)} %get-tuple-element.311) | copy-start | bytes 393220
  712.5 10.8 %copy-start.28 = (f32[32,1024]{1,0:T(8,128)S(1)}, f32[32,1024]{1,0:T(8,128)}, u32[]{:S(2)}) copy-start(f32[32,1024]{1,0:T(8,128)} %get-tuple-element.312) | copy-start | bytes 393220
  712.5 11.4 %copy-start.26 = (f32[32,1024]{1,0:T(8,128)S(1)}, f32[32,1024]{1,0:T(8,128)}, u32[]{:S(2)}) copy-start(f32[32,1024]{1,0:T(8,128)} %get-tuple-element.313) | copy-start | bytes 393220
  715.2 9.4 %copy-start.25 = (f32[32,2816]{1,0:T(8,128)S(1)}, f32[32,2816]{1,0:T(8,128)}, u32[]{:S(2)}) copy-start(f32[32,2816]{1,0:T(8,128)} %get-tuple-element.315) | copy-start | bytes 1081348
  715.2 10.2 %copy-start.24 = (f32[32,2816]{1,0:T(8,128)S(1)}, f32[32,2816]{1,0:T(8,128)}, u32[]{:S(2)}) copy-start(f32[32,2816]{1,0:T(8,128)} %get-tuple-element.316) | copy-start | bytes 1081348
  715.2 10.9 %copy-start.23 = (f32[88,1024]{1,0:T(8,128)S(1)}, f32[88,1024]{1,0:T(8,128)}, u32[]{:S(2)}) copy-start(f32[88,1024]{1,0:T(8,128)} %get-tuple-element.317) | copy-start | bytes 1081348
  (20 other events, 57.7 us)

commit v6 on v5

--- a/solution.py
+++ b/solution.py
@@ -938,8 +938,9 @@
 
 
 class Gather:
-    def __init__(self, links, shards, wholes, local_sem, send_sem, recv_sem):
+    def __init__(self, links, shards, wholes, local_sem, send_sem, recv_sem, plane_first=()):
         self.links, self.shards, self.wholes = links, shards, wholes
+        self.plane_first = plane_first
         self.along_z = [len(shard.shape) == 3 for shard in shards]
         self.local_sem, self.send_sem, self.recv_sem = local_sem, send_sem, recv_sem
 
@@ -951,6 +952,18 @@
         z, core, y, x = links.z, links.core, links.y, links.x
         half = whole.shape[-1] // 2
         left, right = pl.ds(0, half), pl.ds(half, half)
+        if w in self.plane_first and stage < 3:
+            if stage == 0:
+                own, shard = whole.at[z, core, y, x], self.shards[w]
+                return [
+                    self.copy(w, 0, shard.at[:, left], own.at[:, left], links.at_x),
+                    self.copy(w, 1, shard.at[:, right], own.at[:, right], links.at_y),
+                ]
+            if stage == 1:
+                one, two = whole.at[z, core, y, :, :, left], whole.at[z, core, :, x, :, right]
+                return [self.copy(w, 2, one, one, links.at_y), self.copy(w, 3, two, two, links.at_x)]
+            plane = whole.at[z, core]
+            return [self.copy(w, 4 + k, plane, plane, links.at_z[k]) for k in range(3)]
         if stage == 0:
             own = whole.at[z, core, y, x]
             return [self.copy(w, k, self.shards[w], own, links.at_z[k]) for k in range(3)]
@@ -976,7 +989,8 @@
         return pltpu.make_async_copy(self.shards[w], own, self.local_sem.at[w])
 
     def begin(self):
-        for w in range(len(self.shards)):
+        count = len(self.shards)
+        for w in [*self.plane_first, *(w for w in range(count) if w not in self.plane_first)]:
             self.local(w).start()
             for copy in self.copies(1 if self.along_z[w] else 0, w):
                 copy.start()
@@ -1041,7 +1055,7 @@
     shards = refs[count + 8 : 2 * count + 8]
     load_sem, local_sem, send_sem, recv_sem = refs[2 * count + 8 :]
     links = Links()
-    gather = Gather(links, shards, wholes, local_sem, send_sem, recv_sem)
+    gather = Gather(links, shards, wholes, local_sem, send_sem, recv_sem, PLANE_FIRST)
     step = pl.program_id(0) * pl.num_programs(1) + pl.program_id(1)
     total = (HEADS * HEAD_DIM // q_ref.shape[1]) * 4
     @pl.when(step == 0)
@@ -1066,10 +1080,11 @@
                     gather.end()
 
 
+PLANE_FIRST = (5, 6, 7)
 GATHER_PLAN = (
-    (0, (1, 3)), (1, (2, 0)), (1, (1, 4)), (2, (2, 1)), (2, (1, 5)), (3, (2, 2)), (3, (1, 6)), (4, (1, 7)),
-    (5, (2, 3)), (5, (3, 0)), (6, (2, 4)), (6, (2, 5)), (7, (3, 1)), (7, (2, 6)), (7, (2, 7)), (7, (3, 2)),
-    (7, (3, 3)), (7, (3, 4)), (7, (3, 5)), (7, (3, 6)), (7, (3, 7)),
+    (0, (1, 5)), (0, (1, 6)), (0, (1, 7)), (0, (2, 5)), (1, (2, 6)), (1, (2, 7)), (1, (1, 3)), (1, (2, 0)),
+    (2, (1, 4)), (3, (2, 1)), (4, (2, 2)), (5, (2, 3)), (5, (3, 0)), (6, (2, 4)), (6, (3, 5)), (7, (3, 1)),
+    (7, (3, 6)), (7, (3, 2)), (7, (3, 3)), (7, (3, 4)), (7, (3, 7)),
 )
 
 
@@ -1383,9 +1398,9 @@
 
 
 SCATTER_PACE = (
-    (1, (1, 0)), (3, (1, 1)), (4, (2, 0)), (4, (1, 2)), (7, (2, 1)), (7, (1, 3)), (8, (3, 0)), (9, (1, 4)),
-    (11, (2, 2)), (12, (3, 1)), (12, (2, 3)), (13, (4, 0)), (13, (2, 4)), (14, (3, 2)), (14, (3, 3)),
-    (15, (3, 4)), (15, (4, 1)), (15, (4, 2)), (15, (4, 3)), (15, (4, 4)),
+    (1, (1, 0)), (3, (1, 1)), (4, (2, 0)), (7, (2, 1)), (7, (1, 2)), (8, (3, 0)), (10, (3, 1)), (10, (1, 3)),
+    (12, (2, 2)), (12, (1, 4)), (13, (4, 0)), (13, (2, 3)), (14, (3, 2)), (14, (3, 3)), (15, (2, 4)),
+    (15, (4, 1)), (15, (3, 4)), (15, (4, 2)), (15, (4, 3)), (15, (4, 4)),
 )
 
 

time: 734 us -> 715 us (0.974)
  Pallas kernels: 463 us -> 444 us
    pallas_call x1, Pallas kernels: 128 us -> 115 us  [attend_gather(): pl.pallas_call(functools.partial(attend_gather_kernel, count), grid=(grou...]
  transfers between devices with their start and end apart: 12 -> 12, of which waited for: 0 -> 0; matrix products, arithmetic and copies ran while one was open for 10% -> 11% of each run, Pallas kernels for 7% -> 7%
where the time goes in v6:
time: 715 us; the launch traced here: 709 us
  Pallas kernels  444 us (62%)
  matrix products  181 us (25%)
  other arithmetic  39 us (5%)
  local copies, waits for them, and re-layouts  26 us (4%)
  starting transfers between devices  16.4 us (2%)
    pallas_call x1, Pallas kernels, attend_scatter(): pl.pallas_call(functools.partial(attend_scatter_kernel, count), grid=(gro...  120 us
    pallas_call x1, Pallas kernels, attend_gather(): pl.pallas_call(functools.partial(attend_gather_kernel, count), grid=(grou...  115 us
    dot_general x22, matrix products, contract(): lax.dot_general(left, right, (((left_dim,), (right_dim,)), ((), ())), pre...  106 us
    pallas_call x1, Pallas kernels, scatter_grads(): pl.pallas_call(functools.partial(scatter_kernel, count, part), in_specs=[...  90.8 us
    dot_general x11, matrix products, dot(): return jnp.dot(rows, weight, preferred_element_type=F32)  74.8 us
    pallas_call x1, Pallas kernels, gather_weights(): pl.pallas_call(functools.partial(gather_kernel, count, later, parts), in_...  70.1 us
    pallas_call x1, Pallas kernels, attend_back_fast(): pl.pallas_call(functools.partial(attend_back_kernel, causal), grid_spec=p...  28.3 us
    pallas_call x1, Pallas kernels, attend_fast(): pl.pallas_call(functools.partial(attend_kernel, causal), grid_spec=pltpu....  19.6 us
  transfers between devices with their start and end apart: 12, of which 0 were waited for; matrix products, arithmetic and copies ran while one was open for 11% of the time, Pallas kernels for 7%

profile of v6, /device:TPU:0, one launch (start us, length us, event | category | flops | bytes accessed | tf_op | source)
XLA Modules:
  0.0 708.9 jit_solution(11400908492173609346)
XLA Ops:
  4.1 70.1 %gather_weights.1 = (bf16[4,2,2,2,8,256]{5,4,3,2,1,0:T(8,128)(2,1)}, bf16[4,2,2,2,32,1024]{5,4,3,2,1,0:T(8,128)(2,1)}, bf16[4,2,2,2,32,1024]{5,4,3,2,1,0:T(8,128...) custom-call(bf16[8,256]{1,0:T(8,128)(2,1)} %broadcast_in_dim.108.ref, ...), custom_call_target="tpu_custom_call" | custom-call | bytes 100352000 | tf_op jit(solution)/shard_map/gather_weights/pallas_call | solution.py:1139
  74.2 0.9 slice.181
  75.3 2.2 fusion.7
  78.1 2.1 fusion.9
  80.3 2.4 convolution_convert_fusion.15
  82.6 2.4 convolution_convert_fusion.14
  85.0 2.5 pad_maximum_fusion.ko.vo.refs_1_.refs_2_
  93.4 1.9 broadcast_select_fusion.1
  95.3 1.1 pad_maximum_fusion.2.kext_ref.refs_6_
  96.4 3.7 convolution_convert_fusion.16.q_ref.refs_0_
  100.1 115.2 %attend_gather.1 = (bf16[1024,1024]{1,0:T(8,128)(2,1)}, f32[2,8,1024]{2,1,0:T(8,128)}, bf16[4,2,2,2,32,2816]{5,4,3,2,1,0:T(8,128)(2,1)}, bf16[4,2,2,2,32,2816]{5...) custom-call(bf16[1024,1024]{1,0:T(8,128)(2,1)} %convolution_convert_, ...), custom_call_target="tpu_custom_call" | custom-call | flops 9663676416 | bytes 13631488 | tf_op jit(solution)/shard_map/attend_gather/pallas_call | solution.py:1097
  215.4 2.5 convolution_convert_fusion.18
  217.8 2.3 convolution_convert_fusion.17
  220.7 4.4 multiply_reduce_fusion.5
  226.4 6.7 convolution_convert_fusion.13.q_ref
  234.9 1.9 collective-permute-start.3
  236.8 1.1 collective-permute-start.4
  237.9 3.3 collective-permute-start.5
  241.2 19.6 %attend_cross.1 = (bf16[1024,1024]{1,0:T(8,128)(2,1)}, f32[2,8,1024]{2,1,0:T(8,128)}) custom-call(s32[12]{0:T(128)} %pad_add_fusion.1.meta_ref, bf16[1024,1024]{1,0:T(8,128)(2,1)} %convolution_convert_fusion.13.q_ref, bf16[256,2048]{1,0:T(8,128)(2,1)} %copy-done.21, bf16[256,2048]{1,0:T(8,128)(2,1)} %copy-done.21, ...), custom_call_target="tpu_custom_call" | custom-call | flops 2147483648 | bytes 6291456 | tf_op jit(solution)/shard_map/attend_cross/pallas_call | solution.py:746
  260.9 6.0 multiply_reduce_fusion.4
  266.9 2.0 copy-done.5
  269.4 8.8 %fusion.81 = f32[1024,2816]{1,0:T(8,128)} fusion(bf16[1024,1024]{1,0:T(8,128)(2,1)S(1)} %multiply_convert_fusion.2, bf16[1024,2816]{1,0:T(8,128)(2,1)S(1)} %bitcast.253), kind=kOutput, calls=%fused_computation.248 | convolution fusion | flops 5905580032 | bytes 19398656 | tf_op jit(solution)/shard_map/dot_general | solution.py:1506
  278.8 8.9 %fusion.80 = f32[1024,2816]{1,0:T(8,128)} fusion(bf16[1024,1024]{1,0:T(8,128)(2,1)S(1)} %bitcast.205, bf16[2816,1024]{1,0:T(8,128)(2,1)S(1)} %bitcast.262), kind=kOutput, calls=%fused_computation.247 | convolution fusion | flops 5905580032 | bytes 19398656 | tf_op jit(solution)/shard_map/dot_general | solution.py:398
  287.6 25.2 %multiply_convert_fusion = (bf16[1024,2816]{1,0:T(8,128)(2,1)}, bf16[1024,2816]{1,0:T(8,128)(2,1)}, bf16[1024,2816]{1,0:T(8,128)(2,1)}) fusion(f32[1024,2816]{1,0:T(8,128)} %fusion.81, f32[1024,2816]{1,0:T(8,128)} %fusion.80, bf16[1024,1024]{1,0:T(8,128)(2,1)} %copy-done.16, bf16[1024,2816]{1,0:T(8,128)(2,1)} %bitcast.257), kind=kOutput, calls=%fused_computation.9 | convolution fusion | flops 5980553216 | bytes 48234496 | tf_op jit(solution)/shard_map/dot_general | solution.py:1506
  312.8 10.6 %add_convert_fusion.1 = bf16[1024,1024]{1,0:T(8,128)(2,1)S(1)} fusion(f32[1024,1024]{1,0:T(8,128)} %copy-done.5, bf16[1024,2816]{1,0:T(8,128)(2,1)} %get-tuple-element.212, bf16[2816,1024]{1,0:T(8,128)(2,1)} %bitcast.259), kind=kOutput, calls=%fused_computation.41 | convolution fusion | flops 5907677184 | bytes 17825792 | tf_op jit(solution)/shard_map/dot_general | solution.py:1506
  323.4 8.1 %convolution_convert_fusion = bf16[2816,1024]{1,0:T(8,128)(2,1)} fusion(bf16[1024,2816]{1,0:T(8,128)(2,1)S(1)} %copy-done.63, bf16[1024,1024]{1,0:T(8,128)(2,1)S(1)} %bitcast.206), kind=kOutput, calls=%fused_computation.13 | convolution fusion | flops 5908463616 | bytes 13631488 | tf_op jit(solution)/shard_map/dot_general | solution.py:398
  331.6 10.0 %fusion.82 = f32[1024,1024]{1,0:T(8,128)} fusion(bf16[1024,2816]{1,0:T(8,128)(2,1)S(1)} %copy-done.61, bf16[1024,2816]{1,0:T(8,128)(2,1)} %bitcast.258), kind=kOutput, calls=%fused_computation.249 | convolution fusion | flops 5905580032 | bytes 15728640 | tf_op jit(solution)/shard_map/dot_general | solution.py:398
  341.5 8.3 %convolution_convert_fusion.1 = bf16[1024,2816]{1,0:T(8,128)(2,1)} fusion(bf16[1024,1024]{1,0:T(8,128)(2,1)S(1)} %copy-done.17, bf16[1024,2816]{1,0:T(8,128)(2,1)S(1)} %copy-done.61), kind=kOutput, calls=%fused_computation.14 | convolution fusion | flops 5908463616 | bytes 13631488 | tf_op jit(solution)/shard_map/dot_general | solution.py:398
  349.8 8.5 %convolution_convert_fusion.2 = bf16[1024,2816]{1,0:T(8,128)(2,1)} fusion(bf16[1024,1024]{1,0:T(8,128)(2,1)S(1)} %copy-done.17, bf16[1024,2816]{1,0:T(8,128)(2,1)S(1)} %bitcast.272), kind=kOutput, calls=%fused_computation.15 | convolution fusion | flops 5908463616 | bytes 13631488 | tf_op jit(solution)/shard_map/dot_general | solution.py:398
  358.3 9.5 %multiply_reduce_fusion = (f32[1024]{0:T(1024)}, f32[1024]{0:T(1024)S(1)}, f32[1024,1024]{1,0:T(8,128)S(1)}) fusion(f32[1024,1024]{1,0:T(8,128)S(1)} %copy-done.6, f32[1024]{0:T(1024)S(1)} %get-tuple-element.254, f32[1024]{0:T(1024)S(1)} %mul.346, f32[1024,1024]{1,0:T(8,128)S(1)} %copy-done.62, bf16[1024,2816]{1,0:T(8,128)(2,1)} %get-tuple-element.213, ...), kind=kOutput, calls=%fused_computation.36 | convolution fusion | flops 5912918016 | bytes 24133632 | tf_op jit(solution)/shard_map/dot_general | solution.py:398
  367.8 2.0 subtract_add_fusion.1
  369.8 3.7 convolution_convert_fusion.12.do_ref
  373.5 1.0 dynamic-slice_bitcast_fusion.2
  374.5 1.7 collective-permute-start.6
  376.2 2.1 collective-permute-start.7
  378.2 3.8 convolution_convert_fusion.8
  382.0 1.5 collective-permute-start.8
  383.5 2.0 collective-permute-start.9
  385.5 28.3 %attend_cross_back.1 = (bf16[1024,1024]{1,0:T(8,128)(2,1)}, bf16[2,256,1024]{2,1,0:T(8,128)(2,1)}, bf16[2,256,1024]{2,1,0:T(8,128)(2,1)}, f32[16,1,256]{2,1,0:T(1,128)}, f32[16,1,256]{2,1,0:T(1,128)}) custom-call(s32[12]{0:T(128)} %pad_add_fusion.1.meta_ref, bf16[1024,1024]{1,0:T(8,128)(2,1)} %convolution_convert_fusion.13.q_ref, ...), custom_call_target="tpu_custom_call" | custom-call | flops 5368709120 | bytes 15728640 | tf_op jit(solution)/shard_map/attend_cross_back/pallas_call | solution.py:799
  413.7 1.6 collective-permute-start.10
  415.8 1.5 maximum_bitcast_fusion
  417.7 1.4 copy-done.9
  419.8 3.2 multiply_reduce_fusion.1
  423.0 1.4 subtract_add_fusion
  424.6 3.7 convolution_convert_fusion.9.refs_8_
  428.3 3.9 convolution_convert_fusion.7
  434.2 1.5 fusion.21
  435.7 120.2 %attend_scatter.1 = (bf16[1024,1024]{1,0:T(8,128)(2,1)}, bf16[2,1024,1024]{2,1,0:T(8,128)(2,1)}, bf16[2,1024,1024]{2,1,0:T(8,128)(2,1)}, f32[16,1,256]{2,1,0:T(1...) custom-call(bf16[1024,1024]{1,0:T(8,128)(2,1)} %convolution_convert_, ...), custom_call_target="tpu_custom_call" | custom-call | flops 24159191040 | bytes 34078720 | tf_op jit(solution)/shard_map/attend_scatter/pallas_call | solution.py:1416
  558.2 6.7 convolution_convert_fusion.4
  565.9 1.1 bitcast_convert_fusion.1
  567.0 2.1 convolution_convert_fusion.10
  569.0 2.1 convolution_convert_fusion.11
  571.1 2.4 fusion.83
  573.5 4.4 add_convert_fusion
  578.0 2.4 fusion.19
  580.4 3.8 convolution_convert_fusion.5
  584.1 3.8 convolution_convert_fusion.6
  587.9 5.2 fusion.18
  593.3 5.5 fusion.17
  598.8 3.7 convolution_convert_fusion.3
  603.2 90.8 %scatter_grads.1 = (f32[32,1024]{1,0:T(8,128)}, f32[32,1024]{1,0:T(8,128)}, f32[32,1024]{1,0:T(8,128)}, f32[32,1024]{1,0:T(8,128)}, f32[32,1024]{1,0:T(8,128)}, ...) custom-call(bf16[4,2,2,2,32,1024]{5,4,3,2,1,0:T(8,128)(2,1)} %bitcast.203, ...), custom_call_target="tpu_custom_call" | custom-call | bytes 101711872 | tf_op jit(solution)/shard_map/scatter_grads/pallas_call | solution.py:1465
  694.1 1.4 slice_bitcast_fusion.14
  695.5 1.3 slice_bitcast_fusion.16
  696.8 4.2 bitcast_convert_fusion
  (265 shorter events, 29.8 us)
Async XLA Ops:
  75.3 7.4 %copy-start.35 = (f32[1024]{0:T(1024)}, f32[1024]{0:T(1024)S(1)}, u32[]{:S(2)}) copy-start(f32[1024]{0:T(1024)S(1)} %mul.332) | copy-start | bytes 12292
  75.3 5.0 copy-start.46
  80.2 16.2 %copy-start.13 = (bf16[4,256,1024]{2,1,0:T(8,128)(2,1)}, bf16[4,256,1024]{2,1,0:T(8,128)(2,1)S(1)}, u32[]{:S(2)}) copy-start(bf16[4,256,1024]{2,1,0:T(8,128)(2,1)S(1)} %fusion.9) | copy-start | bytes 6291460
  87.5 12.6 %collective-permute-start = (bf16[1024,2048]{1,0:T(8,128)(2,1)}, bf16[1024,2048]{1,0:T(8,128)(2,1)}, u32[]{:S(2)}, u32[]{:S(2)}) collective-permute-start(bf16[1024,2048]{1,0:T(8,128)(2,1)} %pad_maximum_fusion.ko.vo.refs_1_.refs_2_), channel_id=1, source_target_pairs={{0,4},{1,5},{2,6},{3,7},{4,0},{5,1},{6,2},{7,3},{8,12},{9,13},{10,... | collective-permute-start | bytes 12582920 | tf_op jit(solution)/shard_map/ppermute | solution.py:838
  88.4 11.7 %copy-start.54 = (s32[256]{0:T(256)}, s32[256]{0:T(256)S(1)}, u32[]{:S(2)}) copy-start(s32[256]{0:T(256)S(1)} %iota_select_fusion) | copy-start | bytes 3076
  90.1 136.2 %copy-start.37 = (f32[1024]{0:T(1024)}, f32[1024]{0:T(1024)S(1)}, u32[]{:S(2)}) copy-start(f32[1024]{0:T(1024)S(1)} %mul.338) | copy-start | bytes 12292
  90.4 6.1 copy-start.48
  100.1 115.3 %copy-start.18 = (bf16[4,64,1024]{2,1,0:T(8,128)(2,1)S(1)}, bf16[4,64,1024]{2,1,0:T(8,128)(2,1)}, u32[]{:S(2)}) copy-start(bf16[4,64,1024]{2,1,0:T(8,128)(2,1)} %get-tuple-element.90) | copy-start | bytes 1572868
  215.4 5.4 copy-start
  215.4 5.3 copy-start.50
  215.4 5.3 copy-start.58
  220.2 4.8 copy-start.21
  220.3 12.8 %collective-permute-start.1 = (bf16[256,2048]{1,0:T(8,128)(2,1)S(1)}, bf16[256,2048]{1,0:T(8,128)(2,1)}, u32[]{:S(2)}, u32[]{:S(2)}) collective-permute-start(bf16[256,2048]{1,0:T(8,128)(2,1)S(1)} %pad_maximum_fusion.3.ko.vo), channel_id=1, source_target_pairs={{0,4},{1,5},{2,6},{3,7},{4,0},{5,1},{6,2},{7,3},{8,12},{9,13},{10,... | collective-permute-start | bytes 3145736 | tf_op jit(solution)/shard_map/ppermute | solution.py:838
  220.7 4.4 copy-start.34
  226.3 6.7 copy-start.39
  226.4 6.7 copy-start.12
  233.4 44.8 %collective-permute-start.2 = (bf16[256,1024]{1,0:T(8,128)(2,1)S(1)}, bf16[256,1024]{1,0:T(8,128)(2,1)S(1)}, u32[]{:S(2)}, u32[]{:S(2)}) collective-permute-start(bf16[256,1024]{1,0:T(8,128)(2,1)S(1)} %get-tuple-element.233), channel_id=1, source_target_pairs={{0,0},{1,4},{2,1},{3,5},{4,2},{5,6},{6,3},{7,7},{8,8},{9,12},{10,9... | collective-permute-start | bytes 1572872 | tf_op jit(solution)/shard_map/ppermute | solution.py:1549
  234.9 43.2 %collective-permute-start.3 = (bf16[256,1024]{1,0:T(8,128)(2,1)}, bf16[256,1024]{1,0:T(8,128)(2,1)S(1)}, u32[]{:S(2)}, u32[]{:S(2)}) collective-permute-start(bf16[256,1024]{1,0:T(8,128)(2,1)} %get-tuple-element.231), channel_id=1, source_target_pairs={{0,4},{1,0},{2,5},{3,1},{4,6},{5,2},{6,7},{7,3},{8,12},{9,8},{10,1... | collective-permute-start | bytes 1572872 | tf_op jit(solution)/shard_map/ppermute | solution.py:1549
  236.8 41.4 %collective-permute-start.4 = (bf16[256,1024]{1,0:T(8,128)(2,1)S(1)}, bf16[256,1024]{1,0:T(8,128)(2,1)S(1)}, u32[]{:S(2)}, u32[]{:S(2)}) collective-permute-start(bf16[256,1024]{1,0:T(8,128)(2,1)S(1)} %get-tuple-element.234), channel_id=1, source_target_pairs={{0,1},{1,5},{2,0},{3,4},{4,3},{5,7},{6,2},{7,6},{8,9},{9,13},{10,8... | collective-permute-start | bytes 1572872 | tf_op jit(solution)/shard_map/ppermute | solution.py:1549
  237.9 40.3 %collective-permute-start.5 = (bf16[256,1024]{1,0:T(8,128)(2,1)S(1)}, bf16[256,1024]{1,0:T(8,128)(2,1)S(1)}, u32[]{:S(2)}, u32[]{:S(2)}) collective-permute-start(bf16[256,1024]{1,0:T(8,128)(2,1)S(1)} %get-tuple-element.232), channel_id=1, source_target_pairs={{0,5},{1,1},{2,4},{3,0},{4,7},{5,3},{6,6},{7,2},{8,13},{9,9},{10,1... | collective-permute-start | bytes 1572872 | tf_op jit(solution)/shard_map/ppermute | solution.py:1549
  260.9 8.4 %slice-start = ((s8[5767168]{0:T(1024)(128)(4,1)}), s8[4194304]{0:T(1024)(128)(4,1)S(1)}, s32[]{:S(2)}) async-start(s8[5767168]{0:T(1024)(128)(4,1)} %bitcast.251), calls=%async_computation | async-start | bytes 8388608
  260.9 8.5 %slice-start.1 = ((s8[5767168]{0:T(1024)(128)(4,1)}), s8[1572864]{0:T(1024)(128)(4,1)S(1)}, s32[]{:S(2)}) async-start(s8[5767168]{0:T(1024)(128)(4,1)} %bitcast.251), calls=%async_computation.1 | async-start | bytes 3145728
  269.3 8.9 %copy-start.16 = (bf16[1024,1024]{1,0:T(8,128)(2,1)}, bf16[1024,1024]{1,0:T(8,128)(2,1)S(1)}, u32[]{:S(2)}) copy-start(bf16[1024,1024]{1,0:T(8,128)(2,1)S(1)} %multiply_convert_fusion.2) | copy-start | bytes 6291460
  269.3 9.4 %slice-start.4 = ((s8[5767168]{0:T(1024)(128)(4,1)}), s8[4194304]{0:T(1024)(128)(4,1)S(1)}, s32[]{:S(2)}) async-start(s8[5767168]{0:T(1024)(128)(4,1)} %bitcast.260), calls=%async_computation.4 | async-start | bytes 8388608
  269.4 9.4 %slice-start.5 = ((s8[5767168]{0:T(1024)(128)(4,1)}), s8[1572864]{0:T(1024)(128)(4,1)S(1)}, s32[]{:S(2)}) async-start(s8[5767168]{0:T(1024)(128)(4,1)} %bitcast.260), calls=%async_computation.5 | async-start | bytes 3145728
  312.8 10.6 %copy-start.63 = (bf16[1024,2816]{1,0:T(8,128)(2,1)S(1)}, bf16[1024,2816]{1,0:T(8,128)(2,1)}, u32[]{:S(2)}) copy-start(bf16[1024,2816]{1,0:T(8,128)(2,1)} %get-tuple-element.212) | copy-start | bytes 17301508
  323.4 8.1 %copy-start.61 = (bf16[1024,2816]{1,0:T(8,128)(2,1)S(1)}, bf16[1024,2816]{1,0:T(8,128)(2,1)}, u32[]{:S(2)}) copy-start(bf16[1024,2816]{1,0:T(8,128)(2,1)} %get-tuple-element.214) | copy-start | bytes 17301508
  331.6 10.0 %copy-start.17 = (bf16[1024,1024]{1,0:T(8,128)(2,1)S(1)}, bf16[1024,1024]{1,0:T(8,128)(2,1)}, u32[]{:S(2)}) copy-start(bf16[1024,1024]{1,0:T(8,128)(2,1)} %copy-done.16) | copy-start | bytes 6291460
  331.6 18.3 %slice-start.6 = ((s8[5767168]{0:T(1024)(128)(4,1)}), s8[4194304]{0:T(1024)(128)(4,1)S(1)}, s32[]{:S(2)}) async-start(s8[5767168]{0:T(1024)(128)(4,1)} %bitcast.271), calls=%async_computation.6 | async-start | bytes 8388608
  341.5 8.3 %slice-start.7 = ((s8[5767168]{0:T(1024)(128)(4,1)}), s8[1572864]{0:T(1024)(128)(4,1)S(1)}, s32[]{:S(2)}) async-start(s8[5767168]{0:T(1024)(128)(4,1)} %bitcast.271), calls=%async_computation.7 | async-start | bytes 3145728
  341.5 16.8 %slice-start.2 = ((s8[5767168]{0:T(1024)(128)(4,1)}), s8[4194304]{0:T(1024)(128)(4,1)S(1)}, s32[]{:S(2)}) async-start(s8[5767168]{0:T(1024)(128)(4,1)} %bitcast.254), calls=%async_computation.2 | async-start | bytes 8388608
  349.8 8.5 %slice-start.3 = ((s8[5767168]{0:T(1024)(128)(4,1)}), s8[1572864]{0:T(1024)(128)(4,1)S(1)}, s32[]{:S(2)}) async-start(s8[5767168]{0:T(1024)(128)(4,1)} %bitcast.254), calls=%async_computation.3 | async-start | bytes 3145728
  349.8 8.5 %copy-start.6 = (f32[1024,1024]{1,0:T(8,128)S(1)}, f32[1024,1024]{1,0:T(8,128)}, u32[]{:S(2)}) copy-start(f32[1024,1024]{1,0:T(8,128)} %copy-done.5) | copy-start | bytes 12582916
  349.8 8.5 %copy-start.62 = (f32[1024,1024]{1,0:T(8,128)S(1)}, f32[1024,1024]{1,0:T(8,128)}, u32[]{:S(2)}) copy-start(f32[1024,1024]{1,0:T(8,128)} %fusion.82) | copy-start | bytes 12582916
  369.8 8.5 %copy-start.3 = (f32[1024,1024]{1,0:T(8,128)}, f32[1024,1024]{1,0:T(8,128)S(1)}, u32[]{:S(2)}) copy-start(f32[1024,1024]{1,0:T(8,128)S(1)} %subtract_add_fusion.1) | copy-start | bytes 12582916
  373.5 4.7 copy-start.56
  374.5 40.9 %collective-permute-start.6 = (bf16[256,1024]{1,0:T(8,128)(2,1)}, bf16[256,1024]{1,0:T(8,128)(2,1)S(1)}, u32[]{:S(2)}, u32[]{:S(2)}) collective-permute-start(bf16[256,1024]{1,0:T(8,128)(2,1)} %get-tuple-element.220), channel_id=1, source_target_pairs={{0,0},{4,1},{1,2},{5,3},{2,4},{6,5},{3,6},{7,7},{8,8},{12,9},{9,10... | collective-permute-start | bytes 1572872 | tf_op jit(solution)/shard_map/ppermute | solution.py:1564
  376.2 39.2 %collective-permute-start.7 = (bf16[256,1024]{1,0:T(8,128)(2,1)S(1)}, bf16[256,1024]{1,0:T(8,128)(2,1)S(1)}, u32[]{:S(2)}, u32[]{:S(2)}) collective-permute-start(bf16[256,1024]{1,0:T(8,128)(2,1)S(1)} %get-tuple-element.217), channel_id=1, source_target_pairs={{1,0},{5,1},{0,2},{4,3},{3,4},{7,5},{2,6},{6,7},{9,8},{13,9},{8,10... | collective-permute-start | bytes 1572872 | tf_op jit(solution)/shard_map/ppermute | solution.py:1564
  382.0 33.5 %collective-permute-start.8 = (bf16[256,1024]{1,0:T(8,128)(2,1)S(1)}, bf16[256,1024]{1,0:T(8,128)(2,1)S(1)}, u32[]{:S(2)}, u32[]{:S(2)}) collective-permute-start(bf16[256,1024]{1,0:T(8,128)(2,1)S(1)} %get-tuple-element.219), channel_id=1, source_target_pairs={{4,0},{0,1},{5,2},{1,3},{6,4},{2,5},{7,6},{3,7},{12,8},{8,9},{13,1... | collective-permute-start | bytes 1572872 | tf_op jit(solution)/shard_map/ppermute | solution.py:1564
  383.5 32.0 %collective-permute-start.9 = (bf16[256,1024]{1,0:T(8,128)(2,1)S(1)}, bf16[256,1024]{1,0:T(8,128)(2,1)S(1)}, u32[]{:S(2)}, u32[]{:S(2)}) collective-permute-start(bf16[256,1024]{1,0:T(8,128)(2,1)S(1)} %get-tuple-element.218), channel_id=1, source_target_pairs={{5,0},{1,1},{4,2},{0,3},{7,4},{3,5},{6,6},{2,7},{13,8},{9,9},{12,1... | collective-permute-start | bytes 1572872 | tf_op jit(solution)/shard_map/ppermute | solution.py:1564
  413.7 18.5 %collective-permute-start.10 = (bf16[2,256,1024]{2,1,0:T(8,128)(2,1)}, bf16[2,256,1024]{2,1,0:T(8,128)(2,1)S(1)}, u32[]{:S(2)}, u32[]{:S(2)}) collective-permute-start(bf16[2,256,1024]{2,1,0:T(8,128)(2,1)} %get-tuple-element.104), channel_id=1, source_target_pairs={{0,4},{1,5},{2,6},{3,7},{4,0},{5,1},{6,2},{7,3},{8,12},{9,13},{10,... | collective-permute-start | bytes 3145736 | tf_op jit(solution)/shard_map/ppermute | solution.py:838
  428.3 4.3 copy-start.11
  555.9 17.6 %collective-permute-start.11 = (bf16[2,1024,1024]{2,1,0:T(8,128)(2,1)}, bf16[2,1024,1024]{2,1,0:T(8,128)(2,1)}, u32[]{:S(2)}, u32[]{:S(2)}) collective-permute-start(bf16[2,1024,1024]{2,1,0:T(8,128)(2,1)} %get-tuple-element.108), channel_id=1, source_target_pairs={{0,4},{1,5},{2,6},{3,7},{4,0},{5,1},{6,2},{7,3},{8,12},{9,13},{10,... | collective-permute-start | bytes 12582920 | tf_op jit(solution)/shard_map/ppermute | solution.py:838
  558.2 6.7 copy-start.42
  558.2 6.7 copy-start.43
  558.2 7.0 copy-start.55
  558.2 7.7 %copy-start.22 = (bf16[2,128,1024]{2,1,0:T(8,128)(2,1)S(1)}, bf16[2,128,1024]{2,1,0:T(8,128)(2,1)}, u32[]{:S(2)}) copy-start(bf16[2,128,1024]{2,1,0:T(8,128)(2,1)} %get-tuple-element.113) | copy-start | bytes 1572868
  558.2 8.8 %copy-start.8 = (bf16[2,256,1024]{2,1,0:T(8,128)(2,1)S(1)}, bf16[2,256,1024]{2,1,0:T(8,128)(2,1)}, u32[]{:S(2)}) copy-start(bf16[2,256,1024]{2,1,0:T(8,128)(2,1)} %copy-done.7) | copy-start | bytes 3145732
  558.2 8.8 %copy-start.19 = (bf16[4,64,1024]{2,1,0:T(8,128)(2,1)S(1)}, bf16[4,64,1024]{2,1,0:T(8,128)(2,1)}, u32[]{:S(2)}) copy-start(bf16[4,64,1024]{2,1,0:T(8,128)(2,1)} %get-tuple-element.90) | copy-start | bytes 1572868
  565.9 5.2 copy-start.49
  565.9 5.2 copy-start.59
  573.5 4.5 copy-start.47
  593.3 5.5 copy-start.60
  694.1 6.9 copy-start.33
  694.1 7.6 %copy-start.32 = (f32[32,1024]{1,0:T(8,128)S(1)}, f32[32,1024]{1,0:T(8,128)}, u32[]{:S(2)}) copy-start(f32[32,1024]{1,0:T(8,128)} %get-tuple-element.305) | copy-start | bytes 393220
  694.1 8.2 %copy-start.31 = (f32[32,1024]{1,0:T(8,128)S(1)}, f32[32,1024]{1,0:T(8,128)}, u32[]{:S(2)}) copy-start(f32[32,1024]{1,0:T(8,128)} %get-tuple-element.306) | copy-start | bytes 393220
  694.1 8.8 %copy-start.30 = (f32[32,1024]{1,0:T(8,128)S(1)}, f32[32,1024]{1,0:T(8,128)}, u32[]{:S(2)}) copy-start(f32[32,1024]{1,0:T(8,128)} %get-tuple-element.307) | copy-start | bytes 393220
  694.1 9.5 %copy-start.27 = (f32[32,1024]{1,0:T(8,128)S(1)}, f32[32,1024]{1,0:T(8,128)}, u32[]{:S(2)}) copy-start(f32[32,1024]{1,0:T(8,128)} %get-tuple-element.310) | copy-start | bytes 393220
  694.1 10.1 %copy-start.29 = (f32[32,1024]{1,0:T(8,128)S(1)}, f32[32,1024]{1,0:T(8,128)}, u32[]{:S(2)}) copy-start(f32[32,1024]{1,0:T(8,128)} %get-tuple-element.311) | copy-start | bytes 393220
  694.1 10.8 %copy-start.28 = (f32[32,1024]{1,0:T(8,128)S(1)}, f32[32,1024]{1,0:T(8,128)}, u32[]{:S(2)}) copy-start(f32[32,1024]{1,0:T(8,128)} %get-tuple-element.312) | copy-start | bytes 393220
  694.1 11.4 %copy-start.26 = (f32[32,1024]{1,0:T(8,128)S(1)}, f32[32,1024]{1,0:T(8,128)}, u32[]{:S(2)}) copy-start(f32[32,1024]{1,0:T(8,128)} %get-tuple-element.313) | copy-start | bytes 393220
  696.8 9.4 %copy-start.25 = (f32[32,2816]{1,0:T(8,128)S(1)}, f32[32,2816]{1,0:T(8,128)}, u32[]{:S(2)}) copy-start(f32[32,2816]{1,0:T(8,128)} %get-tuple-element.315) | copy-start | bytes 1081348
  696.8 10.2 %copy-start.24 = (f32[32,2816]{1,0:T(8,128)S(1)}, f32[32,2816]{1,0:T(8,128)}, u32[]{:S(2)}) copy-start(f32[32,2816]{1,0:T(8,128)} %get-tuple-element.316) | copy-start | bytes 1081348
  696.8 10.9 %copy-start.23 = (f32[88,1024]{1,0:T(8,128)S(1)}, f32[88,1024]{1,0:T(8,128)}, u32[]{:S(2)}) copy-start(f32[88,1024]{1,0:T(8,128)} %get-tuple-element.317) | copy-start | bytes 1081348
  (20 other events, 58.1 us)

commit v7 on v6

--- a/solution.py
+++ b/solution.py
@@ -1355,10 +1355,11 @@
     scatter = Scatter(links, grads, sums, scratch)
     scatter.begin()
     starts, finish = return_tokens_kernel(links, tokens, returned, part, back_local, back_send, back_recv)
-    for start in starts:
-        start()
     for stage, w in scatter.steps():
         scatter.advance(stage, w)
+        if (stage, w) == (2, count - 1):
+            for start in starts:
+                start()
     scatter.end()
     finish()
 

time: 715 us -> 707 us (0.989)
  Pallas kernels: 444 us -> 435 us
    pallas_call x1, Pallas kernels: 90.8 us -> 81.8 us  [scatter_grads(): pl.pallas_call(functools.partial(scatter_kernel, count, part), in_specs=[...]
where the time goes in v7:
time: 707 us; the launch traced here: 700 us
  Pallas kernels  435 us (62%)
  matrix products  181 us (26%)
  other arithmetic  39 us (6%)
  local copies, waits for them, and re-layouts  26 us (4%)
  starting transfers between devices  16.4 us (2%)
    pallas_call x1, Pallas kernels, attend_scatter(): pl.pallas_call(functools.partial(attend_scatter_kernel, count), grid=(gro...  120 us
    pallas_call x1, Pallas kernels, attend_gather(): pl.pallas_call(functools.partial(attend_gather_kernel, count), grid=(grou...  115 us
    dot_general x22, matrix products, contract(): lax.dot_general(left, right, (((left_dim,), (right_dim,)), ((), ())), pre...  106 us
    pallas_call x1, Pallas kernels, scatter_grads(): pl.pallas_call(functools.partial(scatter_kernel, count, part), in_specs=[...  81.8 us
    dot_general x11, matrix products, dot(): return jnp.dot(rows, weight, preferred_element_type=F32)  74.8 us
    pallas_call x1, Pallas kernels, gather_weights(): pl.pallas_call(functools.partial(gather_kernel, count, later, parts), in_...  70.1 us
    pallas_call x1, Pallas kernels, attend_back_fast(): pl.pallas_call(functools.partial(attend_back_kernel, causal), grid_spec=p...  28.3 us
    pallas_call x1, Pallas kernels, attend_fast(): pl.pallas_call(functools.partial(attend_kernel, causal), grid_spec=pltpu....  19.6 us
  transfers between devices with their start and end apart: 12, of which 0 were waited for; matrix products, arithmetic and copies ran while one was open for 11% of the time, Pallas kernels for 7%

profile of v7, /device:TPU:0, one launch (start us, length us, event | category | flops | bytes accessed | tf_op | source)
XLA Modules:
  0.0 699.9 jit_solution(1382824738602735366)
XLA Ops:
  4.1 70.1 %gather_weights.1 = (bf16[4,2,2,2,8,256]{5,4,3,2,1,0:T(8,128)(2,1)}, bf16[4,2,2,2,32,1024]{5,4,3,2,1,0:T(8,128)(2,1)}, bf16[4,2,2,2,32,1024]{5,4,3,2,1,0:T(8,128...) custom-call(bf16[8,256]{1,0:T(8,128)(2,1)} %broadcast_in_dim.108.ref, ...), custom_call_target="tpu_custom_call" | custom-call | bytes 100352000 | tf_op jit(solution)/shard_map/gather_weights/pallas_call | solution.py:1139
  74.2 0.9 slice.181
  75.3 2.2 fusion.7
  78.1 2.1 fusion.9
  80.3 2.4 convolution_convert_fusion.15
  82.6 2.4 convolution_convert_fusion.14
  85.0 2.5 pad_maximum_fusion.ko.vo.refs_1_.refs_2_
  93.4 1.9 broadcast_select_fusion.1
  95.3 1.1 pad_maximum_fusion.2.kext_ref.refs_6_
  96.4 3.7 convolution_convert_fusion.16.q_ref.refs_0_
  100.1 115.2 %attend_gather.1 = (bf16[1024,1024]{1,0:T(8,128)(2,1)}, f32[2,8,1024]{2,1,0:T(8,128)}, bf16[4,2,2,2,32,2816]{5,4,3,2,1,0:T(8,128)(2,1)}, bf16[4,2,2,2,32,2816]{5...) custom-call(bf16[1024,1024]{1,0:T(8,128)(2,1)} %convolution_convert_, ...), custom_call_target="tpu_custom_call" | custom-call | flops 9663676416 | bytes 13631488 | tf_op jit(solution)/shard_map/attend_gather/pallas_call | solution.py:1097
  215.4 2.5 convolution_convert_fusion.18
  217.8 2.3 convolution_convert_fusion.17
  220.7 4.4 multiply_reduce_fusion.5
  226.4 6.7 convolution_convert_fusion.13.q_ref
  234.9 1.9 collective-permute-start.3
  236.8 1.1 collective-permute-start.4
  237.9 3.3 collective-permute-start.5
  241.2 19.6 %attend_cross.1 = (bf16[1024,1024]{1,0:T(8,128)(2,1)}, f32[2,8,1024]{2,1,0:T(8,128)}) custom-call(s32[12]{0:T(128)} %pad_add_fusion.1.meta_ref, bf16[1024,1024]{1,0:T(8,128)(2,1)} %convolution_convert_fusion.13.q_ref, bf16[256,2048]{1,0:T(8,128)(2,1)} %copy-done.21, bf16[256,2048]{1,0:T(8,128)(2,1)} %copy-done.21, ...), custom_call_target="tpu_custom_call" | custom-call | flops 2147483648 | bytes 6291456 | tf_op jit(solution)/shard_map/attend_cross/pallas_call | solution.py:746
  260.9 6.0 multiply_reduce_fusion.4
  266.9 2.0 copy-done.5
  269.4 8.8 %fusion.81 = f32[1024,2816]{1,0:T(8,128)} fusion(bf16[1024,1024]{1,0:T(8,128)(2,1)S(1)} %multiply_convert_fusion.2, bf16[1024,2816]{1,0:T(8,128)(2,1)S(1)} %bitcast.253), kind=kOutput, calls=%fused_computation.248 | convolution fusion | flops 5905580032 | bytes 19398656 | tf_op jit(solution)/shard_map/dot_general | solution.py:1507
  278.8 8.9 %fusion.80 = f32[1024,2816]{1,0:T(8,128)} fusion(bf16[1024,1024]{1,0:T(8,128)(2,1)S(1)} %bitcast.205, bf16[2816,1024]{1,0:T(8,128)(2,1)S(1)} %bitcast.262), kind=kOutput, calls=%fused_computation.247 | convolution fusion | flops 5905580032 | bytes 19398656 | tf_op jit(solution)/shard_map/dot_general | solution.py:398
  287.6 25.2 %multiply_convert_fusion = (bf16[1024,2816]{1,0:T(8,128)(2,1)}, bf16[1024,2816]{1,0:T(8,128)(2,1)}, bf16[1024,2816]{1,0:T(8,128)(2,1)}) fusion(f32[1024,2816]{1,0:T(8,128)} %fusion.81, f32[1024,2816]{1,0:T(8,128)} %fusion.80, bf16[1024,1024]{1,0:T(8,128)(2,1)} %copy-done.16, bf16[1024,2816]{1,0:T(8,128)(2,1)} %bitcast.257), kind=kOutput, calls=%fused_computation.9 | convolution fusion | flops 5980553216 | bytes 48234496 | tf_op jit(solution)/shard_map/dot_general | solution.py:1507
  312.8 10.6 %add_convert_fusion.1 = bf16[1024,1024]{1,0:T(8,128)(2,1)S(1)} fusion(f32[1024,1024]{1,0:T(8,128)} %copy-done.5, bf16[1024,2816]{1,0:T(8,128)(2,1)} %get-tuple-element.212, bf16[2816,1024]{1,0:T(8,128)(2,1)} %bitcast.259), kind=kOutput, calls=%fused_computation.41 | convolution fusion | flops 5907677184 | bytes 17825792 | tf_op jit(solution)/shard_map/dot_general | solution.py:1507
  323.4 8.1 %convolution_convert_fusion = bf16[2816,1024]{1,0:T(8,128)(2,1)} fusion(bf16[1024,2816]{1,0:T(8,128)(2,1)S(1)} %copy-done.63, bf16[1024,1024]{1,0:T(8,128)(2,1)S(1)} %bitcast.206), kind=kOutput, calls=%fused_computation.13 | convolution fusion | flops 5908463616 | bytes 13631488 | tf_op jit(solution)/shard_map/dot_general | solution.py:398
  331.6 10.0 %fusion.82 = f32[1024,1024]{1,0:T(8,128)} fusion(bf16[1024,2816]{1,0:T(8,128)(2,1)S(1)} %copy-done.61, bf16[1024,2816]{1,0:T(8,128)(2,1)} %bitcast.258), kind=kOutput, calls=%fused_computation.249 | convolution fusion | flops 5905580032 | bytes 15728640 | tf_op jit(solution)/shard_map/dot_general | solution.py:398
  341.5 8.3 %convolution_convert_fusion.1 = bf16[1024,2816]{1,0:T(8,128)(2,1)} fusion(bf16[1024,1024]{1,0:T(8,128)(2,1)S(1)} %copy-done.17, bf16[1024,2816]{1,0:T(8,128)(2,1)S(1)} %copy-done.61), kind=kOutput, calls=%fused_computation.14 | convolution fusion | flops 5908463616 | bytes 13631488 | tf_op jit(solution)/shard_map/dot_general | solution.py:398
  349.8 8.5 %convolution_convert_fusion.2 = bf16[1024,2816]{1,0:T(8,128)(2,1)} fusion(bf16[1024,1024]{1,0:T(8,128)(2,1)S(1)} %copy-done.17, bf16[1024,2816]{1,0:T(8,128)(2,1)S(1)} %bitcast.272), kind=kOutput, calls=%fused_computation.15 | convolution fusion | flops 5908463616 | bytes 13631488 | tf_op jit(solution)/shard_map/dot_general | solution.py:398
  358.3 9.5 %multiply_reduce_fusion = (f32[1024]{0:T(1024)}, f32[1024]{0:T(1024)S(1)}, f32[1024,1024]{1,0:T(8,128)S(1)}) fusion(f32[1024,1024]{1,0:T(8,128)S(1)} %copy-done.6, f32[1024]{0:T(1024)S(1)} %get-tuple-element.254, f32[1024]{0:T(1024)S(1)} %mul.346, f32[1024,1024]{1,0:T(8,128)S(1)} %copy-done.62, bf16[1024,2816]{1,0:T(8,128)(2,1)} %get-tuple-element.213, ...), kind=kOutput, calls=%fused_computation.36 | convolution fusion | flops 5912918016 | bytes 24133632 | tf_op jit(solution)/shard_map/dot_general | solution.py:398
  367.8 2.0 subtract_add_fusion.1
  369.8 3.7 convolution_convert_fusion.12.do_ref
  373.5 1.0 dynamic-slice_bitcast_fusion.2
  374.5 1.7 collective-permute-start.6
  376.2 2.1 collective-permute-start.7
  378.2 3.8 convolution_convert_fusion.8
  382.0 1.5 collective-permute-start.8
  383.5 2.0 collective-permute-start.9
  385.5 28.3 %attend_cross_back.1 = (bf16[1024,1024]{1,0:T(8,128)(2,1)}, bf16[2,256,1024]{2,1,0:T(8,128)(2,1)}, bf16[2,256,1024]{2,1,0:T(8,128)(2,1)}, f32[16,1,256]{2,1,0:T(1,128)}, f32[16,1,256]{2,1,0:T(1,128)}) custom-call(s32[12]{0:T(128)} %pad_add_fusion.1.meta_ref, bf16[1024,1024]{1,0:T(8,128)(2,1)} %convolution_convert_fusion.13.q_ref, ...), custom_call_target="tpu_custom_call" | custom-call | flops 5368709120 | bytes 15728640 | tf_op jit(solution)/shard_map/attend_cross_back/pallas_call | solution.py:799
  413.7 1.6 collective-permute-start.10
  415.8 1.5 maximum_bitcast_fusion
  417.7 1.4 copy-done.9
  419.8 3.2 multiply_reduce_fusion.1
  423.0 1.4 subtract_add_fusion
  424.6 3.7 convolution_convert_fusion.9.refs_8_
  428.3 3.9 convolution_convert_fusion.7
  434.2 1.5 fusion.21
  435.7 120.2 %attend_scatter.1 = (bf16[1024,1024]{1,0:T(8,128)(2,1)}, bf16[2,1024,1024]{2,1,0:T(8,128)(2,1)}, bf16[2,1024,1024]{2,1,0:T(8,128)(2,1)}, f32[16,1,256]{2,1,0:T(1...) custom-call(bf16[1024,1024]{1,0:T(8,128)(2,1)} %convolution_convert_, ...), custom_call_target="tpu_custom_call" | custom-call | flops 24159191040 | bytes 34078720 | tf_op jit(solution)/shard_map/attend_scatter/pallas_call | solution.py:1417
  558.2 6.7 convolution_convert_fusion.4
  565.9 1.1 bitcast_convert_fusion.1
  567.0 2.1 convolution_convert_fusion.10
  569.0 2.1 convolution_convert_fusion.11
  571.1 2.4 fusion.83
  573.5 4.4 add_convert_fusion
  578.0 2.4 fusion.19
  580.4 3.8 convolution_convert_fusion.5
  584.1 3.8 convolution_convert_fusion.6
  587.9 5.2 fusion.18
  593.3 5.5 fusion.17
  598.8 3.7 convolution_convert_fusion.3
  603.2 81.8 %scatter_grads.1 = (f32[32,1024]{1,0:T(8,128)}, f32[32,1024]{1,0:T(8,128)}, f32[32,1024]{1,0:T(8,128)}, f32[32,1024]{1,0:T(8,128)}, f32[32,1024]{1,0:T(8,128)}, ...) custom-call(bf16[4,2,2,2,32,1024]{5,4,3,2,1,0:T(8,128)(2,1)} %bitcast.203, ...), custom_call_target="tpu_custom_call" | custom-call | bytes 101711872 | tf_op jit(solution)/shard_map/scatter_grads/pallas_call | solution.py:1466
  685.1 1.4 slice_bitcast_fusion.14
  686.5 1.3 slice_bitcast_fusion.16
  687.8 4.2 bitcast_convert_fusion
  (265 shorter events, 29.8 us)
Async XLA Ops:
  75.3 7.4 %copy-start.35 = (f32[1024]{0:T(1024)}, f32[1024]{0:T(1024)S(1)}, u32[]{:S(2)}) copy-start(f32[1024]{0:T(1024)S(1)} %mul.332) | copy-start | bytes 12292
  75.3 5.0 copy-start.46
  80.2 16.2 %copy-start.13 = (bf16[4,256,1024]{2,1,0:T(8,128)(2,1)}, bf16[4,256,1024]{2,1,0:T(8,128)(2,1)S(1)}, u32[]{:S(2)}) copy-start(bf16[4,256,1024]{2,1,0:T(8,128)(2,1)S(1)} %fusion.9) | copy-start | bytes 6291460
  87.5 12.6 %collective-permute-start = (bf16[1024,2048]{1,0:T(8,128)(2,1)}, bf16[1024,2048]{1,0:T(8,128)(2,1)}, u32[]{:S(2)}, u32[]{:S(2)}) collective-permute-start(bf16[1024,2048]{1,0:T(8,128)(2,1)} %pad_maximum_fusion.ko.vo.refs_1_.refs_2_), channel_id=1, source_target_pairs={{0,4},{1,5},{2,6},{3,7},{4,0},{5,1},{6,2},{7,3},{8,12},{9,13},{10,... | collective-permute-start | bytes 12582920 | tf_op jit(solution)/shard_map/ppermute | solution.py:838
  88.4 11.7 %copy-start.54 = (s32[256]{0:T(256)}, s32[256]{0:T(256)S(1)}, u32[]{:S(2)}) copy-start(s32[256]{0:T(256)S(1)} %iota_select_fusion) | copy-start | bytes 3076
  90.1 136.2 %copy-start.37 = (f32[1024]{0:T(1024)}, f32[1024]{0:T(1024)S(1)}, u32[]{:S(2)}) copy-start(f32[1024]{0:T(1024)S(1)} %mul.338) | copy-start | bytes 12292
  90.4 6.1 copy-start.48
  100.1 115.3 %copy-start.18 = (bf16[4,64,1024]{2,1,0:T(8,128)(2,1)S(1)}, bf16[4,64,1024]{2,1,0:T(8,128)(2,1)}, u32[]{:S(2)}) copy-start(bf16[4,64,1024]{2,1,0:T(8,128)(2,1)} %get-tuple-element.90) | copy-start | bytes 1572868
  215.4 5.4 copy-start
  215.4 5.3 copy-start.50
  215.4 5.3 copy-start.58
  220.2 4.8 copy-start.21
  220.3 12.8 %collective-permute-start.1 = (bf16[256,2048]{1,0:T(8,128)(2,1)S(1)}, bf16[256,2048]{1,0:T(8,128)(2,1)}, u32[]{:S(2)}, u32[]{:S(2)}) collective-permute-start(bf16[256,2048]{1,0:T(8,128)(2,1)S(1)} %pad_maximum_fusion.3.ko.vo), channel_id=1, source_target_pairs={{0,4},{1,5},{2,6},{3,7},{4,0},{5,1},{6,2},{7,3},{8,12},{9,13},{10,... | collective-permute-start | bytes 3145736 | tf_op jit(solution)/shard_map/ppermute | solution.py:838
  220.7 4.4 copy-start.34
  226.3 6.7 copy-start.39
  226.4 6.7 copy-start.12
  233.4 44.8 %collective-permute-start.2 = (bf16[256,1024]{1,0:T(8,128)(2,1)S(1)}, bf16[256,1024]{1,0:T(8,128)(2,1)S(1)}, u32[]{:S(2)}, u32[]{:S(2)}) collective-permute-start(bf16[256,1024]{1,0:T(8,128)(2,1)S(1)} %get-tuple-element.233), channel_id=1, source_target_pairs={{0,0},{1,4},{2,1},{3,5},{4,2},{5,6},{6,3},{7,7},{8,8},{9,12},{10,9... | collective-permute-start | bytes 1572872 | tf_op jit(solution)/shard_map/ppermute | solution.py:1550
  234.9 43.2 %collective-permute-start.3 = (bf16[256,1024]{1,0:T(8,128)(2,1)}, bf16[256,1024]{1,0:T(8,128)(2,1)S(1)}, u32[]{:S(2)}, u32[]{:S(2)}) collective-permute-start(bf16[256,1024]{1,0:T(8,128)(2,1)} %get-tuple-element.231), channel_id=1, source_target_pairs={{0,4},{1,0},{2,5},{3,1},{4,6},{5,2},{6,7},{7,3},{8,12},{9,8},{10,1... | collective-permute-start | bytes 1572872 | tf_op jit(solution)/shard_map/ppermute | solution.py:1550
  236.8 41.4 %collective-permute-start.4 = (bf16[256,1024]{1,0:T(8,128)(2,1)S(1)}, bf16[256,1024]{1,0:T(8,128)(2,1)S(1)}, u32[]{:S(2)}, u32[]{:S(2)}) collective-permute-start(bf16[256,1024]{1,0:T(8,128)(2,1)S(1)} %get-tuple-element.234), channel_id=1, source_target_pairs={{0,1},{1,5},{2,0},{3,4},{4,3},{5,7},{6,2},{7,6},{8,9},{9,13},{10,8... | collective-permute-start | bytes 1572872 | tf_op jit(solution)/shard_map/ppermute | solution.py:1550
  237.9 40.3 %collective-permute-start.5 = (bf16[256,1024]{1,0:T(8,128)(2,1)S(1)}, bf16[256,1024]{1,0:T(8,128)(2,1)S(1)}, u32[]{:S(2)}, u32[]{:S(2)}) collective-permute-start(bf16[256,1024]{1,0:T(8,128)(2,1)S(1)} %get-tuple-element.232), channel_id=1, source_target_pairs={{0,5},{1,1},{2,4},{3,0},{4,7},{5,3},{6,6},{7,2},{8,13},{9,9},{10,1... | collective-permute-start | bytes 1572872 | tf_op jit(solution)/shard_map/ppermute | solution.py:1550
  260.9 8.4 %slice-start = ((s8[5767168]{0:T(1024)(128)(4,1)}), s8[4194304]{0:T(1024)(128)(4,1)S(1)}, s32[]{:S(2)}) async-start(s8[5767168]{0:T(1024)(128)(4,1)} %bitcast.251), calls=%async_computation | async-start | bytes 8388608
  260.9 8.5 %slice-start.1 = ((s8[5767168]{0:T(1024)(128)(4,1)}), s8[1572864]{0:T(1024)(128)(4,1)S(1)}, s32[]{:S(2)}) async-start(s8[5767168]{0:T(1024)(128)(4,1)} %bitcast.251), calls=%async_computation.1 | async-start | bytes 3145728
  269.3 8.9 %copy-start.16 = (bf16[1024,1024]{1,0:T(8,128)(2,1)}, bf16[1024,1024]{1,0:T(8,128)(2,1)S(1)}, u32[]{:S(2)}) copy-start(bf16[1024,1024]{1,0:T(8,128)(2,1)S(1)} %multiply_convert_fusion.2) | copy-start | bytes 6291460
  269.3 9.4 %slice-start.4 = ((s8[5767168]{0:T(1024)(128)(4,1)}), s8[4194304]{0:T(1024)(128)(4,1)S(1)}, s32[]{:S(2)}) async-start(s8[5767168]{0:T(1024)(128)(4,1)} %bitcast.260), calls=%async_computation.4 | async-start | bytes 8388608
  269.4 9.4 %slice-start.5 = ((s8[5767168]{0:T(1024)(128)(4,1)}), s8[1572864]{0:T(1024)(128)(4,1)S(1)}, s32[]{:S(2)}) async-start(s8[5767168]{0:T(1024)(128)(4,1)} %bitcast.260), calls=%async_computation.5 | async-start | bytes 3145728
  312.8 10.6 %copy-start.63 = (bf16[1024,2816]{1,0:T(8,128)(2,1)S(1)}, bf16[1024,2816]{1,0:T(8,128)(2,1)}, u32[]{:S(2)}) copy-start(bf16[1024,2816]{1,0:T(8,128)(2,1)} %get-tuple-element.212) | copy-start | bytes 17301508
  323.4 8.1 %copy-start.61 = (bf16[1024,2816]{1,0:T(8,128)(2,1)S(1)}, bf16[1024,2816]{1,0:T(8,128)(2,1)}, u32[]{:S(2)}) copy-start(bf16[1024,2816]{1,0:T(8,128)(2,1)} %get-tuple-element.214) | copy-start | bytes 17301508
  331.6 10.0 %copy-start.17 = (bf16[1024,1024]{1,0:T(8,128)(2,1)S(1)}, bf16[1024,1024]{1,0:T(8,128)(2,1)}, u32[]{:S(2)}) copy-start(bf16[1024,1024]{1,0:T(8,128)(2,1)} %copy-done.16) | copy-start | bytes 6291460
  331.6 18.3 %slice-start.6 = ((s8[5767168]{0:T(1024)(128)(4,1)}), s8[4194304]{0:T(1024)(128)(4,1)S(1)}, s32[]{:S(2)}) async-start(s8[5767168]{0:T(1024)(128)(4,1)} %bitcast.271), calls=%async_computation.6 | async-start | bytes 8388608
  341.5 8.3 %slice-start.7 = ((s8[5767168]{0:T(1024)(128)(4,1)}), s8[1572864]{0:T(1024)(128)(4,1)S(1)}, s32[]{:S(2)}) async-start(s8[5767168]{0:T(1024)(128)(4,1)} %bitcast.271), calls=%async_computation.7 | async-start | bytes 3145728
  341.5 16.8 %slice-start.2 = ((s8[5767168]{0:T(1024)(128)(4,1)}), s8[4194304]{0:T(1024)(128)(4,1)S(1)}, s32[]{:S(2)}) async-start(s8[5767168]{0:T(1024)(128)(4,1)} %bitcast.254), calls=%async_computation.2 | async-start | bytes 8388608
  349.8 8.5 %slice-start.3 = ((s8[5767168]{0:T(1024)(128)(4,1)}), s8[1572864]{0:T(1024)(128)(4,1)S(1)}, s32[]{:S(2)}) async-start(s8[5767168]{0:T(1024)(128)(4,1)} %bitcast.254), calls=%async_computation.3 | async-start | bytes 3145728
  349.8 8.5 %copy-start.6 = (f32[1024,1024]{1,0:T(8,128)S(1)}, f32[1024,1024]{1,0:T(8,128)}, u32[]{:S(2)}) copy-start(f32[1024,1024]{1,0:T(8,128)} %copy-done.5) | copy-start | bytes 12582916
  349.8 8.5 %copy-start.62 = (f32[1024,1024]{1,0:T(8,128)S(1)}, f32[1024,1024]{1,0:T(8,128)}, u32[]{:S(2)}) copy-start(f32[1024,1024]{1,0:T(8,128)} %fusion.82) | copy-start | bytes 12582916
  369.8 8.5 %copy-start.3 = (f32[1024,1024]{1,0:T(8,128)}, f32[1024,1024]{1,0:T(8,128)S(1)}, u32[]{:S(2)}) copy-start(f32[1024,1024]{1,0:T(8,128)S(1)} %subtract_add_fusion.1) | copy-start | bytes 12582916
  373.5 4.7 copy-start.56
  374.5 40.9 %collective-permute-start.6 = (bf16[256,1024]{1,0:T(8,128)(2,1)}, bf16[256,1024]{1,0:T(8,128)(2,1)S(1)}, u32[]{:S(2)}, u32[]{:S(2)}) collective-permute-start(bf16[256,1024]{1,0:T(8,128)(2,1)} %get-tuple-element.220), channel_id=1, source_target_pairs={{0,0},{4,1},{1,2},{5,3},{2,4},{6,5},{3,6},{7,7},{8,8},{12,9},{9,10... | collective-permute-start | bytes 1572872 | tf_op jit(solution)/shard_map/ppermute | solution.py:1565
  376.2 39.2 %collective-permute-start.7 = (bf16[256,1024]{1,0:T(8,128)(2,1)S(1)}, bf16[256,1024]{1,0:T(8,128)(2,1)S(1)}, u32[]{:S(2)}, u32[]{:S(2)}) collective-permute-start(bf16[256,1024]{1,0:T(8,128)(2,1)S(1)} %get-tuple-element.217), channel_id=1, source_target_pairs={{1,0},{5,1},{0,2},{4,3},{3,4},{7,5},{2,6},{6,7},{9,8},{13,9},{8,10... | collective-permute-start | bytes 1572872 | tf_op jit(solution)/shard_map/ppermute | solution.py:1565
  382.0 33.5 %collective-permute-start.8 = (bf16[256,1024]{1,0:T(8,128)(2,1)S(1)}, bf16[256,1024]{1,0:T(8,128)(2,1)S(1)}, u32[]{:S(2)}, u32[]{:S(2)}) collective-permute-start(bf16[256,1024]{1,0:T(8,128)(2,1)S(1)} %get-tuple-element.219), channel_id=1, source_target_pairs={{4,0},{0,1},{5,2},{1,3},{6,4},{2,5},{7,6},{3,7},{12,8},{8,9},{13,1... | collective-permute-start | bytes 1572872 | tf_op jit(solution)/shard_map/ppermute | solution.py:1565
  383.5 32.0 %collective-permute-start.9 = (bf16[256,1024]{1,0:T(8,128)(2,1)S(1)}, bf16[256,1024]{1,0:T(8,128)(2,1)S(1)}, u32[]{:S(2)}, u32[]{:S(2)}) collective-permute-start(bf16[256,1024]{1,0:T(8,128)(2,1)S(1)} %get-tuple-element.218), channel_id=1, source_target_pairs={{5,0},{1,1},{4,2},{0,3},{7,4},{3,5},{6,6},{2,7},{13,8},{9,9},{12,1... | collective-permute-start | bytes 1572872 | tf_op jit(solution)/shard_map/ppermute | solution.py:1565
  413.7 18.5 %collective-permute-start.10 = (bf16[2,256,1024]{2,1,0:T(8,128)(2,1)}, bf16[2,256,1024]{2,1,0:T(8,128)(2,1)S(1)}, u32[]{:S(2)}, u32[]{:S(2)}) collective-permute-start(bf16[2,256,1024]{2,1,0:T(8,128)(2,1)} %get-tuple-element.104), channel_id=1, source_target_pairs={{0,4},{1,5},{2,6},{3,7},{4,0},{5,1},{6,2},{7,3},{8,12},{9,13},{10,... | collective-permute-start | bytes 3145736 | tf_op jit(solution)/shard_map/ppermute | solution.py:838
  428.3 4.3 copy-start.11
  555.9 17.6 %collective-permute-start.11 = (bf16[2,1024,1024]{2,1,0:T(8,128)(2,1)}, bf16[2,1024,1024]{2,1,0:T(8,128)(2,1)}, u32[]{:S(2)}, u32[]{:S(2)}) collective-permute-start(bf16[2,1024,1024]{2,1,0:T(8,128)(2,1)} %get-tuple-element.108), channel_id=1, source_target_pairs={{0,4},{1,5},{2,6},{3,7},{4,0},{5,1},{6,2},{7,3},{8,12},{9,13},{10,... | collective-permute-start | bytes 12582920 | tf_op jit(solution)/shard_map/ppermute | solution.py:838
  558.2 6.7 copy-start.42
  558.2 6.7 copy-start.43
  558.2 7.0 copy-start.55
  558.2 7.7 %copy-start.22 = (bf16[2,128,1024]{2,1,0:T(8,128)(2,1)S(1)}, bf16[2,128,1024]{2,1,0:T(8,128)(2,1)}, u32[]{:S(2)}) copy-start(bf16[2,128,1024]{2,1,0:T(8,128)(2,1)} %get-tuple-element.113) | copy-start | bytes 1572868
  558.2 8.8 %copy-start.8 = (bf16[2,256,1024]{2,1,0:T(8,128)(2,1)S(1)}, bf16[2,256,1024]{2,1,0:T(8,128)(2,1)}, u32[]{:S(2)}) copy-start(bf16[2,256,1024]{2,1,0:T(8,128)(2,1)} %copy-done.7) | copy-start | bytes 3145732
  558.2 8.8 %copy-start.19 = (bf16[4,64,1024]{2,1,0:T(8,128)(2,1)S(1)}, bf16[4,64,1024]{2,1,0:T(8,128)(2,1)}, u32[]{:S(2)}) copy-start(bf16[4,64,1024]{2,1,0:T(8,128)(2,1)} %get-tuple-element.90) | copy-start | bytes 1572868
  565.9 5.2 copy-start.49
  565.9 5.2 copy-start.59
  573.5 4.5 copy-start.47
  593.3 5.5 copy-start.60
  685.0 6.9 copy-start.33
  685.0 7.6 %copy-start.32 = (f32[32,1024]{1,0:T(8,128)S(1)}, f32[32,1024]{1,0:T(8,128)}, u32[]{:S(2)}) copy-start(f32[32,1024]{1,0:T(8,128)} %get-tuple-element.305) | copy-start | bytes 393220
  685.1 8.2 %copy-start.31 = (f32[32,1024]{1,0:T(8,128)S(1)}, f32[32,1024]{1,0:T(8,128)}, u32[]{:S(2)}) copy-start(f32[32,1024]{1,0:T(8,128)} %get-tuple-element.306) | copy-start | bytes 393220
  685.1 8.8 %copy-start.30 = (f32[32,1024]{1,0:T(8,128)S(1)}, f32[32,1024]{1,0:T(8,128)}, u32[]{:S(2)}) copy-start(f32[32,1024]{1,0:T(8,128)} %get-tuple-element.307) | copy-start | bytes 393220
  685.1 9.5 %copy-start.27 = (f32[32,1024]{1,0:T(8,128)S(1)}, f32[32,1024]{1,0:T(8,128)}, u32[]{:S(2)}) copy-start(f32[32,1024]{1,0:T(8,128)} %get-tuple-element.310) | copy-start | bytes 393220
  685.1 10.1 %copy-start.29 = (f32[32,1024]{1,0:T(8,128)S(1)}, f32[32,1024]{1,0:T(8,128)}, u32[]{:S(2)}) copy-start(f32[32,1024]{1,0:T(8,128)} %get-tuple-element.311) | copy-start | bytes 393220
  685.1 10.8 %copy-start.28 = (f32[32,1024]{1,0:T(8,128)S(1)}, f32[32,1024]{1,0:T(8,128)}, u32[]{:S(2)}) copy-start(f32[32,1024]{1,0:T(8,128)} %get-tuple-element.312) | copy-start | bytes 393220
  685.1 11.4 %copy-start.26 = (f32[32,1024]{1,0:T(8,128)S(1)}, f32[32,1024]{1,0:T(8,128)}, u32[]{:S(2)}) copy-start(f32[32,1024]{1,0:T(8,128)} %get-tuple-element.313) | copy-start | bytes 393220
  687.8 9.4 %copy-start.25 = (f32[32,2816]{1,0:T(8,128)S(1)}, f32[32,2816]{1,0:T(8,128)}, u32[]{:S(2)}) copy-start(f32[32,2816]{1,0:T(8,128)} %get-tuple-element.315) | copy-start | bytes 1081348
  687.8 10.2 %copy-start.24 = (f32[32,2816]{1,0:T(8,128)S(1)}, f32[32,2816]{1,0:T(8,128)}, u32[]{:S(2)}) copy-start(f32[32,2816]{1,0:T(8,128)} %get-tuple-element.316) | copy-start | bytes 1081348
  687.8 10.9 %copy-start.23 = (f32[88,1024]{1,0:T(8,128)S(1)}, f32[88,1024]{1,0:T(8,128)}, u32[]{:S(2)}) copy-start(f32[88,1024]{1,0:T(8,128)} %get-tuple-element.317) | copy-start | bytes 1081348
  (20 other events, 58.1 us)
